TPU v7x, 32 devices: a whole 2x2x4 slice. The times are simulated.
32 devices in a mesh: dp: 8 (over y, x, core), tensor: 4 (over z).
Axes of the slice: x: 2, y: 2, z: 4, core: 2. Of those that a mesh axis runs over, the one named last changes fastest.
Arguments:
- tokens: bfloat16 [32768, 1024], P(('dp', 'tensor')), may hold values from -6 to 6
- first_values: bfloat16 [32768, 1024], P('dp', 'tensor'), may hold values from -6 to 6
- doc_lengths: int32 [16, 8], P('dp'), may hold values from 1 to 1024, 2048 in all within a row
- cotangent: bfloat16 [32768, 1024], P(('dp', 'tensor')), may hold values from -6 to 6
- w_query: bfloat16 [1024, 1024], P('dp', 'tensor'), may hold values from -0.1875 to 0.1875
- w_key: bfloat16 [1024, 1024], P('dp', 'tensor'), may hold values from -0.1875 to 0.1875
- w_value: bfloat16 [1024, 1024], P('dp', 'tensor'), may hold values from -0.1875 to 0.1875
- w_out: bfloat16 [1024, 1024], P('tensor', 'dp'), may hold values from -1 to 1
- w_gate: bfloat16 [1024, 2816], P('dp', 'tensor'), may hold values from -0.1875 to 0.1875
- w_up: bfloat16 [1024, 2816], P('dp', 'tensor'), may hold values from -0.1875 to 0.1875
- w_down: bfloat16 [2816, 1024], P('tensor', 'dp'), may hold values from -0.109375 to 0.109375
- gain_attn: float32 [1024], replicated, may hold values from 0.1 to 1.9
- gain_mlp: float32 [1024], replicated, may hold values from 0.1 to 1.9
Outputs:
- layer_out: bfloat16 [32768, 1024], P(('dp', 'tensor'))
- grad_tokens: float32 [32768, 1024], P(('dp', 'tensor'))
- grad_first_values: float32 [32768, 1024], P('dp', 'tensor')
- grad_w_query: float32 [1024, 1024], P('dp', 'tensor')
- grad_w_key: float32 [1024, 1024], P('dp', 'tensor')
- grad_w_value: float32 [1024, 1024], P('dp', 'tensor')
- grad_w_out: float32 [1024, 1024], P('tensor', 'dp')
- grad_w_gate: float32 [1024, 2816], P('dp', 'tensor')
- grad_w_up: float32 [1024, 2816], P('dp', 'tensor')
- grad_w_down: float32 [2816, 1024], P('tensor', 'dp')
- grad_gain_attn: float32 [1024], replicated
- grad_gain_mlp: float32 [1024], replicated
Inputs may be any that keep to these rules, and one draw needn't show every extreme that they name: `doc_lengths`: each row's 8 lengths sum to 2048, and the largest in each row is 1024.
All inputs are finite; a program needn't handle non-finite values.
Results may differ from a plain program's by a relative error of at most 0.013.
Values may be sent and summed in bfloat16 or wider, within the bound.
A program may use at most 256 MiB of HBM per device.

v0:
```python
import jax
import jax.numpy as jnp
from jax import lax
from jax.sharding import PartitionSpec as P

HEAD = 64
SEQ = 2048
DOCS = 8


EPSILON = 1e-05


def rms_norm(values, gain):
    factor = lax.rsqrt(jnp.mean(values * values, axis=1, keepdims=True) + EPSILON)
    return values * factor * gain


def documents(doc_lengths):
    ends = jnp.cumsum(doc_lengths, axis=1)
    starts = ends - doc_lengths
    places = jnp.arange(SEQ, dtype=jnp.int32)
    segment = jnp.sum((places[None, :, None] >= ends[:, None, :]).astype(jnp.int32), axis=2)
    member = segment[:, :, None] == jnp.arange(DOCS, dtype=jnp.int32)[None, None, :]
    offset = jnp.sum(jnp.where(member, starts[:, None, :], 0), axis=2)
    return (segment, (places[None, :] - offset).astype(jnp.float32))


def rotation(positions):
    half = HEAD // 2
    freqs = 10000.0 ** (-(jnp.arange(half, dtype=jnp.float32) * 2.0 / HEAD))
    angles = positions[:, None] * freqs[None, :]
    return (jnp.cos(angles), jnp.sin(angles))


def rotate(values, cosine, sine):
    shaped = values.reshape(values.shape[0], -1, HEAD)
    half = HEAD // 2
    first = shaped[:, :, :half]
    second = shaped[:, :, half:]
    cos_rows = cosine[:, None, :]
    sin_rows = sine[:, None, :]
    turned = jnp.concatenate(
        [first * cos_rows - second * sin_rows, second * cos_rows + first * sin_rows], axis=2
    )
    return turned.reshape(values.shape)


def rotate_back(grads, cosine, sine):
    shaped = grads.reshape(grads.shape[0], -1, HEAD)
    half = HEAD // 2
    first = shaped[:, :, :half]
    second = shaped[:, :, half:]
    cos_rows = cosine[:, None, :]
    sin_rows = sine[:, None, :]
    turned = jnp.concatenate(
        [first * cos_rows + second * sin_rows, second * cos_rows - first * sin_rows], axis=2
    )
    return turned.reshape(grads.shape)


def swiglu(gate, up_val):
    return jax.nn.silu(gate) * up_val


def product(left, right):
    return jnp.dot(left, right, preferred_element_type=jnp.float32)


def inner(left, right):
    return lax.dot_general(
        left, right, (((0,), (0,)), ((), ())), preferred_element_type=jnp.float32
    )


def outer(left, right):
    return lax.dot_general(
        left, right, (((1,), (1,)), ((), ())), preferred_element_type=jnp.float32
    )


def block_scores(queries, keys_all, segment, start, width):
    query_block = lax.dynamic_slice_in_dim(queries, start, width, 0)
    query_seg = lax.dynamic_slice_in_dim(segment, start, width, 0)
    scores = (
        jnp.einsum("qhd,khd->hqk", query_block, keys_all, preferred_element_type=jnp.float32)
        * 0.125
    )
    places = jnp.arange(SEQ, dtype=jnp.int32)
    rows_at = start + jnp.arange(width, dtype=jnp.int32)
    allowed = (query_seg[:, None] == segment[None, :]) & (places[None, :] <= rows_at[:, None])
    return (query_block, jnp.where(allowed[None], scores, -1e30))


def forward_row(pieces):
    queries, keys_all, values_all, segment = pieces
    width = min(512, SEQ)
    count = SEQ // width

    def forward_one_block(index):
        unused, scores = block_scores(queries, keys_all, segment, index * width, width)
        top = jnp.max(scores, axis=2, keepdims=True)
        expo = jnp.exp(scores - top)
        total = jnp.sum(expo, axis=2, keepdims=True)
        weights = (expo / total).astype(jnp.bfloat16)
        result = jnp.einsum("hqk,khd->qhd", weights, values_all, preferred_element_type=jnp.float32)
        return (result, (top + jnp.log(total))[:, :, 0])

    results, logsums = lax.map(forward_one_block, jnp.arange(count, dtype=jnp.int32))
    return (results.reshape(SEQ, queries.shape[1], HEAD), logsums)


def backward_row(pieces):
    queries, keys_all, values_all, segment, grad_rows, logsums = pieces
    width = min(512, SEQ)
    count = SEQ // width

    def backward_one_block(carry, extra):
        index, logsum = extra
        start = index * width
        query_block, scores = block_scores(queries, keys_all, segment, start, width)
        probs = jnp.exp(scores - logsum[:, :, None])
        grad_block = lax.dynamic_slice_in_dim(grad_rows, start, width, 0)
        grad_probs = jnp.einsum(
            "qhd,khd->hqk", grad_block, values_all, preferred_element_type=jnp.float32
        )
        delta = jnp.sum(probs * grad_probs, axis=2, keepdims=True)
        grad_scores = (probs * (grad_probs - delta)).astype(jnp.bfloat16)
        grad_query = (
            jnp.einsum("hqk,khd->qhd", grad_scores, keys_all, preferred_element_type=jnp.float32)
            * 0.125
        )
        grad_keys = (
            carry[0]
            + jnp.einsum(
                "hqk,qhd->khd", grad_scores, query_block, preferred_element_type=jnp.float32
            )
            * 0.125
        )
        grad_values = carry[1] + jnp.einsum(
            "hqk,qhd->khd",
            probs.astype(jnp.bfloat16),
            grad_block,
            preferred_element_type=jnp.float32,
        )
        return ((grad_keys, grad_values), grad_query)

    zeros = jnp.zeros(keys_all.shape, jnp.float32)
    sums, grad_queries = lax.scan(
        backward_one_block, (zeros, zeros), (jnp.arange(count, dtype=jnp.int32), logsums)
    )
    return (grad_queries.reshape(SEQ, queries.shape[1], HEAD), sums[0], sums[1])


def body(
    tokens,
    first_values,
    doc_lengths,
    cotangent,
    w_query,
    w_key,
    w_value,
    w_out,
    w_gate,
    w_up,
    w_down,
    gain_attn,
    gain_mlp,
):
    query_mat, key_mat, value_mat, out_mat, gate_mat, up_mat, down_mat = (
        lax.all_gather(w_query, "dp", axis=0, tiled=True),
        lax.all_gather(w_key, "dp", axis=0, tiled=True),
        lax.all_gather(w_value, "dp", axis=0, tiled=True),
        lax.all_gather(w_out, "dp", axis=1, tiled=True),
        lax.all_gather(w_gate, "dp", axis=0, tiled=True),
        lax.all_gather(w_up, "dp", axis=0, tiled=True),
        lax.all_gather(w_down, "dp", axis=1, tiled=True),
    )
    local_heads = query_mat.shape[1] // HEAD
    row_count = doc_lengths.shape[0]
    group = row_count * SEQ
    segment, positions = documents(doc_lengths)
    cosine, sine = rotation(positions.reshape(-1))

    def heads(matrix):
        return matrix.reshape(row_count, SEQ, local_heads, HEAD)

    inputs = tokens.astype(jnp.float32)
    normed_one, norm_one_back = jax.vjp(rms_norm, inputs, gain_attn)
    gathered_one = lax.all_gather(normed_one.astype(jnp.bfloat16), "tensor", axis=0, tiled=True)
    query_raw = product(gathered_one, query_mat)
    key_raw = product(gathered_one, key_mat)
    value_raw = product(gathered_one, value_mat)
    queries = rotate(query_raw, cosine, sine).astype(jnp.bfloat16)
    keys_low = rotate(key_raw, cosine, sine).astype(jnp.bfloat16)
    mixed_values = (0.5 * value_raw + 0.5 * first_values.astype(jnp.float32)).astype(jnp.bfloat16)
    attended, logsums = lax.map(
        forward_row, (heads(queries), heads(keys_low), heads(mixed_values), segment)
    )
    attended_low = attended.reshape(group, -1).astype(jnp.bfloat16)
    hidden_in = inputs + lax.psum_scatter(
        product(attended_low, out_mat), "tensor", scatter_dimension=0, tiled=True
    )
    normed_two, norm_two_back = jax.vjp(rms_norm, hidden_in, gain_mlp)
    normed_low_two = normed_two.astype(jnp.bfloat16)
    grad_out = cotangent.astype(jnp.float32)
    gathered_two = lax.all_gather(normed_low_two, "tensor", axis=0, tiled=True)
    activated, swiglu_back = jax.vjp(
        swiglu, product(gathered_two, gate_mat), product(gathered_two, up_mat)
    )
    act_low = activated.astype(jnp.bfloat16)
    layer_out = hidden_in + lax.psum_scatter(
        product(act_low, down_mat).astype(jnp.bfloat16), "tensor", scatter_dimension=0, tiled=True
    ).astype(jnp.float32)
    grad_rows = lax.all_gather(cotangent, "tensor", axis=0, tiled=True)
    grad_gate, grad_up = swiglu_back(outer(grad_rows, down_mat))
    gate_low = grad_gate.astype(jnp.bfloat16)
    up_low = grad_up.astype(jnp.bfloat16)
    grad_normed_two = lax.psum_scatter(
        outer(gate_low, gate_mat) + outer(up_low, up_mat), "tensor", scatter_dimension=0, tiled=True
    )
    grad_gate_mat = inner(gathered_two, gate_low)
    grad_up_mat = inner(gathered_two, up_low)
    grad_down_mat = inner(act_low, grad_rows)
    grad_hidden_two, grad_gain_two = norm_two_back(grad_normed_two)
    grad_hidden = grad_out + grad_hidden_two
    grad_branch = lax.all_gather(grad_hidden.astype(jnp.bfloat16), "tensor", axis=0, tiled=True)
    grad_attended = outer(grad_branch, out_mat).astype(jnp.bfloat16)
    grad_out_mat = inner(attended_low, grad_branch)
    grad_rot_query, grad_rot_key, grad_mixed = lax.map(
        backward_row,
        (
            heads(queries),
            heads(keys_low),
            heads(mixed_values),
            segment,
            heads(grad_attended),
            logsums,
        ),
    )
    grad_query_low = rotate_back(grad_rot_query.reshape(group, -1), cosine, sine).astype(
        jnp.bfloat16
    )
    grad_key_low = rotate_back(grad_rot_key.reshape(group, -1), cosine, sine).astype(jnp.bfloat16)
    grad_first = 0.5 * grad_mixed.reshape(group, -1)
    grad_value_low = grad_first.astype(jnp.bfloat16)
    grad_normed_one = lax.psum_scatter(
        outer(grad_query_low, query_mat)
        + outer(grad_key_low, key_mat)
        + outer(grad_value_low, value_mat),
        "tensor",
        scatter_dimension=0,
        tiled=True,
    )
    grad_query_mat = inner(gathered_one, grad_query_low)
    grad_key_mat = inner(gathered_one, grad_key_low)
    grad_value_mat = inner(gathered_one, grad_value_low)
    grad_inputs_one, grad_gain_one = norm_one_back(grad_normed_one)
    grad_tokens = grad_hidden + grad_inputs_one
    summed = (
        lax.psum_scatter(grad_query_mat, "dp", scatter_dimension=0, tiled=True),
        lax.psum_scatter(grad_key_mat, "dp", scatter_dimension=0, tiled=True),
        lax.psum_scatter(grad_value_mat, "dp", scatter_dimension=0, tiled=True),
        lax.psum_scatter(grad_out_mat, "dp", scatter_dimension=1, tiled=True),
        lax.psum_scatter(grad_gate_mat, "dp", scatter_dimension=0, tiled=True),
        lax.psum_scatter(grad_up_mat, "dp", scatter_dimension=0, tiled=True),
        lax.psum_scatter(grad_down_mat, "dp", scatter_dimension=1, tiled=True),
    )
    gain_sums = lax.psum((grad_gain_one, grad_gain_two), ("dp", "tensor"))
    return (
        layer_out.astype(jnp.bfloat16),
        grad_tokens,
        grad_first,
        summed[0],
        summed[1],
        summed[2],
        summed[3],
        summed[4],
        summed[5],
        summed[6],
        gain_sums[0],
        gain_sums[1],
    )


def solution(mesh):
    placed = (
        P(("dp", "tensor"), None),
        P("dp", "tensor"),
        P("dp", None),
        P(("dp", "tensor"), None),
        P("dp", "tensor"),
        P("dp", "tensor"),
        P("dp", "tensor"),
        P("tensor", "dp"),
        P("dp", "tensor"),
        P("dp", "tensor"),
        P("tensor", "dp"),
        P(),
        P(),
    )
    return jax.shard_map(
        body,
        mesh=mesh,
        in_specs=placed,
        out_specs=(
            P(("dp", "tensor"), None),
            P(("dp", "tensor"), None),
            P("dp", "tensor"),
            P("dp", "tensor"),
            P("dp", "tensor"),
            P("dp", "tensor"),
            P("tensor", "dp"),
            P("dp", "tensor"),
            P("dp", "tensor"),
            P("tensor", "dp"),
            P(),
            P(),
        ),
        check_vma=False,
    )
```

profile of v0, /device:TPU:11, one launch (start us, length us, event | category | flops | bytes accessed | tf_op | source)
XLA Modules:
  0.0 2841.7 jit_solution(16840043710271536460)
XLA Ops:
  59.4 103.7 %all-gather.8.cloned.1.call-done = bf16[4096,1024]{1,0:T(8,128)(2,1)} async-done(((bf16[1024,1024]{1,0:T(8,128)(2,1)}), bf16[4096,1024]{1,0:T(8,128)(2,1)}) %all-gather.8.cloned.1.call-update) | async-done | bytes 8388624 | tf_op jit(solution)/shard_map/all_gather | solution.py:190
  201.0 142.8 %while.60 = (s32[]{:T(128)}, bf16[2,2048,4,64]{3,2,1,0:T(4,128)(2,1)}, f32[2,4,4,512]{3,2,1,0:T(4,128)}, bf16[2,2048,4,64]{1,3,2,0:T(8,128)(2,1)}, s32[2,2048]{1...) while((s32[]{:T(128)}, ...), condition=%wide.region_9.10_spmd.clone, body=%wide.region_4.9_spmd.sunk.clone | while | flops 1127217664 | bytes 78154360 | solution.py:197
  204.4 63.5 %while.59 = (s32[]{:T(128)}, bf16[4,512,4,64]{1,3,2,0:T(8,128)(2,1)}, f32[4,4,512]{2,1,0:T(4,128)S(1)}, s32[4]{0:T(128)S(1)}, s32[2048]{0:T(1024)S(1)}, /*index=...) while((s32[]{:T(128)}, ...), condition=%wide.region_8.8_spmd, body=%wide.region_5.7_spmd.sunk | while | flops 1127217664 | bytes 65882372 | solution.py:109
  275.6 63.5 %while.59 = (s32[]{:T(128)}, bf16[4,512,4,64]{1,3,2,0:T(8,128)(2,1)}, f32[4,4,512]{2,1,0:T(4,128)S(1)}, s32[4]{0:T(128)S(1)}, s32[2048]{0:T(1024)S(1)}, /*index=...) while((s32[]{:T(128)}, ...), condition=%wide.region_8.8_spmd, body=%wide.region_5.7_spmd.sunk | while | flops 1127217664 | bytes 65882372 | solution.py:109
  358.7 277.8 %reduce-scatter.12.cloned.1.call-done = f32[1024,1024]{1,0:T(8,128)} async-done(((f32[4096,1024]{1,0:T(8,128)}), f32[1024,1024]{1,0:T(8,128)}) %reduce-scatter.12.cloned.1.call-update) | async-done | bytes 4194320 | tf_op jit(solution)/shard_map/reduce_scatter | solution.py:201
  645.3 148.3 %all-gather.10.cloned.1.call-done = bf16[4096,1024]{1,0:T(8,128)(2,1)} async-done(((bf16[1024,1024]{1,0:T(8,128)(2,1)}), bf16[4096,1024]{1,0:T(8,128)(2,1)}) %all-gather.10.cloned.1.call-update) | async-done | bytes 8388624 | tf_op jit(solution)/shard_map/all_gather | solution.py:207
  849.3 147.9 %all-gather.18.cloned.1.call-done = bf16[4096,1024]{1,0:T(8,128)(2,1)} async-done(((bf16[1024,1024]{1,0:T(8,128)(2,1)}), bf16[4096,1024]{1,0:T(8,128)(2,1)}) %all-gather.18.cloned.1.call-update) | async-done | bytes 8388624 | tf_op jit(solution)/shard_map/all_gather | solution.py:215
  1047.1 278.3 %reduce-scatter.16.cloned.1.call-done = f32[1024,1024]{1,0:T(8,128)} async-done(((f32[4096,1024]{1,0:T(8,128)}), f32[1024,1024]{1,0:T(8,128)}) %reduce-scatter.16.cloned.1.call-update) | async-done | bytes 4194320 | tf_op jit(solution)/shard_map/reduce_scatter | solution.py:219
  1333.8 150.8 %all-gather.20.cloned.1.call-done = bf16[4096,1024]{1,0:T(8,128)(2,1)} async-done(((bf16[1024,1024]{1,0:T(8,128)(2,1)}), bf16[4096,1024]{1,0:T(8,128)(2,1)}) %all-gather.20.cloned.1.call-update) | async-done | bytes 8388624 | tf_op jit(solution)/shard_map/all_gather | solution.py:227
  1499.2 508.5 %while.62 = (s32[]{:T(128)}, f32[2,2048,4,64]{3,2,1,0:T(4,128)}, f32[2,2048,4,64]{1,0,3,2:T(2,128)}, f32[2,2048,4,64]{1,3,2,0:T(8,128)}, f32[2,4,4,512]{3,2,1,0:...) while((s32[]{:T(128)}, f32[2,2048,4,64]{3,2,1,0:T(4,128)}, ...), condition=%wide.region_19.20_spmd.clone, body=%wide.region_15.19_spmd.sunk.clone | while | flops 2753165824 | bytes 265382816 | solution.py:230
  1506.2 193.8 %while.61 = (s32[]{:T(128)}, f32[2048,4,64]{0,2,1:T(8,128)}, f32[2048,4,64]{0,2,1:T(8,128)}, f32[4,512,4,64]{1,3,2,0:T(8,128)}, s32[4]{0:T(128)S(1)}, /*index=5*...) while((s32[]{:T(128)}, f32[2048,4,64]{0,2,1:T(8,128)}, ...), condition=%wide.region_18.18_spmd.clone, body=%wide.region_16.17_spmd.clone.sunk | while | flops 2753165824 | bytes 181283248 | solution.py:149
  1703.8 35.8 %dynamic_update_slice.56 = f32[2,2048,4,64]{1,0,3,2:T(2,128)} dynamic-update-slice(f32[2,2048,4,64]{1,0,3,2:T(2,128)} %get-tuple-element.932, f32[1,2048,4,64]{1,0,3,2:T(1,128)S(1)} %copy.103, s32[]{:T(128)S(6)} %copy.146, s32[]{:T(128)} %constant.105.clone.1..sunk.6, s32[]{:T(128)} %constant.105.clone.1..sunk.6, s32[]{:T(128)} %constant.105.clone.1..sunk.6) | dynamic-update-slice | bytes 4194308 | tf_op jit(solution)/shard_map/while/body/jit(dynamic_update_index_in_dim)/dynamic_update_slice | solution.py:197
  1760.2 193.8 %while.61 = (s32[]{:T(128)}, f32[2048,4,64]{0,2,1:T(8,128)}, f32[2048,4,64]{0,2,1:T(8,128)}, f32[4,512,4,64]{1,3,2,0:T(8,128)}, s32[4]{0:T(128)S(1)}, /*index=5*...) while((s32[]{:T(128)}, f32[2048,4,64]{0,2,1:T(8,128)}, ...), condition=%wide.region_18.18_spmd.clone, body=%wide.region_16.17_spmd.clone.sunk | while | flops 2753165824 | bytes 181283248 | solution.py:149
  1957.8 35.8 %dynamic_update_slice.56 = f32[2,2048,4,64]{1,0,3,2:T(2,128)} dynamic-update-slice(f32[2,2048,4,64]{1,0,3,2:T(2,128)} %get-tuple-element.932, f32[1,2048,4,64]{1,0,3,2:T(1,128)S(1)} %copy.103, s32[]{:T(128)S(6)} %copy.146, s32[]{:T(128)} %constant.105.clone.1..sunk.6, s32[]{:T(128)} %constant.105.clone.1..sunk.6, s32[]{:T(128)} %constant.105.clone.1..sunk.6) | dynamic-update-slice | bytes 4194308 | tf_op jit(solution)/shard_map/while/body/jit(dynamic_update_index_in_dim)/dynamic_update_slice | solution.py:197
  2182.4 193.2 %reduce-scatter.18.cloned.1.call-done = f32[1024,1024]{1,0:T(8,128)} async-done(((f32[4096,1024]{1,0:T(8,128)}), f32[1024,1024]{1,0:T(8,128)}) %reduce-scatter.18.cloned.1.call-update) | async-done | bytes 4194320 | tf_op jit(solution)/shard_map/reduce_scatter | solution.py:247
  2379.2 46.9 %all-reduce = (f32[1024]{0:T(1024)}, f32[1024]{0:T(1024)}) all-reduce(f32[1024]{0:T(1024)S(1)} %get-tuple-element.324, f32[1024]{0:T(1024)S(1)} %copy-done.55), channel_id=1, replica_groups=mesh['dp'=8,'tensor'=4] {'dp','tensor'}, use_global_device_ids=true, to_apply=%region_30.31 | all-reduce | flops 2048 | bytes 16384 | tf_op jit(solution)/shard_map/psum | solution.py:269
  2426.1 100.8 %reduce-scatter.14.cloned.1.call-done = bf16[1024,1024]{1,0:T(8,128)(2,1)} async-done(((bf16[4096,1024]{1,0:T(8,128)(2,1)}), bf16[1024,1024]{1,0:T(8,128)(2,1)}) %reduce-scatter.14.cloned.1.call-update) | async-done | bytes 2097168 | tf_op jit(solution)/shard_map/reduce_scatter | solution.py:212
  2535.9 41.0 %reduce-scatter.32.cloned.1.call-done = f32[704,128]{1,0:T(8,128)} async-done(((f32[704,1024]{1,0:T(8,128)}), f32[704,128]{1,0:T(8,128)}) %reduce-scatter.32.cloned.1.call-update) | async-done | bytes 360464 | tf_op jit(solution)/shard_map/reduce_scatter | solution.py:267
  2576.9 48.9 %reduce-scatter.28.cloned.1.call-done = f32[128,704]{0,1:T(8,128)} async-done(((f32[1024,704]{0,1:T(8,128)}), f32[128,704]{0,1:T(8,128)}) %reduce-scatter.28.cloned.1.call-update) | async-done | bytes 360464 | tf_op jit(solution)/shard_map/reduce_scatter | solution.py:265
  2625.8 49.3 %reduce-scatter.30.cloned.1.call-done = f32[128,704]{0,1:T(8,128)} async-done(((f32[1024,704]{0,1:T(8,128)}), f32[128,704]{0,1:T(8,128)}) %reduce-scatter.30.cloned.1.call-update) | async-done | bytes 360464 | tf_op jit(solution)/shard_map/reduce_scatter | solution.py:266
  2675.0 39.7 %reduce-scatter.26.cloned.1.call-done = f32[256,128]{1,0:T(8,128)} async-done(((f32[256,1024]{1,0:T(8,128)}), f32[256,128]{1,0:T(8,128)}) %reduce-scatter.26.cloned.1.call-update) | async-done | bytes 131088 | tf_op jit(solution)/shard_map/reduce_scatter | solution.py:264
  2714.7 39.7 %reduce-scatter.24.cloned.1.call-done = f32[128,256]{1,0:T(8,128)} async-done(((f32[1024,256]{1,0:T(8,128)}), f32[128,256]{1,0:T(8,128)}) %reduce-scatter.24.cloned.1.call-update) | async-done | bytes 131088 | tf_op jit(solution)/shard_map/reduce_scatter | solution.py:263
  2754.4 39.8 %reduce-scatter.22.cloned.1.call-done = f32[128,256]{1,0:T(8,128)} async-done(((f32[1024,256]{1,0:T(8,128)}), f32[128,256]{1,0:T(8,128)}) %reduce-scatter.22.cloned.1.call-update) | async-done | bytes 131088 | tf_op jit(solution)/shard_map/reduce_scatter | solution.py:262
  2794.1 39.7 %reduce-scatter.20.cloned.1.call-done = f32[128,256]{1,0:T(8,128)} async-done(((f32[1024,256]{1,0:T(8,128)}), f32[128,256]{1,0:T(8,128)}) %reduce-scatter.20.cloned.1.call-update) | async-done | bytes 131088 | tf_op jit(solution)/shard_map/reduce_scatter | solution.py:261
  (557 shorter events, 995.1 us)
Async XLA Ops:
  8.0 155.0 %all-gather.8.cloned.1.call-start = ((), (), s32[]{:S(2)}) async-start(), calls=%async_computation.11 | async-start | bytes 10485760 | tf_op jit(solution)/shard_map/all_gather | solution.py:190
  14.9 621.6 %reduce-scatter.12.cloned.1.call-start = ((), (), s32[]{:S(2)}) async-start(), calls=%async_computation.12 | async-start | bytes 20971520 | tf_op jit(solution)/shard_map/reduce_scatter | solution.py:201
  358.0 287.2 %all-gather.14.cloned.1.call-start = ((), (), s32[]{:S(2)}) async-start(), calls=%async_computation.15 | async-start | bytes 1622016 | tf_op jit(solution)/shard_map/all_gather | solution.py:176
  358.6 282.7 %copy-start.42 = (f32[1024]{0:T(1024)S(1)}, f32[1024]{0:T(1024)}, u32[]{:S(2)}) copy-start(f32[1024]{0:T(1024)} %param.33) | copy-start | bytes 12292
  358.6 434.9 %all-gather.10.cloned.1.call-start = ((), (), s32[]{:S(2)}) async-start(), calls=%async_computation.13 | async-start | bytes 10485760 | tf_op jit(solution)/shard_map/all_gather | solution.py:207
  639.3 691.3 %copy-start.40 = (f32[1024]{0:T(1024)}, f32[1024]{0:T(1024)S(1)}, u32[]{:S(2)}) copy-start(f32[1024]{0:T(1024)S(1)} %fusion.56) | copy-start | bytes 12292
  643.1 179.0 %all-gather.12.cloned.1.call-start = ((), (), s32[]{:S(2)}) async-start(), calls=%async_computation.14 | async-start | bytes 1622016 | tf_op jit(solution)/shard_map/all_gather | solution.py:175
  643.7 205.6 %all-gather.16.cloned.1.call-start = ((), (), s32[]{:S(2)}) async-start(), calls=%async_computation.16 | async-start | bytes 1622016 | tf_op jit(solution)/shard_map/all_gather | solution.py:177
  644.4 352.8 %all-gather.18.cloned.1.call-start = ((), (), s32[]{:S(2)}) async-start(), calls=%async_computation.18 | async-start | bytes 10485760 | tf_op jit(solution)/shard_map/all_gather | solution.py:215
  645.2 680.2 %reduce-scatter.16.cloned.1.call-start = ((), (), s32[]{:S(2)}) async-start(), calls=%async_computation.19 | async-start | bytes 20971520 | tf_op jit(solution)/shard_map/reduce_scatter | solution.py:219
  1047.0 284.2 %copy-start.13 = (bf16[1024,1024]{1,0:T(8,128)(2,1)S(1)}, bf16[1024,1024]{1,0:T(8,128)(2,1)}, u32[]{:S(2)}) copy-start(bf16[1024,1024]{1,0:T(8,128)(2,1)} %param.24) | copy-start | bytes 6291460
  1047.0 437.6 %all-gather.20.cloned.1.call-start = ((), (), s32[]{:S(2)}) async-start(), calls=%async_computation.20 | async-start | bytes 10485760 | tf_op jit(solution)/shard_map/all_gather | solution.py:227
  1333.8 1041.8 %reduce-scatter.18.cloned.1.call-start = ((), (), s32[]{:S(2)}) async-start(), calls=%async_computation.21 | async-start | bytes 20971520 | tf_op jit(solution)/shard_map/reduce_scatter | solution.py:247
  2097.1 429.8 %reduce-scatter.14.cloned.1.call-start = ((), (), s32[]{:S(2)}) async-start(), calls=%async_computation.17 | async-start | bytes 10485760 | tf_op jit(solution)/shard_map/reduce_scatter | solution.py:212
  2110.3 466.6 %reduce-scatter.32.cloned.1.call-start = ((), (), s32[]{:S(2)}) async-start(), calls=%async_computation.28 | async-start | bytes 3244032 | tf_op jit(solution)/shard_map/reduce_scatter | solution.py:267
  2122.0 503.7 %reduce-scatter.28.cloned.1.call-start = ((), (), s32[]{:S(2)}) async-start(), calls=%async_computation.26 | async-start | bytes 3244032 | tf_op jit(solution)/shard_map/reduce_scatter | solution.py:265
  2133.6 541.4 %reduce-scatter.30.cloned.1.call-start = ((), (), s32[]{:S(2)}) async-start(), calls=%async_computation.27 | async-start | bytes 3244032 | tf_op jit(solution)/shard_map/reduce_scatter | solution.py:266
  2145.0 569.7 %reduce-scatter.26.cloned.1.call-start = ((), (), s32[]{:S(2)}) async-start(), calls=%async_computation.25 | async-start | bytes 1179648 | tf_op jit(solution)/shard_map/reduce_scatter | solution.py:264
  2153.5 600.9 %reduce-scatter.24.cloned.1.call-start = ((), (), s32[]{:S(2)}) async-start(), calls=%async_computation.24 | async-start | bytes 1179648 | tf_op jit(solution)/shard_map/reduce_scatter | solution.py:263
  2161.6 632.5 %reduce-scatter.22.cloned.1.call-start = ((), (), s32[]{:S(2)}) async-start(), calls=%async_computation.23 | async-start | bytes 1179648 | tf_op jit(solution)/shard_map/reduce_scatter | solution.py:262
  2169.0 664.8 %reduce-scatter.20.cloned.1.call-start = ((), (), s32[]{:S(2)}) async-start(), calls=%async_computation.22 | async-start | bytes 1179648 | tf_op jit(solution)/shard_map/reduce_scatter | solution.py:261
  2182.4 344.5 %copy-start.41 = (f32[1024]{0:T(1024)S(1)}, f32[1024]{0:T(1024)}, u32[]{:S(2)}) copy-start(f32[1024]{0:T(1024)} %copy-done.40) | copy-start | bytes 12292
  2182.4 344.5 %copy-start.43 = (f32[1024]{0:T(1024)S(1)}, f32[1024]{0:T(1024)}, u32[]{:S(2)}) copy-start(f32[1024]{0:T(1024)} %param.33) | copy-start | bytes 12292
  2182.4 344.5 %copy-start.51 = (f32[1024]{0:T(1024)S(1)}, f32[1024]{0:T(1024)}, u32[]{:S(2)}) copy-start(f32[1024]{0:T(1024)} %copy-done.50) | copy-start | bytes 12292
  (121 other events, 2869.3 us)
Sparse Core Ops, SparseCore 0:
  15.0 148.0 all-gather.7
  358.2 278.3 reduce-scatter.11
  1333.9 150.6 all-gather.19
  2097.3 278.3 reduce-scatter.17
  2377.9 148.9 reduce-scatter.13
  2531.1 45.7 reduce-scatter.31
  2580.8 44.8 reduce-scatter.27
  2630.1 44.8 reduce-scatter.29
  2678.8 35.8 reduce-scatter.25
  2718.3 36.0 reduce-scatter.23
  2758.1 35.9 reduce-scatter.21
  2797.7 36.0 reduce-scatter.19
Sparse Core Ops, SparseCore 1:
  360.5 26.5 all-gather.13
  643.2 150.3 all-gather.9
  795.4 26.6 all-gather.11
  824.2 25.1 all-gather.15
  851.0 146.2 all-gather.17
  1047.1 278.2 reduce-scatter.15
where the time goes:
time: 2860 us; the launch traced here: 2840 us
  waiting for transfers between devices  1730 us (60%)
  matrix products  558 us (20%)
  local copies, waits for them, and re-layouts  271 us (9%)
  other arithmetic  164 us (6%)
  blocking collectives  86.1 us (3%)
    reduce_scatter x1, waiting for transfers between devices, body(): lax.psum_scatter(outer(gate_low, gate_mat) + outer(up_low, up_mat), 'tens...  278 us
    reduce_scatter x1, waiting for transfers between devices, body(): lax.psum_scatter(product(attended_low, out_mat), 'tensor', scatter_dimens...  278 us
    reduce_scatter x1, waiting for transfers between devices, body(): lax.psum_scatter(outer(grad_query_low, query_mat) + outer(grad_key_low, k...  193 us
    all_gather x1, waiting for transfers between devices, body(): lax.all_gather(grad_hidden.astype(jnp.bfloat16), 'tensor', axis=0, tiled=...  151 us
    all_gather x1, waiting for transfers between devices, body(): gathered_two = lax.all_gather(normed_low_two, 'tensor', axis=0, tiled=True)  148 us
    all_gather x1, waiting for transfers between devices, body(): grad_rows = lax.all_gather(cotangent, 'tensor', axis=0, tiled=True)  148 us
    all_gather x1, waiting for transfers between devices, body(): lax.all_gather(normed_one.astype(jnp.bfloat16), 'tensor', axis=0, tiled=T...  104 us
    reduce_scatter x1, waiting for transfers between devices, body(): lax.psum_scatter(product(act_low, down_mat).astype(jnp.bfloat16), 'tensor...  101 us
  transfers between devices with their start and end apart: 18, of which 17 were waited for; matrix products, arithmetic and copies ran while one was open for 5% of the time, Pallas kernels for 0%

commit v1 on v0

--- a/solution.py
+++ b/solution.py
@@ -1,13 +1,15 @@
+import functools
+
 import jax
 import jax.numpy as jnp
 from jax import lax
+from jax.experimental import pallas as pl
+from jax.experimental.pallas import tpu as pltpu
 from jax.sharding import PartitionSpec as P
 
 HEAD = 64
 SEQ = 2048
 DOCS = 8
-
-
 EPSILON = 1e-05
 
 
@@ -152,7 +154,7 @@
     return (grad_queries.reshape(SEQ, queries.shape[1], HEAD), sums[0], sums[1])
 
 
-def body(
+def general_body(
     tokens,
     first_values,
     doc_lengths,
@@ -283,7 +285,796 @@
     )
 
 
+AXES = ("dp", "tensor")
+TILE = 256
+NEG = -1e30
+F32 = jnp.float32
+BF16 = jnp.bfloat16
+
+
+def flat(y, x, c, t):
+    return ((y * 2 + x) * 2 + c) * 4 + t
+
+
+def move(values, to):
+    pairs = []
+    for y in range(2):
+        for x in range(2):
+            for c in range(2):
+                for t in range(4):
+                    pairs.append((flat(y, x, c, t), flat(*to(y, x, c, t))))
+    return lax.ppermute(values, AXES, pairs)
+
+
+def across_x(values):
+    return move(values, lambda y, x, c, t: (y, 1 - x, c, t))
+
+
+def across_y(values):
+    return move(values, lambda y, x, c, t: (1 - y, x, c, t))
+
+
+def across_c(values):
+    return move(values, lambda y, x, c, t: (y, x, 1 - c, t))
+
+
+def along_t(values, step):
+    return move(values, lambda y, x, c, t: (y, x, c, (t + step) % 4))
+
+
+def swap_halves(values):
+    return move(values, lambda y, x, c, t: (y, x, t % 2, (t // 2) * 2 + c))
+
+
+PIECES = []
+for _c in range(2):
+    PIECES += [
+        [[(_c + 2 * i, j) for j in range(2)] for i in range(2)],
+        [[(_c + 4 + 2 * i, j) for j in range(2)] for i in range(2)],
+        [[(_c + 4 * i, 2 + j) for j in range(2)] for i in range(2)],
+        [[(_c + 2 + 4 * i, 2 + j) for j in range(2)] for i in range(2)],
+    ]
+
+
+def gather_pieces(shard):
+    along = [shard] + [along_t(shard, d) for d in (1, 2, 3)]
+    first = jnp.stack(along[:2])
+    second = jnp.stack(along[2:])
+    first = jnp.stack([first, across_x(first)])
+    second = jnp.stack([second, across_y(second)])
+    own = [first, across_y(first), second, across_x(second)]
+    return own + [across_c(piece) for piece in own]
+
+
+def start_loads(pieces, which, held, sem, me, t):
+    for array, places in zip(pieces, PIECES, strict=True):
+        for i in range(2):
+            for j in range(2):
+                rel, dist = places[i][j]
+                block = (me ^ rel) * 128
+                pltpu.make_async_copy(
+                    array.at[i, j, which],
+                    held.at[(t - dist) & 3, pl.ds(pl.multiple_of(block, 128), 128), :],
+                    sem,
+                ).start()
+
+
+def wait_loads(held, sem):
+    pltpu.make_async_copy(held, held, sem).wait()
+
+
+def dot(left, right):
+    return jnp.dot(left, right, preferred_element_type=F32)
+
+
+def dot_nt(left, right):
+    return lax.dot_general(left, right, (((1,), (1,)), ((), ())), preferred_element_type=F32)
+
+
+def dot_tn(left, right):
+    return lax.dot_general(left, right, (((0,), (0,)), ((), ())), preferred_element_type=F32)
+
+
+def any_spec():
+    return pl.BlockSpec(memory_space=pl.ANY)
+
+
+def params(**more):
+    return pltpu.CompilerParams(vmem_limit_bytes=62 * 1024 * 1024, **more)
+
+
+def cost(flops, size, exps=0):
+    return pl.CostEstimate(flops=int(flops), bytes_accessed=int(size), transcendentals=int(exps))
+
+
+def project_kernel(at, own, other, fv0, fv1, cosine, sine, gain, *rest):
+    pieces, (normed_out, q_out, k_out, v_out, wq, wk, wv, sems) = rest[:8], rest[8:]
+    step = pl.program_id(0)
+    me, t = at[0], at[1]
+    c, pair = me & 1, t >> 1
+
+    @pl.when(step == 0)
+    def _():
+        for n, held in enumerate((wq, wk, wv)):
+            start_loads(pieces, n, held, sems.at[n], me, t)
+        for n, held in enumerate((wq, wk, wv)):
+            wait_loads(held, sems.at[n])
+
+    values = jnp.where(step < 2, own[...], other[...]).astype(F32)
+    factor = lax.rsqrt(jnp.mean(values * values, axis=1, keepdims=True) + EPSILON)
+    normed = (values * factor * gain[...]).astype(BF16)
+    normed_out[...] = normed
+    cos, sin = cosine[...], sine[...]
+    for u in range(2):
+        shard = 2 * c + u
+        for held, out, scale in ((wq, q_out, 0.125), (wk, k_out, 1.0)):
+            raw = dot(normed, held[shard])
+            a, b = raw[:, :128], raw[:, 128:]
+            out[:, u * 256 : u * 256 + 128] = ((a * cos - b * sin) * scale).astype(BF16)
+            out[:, u * 256 + 128 : u * 256 + 256] = ((b * cos + a * sin) * scale).astype(BF16)
+        raw = dot(normed, wv[shard])
+        first = jnp.where(pair == u, fv0[...], fv1[...]).astype(F32)
+        v_out[:, u * 256 : u * 256 + 256] = (0.5 * raw + 0.5 * first).astype(BF16)
+
+
+def project(at, own, other, fv, cosine, sine, gain, pieces):
+    rows, wide = 512, own.shape[1]
+
+    def place(i, at):
+        half = jnp.where(i < 2, at[0] & 1, 1 - (at[0] & 1))
+        return half * 2 + (i & 1)
+
+    row = lambda width: pl.BlockSpec((rows, width), lambda i, at: (place(i, at), 0))
+    grid = pltpu.PrefetchScalarGridSpec(
+        num_scalar_prefetch=1,
+        grid=(4,),
+        in_specs=[
+            pl.BlockSpec((rows, wide), lambda i, at: (jnp.minimum(i, 1), 0)),
+            pl.BlockSpec((rows, wide), lambda i, at: (jnp.maximum(i - 2, 0), 0)),
+            row(256),
+            row(256),
+            row(128),
+            row(128),
+            pl.BlockSpec((1, wide), lambda i, at: (0, 0)),
+        ]
+        + [any_spec()] * 8,
+        out_specs=[row(wide), row(512), row(512), row(512)],
+        scratch_shapes=[pltpu.VMEM((4, wide, 256), BF16)] * 3 + [pltpu.SemaphoreType.DMA((3,))],
+    )
+    return pl.pallas_call(
+        project_kernel,
+        out_shape=[jax.ShapeDtypeStruct((SEQ, wide), BF16)]
+        + [jax.ShapeDtypeStruct((SEQ, 512), BF16)] * 3,
+        grid_spec=grid,
+        compiler_params=params(),
+        cost_estimate=cost(2 * SEQ * wide * 1536, 24e6),
+        name="project",
+    )(at, own, other, fv[0], fv[1], cosine, sine, gain, *pieces)
+
+
+def head_masks(rows):
+    lane = lax.broadcasted_iota(jnp.int32, (rows, 256), 1)
+    return (lane & 127) >> 5, lane >> 6
+
+
+def attend_kernel(bounds, q_ref, k_ref, v_ref, starts, o_ref, lse_ref, kept, top, total, acc):
+    of_qk, of_v = head_masks(TILE)
+    row = lax.broadcasted_iota(jnp.int32, (TILE, TILE), 0)
+    lane = lax.broadcasted_iota(jnp.int32, (TILE, TILE), 1)
+
+    def query_tile(i, carry):
+        here = pl.ds(pl.multiple_of(i * TILE, TILE), TILE)
+        q = q_ref[here, :]
+        zero = jnp.zeros_like(q)
+        q4 = jnp.concatenate([jnp.where(of_qk == h, q, zero) for h in range(4)], axis=0)
+        begin = starts[here, :]
+        begin = jnp.concatenate([begin, begin], axis=1)
+        at_row = row + i * TILE
+        low = bounds[i]
+        top[...] = jnp.full_like(top, NEG)
+
+        def score(j, carry):
+            keys = k_ref[pl.ds(pl.multiple_of(j * TILE, TILE), TILE), :]
+            s = dot_nt(q4, keys)
+            at_lane = lane + j * TILE
+            ok = (at_lane >= begin) & (at_lane <= at_row)
+            for h in range(4):
+                part = slice(h * TILE, (h + 1) * TILE)
+                one = jnp.where(ok, s[part], NEG)
+                kept[j - low, part, :] = one
+                top[part] = jnp.maximum(top[part], jnp.maximum(one[:, :128], one[:, 128:]))
+            return carry
+
+        lax.fori_loop(low, i + 1, score, 0)
+        highest = jnp.max(top[...], axis=1, keepdims=True)
+        top[...] = jnp.broadcast_to(highest, top.shape)
+        total[...] = jnp.zeros_like(total)
+        acc[...] = jnp.zeros_like(acc)
+
+        def weigh(j, carry):
+            values = v_ref[pl.ds(pl.multiple_of(j * TILE, TILE), TILE), :]
+            zero = jnp.zeros_like(values)
+            exps, parts = [], []
+            for h in range(4):
+                part = slice(h * TILE, (h + 1) * TILE)
+                peak = top[part]
+                e = jnp.exp(kept[j - low, part, :] - jnp.concatenate([peak, peak], axis=1))
+                total[part] += e[:, :128] + e[:, 128:]
+                exps.append(e.astype(BF16))
+                parts.append(jnp.where(of_v == h, values, zero))
+            acc[...] += dot(jnp.concatenate(exps, axis=1), jnp.concatenate(parts, axis=0))
+            return carry
+
+        lax.fori_loop(low, i + 1, weigh, 0)
+        sums = jnp.sum(total[...], axis=1, keepdims=True)
+        inverse = 1.0 / sums
+        scale = jnp.broadcast_to(inverse[:TILE], (TILE, 256))
+        for h in range(1, 4):
+            scale = jnp.where(of_v == h, inverse[h * TILE : (h + 1) * TILE], scale)
+        o_ref[here, :] = (acc[...] * scale).astype(BF16)
+        logs = top[...] + jnp.log(jnp.broadcast_to(sums, top.shape))
+        for h in range(4):
+            turned = logs[h * TILE : (h + 1) * TILE].T
+            lse_ref[0, pl.ds(i, 1), h * TILE : (h + 1) * TILE] = turned[:1]
+        return carry
+
+    lax.fori_loop(0, SEQ // TILE, query_tile, 0)
+
+
+def attend(bounds, q, k, v, starts):
+    slab = pl.BlockSpec((SEQ, 256), lambda u, b: (0, u))
+    tiles = SEQ // TILE
+    grid = pltpu.PrefetchScalarGridSpec(
+        num_scalar_prefetch=1,
+        grid=(2,),
+        in_specs=[slab, slab, slab, pl.BlockSpec((SEQ, 128), lambda u, b: (0, 0))],
+        out_specs=[slab, pl.BlockSpec((1, tiles, 4 * TILE), lambda u, b: (u, 0, 0))],
+        scratch_shapes=[
+            pltpu.VMEM((tiles, 4 * TILE, TILE), F32),
+            pltpu.VMEM((4 * TILE, 128), F32),
+            pltpu.VMEM((4 * TILE, 128), F32),
+            pltpu.VMEM((TILE, 256), F32),
+        ],
+    )
+    return pl.pallas_call(
+        attend_kernel,
+        out_shape=[
+            jax.ShapeDtypeStruct((SEQ, 512), BF16),
+            jax.ShapeDtypeStruct((2, tiles, 4 * TILE), F32),
+        ],
+        grid_spec=grid,
+        compiler_params=params(),
+        cost_estimate=cost(20e9, 12e6, 1e7),
+        name="attend",
+    )(bounds, q, k, v, starts)
+
+
+def attend_back_kernel(
+    bounds, q_ref, k_ref, v_ref, do_ref, o_ref, lse_ref, starts, cosine, sine, dq_ref, dk_ref, dv_ref, dq_acc, delta, dk_acc, dv_acc
+):
+    tiles = SEQ // TILE
+    of_qk, of_v = head_masks(TILE)
+    row = lax.broadcasted_iota(jnp.int32, (TILE, TILE), 0)
+    lane = lax.broadcasted_iota(jnp.int32, (TILE, TILE), 1)
+    pick = (lax.broadcasted_iota(jnp.int32, (8, 256), 1) >> 6) == lax.broadcasted_iota(
+        jnp.int32, (8, 256), 0
+    )
+    pick = pick.astype(F32)
+    dq_acc[...] = jnp.zeros_like(dq_acc)
+
+    def prepare(i, carry):
+        here = pl.ds(pl.multiple_of(i * TILE, TILE), TILE)
+        both = do_ref[here, :].astype(F32) * o_ref[here, :].astype(F32)
+        sums = lax.dot_general(
+            pick, both, (((1,), (1,)), ((), ())), precision=lax.Precision.HIGHEST, preferred_element_type=F32
+        )
+        for h in range(4):
+            delta[pl.ds(i, 1), h * TILE : (h + 1) * TILE] = sums[h : h + 1]
+        return carry
+
+    lax.fori_loop(0, tiles, prepare, 0)
+
+    def rotate_out(values, here, out, scale):
+        a, b = values[:, :128], values[:, 128:]
+        cos, sin = cosine[here, :], sine[here, :]
+        out[here, :128] = ((a * cos + b * sin) * scale).astype(BF16)
+        out[here, 128:] = ((b * cos - a * sin) * scale).astype(BF16)
+
+    def split(values, of):
+        zero = jnp.zeros_like(values)
+        return jnp.concatenate([jnp.where(of == h, values, zero) for h in range(4)], axis=0)
+
+    def key_tile(j, carry):
+        there = pl.ds(pl.multiple_of(j * TILE, TILE), TILE)
+        keys, values = k_ref[there, :], v_ref[there, :]
+        k4 = split(keys, of_qk)
+        at_row = row + j * TILE
+        dk_acc[...] = jnp.zeros_like(dk_acc)
+        dv_acc[...] = jnp.zeros_like(dv_acc)
+
+        def query_tile(i, carry):
+            here = pl.ds(pl.multiple_of(i * TILE, TILE), TILE)
+            q4 = split(q_ref[here, :], of_qk)
+            do4 = split(do_ref[here, :], of_v)
+            s = dot_nt(keys, q4)
+            dp = dot_nt(values, do4)
+            at_lane = lane + i * TILE
+            ok = (at_row >= starts[pl.ds(i, 1), :]) & (at_row <= at_lane)
+            lse, shift = lse_ref[0, pl.ds(i, 1), :], delta[pl.ds(i, 1), :]
+            ps, dss = [], []
+            for h in range(4):
+                part = slice(h * TILE, (h + 1) * TILE)
+                p = jnp.exp(jnp.where(ok, s[:, part] - lse[:, part], NEG))
+                ds = p * (dp[:, part] - shift[:, part])
+                ps.append(p.astype(BF16))
+                dss.append(ds.astype(BF16))
+            dv_acc[...] += dot(jnp.concatenate(ps, axis=1), do4)
+            dk_acc[...] += dot(jnp.concatenate(dss, axis=1), q4)
+            dq_acc[here, :] += dot_tn(jnp.concatenate(dss, axis=0), k4)
+            return carry
+
+        lax.fori_loop(j, bounds[tiles + j] + 1, query_tile, 0)
+        rotate_out(dk_acc[...], there, dk_ref, 1.0)
+        dv_ref[there, :] = (0.5 * dv_acc[...]).astype(BF16)
+        return carry
+
+    lax.fori_loop(0, tiles, key_tile, 0)
+
+    def finish(i, carry):
+        here = pl.ds(pl.multiple_of(i * TILE, TILE), TILE)
+        rotate_out(dq_acc[here, :], here, dq_ref, 0.125)
+        return carry
+
+    lax.fori_loop(0, tiles, finish, 0)
+
+
+def attend_back(bounds, q, k, v, do, o, lse, starts, cosine, sine):
+    slab = pl.BlockSpec((SEQ, 256), lambda u, b: (0, u))
+    whole = lambda shape: pl.BlockSpec(shape, lambda u, b: (0,) * len(shape))
+    tiles = SEQ // TILE
+    grid = pltpu.PrefetchScalarGridSpec(
+        num_scalar_prefetch=1,
+        grid=(2,),
+        in_specs=[slab] * 5
+        + [
+            pl.BlockSpec((1, tiles, 4 * TILE), lambda u, b: (u, 0, 0)),
+            whole((tiles, TILE)),
+            whole((SEQ, 128)),
+            whole((SEQ, 128)),
+        ],
+        out_specs=[slab] * 3,
+        scratch_shapes=[
+            pltpu.VMEM((SEQ, 256), F32),
+            pltpu.VMEM((tiles, 4 * TILE), F32),
+            pltpu.VMEM((TILE, 256), F32),
+            pltpu.VMEM((TILE, 256), F32),
+        ],
+    )
+    return pl.pallas_call(
+        attend_back_kernel,
+        out_shape=[jax.ShapeDtypeStruct((SEQ, 512), BF16)] * 3,
+        grid_spec=grid,
+        compiler_params=params(),
+        cost_estimate=cost(50e9, 20e6, 1e7),
+        name="attend_back",
+    )(bounds, q, k, v, do, o, lse, starts, cosine, sine)
+
+
+def mlp_kernel(at, att_own, att_other, tok, cot, gain, *rest):
+    small, big, rest = rest[:8], rest[8:16], rest[16:]
+    (out, gh_out, gb_out, n2_out, hid_out, ga_own, ga_other, gg_out) = rest[:8]
+    (wo, wg, wu, wd, sems) = rest[8:]
+    step = pl.program_id(0)
+    me, t = at[0], at[1]
+    c = me & 1
+
+    @pl.when(step == 0)
+    def _():
+        start_loads(small, 3, wo, sems.at[0], me, t)
+        for n, held in enumerate((wg, wu, wd)):
+            start_loads(big, n, held, sems.at[1 + n], me, t)
+        wait_loads(wo, sems.at[0])
+        gg_out[...] = jnp.zeros_like(gg_out)
+
+    hidden = tok[...].astype(F32)
+    for e, att in enumerate((att_own, att_other)):
+        for u in range(2):
+            hidden += dot_nt(att[:, u * 256 : u * 256 + 256], wo[2 * (c ^ e) + u])
+    factor = lax.rsqrt(jnp.mean(hidden * hidden, axis=1, keepdims=True) + EPSILON)
+    gains = gain[...]
+    normed = (hidden * factor * gains).astype(BF16)
+    n2_out[...] = normed
+    g = cot[...]
+
+    @pl.when(step == 0)
+    def _():
+        for n, held in enumerate((wg, wu, wd)):
+            wait_loads(held, sems.at[1 + n])
+
+    down = jnp.zeros_like(hidden)
+    back = jnp.zeros_like(hidden)
+    for k in range(4):
+        gate, up, grad_act = dot(normed, wg[k]), dot(normed, wu[k]), dot(g, wd[k])
+        sig = 1.0 / (1.0 + jnp.exp(-gate))
+        silu = gate * sig
+        act = (silu * up).astype(BF16)
+        grad_up = (grad_act * silu).astype(BF16)
+        grad_gate = (grad_act * up * (sig * (1.0 + gate * (1.0 - sig)))).astype(BF16)
+        hid_out[0, k], hid_out[1, k], hid_out[2, k] = grad_gate, grad_up, act
+        down += dot_nt(act, wd[k])
+        back += dot_nt(grad_gate, wg[k]) + dot_nt(grad_up, wu[k])
+    out[...] = (hidden + down).astype(BF16)
+    gg_out[...] += jnp.sum((back * hidden * factor).reshape(-1, 8, back.shape[1]), axis=0)
+    scaled = back * gains
+    mean = jnp.mean(scaled * hidden, axis=1, keepdims=True)
+    grad_hidden = g.astype(F32) + factor * scaled - hidden * (factor * factor * factor * mean)
+    gh_out[...] = grad_hidden
+    branch = grad_hidden.astype(BF16)
+    gb_out[...] = branch
+    for e, ga in enumerate((ga_own, ga_other)):
+        for u in range(2):
+            ga[:, u * 256 : u * 256 + 256] = dot(branch, wo[2 * (c ^ e) + u]).astype(BF16)
+
+
+def mlp(at, att_own, att_other, tok, cot, gain, small, big):
+    count, wide = tok.shape
+    rows, part = 256, big[0].shape[-1]
+    row = lambda width: pl.BlockSpec((rows, width), lambda i, at: (i, 0))
+    one = pl.BlockSpec((1, wide), lambda i, at: (0, 0))
+    grid = pltpu.PrefetchScalarGridSpec(
+        num_scalar_prefetch=1,
+        grid=(count // rows,),
+        in_specs=[row(512), row(512), row(wide), row(wide), one] + [any_spec()] * 16,
+        out_specs=[
+            row(wide),
+            row(wide),
+            row(wide),
+            row(wide),
+            pl.BlockSpec((3, 4, rows, part), lambda i, at: (0, 0, i, 0)),
+            row(512),
+            row(512),
+            pl.BlockSpec((8, wide), lambda i, at: (0, 0)),
+        ],
+        scratch_shapes=[pltpu.VMEM((4, wide, 256), BF16)]
+        + [pltpu.VMEM((4, wide, part), BF16)] * 3
+        + [pltpu.SemaphoreType.DMA((4,))],
+    )
+    tokens = lambda width, kind=BF16: jax.ShapeDtypeStruct((count, width), kind)
+    return pl.pallas_call(
+        mlp_kernel,
+        out_shape=[
+            tokens(wide),
+            tokens(wide, F32),
+            tokens(wide),
+            tokens(wide),
+            jax.ShapeDtypeStruct((3, 4, count, part), BF16),
+            tokens(512),
+            tokens(512),
+            jax.ShapeDtypeStruct((8, wide), F32),
+        ],
+        grid_spec=grid,
+        compiler_params=params(),
+        cost_estimate=cost(2 * count * wide * (6 * 4 * part + 2 * wide), 60e6, 3e6),
+        name="mlp",
+    )(at, att_own, att_other, tok, cot, gain, *small, *big)
+
+
+def turn_rows(source, parity, held):
+    for r in range(4):
+        block = source[:, pl.ds(pl.multiple_of((r * 2 + parity) * 128, 128), 128)]
+        held[r * 128 : (r + 1) * 128, :] = block.T
+
+
+def weight_send_kernel(at, n2, g, hid, out, turned):
+    n, k = pl.program_id(0), pl.program_id(1)
+    parity = 1 - (at[0] & 1)
+
+    @pl.when((n == 0) & (k == 0))
+    def _():
+        turn_rows(n2, parity, turned)
+
+    @pl.when((n == 2) & (k == 0))
+    def _():
+        turn_rows(g, parity, turned)
+
+    out[0, 0] = dot(turned[...], hid[0, 0]).astype(BF16).reshape(out.shape[2:])
+
+
+def weight_send(at, n2, g, hid):
+    count, wide = n2.shape
+    part = hid.shape[-1]
+    whole = pl.BlockSpec((count, wide), lambda n, k, at: (0, 0))
+    grid = pltpu.PrefetchScalarGridSpec(
+        num_scalar_prefetch=1,
+        grid=(3, 4),
+        in_specs=[whole, whole, pl.BlockSpec((1, 1, count, part), lambda n, k, at: (n, k, 0, 0))],
+        out_specs=pl.BlockSpec((1, 1, 4, 128, part), lambda n, k, at: (n, k, 0, 0, 0)),
+        scratch_shapes=[pltpu.VMEM((512, count), BF16)],
+    )
+    return pl.pallas_call(
+        weight_send_kernel,
+        out_shape=jax.ShapeDtypeStruct((3, 4, 4, 128, part), BF16),
+        grid_spec=grid,
+        compiler_params=params(),
+        cost_estimate=cost(2 * count * 512 * part * 12, 30e6),
+        name="weight_send",
+    )(at, n2, g, hid)
+
+
+def weight_keep_kernel(at, n2, g, hid, got, first_send, first_keep, second_send, second_keep, turned):
+    n, d = pl.program_id(0), pl.program_id(1)
+    me = at[0]
+
+    @pl.when((n == 0) & (d == 0))
+    def _():
+        turn_rows(n2, me & 1, turned)
+
+    @pl.when((n == 2) & (d == 0))
+    def _():
+        turn_rows(g, me & 1, turned)
+
+    def block(rel):
+        index = (me >> 1) ^ rel
+        rows = turned[pl.ds(pl.multiple_of(index * 128, 128), 128), :]
+        return rows, got[0, 0, index].astype(F32)
+
+    rows, extra = zip(*[block(rel) for rel in range(4)], strict=True)
+    product = dot(jnp.concatenate(rows, axis=0), hid[0, 0])
+    done = [(product[r * 128 : (r + 1) * 128] + extra[r]).astype(BF16) for r in range(4)]
+
+    @pl.when(d < 2)
+    def _():
+        first_send[0, 0, 0], first_send[0, 1, 0] = done[1], done[3]
+        first_keep[0, 0, 0], first_keep[0, 1, 0] = done[0], done[2]
+
+    @pl.when(d >= 2)
+    def _():
+        second_send[0, 0, 0], second_send[0, 1, 0] = done[2], done[3]
+        second_keep[0, 0, 0], second_keep[0, 1, 0] = done[0], done[1]
+
+
+def weight_keep(at, n2, g, hid, got):
+    count, wide = n2.shape
+    part = hid.shape[-1]
+    whole = pl.BlockSpec((count, wide), lambda n, d, at: (0, 0))
+    first = pl.BlockSpec((1, 2, 1, 128, part), lambda n, d, at: (jnp.minimum(d, 1), 0, n, 0, 0))
+    second = pl.BlockSpec((1, 2, 1, 128, part), lambda n, d, at: (jnp.maximum(d - 2, 0), 0, n, 0, 0))
+    grid = pltpu.PrefetchScalarGridSpec(
+        num_scalar_prefetch=1,
+        grid=(3, 4),
+        in_specs=[
+            whole,
+            whole,
+            pl.BlockSpec((1, 1, count, part), lambda n, d, at: (n, (at[1] + d) & 3, 0, 0)),
+            pl.BlockSpec((1, 1, 4, 128, part), lambda n, d, at: (n, (at[1] + d) & 3, 0, 0, 0)),
+        ],
+        out_specs=[first, first, second, second],
+        scratch_shapes=[pltpu.VMEM((512, count), BF16)],
+    )
+    return pl.pallas_call(
+        weight_keep_kernel,
+        out_shape=[jax.ShapeDtypeStruct((2, 2, 3, 128, part), BF16)] * 4,
+        grid_spec=grid,
+        compiler_params=params(),
+        cost_estimate=cost(2 * count * 512 * part * 12, 40e6),
+        name="weight_keep",
+    )(at, n2, g, hid, got)
+
+
+def add(left, right):
+    return (left.astype(F32) + right.astype(F32)).astype(BF16)
+
+
+def scatter_xy(first_send, first_keep, second_send, second_keep):
+    got = across_x(first_send)
+    send, keep = add(first_keep[:, 1], got[:, 1]), add(first_keep[:, 0], got[:, 0])
+    first = add(keep, across_y(send))
+    got = across_y(second_send)
+    send, keep = add(second_keep[:, 1], got[:, 1]), add(second_keep[:, 0], got[:, 0])
+    return first, add(keep, across_x(send))
+
+
+def scatter_t(pieces):
+    total = pieces[0].astype(F32)
+    for d in (1, 2, 3):
+        total = total + along_t(pieces[d], d).astype(F32)
+    return total
+
+
+def project_back_kernel(at, dq, dk, dv, *rest):
+    pieces, (out, wq, wk, wv, sems) = rest[:8], rest[8:]
+    me, t = at[0], at[1]
+    c = me & 1
+
+    @pl.when(pl.program_id(0) == 0)
+    def _():
+        for n, held in enumerate((wq, wk, wv)):
+            start_loads(pieces, n, held, sems.at[n], me, t)
+        for n, held in enumerate((wq, wk, wv)):
+            wait_loads(held, sems.at[n])
+
+    total = None
+    for u in range(2):
+        for grad, held in ((dq, wq), (dk, wk), (dv, wv)):
+            term = dot_nt(grad[:, u * 256 : u * 256 + 256], held[2 * c + u])
+            total = term if total is None else total + term
+    out[...] = total.astype(out.dtype)
+
+
+def project_back(at, dq, dk, dv, pieces, other, kind):
+    rows, wide = 512, 1024
+    row = pl.BlockSpec((rows, 512), lambda i, at: (((at[0] & 1) ^ other) * 2 + i, 0))
+    grid = pltpu.PrefetchScalarGridSpec(
+        num_scalar_prefetch=1,
+        grid=(2,),
+        in_specs=[row] * 3 + [any_spec()] * 8,
+        out_specs=pl.BlockSpec((rows, wide), lambda i, at: (i, 0)),
+        scratch_shapes=[pltpu.VMEM((4, wide, 256), BF16)] * 3 + [pltpu.SemaphoreType.DMA((3,))],
+    )
+    return pl.pallas_call(
+        project_back_kernel,
+        out_shape=jax.ShapeDtypeStruct((SEQ // 2, wide), kind),
+        grid_spec=grid,
+        compiler_params=params(),
+        cost_estimate=cost(SEQ * wide * 1536, 14e6),
+        name="project_back",
+    )(at, dq, dk, dv, *pieces)
+
+
+def parity_columns(values, parity):
+    shaped = values.reshape(values.shape[0], 4, 2, 128)
+    return lax.dynamic_index_in_dim(shaped, parity, 2, keepdims=False).reshape(values.shape[0], 512)
+
+
+def fast_body(tokens, first_values, doc_lengths, cotangent, w_query, w_key, w_value, w_out, w_gate, w_up, w_down, gain_attn, gain_mlp):
+    me, t = lax.axis_index("dp"), lax.axis_index("tensor")
+    y, x, c = me // 4, (me // 2) % 2, me % 2
+    pair, side = t // 2, t % 2
+    wide = tokens.shape[1]
+    tiles = SEQ // TILE
+    at = jnp.where(jnp.arange(8, dtype=jnp.int32) == 0, me, t).astype(jnp.int32)
+
+    def halves_apart(matrix):
+        return matrix.reshape(-1, 4, 2, 32).swapaxes(1, 2).reshape(-1, 256)
+
+    small_shard = jnp.stack([halves_apart(w_query), halves_apart(w_key), w_value, w_out.T])
+    big_shard = jnp.stack([w_gate, w_up, w_down.T])
+
+    own = swap_halves(tokens)
+    small = gather_pieces(small_shard)
+    other = across_c(own)
+    blocks = first_values.reshape(2, SEQ, 256)
+
+    def first_round(r):
+        block = lax.dynamic_index_in_dim(blocks, r ^ (t % 2), 0, keepdims=False)
+        return move(block, lambda y, x, c, t: (y, x, t // 2, 2 * (r ^ (t % 2)) + c))
+
+    fv = [first_round(0), first_round(1)]
+    big = gather_pieces(big_shard)
+    cot = swap_halves(cotangent)
+
+    lengths = jnp.where(c == side, doc_lengths, across_c(doc_lengths))
+    lengths = lax.dynamic_index_in_dim(lengths, pair, 0, keepdims=False)
+    order = jnp.arange(DOCS, dtype=jnp.int32)
+    ends = jnp.sum(jnp.where(order[None, :] <= order[:, None], lengths[None, :], 0), axis=1)
+    places = jnp.arange(SEQ, dtype=jnp.int32)
+    starts = jnp.max(jnp.where(ends[None, :] <= places[:, None], ends[None, :], 0), axis=1)
+    last = jnp.arange(tiles, dtype=jnp.int32) * TILE + (TILE - 1)
+    finish = jnp.min(jnp.where(ends[None, :] > last[:, None], ends[None, :], SEQ), axis=1)
+    bounds = jnp.concatenate([starts.reshape(tiles, TILE)[:, 0] // TILE, (finish - 1) // TILE])
+    starts_wide = jnp.broadcast_to(starts[:, None], (SEQ, 128))
+    freqs = 10000.0 ** (-(jnp.arange(32, dtype=F32) * 2.0 / HEAD))
+    angles = (places - starts).astype(F32)[:, None] * jnp.tile(freqs, 4)[None, :]
+    cosine, sine = jnp.cos(angles), jnp.sin(angles)
+
+    normed_one, q, k, v = project(at, own, other, fv, cosine, sine, gain_attn[None], small)
+    attended, lse = attend(bounds, q, k, v, starts_wide)
+    by_half = attended.reshape(2, SEQ // 2, 512)
+    att_own = lax.dynamic_index_in_dim(by_half, c, 0, keepdims=False)
+    att_other = across_c(lax.dynamic_index_in_dim(by_half, 1 - c, 0, keepdims=False))
+    out, grad_hidden, branch, normed_two, hid, ga_own, ga_other, gain_two = mlp(
+        at, att_own, att_other, own, cot, gain_mlp[None], small, big
+    )
+    layer_out = swap_halves(out)
+
+    ga_got = across_c(ga_other)
+    do = jnp.where(c == 0, jnp.concatenate([ga_own, ga_got]), jnp.concatenate([ga_got, ga_own]))
+
+    got = across_c(weight_send(at, normed_two, cot, hid))
+    kept = weight_keep(at, normed_two, cot, hid, got)
+    first, second = scatter_xy(*kept)
+    grads = scatter_t([first[0], first[1], second[0], second[1]])
+
+    att_all = jnp.where(c == 0, jnp.concatenate([att_own, att_other], 1), jnp.concatenate([att_other, att_own], 1))
+    shape = (2, 2, 128, 4, 256)
+    sent = dot_tn(parity_columns(branch, 1 - c), att_all).astype(BF16)
+    held = (dot_tn(parity_columns(branch, c), att_all) + across_c(sent).astype(F32)).astype(BF16)
+    held = held.reshape(shape).transpose(3, 0, 1, 2, 4)
+
+    def pick(values, axis, index):
+        return lax.dynamic_index_in_dim(values, index, axis, keepdims=False)
+
+    def relative(values, axis):
+        order = jnp.stack([pick(values, axis, (t + d) % 4) for d in range(4)])
+        return order
+
+    held = relative(held, 0)
+
+    def by_neighbour(values, rows):
+        if rows == "x":
+            send, keep = pick(values, 2, 1 - x), pick(values, 2, x)
+            flip = y
+        else:
+            send, keep = pick(values, 1, 1 - y), pick(values, 1, y)
+            flip = x
+        turn = lambda item: jnp.where(flip == 0, item, item[:, ::-1])
+        return turn(send), turn(keep)
+
+    first, second = scatter_xy(*by_neighbour(held[:2], "x"), *by_neighbour(held[2:], "y"))
+    grad_out = scatter_t([first[0], first[1], second[0], second[1]])
+
+    dq, dk, dv = attend_back(bounds, q, k, v, do, attended, lse, starts.reshape(tiles, TILE), cosine, sine)
+
+    def first_back(r):
+        slab = jnp.where(pair == r, dv[:, :256], dv[:, 256:])
+        return move(slab, lambda y, x, c, t: (y, x, t % 2, 2 * c + ((t // 2) ^ r)))
+
+    fb = [first_back(0), first_back(1)]
+    odd = t % 2
+    grad_first = jnp.concatenate(
+        [jnp.where(odd == 0, fb[0], fb[1]), jnp.where(odd == 0, fb[1], fb[0])]
+    ).astype(F32)
+
+    gn_got = across_c(project_back(at, dq, dk, dv, small, 1, BF16))
+    stacked = jnp.concatenate([dq, dk, dv], axis=1)
+    sent = dot_tn(parity_columns(normed_one, 1 - c), stacked).astype(BF16)
+    mine = dot_tn(parity_columns(normed_one, c), stacked).astype(BF16)
+    got = across_c(sent)
+
+    def arrange(values):
+        return values.reshape(2, 2, 128, 3, 2, 256).transpose(4, 0, 1, 3, 2, 5)
+
+    first, second = scatter_xy(*by_neighbour(arrange(mine), "x"), *by_neighbour(arrange(got), "y"))
+    all_four = jnp.where(c == 0, jnp.concatenate([first, second]), jnp.concatenate([second, first]))
+    gq, gk, gv = scatter_t(list(relative(all_four, 0)))
+
+    def halves_together(matrix):
+        return matrix.reshape(-1, 2, 4, 32).swapaxes(1, 2).reshape(-1, 256)
+
+    gn_keep = project_back(at, dq, dk, dv, small, 0, F32)
+    grad_normed = gn_keep + gn_got.astype(F32)
+    values = own.astype(F32)
+    factor = lax.rsqrt(jnp.mean(values * values, axis=1, keepdims=True) + EPSILON)
+    scaled = grad_normed * gain_attn[None]
+    mean = jnp.mean(scaled * values, axis=1, keepdims=True)
+    grad_tokens = grad_hidden + factor * scaled - values * (factor * factor * factor * mean)
+    grad_tokens = swap_halves(grad_tokens.astype(BF16)).astype(F32)
+    gain_one = jnp.sum(grad_normed * values * factor, axis=0)
+    gains = jnp.stack([gain_one, jnp.sum(gain_two, axis=0)]).reshape(16, 128)
+    gains = gains + across_c(gains)
+    gains = gains + across_x(gains)
+    gains = gains + across_y(gains)
+    gains = gains + move(gains, lambda y, x, c, t: (y, x, c, t ^ 1))
+    gains = gains + move(gains, lambda y, x, c, t: (y, x, c, t ^ 2))
+    gains = gains.reshape(2, wide)
+    return (
+        layer_out,
+        grad_tokens,
+        grad_first,
+        halves_together(gq),
+        halves_together(gk),
+        gv,
+        grad_out.T,
+        grads[0],
+        grads[1],
+        grads[2].T,
+        gains[0],
+        gains[1],
+    )
+
+
 def solution(mesh):
+    fits = dict(mesh.shape) == {"dp": 8, "tensor": 4}
     placed = (
         P(("dp", "tensor"), None),
         P("dp", "tensor"),
@@ -300,7 +1091,7 @@
         P(),
     )
     return jax.shard_map(
-        body,
+        fast_body if fits else general_body,
         mesh=mesh,
         in_specs=placed,
         out_specs=(

time: 2860 us -> 893 us (0.31)
  waiting for transfers between devices: 1730 us -> 215 us
  matrix products: 558 us -> 21.1 us
  Pallas kernels: 0 us -> 240 us
  starting transfers between devices: 1 us -> 121 us
  other arithmetic: 164 us -> 71.4 us
  blocking collectives: 86.1 us -> 0 us
  local copies, waits for them, and re-layouts: 271 us -> 207 us
    reduce_scatter x11 -> x0, waiting for transfers between devices: 1150 us -> none  [the longest x1 278 us: body(): lax.psum_scatter(outer(gate_low, gate_mat) + outer(up_low, up_mat), 'tens...]
    all_gather x7 -> x0, waiting for transfers between devices: 581 us -> none  [the longest x1 151 us: body(): lax.all_gather(grad_hidden.astype(jnp.bfloat16), 'tensor', axis=0, tiled=...]
    dot_general x77 -> x4, matrix products: 558 us -> 21.1 us  [dot_tn(): lax.dot_general(left, right, (((0,), (0,)), ((), ())), preferred_element_...]
    pallas_call x0 -> x8, Pallas kernels: none -> 240 us  [the longest x1 64.2 us: mlp(): pl.pallas_call(mlp_kernel, out_shape=[tokens(wide), tokens(wide, F32), to...]
    ppermute x0 -> x64, waiting for transfers between devices: none -> 215 us  [move(): return lax.ppermute(values, AXES, pairs)]
    ppermute x0 -> x64, starting transfers between devices: none -> 121 us  [move(): return lax.ppermute(values, AXES, pairs)]
    dynamic_update_slice x12 -> x0, local copies, waits for them, and re-layouts: 94.6 us -> none  [body(): lax.map(forward_row, (heads(queries), heads(keys_low), heads(mixed_values...]
    while x174 -> x0, local copies, waits for them, and re-layouts: 68.3 us -> none
  transfers between devices with their start and end apart: 18 -> 64, of which waited for: 17 -> 19; matrix products, arithmetic and copies ran while one was open for 5% -> 30% of each run, Pallas kernels for 0% -> 20%
where the time goes in v1:
time: 893 us; the launch traced here: 878 us
  Pallas kernels  240 us (27%)
  waiting for transfers between devices  215 us (24%)
  local copies, waits for them, and re-layouts  207 us (23%)
  starting transfers between devices  121 us (14%)
  other arithmetic  71.4 us (8%)
  matrix products  21.1 us (2%)
    ppermute x64, waiting for transfers between devices, move(): return lax.ppermute(values, AXES, pairs)  215 us
    ppermute x64, starting transfers between devices, move(): return lax.ppermute(values, AXES, pairs)  121 us
    pallas_call x1, Pallas kernels, mlp(): pl.pallas_call(mlp_kernel, out_shape=[tokens(wide), tokens(wide, F32), to...  64.2 us
    unnamed x106, local copies, waits for them, and re-layouts  60.1 us
    pallas_call x1, Pallas kernels, attend_back(): pl.pallas_call(attend_back_kernel, out_shape=[jax.ShapeDtypeStruct((SEQ,...  55.2 us
    ppermute x17, local copies, waits for them, and re-layouts, move(): return lax.ppermute(values, AXES, pairs)  51.6 us
    pallas_call x1, Pallas kernels, attend(): pl.pallas_call(attend_kernel, out_shape=[jax.ShapeDtypeStruct((SEQ, 512),...  43 us
    pallas_call x1, Pallas kernels, weight_keep(): pl.pallas_call(weight_keep_kernel, out_shape=[jax.ShapeDtypeStruct((2, 2,...  22.9 us
  transfers between devices with their start and end apart: 64, of which 19 were waited for; matrix products, arithmetic and copies ran while one was open for 30% of the time, Pallas kernels for 20%

profile of v1, /device:TPU:11, one launch (start us, length us, event | category | flops | bytes accessed | tf_op | source)
XLA Modules:
  0.0 878.0 jit_solution(1827437457016780626)
XLA Ops:
  11.5 31.8 %collective-permute-done.21 = bf16[3,128,704]{1,2,0:T(8,128)(2,1)S(1)} collective-permute-done((bf16[3,128,704]{1,2,0:T(8,128)(2,1)}, bf16[3,128,704]{1,2,0:T(8,128)(2,1)S(1)}, u32[]{:S(2)}, u32[]{:S(2)}) %collective-permute-start.21) | collective-permute-done | bytes 540704 | tf_op jit(solution)/shard_map/ppermute | solution.py:306
  43.6 18.0 %collective-permute-done.22 = bf16[3,128,704]{1,2,0:T(8,128)(2,1)S(1)} collective-permute-done((bf16[3,128,704]{1,2,0:T(8,128)(2,1)}, bf16[3,128,704]{1,2,0:T(8,128)(2,1)S(1)}, u32[]{:S(2)}, u32[]{:S(2)}) %collective-permute-start.22) | collective-permute-done | bytes 540704 | tf_op jit(solution)/shard_map/ppermute | solution.py:306
  83.5 17.5 %collective-permute-done.10 = bf16[2,4,128,256]{3,2,1,0:T(8,128)(2,1)} collective-permute-done((bf16[2,4,128,256]{3,2,1,0:T(8,128)(2,1)S(1)}, bf16[2,4,128,256]{3,2,1,0:T(8,128)(2,1)}, u32[]{:S(2)}, u32[]{:S(2)}) %collective-permute-start.10) | collective-permute-done | bytes 524320 | tf_op jit(solution)/shard_map/ppermute | solution.py:306
  132.1 17.8 %collective-permute-done.3.fv0 = bf16[2048,256]{1,0:T(8,128)(2,1)} collective-permute-done((bf16[2048,256]{1,0:T(8,128)(2,1)}, bf16[2048,256]{1,0:T(8,128)(2,1)}, u32[]{:S(2)}, u32[]{:S(2)}) %collective-permute-start.3) | collective-permute-done | bytes 1048608 | tf_op jit(solution)/shard_map/ppermute | solution.py:306
  161.3 17.4 %collective-permute-start.17 = (bf16[1024,1024]{1,0:T(8,128)(2,1)}, bf16[1024,1024]{1,0:T(8,128)(2,1)}, u32[]{:S(2)}, u32[]{:S(2)}) collective-permute-start(bf16[1024,1024]{1,0:T(8,128)(2,1)} %param.16), channel_id=1, source_target_pairs={{0,0},{1,4},{2,2},{3,6},{4,1},{5,5},{6,3},{7,7},{8,8},{9,12},{10,1... | collective-permute-start | bytes 6291464 | tf_op jit(solution)/shard_map/ppermute | solution.py:306
  178.8 20.5 %collective-permute-done.24 = bf16[2,2,3,128,704]{3,4,2,1,0:T(8,128)(2,1)} collective-permute-done((bf16[2,2,3,128,704]{3,4,2,1,0:T(8,128)(2,1)}, bf16[2,2,3,128,704]{3,4,2,1,0:T(8,128)(2,1)}, u32[]{:S(2)}, u32[]{:S(2)}) %collective-permute-start.24) | collective-permute-done | bytes 2162720 | tf_op jit(solution)/shard_map/ppermute | solution.py:306
  200.7 15.0 %project.1 = (bf16[2048,1024]{1,0:T(8,128)(2,1)}, bf16[2048,512]{1,0:T(8,128)(2,1)}, bf16[2048,512]{1,0:T(8,128)(2,1)}, bf16[2048,512]{1,0:T(8,128)(2,1)}) custom-call(s32[8]{0:T(128)} %compare_select_fusion.at, bf16[1024,1024]{1,0:T(8,128)(2,1)} %copy-done.3, bf16[1024,1024]{1,0:T(8,128)(2,1)} %collective-permute-done.2.other, ...), custom_call_target="tpu_custom_call" | custom-call | flops 6442450944 | bytes 24000000 | tf_op jit(solution)/shard_map/project/pallas_call | solution.py:444
  217.1 43.0 %attend.1 = (bf16[2048,512]{1,0:T(8,128)(2,1)}, f32[2,8,1024]{2,1,0:T(8,128)}) custom-call(s32[16]{0:T(128)} %pad_add_fusion.bounds, bf16[2048,512]{1,0:T(8,128)(2,1)} %get-tuple-element.33.q_ref, bf16[2048,512]{1,0:T(8,128)(2,1)} %get-tuple-element.34.k_ref, bf16[2048,512]{1,0:T(8,128)(2,1)} %get-tuple-element.35.v_ref, s32[2048,128]{1,0:T(8,128)} %broadcast_in_dim.71.starts), custom_call_target="tpu_custom_call" | custom-call | flops 20000000000 | bytes 12000000 | tf_op jit(solution)/shard_map/attend/pallas_call | solution.py:539
  297.6 64.2 %mlp.1 = (bf16[1024,1024]{1,0:T(8,128)(2,1)}, f32[1024,1024]{1,0:T(8,128)}, bf16[1024,1024]{1,0:T(8,128)(2,1)}, bf16[1024,1024]{1,0:T(8,128)(2,1)}, bf16[3,4,102...) custom-call(s32[8]{0:T(128)} %compare_select_fusion.at, ...), custom_call_target="tpu_custom_call" | custom-call | flops 39728447488 | bytes 60000000 | tf_op jit(solution)/shard_map/mlp/pallas_call | solution.py:743
  390.4 10.7 %copy.284 = bf16[2048,4,1,128]{0,3,1,2:T(8,128)(2,1)} copy(bf16[2048,4,1,128]{3,2,1,0:T(2,128)(2,1)} %get-tuple-element.116) | data formatting | bytes 4194304
  401.0 10.6 %copy.287 = bf16[2048,4,1,128]{0,3,1,2:T(8,128)(2,1)} copy(bf16[2048,4,1,128]{3,2,1,0:T(2,128)(2,1)} %get-tuple-element.117) | data formatting | bytes 4194304
  411.7 20.7 %weight_send.1 = bf16[3,4,4,128,704]{4,3,2,1,0:T(8,128)(2,1)} custom-call(s32[8]{0:T(128)} %compare_select_fusion.at, bf16[1024,1024]{1,0:T(8,128)(2,1)} %get-tuple-element.47.n2, bf16[1024,1024]{1,0:T(8,128)(2,1)} %collective-permute-done.17.cot.g, bf16[3,4,1024,704]{3,2,1,0:T(8,128)(2,1)} %get-tuple-element.48.hid), custom_call_target="tpu_custom_call" | custom-call | flops 8858370048 | bytes 30000000 | tf_op jit(solution)/shard_map/weight_send/pallas_call | solution.py:794
  432.4 12.2 %copy.259 = bf16[3,4,4,128,704]{3,4,2,1,0:T(8,128)(2,1)} copy(bf16[3,4,4,128,704]{4,3,2,1,0:T(8,128)(2,1)} %weight_send.1) | data formatting | bytes 17301504 | tf_op jit(solution)/shard_map/weight_send/pallas_call | solution.py:794
  449.2 17.2 %collective-permute-start.29 = (bf16[1024,1024]{1,0:T(8,128)(2,1)}, bf16[1024,1024]{1,0:T(8,128)(2,1)}, u32[]{:S(2)}, u32[]{:S(2)}) collective-permute-start(bf16[1024,1024]{1,0:T(8,128)(2,1)} %get-tuple-element.37), channel_id=1, source_target_pairs={{0,0},{1,4},{2,2},{3,6},{4,1},{5,5},{6,3},{7,7},{8,8},{9,12},{10,1... | collective-permute-start | bytes 6291464 | tf_op jit(solution)/shard_map/ppermute | solution.py:306
  481.8 55.2 %attend_back.1 = (bf16[2048,512]{1,0:T(8,128)(2,1)}, bf16[2048,512]{1,0:T(8,128)(2,1)}, bf16[2048,512]{1,0:T(8,128)(2,1)}) custom-call(s32[16]{0:T(128)} %pad_add_fusion.bounds, bf16[2048,512]{1,0:T(8,128)(2,1)} %get-tuple-element.33.q_ref, bf16[2048,512]{1,0:T(8,128)(2,1)} %get-tuple-element.34.k_ref, bf16[2048,512]{1,0:T(8,128)(2,1)} %get-tuple-element.35.v_ref, ...), custom_call_target="tpu_custom_call" | custom-call | flops 49999998976 | bytes 20000000 | tf_op jit(solution)/shard_map/attend_back/pallas_call | solution.py:653
  596.4 10.0 %project_back.2 = f32[1024,1024]{1,0:T(8,128)} custom-call(s32[8]{0:T(128)} %compare_select_fusion.at, bf16[2048,512]{1,0:T(8,128)(2,1)} %get-tuple-element.42.dq, bf16[2048,512]{1,0:T(8,128)(2,1)} %get-tuple-element.43.dk, bf16[2048,512]{1,0:T(8,128)(2,1)} %get-tuple-element.44.dv, bf16[2,2,4,128,256]{4,3,2,1,0:T(8,128)(2,1)} %pad_maximum_fusion.4.rest_0_, ...), custom_call_target="tpu_custom_call" | custom-call | flops 3221225472 | bytes 14000000 | tf_op jit(solution)/shard_map/project_back/pallas_call | solution.py:914
  620.5 14.5 %collective-permute-done.34 = bf16[2048,256]{1,0:T(8,128)(2,1)} collective-permute-done((bf16[2048,256]{1,0:T(8,128)(2,1)S(1)}, bf16[2048,256]{1,0:T(8,128)(2,1)}, u32[]{:S(2)}, u32[]{:S(2)}) %collective-permute-start.34) | collective-permute-done | bytes 1048608 | tf_op jit(solution)/shard_map/ppermute | solution.py:306
  647.4 12.1 %copy.260.got = bf16[3,4,4,128,704]{4,3,2,1,0:T(8,128)(2,1)} copy(bf16[3,4,4,128,704]{3,4,2,1,0:T(8,128)(2,1)} %collective-permute-done.51) | data formatting | bytes 17301504 | tf_op jit(solution)/shard_map/ppermute | solution.py:306
  659.5 22.9 %weight_keep.1 = (bf16[2,2,3,128,704]{4,3,2,1,0:T(8,128)(2,1)}, bf16[2,2,3,128,704]{4,3,2,1,0:T(8,128)(2,1)}, bf16[2,2,3,128,704]{4,3,2,1,0:T(8,128)(2,1)}, bf16[2,2,3,128,704]{4,3,2,1,0:T(8,128)(2,1)}) custom-call(s32[8]{0:T(128)} %compare_select_fusion.at, bf16[1024,1024]{1,0:T(8,128)(2,1)} %get-tuple-element.47.n2, ...), custom_call_target="tpu_custom_call" | custom-call | flops 8858370048 | bytes 40000000 | tf_op jit(solution)/shard_map/weight_keep/pallas_call | solution.py:854
  706.9 22.6 %collective-permute-done.60 = f32[16,128]{1,0:T(8,128)S(1)} collective-permute-done((f32[16,128]{1,0:T(8,128)S(1)}, f32[16,128]{1,0:T(8,128)S(1)}, u32[]{:S(2)}, u32[]{:S(2)}) %collective-permute-start.60) | collective-permute-done | bytes 8224 | tf_op jit(solution)/shard_map/ppermute | solution.py:306
  731.5 19.9 %collective-permute-done.61 = f32[16,128]{1,0:T(8,128)S(1)} collective-permute-done((f32[16,128]{1,0:T(8,128)S(1)}, f32[16,128]{1,0:T(8,128)S(1)}, u32[]{:S(2)}, u32[]{:S(2)}) %collective-permute-start.61) | collective-permute-done | bytes 8224 | tf_op jit(solution)/shard_map/ppermute | solution.py:306
  767.2 17.2 %collective-permute-start.32 = (bf16[1024,1024]{1,0:T(8,128)(2,1)}, bf16[1024,1024]{1,0:T(8,128)(2,1)}, u32[]{:S(2)}, u32[]{:S(2)}) collective-permute-start(bf16[1024,1024]{1,0:T(8,128)(2,1)} %fusion.3), channel_id=1, source_target_pairs={{0,0},{1,4},{2,2},{3,6},{4,1},{5,5},{6,3},{7,7},{8,8},{9,12},{10,1... | collective-permute-start | bytes 6291464 | tf_op jit(solution)/shard_map/ppermute | solution.py:306
  824.0 21.3 %collective-permute-done.42 = bf16[3,128,256]{1,2,0:T(8,128)(2,1)} collective-permute-done((bf16[3,128,256]{1,2,0:T(8,128)(2,1)}, bf16[3,128,256]{1,2,0:T(8,128)(2,1)}, u32[]{:S(2)}, u32[]{:S(2)}) %collective-permute-start.42) | collective-permute-done | bytes 196640 | tf_op jit(solution)/shard_map/ppermute | solution.py:306
  854.3 10.8 %collective-permute-done.57 = bf16[3,128,704]{1,2,0:T(8,128)(2,1)} collective-permute-done((bf16[3,128,704]{1,2,0:T(8,128)(2,1)S(1)}, bf16[3,128,704]{1,2,0:T(8,128)(2,1)}, u32[]{:S(2)}, u32[]{:S(2)}) %collective-permute-start.57) | collective-permute-done | bytes 540704 | tf_op jit(solution)/shard_map/ppermute | solution.py:306
  (355 shorter events, 353.0 us)
Async XLA Ops:
  7.4 54.2 %collective-permute-start.22 = (bf16[3,128,704]{1,2,0:T(8,128)(2,1)}, bf16[3,128,704]{1,2,0:T(8,128)(2,1)S(1)}, u32[]{:S(2)}, u32[]{:S(2)}) collective-permute-start(bf16[3,128,704]{1,2,0:T(8,128)(2,1)} %copy.216), channel_id=1, source_target_pairs={{0,3},{1,0},{2,1},{3,2},{4,7},{5,4},{6,5},{7,6},{8,11},{9,8},{10,9... | collective-permute-start | bytes 1622024 | tf_op jit(solution)/shard_map/ppermute | solution.py:306
  7.6 60.9 %collective-permute-start.18 = (bf16[3,128,704]{1,2,0:T(8,128)(2,1)}, bf16[3,128,704]{1,2,0:T(8,128)(2,1)}, u32[]{:S(2)}, u32[]{:S(2)}) collective-permute-start(bf16[3,128,704]{1,2,0:T(8,128)(2,1)} %copy.216), channel_id=1, source_target_pairs={{0,1},{1,2},{2,3},{3,0},{4,5},{5,6},{6,7},{7,4},{8,9},{9,10},{10,1... | collective-permute-start | bytes 1622024 | tf_op jit(solution)/shard_map/ppermute | solution.py:306
  9.6 62.7 %collective-permute-start.8 = (bf16[4,128,256]{2,1,0:T(8,128)(2,1)S(1)}, bf16[4,128,256]{2,1,0:T(8,128)(2,1)}, u32[]{:S(2)}, u32[]{:S(2)}) collective-permute-start(bf16[4,128,256]{2,1,0:T(8,128)(2,1)S(1)} %get-tuple-element.166), channel_id=1, source_target_pairs={{0,2},{1,3},{2,0},{3,1},{4,6},{5,7},{6,4},{7,5},{8,10},{9,11},{10,... | collective-permute-start | bytes 786440 | tf_op jit(solution)/shard_map/ppermute | solution.py:306
  11.5 64.3 %collective-permute-start.9 = (bf16[4,128,256]{2,1,0:T(8,128)(2,1)S(1)}, bf16[4,128,256]{2,1,0:T(8,128)(2,1)}, u32[]{:S(2)}, u32[]{:S(2)}) collective-permute-start(bf16[4,128,256]{2,1,0:T(8,128)(2,1)S(1)} %get-tuple-element.166), channel_id=1, source_target_pairs={{0,3},{1,0},{2,1},{3,2},{4,7},{5,4},{6,5},{7,6},{8,11},{9,8},{10,9... | collective-permute-start | bytes 786440 | tf_op jit(solution)/shard_map/ppermute | solution.py:306
  72.3 79.3 %collective-permute-start.1 = (bf16[1024,1024]{1,0:T(8,128)(2,1)}, bf16[1024,1024]{1,0:T(8,128)(2,1)S(1)}, u32[]{:S(2)}, u32[]{:S(2)}) collective-permute-start(bf16[1024,1024]{1,0:T(8,128)(2,1)} %param.13), channel_id=1, source_target_pairs={{0,0},{1,4},{2,2},{3,6},{4,1},{5,5},{6,3},{7,7},{8,8},{9,12},{10,1... | collective-permute-start | bytes 6291464 | tf_op jit(solution)/shard_map/ppermute | solution.py:306
  101.0 48.9 %collective-permute-start.3 = (bf16[2048,256]{1,0:T(8,128)(2,1)}, bf16[2048,256]{1,0:T(8,128)(2,1)}, u32[]{:S(2)}, u32[]{:S(2)}) collective-permute-start(bf16[2048,256]{1,0:T(8,128)(2,1)} %get-tuple-element.131), channel_id=1, source_target_pairs={{0,0},{1,2},{2,4},{3,6},{4,1},{5,3},{6,5},{7,7},{8,8},{9,10},{10,1... | collective-permute-start | bytes 3145736 | tf_op jit(solution)/shard_map/ppermute | solution.py:306
  150.4 48.9 %collective-permute-start.24 = (bf16[2,2,3,128,704]{3,4,2,1,0:T(8,128)(2,1)}, bf16[2,2,3,128,704]{3,4,2,1,0:T(8,128)(2,1)}, u32[]{:S(2)}, u32[]{:S(2)}) collective-permute-start(bf16[2,2,3,128,704]{3,4,2,1,0:T(8,128)(2,1)} %copy.227), channel_id=1, source_target_pairs={{0,8},{1,9},{2,10},{3,11},{4,12},{5,13},{6,14},{7,15},{8,0},{9,1},... | collective-permute-start | bytes 6488072 | tf_op jit(solution)/shard_map/ppermute | solution.py:306
  150.4 49.8 %collective-permute-start.20 = (bf16[2,2,3,128,704]{3,4,2,1,0:T(8,128)(2,1)}, bf16[2,2,3,128,704]{3,4,2,1,0:T(8,128)(2,1)}, u32[]{:S(2)}, u32[]{:S(2)}) collective-permute-start(bf16[2,2,3,128,704]{3,4,2,1,0:T(8,128)(2,1)} %copy.220), channel_id=1, source_target_pairs={{0,16},{1,17},{2,18},{3,19},{4,20},{5,21},{6,22},{7,23},{8,24},{9,... | collective-permute-start | bytes 6488072 | tf_op jit(solution)/shard_map/ppermute | solution.py:306
  161.3 136.3 %collective-permute-start.17 = (bf16[1024,1024]{1,0:T(8,128)(2,1)}, bf16[1024,1024]{1,0:T(8,128)(2,1)}, u32[]{:S(2)}, u32[]{:S(2)}) collective-permute-start(bf16[1024,1024]{1,0:T(8,128)(2,1)} %param.16), channel_id=1, source_target_pairs={{0,0},{1,4},{2,2},{3,6},{4,1},{5,5},{6,3},{7,7},{8,8},{9,12},{10,1... | collective-permute-start | bytes 6291464 | tf_op jit(solution)/shard_map/ppermute | solution.py:306
  178.7 84.2 %collective-permute-start.27 = (bf16[2,2,3,128,704]{3,4,2,1,0:T(8,128)(2,1)}, bf16[2,2,3,128,704]{3,4,2,1,0:T(8,128)(2,1)}, u32[]{:S(2)}, u32[]{:S(2)}) collective-permute-start(bf16[2,2,3,128,704]{3,4,2,1,0:T(8,128)(2,1)} %copy.227), channel_id=1, source_target_pairs={{0,4},{1,5},{2,6},{3,7},{4,0},{5,1},{6,2},{7,3},{8,12},{9,13},{10,... | collective-permute-start | bytes 6488072 | tf_op jit(solution)/shard_map/ppermute | solution.py:306
  199.3 78.0 %collective-permute-start.25 = (bf16[2,2,3,128,704]{3,4,2,1,0:T(8,128)(2,1)}, bf16[2,2,3,128,704]{3,4,2,1,0:T(8,128)(2,1)}, u32[]{:S(2)}, u32[]{:S(2)}) collective-permute-start(bf16[2,2,3,128,704]{3,4,2,1,0:T(8,128)(2,1)} %copy.220), channel_id=1, source_target_pairs={{0,4},{1,5},{2,6},{3,7},{4,0},{5,1},{6,2},{7,3},{8,12},{9,13},{10,... | collective-permute-start | bytes 6488072 | tf_op jit(solution)/shard_map/ppermute | solution.py:306
  200.2 89.0 %collective-permute-start.28 = (bf16[2,2,3,128,704]{3,4,2,1,0:T(8,128)(2,1)}, bf16[2,2,3,128,704]{3,4,2,1,0:T(8,128)(2,1)}, u32[]{:S(2)}, u32[]{:S(2)}) collective-permute-start(bf16[2,2,3,128,704]{3,4,2,1,0:T(8,128)(2,1)} %collective-permute-done.24), channel_id=1, source_target_pairs={{0,4},{1,5},{2,6},{3,7},{4,0},{5,1},{6,2},{7,3},{8,12},{9,13},{10,... | collective-permute-start | bytes 6488072 | tf_op jit(solution)/shard_map/ppermute | solution.py:306
  200.3 93.2 %collective-permute-start.26 = (bf16[2,2,3,128,704]{3,4,2,1,0:T(8,128)(2,1)}, bf16[2,2,3,128,704]{3,4,2,1,0:T(8,128)(2,1)}, u32[]{:S(2)}, u32[]{:S(2)}) collective-permute-start(bf16[2,2,3,128,704]{3,4,2,1,0:T(8,128)(2,1)} %collective-permute-done.20), channel_id=1, source_target_pairs={{0,4},{1,5},{2,6},{3,7},{4,0},{5,1},{6,2},{7,3},{8,12},{9,13},{10,... | collective-permute-start | bytes 6488072 | tf_op jit(solution)/shard_map/ppermute | solution.py:306
  380.2 86.3 %collective-permute-start.43 = (bf16[512,1024]{1,0:T(8,128)(2,1)}, bf16[512,1024]{1,0:T(8,128)(2,1)}, u32[]{:S(2)}, u32[]{:S(2)}) collective-permute-start(bf16[512,1024]{1,0:T(8,128)(2,1)} %convolution_convert_fusion.2), channel_id=1, source_target_pairs={{0,4},{1,5},{2,6},{3,7},{4,0},{5,1},{6,2},{7,3},{8,12},{9,13},{10,... | collective-permute-start | bytes 3145736 | tf_op jit(solution)/shard_map/ppermute | solution.py:306
  411.6 66.7 %collective-permute-start.30 = (bf16[1024,512]{1,0:T(8,128)(2,1)}, bf16[1024,512]{1,0:T(8,128)(2,1)}, u32[]{:S(2)}, u32[]{:S(2)}) collective-permute-start(bf16[1024,512]{1,0:T(8,128)(2,1)} %get-tuple-element.40), channel_id=1, source_target_pairs={{0,4},{1,5},{2,6},{3,7},{4,0},{5,1},{6,2},{7,3},{8,12},{9,13},{10,... | collective-permute-start | bytes 3145736 | tf_op jit(solution)/shard_map/ppermute | solution.py:306
  444.6 202.8 %collective-permute-start.51 = (bf16[3,4,4,128,704]{3,4,2,1,0:T(8,128)(2,1)}, bf16[3,4,4,128,704]{3,4,2,1,0:T(8,128)(2,1)}, u32[]{:S(2)}, u32[]{:S(2)}) collective-permute-start(bf16[3,4,4,128,704]{3,4,2,1,0:T(8,128)(2,1)} %copy.259), channel_id=1, source_target_pairs={{0,4},{1,5},{2,6},{3,7},{4,0},{5,1},{6,2},{7,3},{8,12},{9,13},{10,... | collective-permute-start | bytes 25952264 | tf_op jit(solution)/shard_map/ppermute | solution.py:306
  449.2 190.3 %collective-permute-start.29 = (bf16[1024,1024]{1,0:T(8,128)(2,1)}, bf16[1024,1024]{1,0:T(8,128)(2,1)}, u32[]{:S(2)}, u32[]{:S(2)}) collective-permute-start(bf16[1024,1024]{1,0:T(8,128)(2,1)} %get-tuple-element.37), channel_id=1, source_target_pairs={{0,0},{1,4},{2,2},{3,6},{4,1},{5,5},{6,3},{7,7},{8,8},{9,12},{10,1... | collective-permute-start | bytes 6291464 | tf_op jit(solution)/shard_map/ppermute | solution.py:306
  474.5 99.3 %collective-permute-start.44 = (bf16[2,2,128,256]{3,2,0,1:T(8,128)(2,1)}, bf16[2,2,128,256]{3,2,0,1:T(8,128)(2,1)}, u32[]{:S(2)}, u32[]{:S(2)}) collective-permute-start(bf16[2,2,128,256]{3,2,0,1:T(8,128)(2,1)} %reverse_select_fusion.6), channel_id=1, source_target_pairs={{0,8},{1,9},{2,10},{3,11},{4,12},{5,13},{6,14},{7,15},{8,0},{9,1},... | collective-permute-start | bytes 786440 | tf_op jit(solution)/shard_map/ppermute | solution.py:306
  476.2 98.7 %collective-permute-start.47 = (bf16[2,2,128,256]{3,2,0,1:T(8,128)(2,1)}, bf16[2,2,128,256]{3,2,0,1:T(8,128)(2,1)}, u32[]{:S(2)}, u32[]{:S(2)}) collective-permute-start(bf16[2,2,128,256]{3,2,0,1:T(8,128)(2,1)} %reverse_select_fusion.4), channel_id=1, source_target_pairs={{0,16},{1,17},{2,18},{3,19},{4,20},{5,21},{6,22},{7,23},{8,24},{9,... | collective-permute-start | bytes 786440 | tf_op jit(solution)/shard_map/ppermute | solution.py:306
  615.1 72.6 %collective-permute-start.31 = (bf16[1024,1024]{1,0:T(8,128)(2,1)}, bf16[1024,1024]{1,0:T(8,128)(2,1)}, u32[]{:S(2)}, u32[]{:S(2)}) collective-permute-start(bf16[1024,1024]{1,0:T(8,128)(2,1)} %project_back.3), channel_id=1, source_target_pairs={{0,4},{1,5},{2,6},{3,7},{4,0},{5,1},{6,2},{7,3},{8,12},{9,13},{10,... | collective-permute-start | bytes 6291464 | tf_op jit(solution)/shard_map/ppermute | solution.py:306
  686.8 100.0 %collective-permute-start.52 = (bf16[2,2,3,128,704]{3,4,2,1,0:T(8,128)(2,1)}, bf16[2,2,3,128,704]{3,4,2,1,0:T(8,128)(2,1)}, u32[]{:S(2)}, u32[]{:S(2)}) collective-permute-start(bf16[2,2,3,128,704]{3,4,2,1,0:T(8,128)(2,1)} %copy.261), channel_id=1, source_target_pairs={{0,8},{1,9},{2,10},{3,11},{4,12},{5,13},{6,14},{7,15},{8,0},{9,1},... | collective-permute-start | bytes 6488072 | tf_op jit(solution)/shard_map/ppermute | solution.py:306
  703.1 91.3 %collective-permute-start.55 = (bf16[2,2,3,128,704]{3,4,2,1,0:T(8,128)(2,1)}, bf16[2,2,3,128,704]{3,4,2,1,0:T(8,128)(2,1)}, u32[]{:S(2)}, u32[]{:S(2)}) collective-permute-start(bf16[2,2,3,128,704]{3,4,2,1,0:T(8,128)(2,1)} %copy.268), channel_id=1, source_target_pairs={{0,16},{1,17},{2,18},{3,19},{4,20},{5,21},{6,22},{7,23},{8,24},{9,... | collective-permute-start | bytes 6488072 | tf_op jit(solution)/shard_map/ppermute | solution.py:306
  731.4 53.0 %collective-permute-start.38 = (bf16[2,2,3,128,256]{3,4,2,0,1:T(8,128)(2,1)S(1)}, bf16[2,2,3,128,256]{3,4,2,0,1:T(8,128)(2,1)S(1)}, u32[]{:S(2)}, u32[]{:S(2)}) collective-permute-start(bf16[2,2,3,128,256]{3,4,2,0,1:T(8,128)(2,1)S(1)} %reverse_select_fusion), channel_id=1, source_target_pairs={{0,16},{1,17},{2,18},{3,19},{4,20},{5,21},{6,22},{7,23},{8,24},{9,... | collective-permute-start | bytes 2359304 | tf_op jit(solution)/shard_map/ppermute | solution.py:306
  767.2 81.7 %collective-permute-start.32 = (bf16[1024,1024]{1,0:T(8,128)(2,1)}, bf16[1024,1024]{1,0:T(8,128)(2,1)}, u32[]{:S(2)}, u32[]{:S(2)}) collective-permute-start(bf16[1024,1024]{1,0:T(8,128)(2,1)} %fusion.3), channel_id=1, source_target_pairs={{0,0},{1,4},{2,2},{3,6},{4,1},{5,5},{6,3},{7,7},{8,8},{9,12},{10,1... | collective-permute-start | bytes 6291464 | tf_op jit(solution)/shard_map/ppermute | solution.py:306
  (77 other events, 1429.4 us)

commit v2 on v1

--- a/solution.py
+++ b/solution.py
@@ -286,6 +286,7 @@
 
 
 AXES = ("dp", "tensor")
+MESH = pl.DeviceIdType.MESH
 TILE = 256
 NEG = -1e30
 F32 = jnp.float32
@@ -302,7 +303,9 @@
         for x in range(2):
             for c in range(2):
                 for t in range(4):
-                    pairs.append((flat(y, x, c, t), flat(*to(y, x, c, t))))
+                    pair = (flat(y, x, c, t), flat(*to(y, x, c, t)))
+                    if pair[0] != pair[1]:
+                        pairs.append(pair)
     return lax.ppermute(values, AXES, pairs)
 
 
@@ -326,41 +329,264 @@
     return move(values, lambda y, x, c, t: (y, x, t % 2, (t // 2) * 2 + c))
 
 
-PIECES = []
-for _c in range(2):
-    PIECES += [
-        [[(_c + 2 * i, j) for j in range(2)] for i in range(2)],
-        [[(_c + 4 + 2 * i, j) for j in range(2)] for i in range(2)],
-        [[(_c + 4 * i, 2 + j) for j in range(2)] for i in range(2)],
-        [[(_c + 2 + 4 * i, 2 + j) for j in range(2)] for i in range(2)],
+def pack_kernel(wq, wk, wv, wo, wg, wu, wd, halves, small, big):
+    small[0] = dot(wq[...], halves[...]).astype(BF16)
+    small[1] = dot(wk[...], halves[...]).astype(BF16)
+    small[2] = wv[...]
+    small[3] = wo[...].T
+    for n, turned in enumerate((wg[...].T, wu[...].T, wd[...])):
+        big[n] = turned.reshape(big.shape[1:])
+
+
+def pack(wq, wk, wv, wo, wg, wu, wd):
+    rows, part = wg.shape
+    lane = jnp.arange(256, dtype=jnp.int32)
+    source = ((lane & 127) >> 5) * 64 + (lane >> 7) * 32 + (lane & 31)
+    halves = (lane[:, None] == source[None, :]).astype(BF16)
+    return pl.pallas_call(
+        pack_kernel,
+        out_shape=[
+            jax.ShapeDtypeStruct((4, rows, 256), BF16),
+            jax.ShapeDtypeStruct((3, 2, part // 2, rows), BF16),
+        ],
+        compiler_params=params(),
+        name="pack",
+    )(wq, wk, wv, wo, wg, wu, wd, halves)
+
+
+def gather_kernel(tok, fv, small, big, row, first, g_small, g_big, send, recv, swap, fsend, frecv, here):
+    dp, t = lax.axis_index("dp"), lax.axis_index("tensor")
+    c, x, y = lax.rem(dp, 2), lax.rem(lax.div(dp, 2), 2), lax.div(dp, 4)
+    pair, side = lax.div(t, 2), lax.rem(t, 2)
+    plane = dp - c
+    dpx, dpy, dpc = dp + 2 - 4 * x, dp + 4 - 8 * y, dp + 1 - 2 * c
+    dpxy = dpx + 4 - 8 * y
+
+    barrier = pltpu.get_barrier_semaphore()
+    for e in range(2):
+        for d in range(4):
+            if e or d:
+                other = plane + (c + e) - 2 * lax.div(c + e, 2)
+                pl.semaphore_signal(barrier, inc=1, device_id=(other, lax.rem(t + d, 4)), device_id_type=MESH)
+    pl.semaphore_signal(barrier, inc=1, device_id=(dpx, t), device_id_type=MESH)
+    pl.semaphore_signal(barrier, inc=1, device_id=(dpy, t), device_id_type=MESH)
+    pl.semaphore_wait(barrier, 9)
+
+    dist = [lax.rem(t + 4 - d, 4) for d in range(4)]
+
+    def slot(k, at, owner, h):
+        if k == 0:
+            return g_small.at[pl.ds(2 * h, 2), at, pl.ds(owner * 128, 128), :]
+        return g_big.at[k - 1, owner, h, at]
+
+    def column(k, owner, h):
+        if k == 0:
+            return g_small.at[pl.ds(2 * h, 2), :, pl.ds(owner * 128, 128), :]
+        return g_big.at[k - 1, owner, h]
+
+    def both(k, at, owner):
+        if k == 0:
+            return g_small.at[:, at, pl.ds(owner * 128, 128), :]
+        return g_big.at[k - 1, owner, :, at]
+
+    def all_of(k, owner):
+        if k == 0:
+            return g_small.at[:, :, pl.ds(owner * 128, 128), :]
+        return g_big.at[k - 1, owner]
+
+    def shard(k):
+        return small if k == 0 else big.at[k - 1]
+
+    def part_of(k, h):
+        return small.at[pl.ds(2 * h, 2)] if k == 0 else big.at[k - 1, h]
+
+    def copy(k, n, src, dst, to, at):
+        return pltpu.make_async_remote_copy(
+            src_ref=src,
+            dst_ref=dst,
+            send_sem=send.at[k, n],
+            recv_sem=recv.at[k, n],
+            device_id=(to, at),
+            device_id_type=MESH,
+        )
+
+    chunks = 4
+    near, far = (dpx, dpy), (dpy, dpx)
+    along = [[copy(k, d - 1, shard(k), both(k, t, dp), dp, lax.rem(t + d, 4)) for d in (1, 2, 3)] for k in range(chunks)]
+    onward = [[[copy(k, 3 + h, part_of(k, h), slot(k, t, dp, h), near[h], t) for h in range(2)]] for k in range(chunks)]
+    kept = [pltpu.make_async_copy(shard(k), both(k, t, dp), here.at[k]) for k in range(chunks)]
+    for k in range(chunks):
+        onward[k] += [
+            [copy(k, 3 + 2 * d + h, slot(k, dist[d], dp, h), slot(k, dist[d], dp, h), near[h], t) for h in range(2)]
+            for d in (1, 2, 3)
+        ]
+    across = [
+        [
+            copy(k, 11 + 2 * h + i, column(k, owner, h), column(k, owner, h), far[h], t)
+            for h in range(2)
+            for i, owner in enumerate((dp, near[h]))
+        ]
+        for k in range(chunks)
     ]
-
-
-def gather_pieces(shard):
-    along = [shard] + [along_t(shard, d) for d in (1, 2, 3)]
-    first = jnp.stack(along[:2])
-    second = jnp.stack(along[2:])
-    first = jnp.stack([first, across_x(first)])
-    second = jnp.stack([second, across_y(second)])
-    own = [first, across_y(first), second, across_x(second)]
-    return own + [across_c(piece) for piece in own]
-
-
-def start_loads(pieces, which, held, sem, me, t):
-    for array, places in zip(pieces, PIECES, strict=True):
-        for i in range(2):
-            for j in range(2):
-                rel, dist = places[i][j]
-                block = (me ^ rel) * 128
-                pltpu.make_async_copy(
-                    array.at[i, j, which],
-                    held.at[(t - dist) & 3, pl.ds(pl.multiple_of(block, 128), 128), :],
-                    sem,
-                ).start()
-
-
-def wait_loads(held, sem):
-    pltpu.make_async_copy(held, held, sem).wait()
+    over = [
+        [copy(k, 15 + i, all_of(k, owner), all_of(k, owner), dpc, t) for i, owner in enumerate((dp, dpx, dpy, dpxy))]
+        for k in range(chunks)
+    ]
+
+    for item in along[0] + onward[0][0] + kept:
+        item.start()
+    for k in range(1, chunks):
+        for item in onward[k][0]:
+            item.start()
+
+    moved = side != c
+    to_own = pltpu.make_async_copy(tok, row.at[c], here.at[4])
+    swapped = pltpu.make_async_remote_copy(
+        src_ref=tok,
+        dst_ref=row.at[side],
+        send_sem=swap.at[0],
+        recv_sem=swap.at[1],
+        device_id=(plane + side, 2 * pair + c),
+        device_id_type=MESH,
+    )
+
+    def start_tokens():
+        @pl.when(moved)
+        def _():
+            swapped.start()
+
+        @pl.when(jnp.logical_not(moved))
+        def _():
+            to_own.start()
+
+    heads_core, slab = pair, side
+
+    def first_copy(p):
+        return pltpu.make_async_remote_copy(
+            src_ref=fv.at[pl.ds(p * SEQ, SEQ), :],
+            dst_ref=first.at[slab],
+            send_sem=fsend.at[p],
+            recv_sem=frecv.at[slab],
+            device_id=(plane + heads_core, 2 * p + c),
+            device_id_type=MESH,
+        )
+
+    def first_local(p):
+        return pltpu.make_async_copy(fv.at[pl.ds(p * SEQ, SEQ), :], first.at[slab], here.at[5])
+
+    stays = [(heads_core == c) & (t == 2 * p + c) for p in range(2)]
+
+    def start_first():
+        for p in range(2):
+
+            @pl.when(stays[p])
+            def _():
+                first_local(p).start()
+
+            @pl.when(jnp.logical_not(stays[p]))
+            def _():
+                first_copy(p).start()
+
+    for step in range(chunks + 2):
+        if step < chunks:
+            for item in along[step]:
+                item.wait_recv()
+            kept[step].wait()
+            if step + 1 < chunks:
+                for item in along[step + 1]:
+                    item.start()
+            if step == 0:
+                start_tokens()
+            if step == 1:
+                start_first()
+            for pair_of in onward[step][1:]:
+                for item in pair_of:
+                    item.start()
+            over[step][0].start()
+        if 0 <= step - 1 < chunks:
+            for pair_of in onward[step - 1]:
+                for item in pair_of:
+                    item.wait_recv()
+            for item in across[step - 1]:
+                item.start()
+        if 0 <= step - 2 < chunks:
+            for item in across[step - 2]:
+                item.wait_recv()
+            for item in over[step - 2][1:]:
+                item.start()
+
+    @pl.when(moved)
+    def _():
+        swapped.wait_send()
+        swapped.wait_recv()
+
+    @pl.when(jnp.logical_not(moved))
+    def _():
+        to_own.wait()
+
+    given = pltpu.make_async_remote_copy(
+        src_ref=row.at[c],
+        dst_ref=row.at[c],
+        send_sem=swap.at[2],
+        recv_sem=swap.at[3],
+        device_id=(dpc, t),
+        device_id_type=MESH,
+    )
+    given.start()
+    for p in range(2):
+
+        @pl.when(stays[p])
+        def _():
+            first_local(p).wait()
+
+        @pl.when(jnp.logical_not(stays[p]))
+        def _():
+            first_copy(p).wait_send()
+
+    for u in range(2):
+        came = pltpu.make_async_remote_copy(
+            src_ref=first.at[u],
+            dst_ref=first.at[u],
+            send_sem=fsend.at[u],
+            recv_sem=frecv.at[u],
+            device_id=(dpc, t),
+            device_id_type=MESH,
+        )
+
+        @pl.when((side != c) | (t != 2 * c + u))
+        def _():
+            came.wait_recv()
+
+    given.wait()
+    for k in range(chunks):
+        for item in over[k]:
+            item.wait_recv()
+        for item in along[k] + across[k] + over[k]:
+            item.wait_send()
+        for pair_of in onward[k]:
+            for item in pair_of:
+                item.wait_send()
+
+
+def gather(tok, fv, small, big):
+    part, rows = big.shape[2:]
+    wide = tok.shape[1]
+    vmem = pl.BlockSpec(memory_space=pltpu.VMEM)
+    sems = pltpu.SemaphoreType.DMA
+    return pl.pallas_call(
+        gather_kernel,
+        out_shape=[
+            jax.ShapeDtypeStruct((2, SEQ // 2, wide), BF16),
+            jax.ShapeDtypeStruct((2, SEQ, 256), BF16),
+            jax.ShapeDtypeStruct((4, 4, wide, 256), BF16),
+            jax.ShapeDtypeStruct((3, 8, 2, 4, part, rows), BF16),
+        ],
+        in_specs=[vmem] * 4,
+        out_specs=[any_spec()] * 4,
+        scratch_shapes=[sems((4, 19)), sems((4, 19)), sems((4,)), sems((2,)), sems((2,)), sems((6,))],
+        compiler_params=params(collective_id=0, has_side_effects=True),
+        name="gather",
+    )(tok, fv, small, big)
 
 
 def dot(left, right):
@@ -387,59 +613,41 @@
     return pl.CostEstimate(flops=int(flops), bytes_accessed=int(size), transcendentals=int(exps))
 
 
-def project_kernel(at, own, other, fv0, fv1, cosine, sine, gain, *rest):
-    pieces, (normed_out, q_out, k_out, v_out, wq, wk, wv, sems) = rest[:8], rest[8:]
-    step = pl.program_id(0)
-    me, t = at[0], at[1]
-    c, pair = me & 1, t >> 1
-
-    @pl.when(step == 0)
-    def _():
-        for n, held in enumerate((wq, wk, wv)):
-            start_loads(pieces, n, held, sems.at[n], me, t)
-        for n, held in enumerate((wq, wk, wv)):
-            wait_loads(held, sems.at[n])
-
-    values = jnp.where(step < 2, own[...], other[...]).astype(F32)
+def project_kernel(at, tok, first, cosine, sine, gain, held, normed_out, q_out, k_out, v_out):
+    values = tok[0].astype(F32)
     factor = lax.rsqrt(jnp.mean(values * values, axis=1, keepdims=True) + EPSILON)
     normed = (values * factor * gain[...]).astype(BF16)
     normed_out[...] = normed
     cos, sin = cosine[...], sine[...]
     for u in range(2):
-        shard = 2 * c + u
-        for held, out, scale in ((wq, q_out, 0.125), (wk, k_out, 1.0)):
-            raw = dot(normed, held[shard])
+        for n, out, scale in ((0, q_out, 0.125), (1, k_out, 1.0)):
+            raw = dot(normed, held[n, u])
             a, b = raw[:, :128], raw[:, 128:]
             out[:, u * 256 : u * 256 + 128] = ((a * cos - b * sin) * scale).astype(BF16)
             out[:, u * 256 + 128 : u * 256 + 256] = ((b * cos + a * sin) * scale).astype(BF16)
-        raw = dot(normed, wv[shard])
-        first = jnp.where(pair == u, fv0[...], fv1[...]).astype(F32)
-        v_out[:, u * 256 : u * 256 + 256] = (0.5 * raw + 0.5 * first).astype(BF16)
-
-
-def project(at, own, other, fv, cosine, sine, gain, pieces):
-    rows, wide = 512, own.shape[1]
-
-    def place(i, at):
-        half = jnp.where(i < 2, at[0] & 1, 1 - (at[0] & 1))
-        return half * 2 + (i & 1)
-
-    row = lambda width: pl.BlockSpec((rows, width), lambda i, at: (place(i, at), 0))
+        raw = dot(normed, held[2, u])
+        v_out[:, u * 256 : u * 256 + 256] = (0.5 * raw + 0.5 * first[u].astype(F32)).astype(BF16)
+
+
+def once(shape, place):
+    return pl.BlockSpec(shape, place, pipeline_mode=pl.Buffered(1))
+
+
+def project(at, tok, first, cosine, sine, gain, small):
+    rows, wide = 512, tok.shape[2]
+    row = lambda width: pl.BlockSpec((rows, width), lambda i, at: (i, 0))
     grid = pltpu.PrefetchScalarGridSpec(
         num_scalar_prefetch=1,
         grid=(4,),
         in_specs=[
-            pl.BlockSpec((rows, wide), lambda i, at: (jnp.minimum(i, 1), 0)),
-            pl.BlockSpec((rows, wide), lambda i, at: (jnp.maximum(i - 2, 0), 0)),
-            row(256),
-            row(256),
+            pl.BlockSpec((1, rows, wide), lambda i, at: (i // 2, i % 2, 0)),
+            pl.BlockSpec((2, rows, 256), lambda i, at: (0, i, 0)),
             row(128),
             row(128),
             pl.BlockSpec((1, wide), lambda i, at: (0, 0)),
-        ]
-        + [any_spec()] * 8,
+            once((4, 2, wide, 256), lambda i, at: (0, at[0] & 1, 0, 0)),
+        ],
         out_specs=[row(wide), row(512), row(512), row(512)],
-        scratch_shapes=[pltpu.VMEM((4, wide, 256), BF16)] * 3 + [pltpu.SemaphoreType.DMA((3,))],
     )
     return pl.pallas_call(
         project_kernel,
@@ -449,7 +657,7 @@
         compiler_params=params(),
         cost_estimate=cost(2 * SEQ * wide * 1536, 24e6),
         name="project",
-    )(at, own, other, fv[0], fv[1], cosine, sine, gain, *pieces)
+    )(at, tok, first, cosine, sine, gain, small)
 
 
 def head_masks(rows):
@@ -660,49 +868,51 @@
     )(bounds, q, k, v, do, o, lse, starts, cosine, sine)
 
 
-def mlp_kernel(at, att_own, att_other, tok, cot, gain, *rest):
-    small, big, rest = rest[:8], rest[8:16], rest[16:]
-    (out, gh_out, gb_out, n2_out, hid_out, ga_own, ga_other, gg_out) = rest[:8]
-    (wo, wg, wu, wd, sems) = rest[8:]
+def mlp_kernel(at, att_own, att_other, tok, cot_here, cot_moved, gain, wo, big, *rest):
+    (out, gh_out, gb_out, n2_out, hid_out, ga_own, ga_other, gg_out, cot_out) = rest[:9]
+    (wg, wu, wd, sems) = rest[9:]
     step = pl.program_id(0)
-    me, t = at[0], at[1]
-    c = me & 1
+    c = at[0] & 1
 
     @pl.when(step == 0)
     def _():
-        start_loads(small, 3, wo, sems.at[0], me, t)
         for n, held in enumerate((wg, wu, wd)):
-            start_loads(big, n, held, sems.at[1 + n], me, t)
-        wait_loads(wo, sems.at[0])
+            for owner in range(8):
+                pltpu.make_async_copy(
+                    big.at[n, owner], held.at[:, owner * 128 : owner * 128 + 128], sems.at[n]
+                ).start()
         gg_out[...] = jnp.zeros_like(gg_out)
 
-    hidden = tok[...].astype(F32)
+    hidden = tok[0].astype(F32)
     for e, att in enumerate((att_own, att_other)):
         for u in range(2):
-            hidden += dot_nt(att[:, u * 256 : u * 256 + 256], wo[2 * (c ^ e) + u])
+            hidden += dot_nt(att[:, u * 256 : u * 256 + 256], wo[0, 2 * (c ^ e) + u])
     factor = lax.rsqrt(jnp.mean(hidden * hidden, axis=1, keepdims=True) + EPSILON)
     gains = gain[...]
     normed = (hidden * factor * gains).astype(BF16)
     n2_out[...] = normed
-    g = cot[...]
+    g = jnp.where((at[1] & 1) == c, cot_here[...], cot_moved[...])
+    cot_out[...] = g
 
     @pl.when(step == 0)
     def _():
         for n, held in enumerate((wg, wu, wd)):
-            wait_loads(held, sems.at[1 + n])
+            pltpu.make_async_copy(held, held, sems.at[n]).wait()
 
     down = jnp.zeros_like(hidden)
     back = jnp.zeros_like(hidden)
-    for k in range(4):
-        gate, up, grad_act = dot(normed, wg[k]), dot(normed, wu[k]), dot(g, wd[k])
+    units = wg.shape[0]
+    for low in range(0, units, 768):
+        part = slice(low, min(low + 768, units))
+        gate, up, grad_act = dot_nt(normed, wg[part]), dot_nt(normed, wu[part]), dot_nt(g, wd[part])
         sig = 1.0 / (1.0 + jnp.exp(-gate))
         silu = gate * sig
         act = (silu * up).astype(BF16)
         grad_up = (grad_act * silu).astype(BF16)
         grad_gate = (grad_act * up * (sig * (1.0 + gate * (1.0 - sig)))).astype(BF16)
-        hid_out[0, k], hid_out[1, k], hid_out[2, k] = grad_gate, grad_up, act
-        down += dot_nt(act, wd[k])
-        back += dot_nt(grad_gate, wg[k]) + dot_nt(grad_up, wu[k])
+        hid_out[0, :, part], hid_out[1, :, part], hid_out[2, :, part] = grad_gate, grad_up, act
+        down += dot(act, wd[part])
+        back += dot(grad_gate, wg[part]) + dot(grad_up, wu[part])
     out[...] = (hidden + down).astype(BF16)
     gg_out[...] += jnp.sum((back * hidden * factor).reshape(-1, 8, back.shape[1]), axis=0)
     scaled = back * gains
@@ -713,31 +923,39 @@
     gb_out[...] = branch
     for e, ga in enumerate((ga_own, ga_other)):
         for u in range(2):
-            ga[:, u * 256 : u * 256 + 256] = dot(branch, wo[2 * (c ^ e) + u]).astype(BF16)
-
-
-def mlp(at, att_own, att_other, tok, cot, gain, small, big):
-    count, wide = tok.shape
-    rows, part = 256, big[0].shape[-1]
+            ga[:, u * 256 : u * 256 + 256] = dot(branch, wo[0, 2 * (c ^ e) + u]).astype(BF16)
+
+
+def mlp(at, att_own, att_other, tok, cot_here, cot_moved, gain, small, big):
+    _, count, wide = tok.shape
+    big = big.reshape(3, 8, -1, 128)
+    rows, units = 256, big.shape[2]
     row = lambda width: pl.BlockSpec((rows, width), lambda i, at: (i, 0))
-    one = pl.BlockSpec((1, wide), lambda i, at: (0, 0))
     grid = pltpu.PrefetchScalarGridSpec(
         num_scalar_prefetch=1,
         grid=(count // rows,),
-        in_specs=[row(512), row(512), row(wide), row(wide), one] + [any_spec()] * 16,
+        in_specs=[
+            row(512),
+            row(512),
+            pl.BlockSpec((1, rows, wide), lambda i, at: (at[0] & 1, i, 0)),
+            row(wide),
+            row(wide),
+            pl.BlockSpec((1, wide), lambda i, at: (0, 0)),
+            once((1, 4, wide, 256), lambda i, at: (3, 0, 0, 0)),
+            any_spec(),
+        ],
         out_specs=[
             row(wide),
             row(wide),
             row(wide),
             row(wide),
-            pl.BlockSpec((3, 4, rows, part), lambda i, at: (0, 0, i, 0)),
+            pl.BlockSpec((3, rows, units), lambda i, at: (0, i, 0)),
             row(512),
             row(512),
             pl.BlockSpec((8, wide), lambda i, at: (0, 0)),
+            row(wide),
         ],
-        scratch_shapes=[pltpu.VMEM((4, wide, 256), BF16)]
-        + [pltpu.VMEM((4, wide, part), BF16)] * 3
-        + [pltpu.SemaphoreType.DMA((4,))],
+        scratch_shapes=[pltpu.VMEM((units, wide), BF16)] * 3 + [pltpu.SemaphoreType.DMA((3,))],
     )
     tokens = lambda width, kind=BF16: jax.ShapeDtypeStruct((count, width), kind)
     return pl.pallas_call(
@@ -747,211 +965,398 @@
             tokens(wide, F32),
             tokens(wide),
             tokens(wide),
-            jax.ShapeDtypeStruct((3, 4, count, part), BF16),
+            jax.ShapeDtypeStruct((3, count, units), BF16),
             tokens(512),
             tokens(512),
             jax.ShapeDtypeStruct((8, wide), F32),
+            tokens(wide),
         ],
         grid_spec=grid,
         compiler_params=params(),
-        cost_estimate=cost(2 * count * wide * (6 * 4 * part + 2 * wide), 60e6, 3e6),
+        cost_estimate=cost(2 * count * wide * (6 * units + 2 * wide), 60e6, 3e6),
         name="mlp",
-    )(at, att_own, att_other, tok, cot, gain, *small, *big)
-
-
-def turn_rows(source, parity, held):
-    for r in range(4):
-        block = source[:, pl.ds(pl.multiple_of((r * 2 + parity) * 128, 128), 128)]
-        held[r * 128 : (r + 1) * 128, :] = block.T
-
-
-def weight_send_kernel(at, n2, g, hid, out, turned):
-    n, k = pl.program_id(0), pl.program_id(1)
-    parity = 1 - (at[0] & 1)
-
-    @pl.when((n == 0) & (k == 0))
+    )(at, att_own, att_other, tok, cot_here, cot_moved, gain, small, big)
+
+
+def turn_rows(source, plane, parity, held):
+    for rel in range(4):
+        block = ((plane ^ rel) * 2 + parity) * 128
+        held[rel * 128 : rel * 128 + 128, :] = source[:, pl.ds(pl.multiple_of(block, 128), 128)].T
+
+
+def place_first(send, keep, done, lanes):
+    for yr in range(2):
+        keep[yr, :, lanes] = done[2 * yr]
+        send[yr, :, lanes] = done[2 * yr + 1]
+
+
+def place_second(send, keep, done, lanes):
+    for xr in range(2):
+        keep[xr, :, lanes] = done[xr]
+        send[xr, :, lanes] = done[2 + xr]
+
+
+def weights_kernel(n2, g, branch, hid, own, other, send1, keep1, send2, keep2, turned, given, got, out_sem, in_sem):
+    step = pl.program_id(0)
+    dp, t = lax.axis_index("dp"), lax.axis_index("tensor")
+    c = lax.rem(dp, 2)
+    plane = lax.div(dp, 2)
+    n = lax.rem(step, 4)
+    units = hid.shape[2] // 2
+
+    @pl.when(step == 0)
     def _():
-        turn_rows(n2, parity, turned)
-
-    @pl.when((n == 2) & (k == 0))
+        barrier = pltpu.get_barrier_semaphore()
+        pl.semaphore_signal(barrier, inc=1, device_id=(dp + 1 - 2 * c, t), device_id_type=MESH)
+        pl.semaphore_wait(barrier, 1)
+
+    def exchange(k):
+        lanes = pl.ds(k * units, units if k < 3 else 512)
+        return pltpu.make_async_remote_copy(
+            src_ref=given.at[:, :, :, lanes],
+            dst_ref=got.at[:, :, :, lanes],
+            send_sem=out_sem.at[k],
+            recv_sem=in_sem.at[k],
+            device_id=(dp + 1 - 2 * c, t),
+            device_id_type=MESH,
+        )
+
+    for phase, parity in ((0, 1 - c), (1, c)):
+        for at_n, source in ((0, n2), (2, g), (3, branch)):
+
+            @pl.when(step == 4 * phase + at_n)
+            def _():
+                x = lax.rem(plane, 2)
+                y = lax.div(plane, 2)
+                for rel in range(4):
+                    yy, xx = (y, 1 - y)[rel // 2], (x, 1 - x)[rel % 2]
+                    block = pl.multiple_of((yy * 4 + xx * 2 + parity) * 128, 128)
+                    turned[rel * 128 : rel * 128 + 128, :] = source[:, pl.ds(block, 128)].T
+
+    def heads(h):
+        return jnp.where(c == h, own[...], other[...])
+
+    @pl.when(step < 3)
     def _():
-        turn_rows(g, parity, turned)
-
-    out[0, 0] = dot(turned[...], hid[0, 0]).astype(BF16).reshape(out.shape[2:])
-
-
-def weight_send(at, n2, g, hid):
+        for h in range(2):
+            product = dot(turned[...], hid[0, :, h * units : h * units + units]).astype(BF16)
+            given[:, h, :, pl.ds(pl.multiple_of(n * units, 128), units)] = product.reshape(4, 128, units)
+
+    @pl.when(step == 3)
+    def _():
+        for h in range(2):
+            product = dot(turned[...], heads(h)).astype(BF16)
+            given[:, h, :, 3 * units : 3 * units + 512] = product.reshape(4, 128, 512)
+
+    for k in range(4):
+
+        @pl.when(step == k + 1)
+        def _():
+            exchange(k).start()
+
+        @pl.when(step == k + 4)
+        def _():
+            exchange(k).wait_recv()
+
+    def keep(product, h, lanes):
+        done = [(product[r * 128 : r * 128 + 128] + got[r, h, :, lanes].astype(F32)).astype(BF16) for r in range(4)]
+        (place_first, place_second)[h](*((send1, keep1), (send2, keep2))[h], done, lanes)
+
+    @pl.when((step >= 4) & (step < 7))
+    def _():
+        for h in range(2):
+            product = dot(turned[...], hid[0, :, h * units : h * units + units])
+            keep(product, h, pl.ds(pl.multiple_of(n * units, 128), units))
+
+    @pl.when(step == 7)
+    def _():
+        for h in range(2):
+            keep(dot(turned[...], heads(h)), h, pl.ds(3 * units, 512))
+        for k in range(4):
+            exchange(k).wait_send()
+
+
+def weights(n2, g, branch, hid, own, other):
     count, wide = n2.shape
-    part = hid.shape[-1]
-    whole = pl.BlockSpec((count, wide), lambda n, k, at: (0, 0))
+    units = hid.shape[2] // 2
+    full = lambda *shape: pl.BlockSpec(shape, lambda s: (0,) * len(shape), pipeline_mode=pl.Buffered(1))
+    length = 3 * units + 512
+    grid = pl.GridSpec(
+        grid=(8,),
+        in_specs=[
+            full(count, wide),
+            full(count, wide),
+            full(count, wide),
+            pl.BlockSpec((1, count, 2 * units), lambda s: (jnp.minimum(lax.rem(s, 4), 2), 0, 0)),
+            full(count, 512),
+            full(count, 512),
+        ],
+        out_specs=[full(2, 128, length)] * 4,
+        scratch_shapes=[
+            pltpu.VMEM((512, count), BF16),
+            pltpu.VMEM((4, 2, 128, length), BF16),
+            pltpu.VMEM((4, 2, 128, length), BF16),
+            pltpu.SemaphoreType.DMA((4,)),
+            pltpu.SemaphoreType.DMA((4,)),
+        ],
+    )
+    return pl.pallas_call(
+        weights_kernel,
+        out_shape=[jax.ShapeDtypeStruct((2, 128, length), BF16)] * 4,
+        grid_spec=grid,
+        compiler_params=params(collective_id=1, has_side_effects=True),
+        cost_estimate=cost(2 * count * 1024 * length * 2, 50e6),
+        name="weights",
+    )(n2, g, branch, hid, own, other)
+
+
+def add(left, right):
+    return (left.astype(F32) + right.astype(F32)).astype(BF16)
+
+
+def scatter_xy(keep1, got1, keep2, got2):
+    last1, last2 = across_y(add(keep1[1], got1[1])), across_x(add(keep2[1], got2[1]))
+    return add(keep1[0], got1[0]), last1, add(keep2[0], got2[0]), last2
+
+
+def turn_kernel(at, kept1, got1, kept2, got2, out, *, units):
+    t = at[1]
+    sums = [kept1[...].astype(F32) + got1[...].astype(F32), kept2[...].astype(F32) + got2[...].astype(F32)]
+    part = units // 4
+    for h in range(2):
+        for n in range(3):
+            turned = sums[h][:, n * units : n * units + units].T.astype(BF16)
+            for i in range(4):
+                rows = slice((2 * n + h) * part, (2 * n + h + 1) * part)
+                out[(i - t) & 3, rows, :] = turned[i * part : (i + 1) * part]
+        turned = sums[h][:, 3 * units :].T.astype(BF16)
+        for i in range(2):
+            out[(2 * h + i - t) & 3, 6 * part :, :] = turned[i * 256 : i * 256 + 256]
+
+
+def turn(at, arrays, units):
+    vmem = pl.BlockSpec(memory_space=pltpu.VMEM)
+    rows = 3 * (units // 2) + 256
+    return pl.pallas_call(
+        functools.partial(turn_kernel, units=units),
+        out_shape=jax.ShapeDtypeStruct((4, rows, 128), BF16),
+        in_specs=[pl.BlockSpec(memory_space=pltpu.SMEM)] + [vmem] * 4,
+        out_specs=vmem,
+        compiler_params=params(),
+        cost_estimate=cost(1e6, 8e6),
+        name="turn",
+    )(at, *arrays)
+
+
+def final_kernel(a, b, c, d, gate, up, down, out):
+    total = a[...].astype(F32) + b[...].astype(F32) + c[...].astype(F32) + d[...].astype(F32)
+    part = down.shape[0]
+    gate[...] = total[:part].T
+    up[...] = total[part : 2 * part].T
+    down[...] = total[2 * part : 3 * part]
+    out[...] = total[3 * part :]
+
+
+def scatter_t(pieces):
+    return [pieces[0]] + [along_t(pieces[d], d) for d in (1, 2, 3)]
+
+
+def final(pieces, part):
+    return pl.pallas_call(
+        final_kernel,
+        out_shape=[
+            jax.ShapeDtypeStruct((128, part), F32),
+            jax.ShapeDtypeStruct((128, part), F32),
+            jax.ShapeDtypeStruct((part, 128), F32),
+            jax.ShapeDtypeStruct((256, 128), F32),
+        ],
+        compiler_params=params(),
+        cost_estimate=cost(1e6, 4e6),
+        name="final",
+    )(*pieces)
+
+
+def project_back_kernel(at, dq, dk, dv, held, out):
+    out[...] = back_product(dq, dk, dv, held).astype(out.dtype)
+
+
+def back_product(dq, dk, dv, held):
+    total = None
+    for u in range(2):
+        for n, grad in enumerate((dq, dk, dv)):
+            term = dot_nt(grad[:, u * 256 : u * 256 + 256], held[n, u])
+            total = term if total is None else total + term
+    return total
+
+
+def back_specs(rows, other, wide):
+    half = SEQ // 2 // rows
+    row = pl.BlockSpec((rows, 512), lambda i, at: (((at[0] & 1) ^ other) * half + i, 0))
+    return [row] * 3 + [once((4, 2, wide, 256), lambda i, at: (0, at[0] & 1, 0, 0))]
+
+
+def project_back_send(at, dq, dk, dv, small):
+    rows, wide = 512, small.shape[2]
     grid = pltpu.PrefetchScalarGridSpec(
         num_scalar_prefetch=1,
-        grid=(3, 4),
-        in_specs=[whole, whole, pl.BlockSpec((1, 1, count, part), lambda n, k, at: (n, k, 0, 0))],
-        out_specs=pl.BlockSpec((1, 1, 4, 128, part), lambda n, k, at: (n, k, 0, 0, 0)),
-        scratch_shapes=[pltpu.VMEM((512, count), BF16)],
+        grid=(SEQ // 2 // rows,),
+        in_specs=back_specs(rows, 1, wide),
+        out_specs=pl.BlockSpec((rows, wide), lambda i, at: (i, 0)),
     )
     return pl.pallas_call(
-        weight_send_kernel,
-        out_shape=jax.ShapeDtypeStruct((3, 4, 4, 128, part), BF16),
+        project_back_kernel,
+        out_shape=jax.ShapeDtypeStruct((SEQ // 2, wide), BF16),
         grid_spec=grid,
         compiler_params=params(),
-        cost_estimate=cost(2 * count * 512 * part * 12, 30e6),
-        name="weight_send",
-    )(at, n2, g, hid)
-
-
-def weight_keep_kernel(at, n2, g, hid, got, first_send, first_keep, second_send, second_keep, turned):
-    n, d = pl.program_id(0), pl.program_id(1)
-    me = at[0]
-
-    @pl.when((n == 0) & (d == 0))
+        cost_estimate=cost(SEQ * wide * 1536, 10e6),
+        name="project_back_send",
+    )(at, dq, dk, dv, small)
+
+
+def project_back_keep_kernel(at, dq, dk, dv, held, got, tok, grad_hidden, gain, out, gain_out):
+    @pl.when(pl.program_id(0) == 0)
     def _():
-        turn_rows(n2, me & 1, turned)
-
-    @pl.when((n == 2) & (d == 0))
-    def _():
-        turn_rows(g, me & 1, turned)
-
-    def block(rel):
-        index = (me >> 1) ^ rel
-        rows = turned[pl.ds(pl.multiple_of(index * 128, 128), 128), :]
-        return rows, got[0, 0, index].astype(F32)
-
-    rows, extra = zip(*[block(rel) for rel in range(4)], strict=True)
-    product = dot(jnp.concatenate(rows, axis=0), hid[0, 0])
-    done = [(product[r * 128 : (r + 1) * 128] + extra[r]).astype(BF16) for r in range(4)]
-
-    @pl.when(d < 2)
-    def _():
-        first_send[0, 0, 0], first_send[0, 1, 0] = done[1], done[3]
-        first_keep[0, 0, 0], first_keep[0, 1, 0] = done[0], done[2]
-
-    @pl.when(d >= 2)
-    def _():
-        second_send[0, 0, 0], second_send[0, 1, 0] = done[2], done[3]
-        second_keep[0, 0, 0], second_keep[0, 1, 0] = done[0], done[1]
-
-
-def weight_keep(at, n2, g, hid, got):
-    count, wide = n2.shape
-    part = hid.shape[-1]
-    whole = pl.BlockSpec((count, wide), lambda n, d, at: (0, 0))
-    first = pl.BlockSpec((1, 2, 1, 128, part), lambda n, d, at: (jnp.minimum(d, 1), 0, n, 0, 0))
-    second = pl.BlockSpec((1, 2, 1, 128, part), lambda n, d, at: (jnp.maximum(d - 2, 0), 0, n, 0, 0))
+        gain_out[...] = jnp.zeros_like(gain_out)
+
+    grad = back_product(dq, dk, dv, held) + got[...].astype(F32)
+    values = tok[0].astype(F32)
+    factor = lax.rsqrt(jnp.mean(values * values, axis=1, keepdims=True) + EPSILON)
+    gain_out[...] += jnp.sum((grad * values * factor).reshape(-1, 8, grad.shape[1]), axis=0)
+    scaled = grad * gain[...]
+    mean = jnp.mean(scaled * values, axis=1, keepdims=True)
+    out[...] = (grad_hidden[...] + factor * scaled - values * (factor * factor * factor * mean)).astype(BF16)
+
+
+def project_back_keep(at, dq, dk, dv, small, got, tok, grad_hidden, gain):
+    rows, wide = 512, small.shape[2]
+    row = pl.BlockSpec((rows, wide), lambda i, at: (i, 0))
     grid = pltpu.PrefetchScalarGridSpec(
         num_scalar_prefetch=1,
-        grid=(3, 4),
-        in_specs=[
-            whole,
-            whole,
-            pl.BlockSpec((1, 1, count, part), lambda n, d, at: (n, (at[1] + d) & 3, 0, 0)),
-            pl.BlockSpec((1, 1, 4, 128, part), lambda n, d, at: (n, (at[1] + d) & 3, 0, 0, 0)),
+        grid=(SEQ // 2 // rows,),
+        in_specs=back_specs(rows, 0, wide)
+        + [
+            row,
+            pl.BlockSpec((1, rows, wide), lambda i, at: (at[0] & 1, i, 0)),
+            row,
+            pl.BlockSpec((1, wide), lambda i, at: (0, 0)),
         ],
-        out_specs=[first, first, second, second],
-        scratch_shapes=[pltpu.VMEM((512, count), BF16)],
+        out_specs=[row, pl.BlockSpec((8, wide), lambda i, at: (0, 0))],
     )
     return pl.pallas_call(
-        weight_keep_kernel,
-        out_shape=[jax.ShapeDtypeStruct((2, 2, 3, 128, part), BF16)] * 4,
+        project_back_keep_kernel,
+        out_shape=[jax.ShapeDtypeStruct((SEQ // 2, wide), BF16), jax.ShapeDtypeStruct((8, wide), F32)],
         grid_spec=grid,
         compiler_params=params(),
-        cost_estimate=cost(2 * count * 512 * part * 12, 40e6),
-        name="weight_keep",
-    )(at, n2, g, hid, got)
-
-
-def add(left, right):
-    return (left.astype(F32) + right.astype(F32)).astype(BF16)
-
-
-def scatter_xy(first_send, first_keep, second_send, second_keep):
-    got = across_x(first_send)
-    send, keep = add(first_keep[:, 1], got[:, 1]), add(first_keep[:, 0], got[:, 0])
-    first = add(keep, across_y(send))
-    got = across_y(second_send)
-    send, keep = add(second_keep[:, 1], got[:, 1]), add(second_keep[:, 0], got[:, 0])
-    return first, add(keep, across_x(send))
-
-
-def scatter_t(pieces):
-    total = pieces[0].astype(F32)
-    for d in (1, 2, 3):
-        total = total + along_t(pieces[d], d).astype(F32)
-    return total
-
-
-def project_back_kernel(at, dq, dk, dv, *rest):
-    pieces, (out, wq, wk, wv, sems) = rest[:8], rest[8:]
-    me, t = at[0], at[1]
-    c = me & 1
-
-    @pl.when(pl.program_id(0) == 0)
+        cost_estimate=cost(SEQ * wide * 1536, 20e6),
+        name="project_back_keep",
+    )(at, dq, dk, dv, small, got, tok, grad_hidden, gain)
+
+
+def heads_send_kernel(at, left, dq, dk, dv, send, keep, turned):
+    n = pl.program_id(0)
+
+    @pl.when(n == 0)
     def _():
-        for n, held in enumerate((wq, wk, wv)):
-            start_loads(pieces, n, held, sems.at[n], me, t)
-        for n, held in enumerate((wq, wk, wv)):
-            wait_loads(held, sems.at[n])
-
-    total = None
-    for u in range(2):
-        for grad, held in ((dq, wq), (dk, wk), (dv, wv)):
-            term = dot_nt(grad[:, u * 256 : u * 256 + 256], held[2 * c + u])
-            total = term if total is None else total + term
-    out[...] = total.astype(out.dtype)
-
-
-def project_back(at, dq, dk, dv, pieces, other, kind):
-    rows, wide = 512, 1024
-    row = pl.BlockSpec((rows, 512), lambda i, at: (((at[0] & 1) ^ other) * 2 + i, 0))
+        turn_rows(left, at[0] >> 1, 1 - (at[0] & 1), turned)
+
+    for k, right in enumerate((dq, dk, dv)):
+
+        @pl.when(n == k)
+        def _():
+            product = dot(turned[...], right[...]).astype(BF16)
+            done = [product[r * 128 : r * 128 + 128] for r in range(4)]
+            place_second(send, keep, done, slice(k * 512, k * 512 + 512))
+
+
+def heads_keep_kernel(at, left, dq, dk, dv, send, keep, turned):
+    n = pl.program_id(0)
+
+    @pl.when(n == 0)
+    def _():
+        turn_rows(left, at[0] >> 1, at[0] & 1, turned)
+
+    for k, right in enumerate((dq, dk, dv)):
+
+        @pl.when(n == k)
+        def _():
+            product = dot(turned[...], right[...]).astype(BF16)
+            done = [product[r * 128 : r * 128 + 128] for r in range(4)]
+            place_first(send, keep, done, slice(k * 512, k * 512 + 512))
+
+
+def heads_gradient(kernel, name, at, left, dq, dk, dv):
+    count, wide = left.shape
+    full = lambda *shape: pl.BlockSpec(shape, lambda n, at: (0,) * len(shape), pipeline_mode=pl.Buffered(1))
     grid = pltpu.PrefetchScalarGridSpec(
         num_scalar_prefetch=1,
-        grid=(2,),
-        in_specs=[row] * 3 + [any_spec()] * 8,
-        out_specs=pl.BlockSpec((rows, wide), lambda i, at: (i, 0)),
-        scratch_shapes=[pltpu.VMEM((4, wide, 256), BF16)] * 3 + [pltpu.SemaphoreType.DMA((3,))],
+        grid=(3,),
+        in_specs=[full(count, wide)] + [full(count, 512)] * 3,
+        out_specs=[full(2, 128, 1536)] * 2,
+        scratch_shapes=[pltpu.VMEM((512, count), BF16)],
     )
     return pl.pallas_call(
-        project_back_kernel,
-        out_shape=jax.ShapeDtypeStruct((SEQ // 2, wide), kind),
+        kernel,
+        out_shape=[jax.ShapeDtypeStruct((2, 128, 1536), BF16)] * 2,
         grid_spec=grid,
         compiler_params=params(),
-        cost_estimate=cost(SEQ * wide * 1536, 14e6),
-        name="project_back",
-    )(at, dq, dk, dv, *pieces)
-
-
-def parity_columns(values, parity):
-    shaped = values.reshape(values.shape[0], 4, 2, 128)
-    return lax.dynamic_index_in_dim(shaped, parity, 2, keepdims=False).reshape(values.shape[0], 512)
+        cost_estimate=cost(2 * count * 512 * 1536, 12e6),
+        name=name,
+    )(at, left, dq, dk, dv)
+
+
+def heads_turn_kernel(at, kept1, got1, kept2, got2, out):
+    c, t = at[0] & 1, at[1]
+    for e, (kept, got) in enumerate(((kept1, got1), (kept2, got2))):
+        total = (kept[...].astype(F32) + got[...].astype(F32)).astype(BF16)
+        for u in range(2):
+            d = (2 * (c ^ e) + u - t) & 3
+            for n in range(3):
+                out[d, n] = total[:, n * 512 + u * 256 : n * 512 + u * 256 + 256]
+
+
+def heads_turn(at, arrays):
+    vmem = pl.BlockSpec(memory_space=pltpu.VMEM)
+    return pl.pallas_call(
+        heads_turn_kernel,
+        out_shape=jax.ShapeDtypeStruct((4, 3, 128, 256), BF16),
+        in_specs=[pl.BlockSpec(memory_space=pltpu.SMEM)] + [vmem] * 4,
+        out_specs=vmem,
+        compiler_params=params(),
+        cost_estimate=cost(1e6, 3e6),
+        name="heads_turn",
+    )(at, *arrays)
+
+
+def heads_final_kernel(a, b, c, d, query, key, value):
+    total = a[...].astype(F32) + b[...].astype(F32) + c[...].astype(F32) + d[...].astype(F32)
+    for n, out in enumerate((query, key)):
+        parts = []
+        for h in range(4):
+            parts += [total[n, :, h * 32 : h * 32 + 32], total[n, :, 128 + h * 32 : 160 + h * 32]]
+        out[...] = jnp.concatenate(parts, axis=1)
+    value[...] = total[2]
+
+
+def heads_final(pieces):
+    return pl.pallas_call(
+        heads_final_kernel,
+        out_shape=[jax.ShapeDtypeStruct((128, 256), F32)] * 3,
+        compiler_params=params(),
+        cost_estimate=cost(1e6, 2e6),
+        name="heads_final",
+    )(*pieces)
 
 
 def fast_body(tokens, first_values, doc_lengths, cotangent, w_query, w_key, w_value, w_out, w_gate, w_up, w_down, gain_attn, gain_mlp):
     me, t = lax.axis_index("dp"), lax.axis_index("tensor")
-    y, x, c = me // 4, (me // 2) % 2, me % 2
+    c = me % 2
     pair, side = t // 2, t % 2
     wide = tokens.shape[1]
     tiles = SEQ // TILE
     at = jnp.where(jnp.arange(8, dtype=jnp.int32) == 0, me, t).astype(jnp.int32)
 
-    def halves_apart(matrix):
-        return matrix.reshape(-1, 4, 2, 32).swapaxes(1, 2).reshape(-1, 256)
-
-    small_shard = jnp.stack([halves_apart(w_query), halves_apart(w_key), w_value, w_out.T])
-    big_shard = jnp.stack([w_gate, w_up, w_down.T])
-
-    own = swap_halves(tokens)
-    small = gather_pieces(small_shard)
-    other = across_c(own)
-    blocks = first_values.reshape(2, SEQ, 256)
-
-    def first_round(r):
-        block = lax.dynamic_index_in_dim(blocks, r ^ (t % 2), 0, keepdims=False)
-        return move(block, lambda y, x, c, t: (y, x, t // 2, 2 * (r ^ (t % 2)) + c))
-
-    fv = [first_round(0), first_round(1)]
-    big = gather_pieces(big_shard)
-    cot = swap_halves(cotangent)
+    small_shard, big_shard = pack(w_query, w_key, w_value, w_out, w_gate, w_up, w_down)
+    row, first, small, big = gather(tokens, first_values, small_shard, big_shard)
 
     lengths = jnp.where(c == side, doc_lengths, across_c(doc_lengths))
     lengths = lax.dynamic_index_in_dim(lengths, pair, 0, keepdims=False)
@@ -967,90 +1372,53 @@
     angles = (places - starts).astype(F32)[:, None] * jnp.tile(freqs, 4)[None, :]
     cosine, sine = jnp.cos(angles), jnp.sin(angles)
 
-    normed_one, q, k, v = project(at, own, other, fv, cosine, sine, gain_attn[None], small)
+    row, cotangent = lax.optimization_barrier((row, cotangent))
+    moved_cot = swap_halves(cotangent)
+    normed_one, q, k, v = project(at, row, first, cosine, sine, gain_attn[None], small)
     attended, lse = attend(bounds, q, k, v, starts_wide)
     by_half = attended.reshape(2, SEQ // 2, 512)
     att_own = lax.dynamic_index_in_dim(by_half, c, 0, keepdims=False)
     att_other = across_c(lax.dynamic_index_in_dim(by_half, 1 - c, 0, keepdims=False))
-    out, grad_hidden, branch, normed_two, hid, ga_own, ga_other, gain_two = mlp(
-        at, att_own, att_other, own, cot, gain_mlp[None], small, big
-    )
-    layer_out = swap_halves(out)
+    out, grad_hidden, branch, normed_two, hid, ga_own, ga_other, gain_two, cot = mlp(
+        at, att_own, att_other, row, cotangent, moved_cot, gain_mlp[None], small, big
+    )
+    stays = c == side
+    layer_out = jnp.where(stays, out, swap_halves(out))
 
     ga_got = across_c(ga_other)
     do = jnp.where(c == 0, jnp.concatenate([ga_own, ga_got]), jnp.concatenate([ga_got, ga_own]))
 
-    got = across_c(weight_send(at, normed_two, cot, hid))
-    kept = weight_keep(at, normed_two, cot, hid, got)
-    first, second = scatter_xy(*kept)
-    grads = scatter_t([first[0], first[1], second[0], second[1]])
-
-    att_all = jnp.where(c == 0, jnp.concatenate([att_own, att_other], 1), jnp.concatenate([att_other, att_own], 1))
-    shape = (2, 2, 128, 4, 256)
-    sent = dot_tn(parity_columns(branch, 1 - c), att_all).astype(BF16)
-    held = (dot_tn(parity_columns(branch, c), att_all) + across_c(sent).astype(F32)).astype(BF16)
-    held = held.reshape(shape).transpose(3, 0, 1, 2, 4)
-
-    def pick(values, axis, index):
-        return lax.dynamic_index_in_dim(values, index, axis, keepdims=False)
-
-    def relative(values, axis):
-        order = jnp.stack([pick(values, axis, (t + d) % 4) for d in range(4)])
-        return order
-
-    held = relative(held, 0)
-
-    def by_neighbour(values, rows):
-        if rows == "x":
-            send, keep = pick(values, 2, 1 - x), pick(values, 2, x)
-            flip = y
-        else:
-            send, keep = pick(values, 1, 1 - y), pick(values, 1, y)
-            flip = x
-        turn = lambda item: jnp.where(flip == 0, item, item[:, ::-1])
-        return turn(send), turn(keep)
-
-    first, second = scatter_xy(*by_neighbour(held[:2], "x"), *by_neighbour(held[2:], "y"))
-    grad_out = scatter_t([first[0], first[1], second[0], second[1]])
+    kept = weights(normed_two, cot, branch, hid, att_own, att_other)
+    kept, do = lax.optimization_barrier((kept, do))
+    got1, got2 = across_x(kept[0]), across_y(kept[2])
 
     dq, dk, dv = attend_back(bounds, q, k, v, do, attended, lse, starts.reshape(tiles, TILE), cosine, sine)
+
+    dq, dk, dv, got1, got2 = lax.optimization_barrier((dq, dk, dv, got1, got2))
+    sums = scatter_xy(kept[1], got1, kept[3], got2)
 
     def first_back(r):
         slab = jnp.where(pair == r, dv[:, :256], dv[:, 256:])
-        return move(slab, lambda y, x, c, t: (y, x, t % 2, 2 * c + ((t // 2) ^ r)))
+        came = move(slab, lambda y, x, c, t: (y, x, t % 2, 2 * c + ((t // 2) ^ r)))
+        return jnp.where(stays & (t == 2 * c + (pair ^ r)), slab, came)
 
     fb = [first_back(0), first_back(1)]
-    odd = t % 2
+    odd = side
     grad_first = jnp.concatenate(
         [jnp.where(odd == 0, fb[0], fb[1]), jnp.where(odd == 0, fb[1], fb[0])]
     ).astype(F32)
 
-    gn_got = across_c(project_back(at, dq, dk, dv, small, 1, BF16))
-    stacked = jnp.concatenate([dq, dk, dv], axis=1)
-    sent = dot_tn(parity_columns(normed_one, 1 - c), stacked).astype(BF16)
-    mine = dot_tn(parity_columns(normed_one, c), stacked).astype(BF16)
-    got = across_c(sent)
-
-    def arrange(values):
-        return values.reshape(2, 2, 128, 3, 2, 256).transpose(4, 0, 1, 3, 2, 5)
-
-    first, second = scatter_xy(*by_neighbour(arrange(mine), "x"), *by_neighbour(arrange(got), "y"))
-    all_four = jnp.where(c == 0, jnp.concatenate([first, second]), jnp.concatenate([second, first]))
-    gq, gk, gv = scatter_t(list(relative(all_four, 0)))
-
-    def halves_together(matrix):
-        return matrix.reshape(-1, 2, 4, 32).swapaxes(1, 2).reshape(-1, 256)
-
-    gn_keep = project_back(at, dq, dk, dv, small, 0, F32)
-    grad_normed = gn_keep + gn_got.astype(F32)
-    values = own.astype(F32)
-    factor = lax.rsqrt(jnp.mean(values * values, axis=1, keepdims=True) + EPSILON)
-    scaled = grad_normed * gain_attn[None]
-    mean = jnp.mean(scaled * values, axis=1, keepdims=True)
-    grad_tokens = grad_hidden + factor * scaled - values * (factor * factor * factor * mean)
-    grad_tokens = swap_halves(grad_tokens.astype(BF16)).astype(F32)
-    gain_one = jnp.sum(grad_normed * values * factor, axis=0)
-    gains = jnp.stack([gain_one, jnp.sum(gain_two, axis=0)]).reshape(16, 128)
+    gn_got = across_c(project_back_send(at, dq, dk, dv, small))
+    send2, keep2 = heads_gradient(heads_send_kernel, "heads_send", at, normed_one, dq, dk, dv)
+    send2, keep2 = across_c(send2), across_c(keep2)
+    send1, keep1 = heads_gradient(heads_keep_kernel, "heads_keep", at, normed_one, dq, dk, dv)
+    grad_gate, grad_up, grad_down, grad_out = final(scatter_t(turn(at, sums, hid.shape[2] // 2)), w_gate.shape[1])
+    head_sums = scatter_xy(keep1, across_x(send1), keep2, across_y(send2))
+    grad_tokens, gain_one = project_back_keep(at, dq, dk, dv, small, gn_got, row, grad_hidden, gain_attn[None])
+    grad_tokens = jnp.where(stays, grad_tokens, swap_halves(grad_tokens)).astype(F32)
+    gq, gk, gv = heads_final(scatter_t(heads_turn(at, head_sums)))
+
+    gains = jnp.stack([jnp.sum(gain_one, axis=0), jnp.sum(gain_two, axis=0)]).reshape(16, 128)
     gains = gains + across_c(gains)
     gains = gains + across_x(gains)
     gains = gains + across_y(gains)
@@ -1061,13 +1429,13 @@
         layer_out,
         grad_tokens,
         grad_first,
-        halves_together(gq),
-        halves_together(gk),
+        gq,
+        gk,
         gv,
-        grad_out.T,
-        grads[0],
-        grads[1],
-        grads[2].T,
+        grad_out,
+        grad_gate,
+        grad_up,
+        grad_down,
         gains[0],
         gains[1],
     )

time: 893 us -> 622 us (0.70); the launches traced: 878 us -> 616 us
  local copies, waits for them, and re-layouts: 207 us -> 20.1 us
  Pallas kernels: 240 us -> 419 us
  waiting for transfers between devices: 215 us -> 70.1 us
  starting transfers between devices: 121 us -> 66.7 us
  other arithmetic: 71.4 us -> 39.1 us
  matrix products: 21.1 us -> 0 us
    pallas_call x4 -> x11, Pallas kernels: 63.1 us -> 261 us  [the longest x1 164 us: gather(): pl.pallas_call(gather_kernel, out_shape=[jax.ShapeDtypeStruct((2, SEQ //...]
    ppermute x64 -> x30, waiting for transfers between devices: 215 us -> 70.1 us  [move(): return lax.ppermute(values, AXES, pairs)]
    ppermute x64 -> x30, starting transfers between devices: 121 us -> 66.7 us  [move(): return lax.ppermute(values, AXES, pairs)]
    ppermute x17 -> x0, local copies, waits for them, and re-layouts: 51.6 us -> none  [move(): return lax.ppermute(values, AXES, pairs)]
    unnamed x106 -> x36, local copies, waits for them, and re-layouts: 60.1 us -> 10.7 us
    dot_general x4 -> x0, matrix products: 21.1 us -> none  [dot_tn(): lax.dot_general(left, right, (((0,), (0,)), ((), ())), preferred_element_...]
    pallas_call x3 -> x0, local copies, waits for them, and re-layouts: 20.8 us -> none  [the longest x1 12.2 us: weight_send(): pl.pallas_call(weight_send_kernel, out_shape=jax.ShapeDtypeStruct((3, 4,...]
    another operation x11 -> x0, local copies, waits for them, and re-layouts: 19.6 us -> none
  transfers between devices with their start and end apart: 64 -> 30, of which waited for: 19 -> 10; matrix products, arithmetic and copies ran while one was open for 30% -> 8% of each run, Pallas kernels for 20% -> 57%
where the time goes in v2:
time: 622 us; the launch traced here: 616 us
  Pallas kernels  419 us (67%)
  waiting for transfers between devices  70.1 us (11%)
  starting transfers between devices  66.7 us (11%)
  other arithmetic  39.1 us (6%)
  local copies, waits for them, and re-layouts  20.1 us (3%)
    pallas_call x1, Pallas kernels, gather(): pl.pallas_call(gather_kernel, out_shape=[jax.ShapeDtypeStruct((2, SEQ //...  164 us
    ppermute x30, waiting for transfers between devices, move(): return lax.ppermute(values, AXES, pairs)  70.1 us
    ppermute x30, starting transfers between devices, move(): return lax.ppermute(values, AXES, pairs)  66.7 us
    pallas_call x1, Pallas kernels, mlp(): pl.pallas_call(mlp_kernel, out_shape=[tokens(wide), tokens(wide, F32), to...  60.2 us
    pallas_call x1, Pallas kernels, attend_back(): pl.pallas_call(attend_back_kernel, out_shape=[jax.ShapeDtypeStruct((SEQ,...  47.6 us
    pallas_call x1, Pallas kernels, weights(): pl.pallas_call(weights_kernel, out_shape=[jax.ShapeDtypeStruct((2, 128, l...  43.6 us
    pallas_call x1, Pallas kernels, attend(): pl.pallas_call(attend_kernel, out_shape=[jax.ShapeDtypeStruct((SEQ, 512),...  37.6 us
    pallas_call x2, Pallas kernels, heads_gradient(): pl.pallas_call(kernel, out_shape=[jax.ShapeDtypeStruct((2, 128, 1536), BF...  19.5 us
  transfers between devices with their start and end apart: 30, of which 10 were waited for; matrix products, arithmetic and copies ran while one was open for 8% of the time, Pallas kernels for 57%

profile of v2, /device:TPU:11, one launch (start us, length us, event | category | flops | bytes accessed | tf_op | source)
XLA Modules:
  0.0 616.0 jit_solution(1351303660225573)
XLA Ops:
  7.9 163.6 %gather.1 = (bf16[2,1024,1024]{2,1,0:T(8,128)(2,1)}, bf16[2,2048,256]{2,1,0:T(8,128)(2,1)}, bf16[4,4,1024,256]{3,2,1,0:T(8,128)(2,1)}, bf16[3,8,2,4,352,128]{5,4,3,2,1,0:T(8,128)(2,1)}) custom-call(bf16[1024,1024]{1,0:T(8,128)(2,1)} %tok.1, bf16[4096,256]{1,0:T(8,128)(2,1)} %fv.1, bf16[4,128,256]{2,1,0:T(8,128)(2,1)} %get-tuple-element.65.small, ...), custom_call_target="tpu_custom_call" | custom-call | tf_op jit(solution)/shard_map/gather/pallas_call | solution.py:576
  174.7 5.6 multiply_sine_fusion
  180.9 12.8 %project.1 = (bf16[2048,1024]{1,0:T(8,128)(2,1)}, bf16[2048,512]{1,0:T(8,128)(2,1)}, bf16[2048,512]{1,0:T(8,128)(2,1)}, bf16[2048,512]{1,0:T(8,128)(2,1)}) custom-call(s32[8]{0:T(128)} %compare_select_fusion.at, bf16[2,1024,1024]{2,1,0:T(8,128)(2,1)} %get-tuple-element.68.tok, bf16[2,2048,256]{2,1,0:T(8,128)(2,1)} %get-tuple-element.69.first, ...), custom_call_target="tpu_custom_call" | custom-call | flops 6442450944 | bytes 24000000 | tf_op jit(solution)/shard_map/project/pallas_call | solution.py:652
  195.0 37.6 %attend.1 = (bf16[2048,512]{1,0:T(8,128)(2,1)}, f32[2,8,1024]{2,1,0:T(8,128)}) custom-call(s32[16]{0:T(128)} %pad_add_fusion.bounds, bf16[2048,512]{1,0:T(8,128)(2,1)} %get-tuple-element.71.q_ref, bf16[2048,512]{1,0:T(8,128)(2,1)} %get-tuple-element.72.k_ref, bf16[2048,512]{1,0:T(8,128)(2,1)} %get-tuple-element.73.v_ref, s32[2048,128]{1,0:T(8,128)} %broadcast_in_dim.71.starts), custom_call_target="tpu_custom_call" | custom-call | flops 20000000000 | bytes 12000000 | tf_op jit(solution)/shard_map/attend/pallas_call | solution.py:747
  238.9 60.2 %mlp.1 = (bf16[1024,1024]{1,0:T(8,128)(2,1)}, f32[1024,1024]{1,0:T(8,128)}, bf16[1024,1024]{1,0:T(8,128)(2,1)}, bf16[1024,1024]{1,0:T(8,128)(2,1)}, bf16[3,1024,...) custom-call(s32[8]{0:T(128)} %compare_select_fusion.at, ...), custom_call_target="tpu_custom_call" | custom-call | flops 39728447488 | bytes 60000000 | tf_op jit(solution)/shard_map/mlp/pallas_call | solution.py:961
  302.1 43.6 %weights.1 = (bf16[2,128,4736]{2,1,0:T(8,128)(2,1)}, bf16[2,128,4736]{2,1,0:T(8,128)(2,1)}, bf16[2,128,4736]{2,1,0:T(8,128)(2,1)}, bf16[2,128,4736]{2,1,0:T(8,128)(2,1)}) custom-call(bf16[1024,1024]{1,0:T(8,128)(2,1)} %get-tuple-element.78.n2, bf16[1024,1024]{1,0:T(8,128)(2,1)} %get-tuple-element.79.g, bf16[1024,1024]{1,0:T(8,128)(2,1)} %get-tuple-element.80.branch, ...), custom_call_target="tpu_custom_call" | custom-call | flops 19864223744 | bytes 50000000 | tf_op jit(solution)/shard_map/weights/pallas_call | solution.py:1103
  349.2 47.6 %attend_back.1 = (bf16[2048,512]{1,0:T(8,128)(2,1)}, bf16[2048,512]{1,0:T(8,128)(2,1)}, bf16[2048,512]{1,0:T(8,128)(2,1)}) custom-call(s32[16]{0:T(128)} %pad_add_fusion.bounds, bf16[2048,512]{1,0:T(8,128)(2,1)} %get-tuple-element.71.q_ref, bf16[2048,512]{1,0:T(8,128)(2,1)} %get-tuple-element.72.k_ref, bf16[2048,512]{1,0:T(8,128)(2,1)} %get-tuple-element.73.v_ref, ...), custom_call_target="tpu_custom_call" | custom-call | flops 49999998976 | bytes 20000000 | tf_op jit(solution)/shard_map/attend_back/pallas_call | solution.py:861
  400.0 3.8 collective-permute-done.5
  403.8 8.6 %project_back_send.1 = bf16[1024,1024]{1,0:T(8,128)(2,1)} custom-call(s32[8]{0:T(128)} %compare_select_fusion.at, bf16[2048,512]{1,0:T(8,128)(2,1)} %get-tuple-element.95.dq, bf16[2048,512]{1,0:T(8,128)(2,1)} %get-tuple-element.96.dk, bf16[2048,512]{1,0:T(8,128)(2,1)} %get-tuple-element.97.dv, bf16[4,4,1024,256]{3,2,1,0:T(8,128)(2,1)} %get-tuple-element.70.held.wo), custom_call_target="tpu_custom_call" | custom-call | flops 3221225472 | bytes 10000000 | tf_op jit(solution)/shard_map/project_back_send/pallas_call | solution.py:1206
  413.2 4.4 fusion.3
  422.6 9.7 %heads_send.1 = (bf16[2,128,1536]{2,1,0:T(8,128)(2,1)}, bf16[2,128,1536]{2,1,0:T(8,128)(2,1)}) custom-call(s32[8]{0:T(128)} %compare_select_fusion.at, bf16[2048,1024]{1,0:T(8,128)(2,1)} %get-tuple-element.100.left, bf16[2048,512]{1,0:T(8,128)(2,1)} %get-tuple-element.95.dq, bf16[2048,512]{1,0:T(8,128)(2,1)} %get-tuple-element.96.dk, ...), custom_call_target="tpu_custom_call" | custom-call | flops 3221225472 | bytes 12000000 | tf_op jit(solution)/shard_map/heads_send/pallas_call | solution.py:1297
  433.1 9.7 %heads_keep.1 = (bf16[2,128,1536]{2,1,0:T(8,128)(2,1)}, bf16[2,128,1536]{2,1,0:T(8,128)(2,1)}) custom-call(s32[8]{0:T(128)} %compare_select_fusion.at, bf16[2048,1024]{1,0:T(8,128)(2,1)} %get-tuple-element.100.left, bf16[2048,512]{1,0:T(8,128)(2,1)} %get-tuple-element.95.dq, bf16[2048,512]{1,0:T(8,128)(2,1)} %get-tuple-element.96.dk, ...), custom_call_target="tpu_custom_call" | custom-call | flops 3221225472 | bytes 12000000 | tf_op jit(solution)/shard_map/heads_keep/pallas_call | solution.py:1297
  445.5 14.8 %collective-permute-start.10 = (bf16[2048,256]{1,0:T(8,128)(2,1)S(1)}, bf16[2048,256]{1,0:T(8,128)(2,1)}, u32[]{:S(2)}, u32[]{:S(2)}) collective-permute-start(bf16[2048,256]{1,0:T(8,128)(2,1)S(1)} %get-tuple-element.164), channel_id=1, source_target_pairs={{0,1},{1,5},{2,0},{3,4},{4,3},{5,7},{6,2},{7,6},{8,9},{9,13},{10,8... | collective-permute-start | bytes 3145736 | tf_op jit(solution)/shard_map/ppermute | solution.py:309
  460.4 10.9 %project_back_keep.1 = (bf16[1024,1024]{1,0:T(8,128)(2,1)}, f32[8,1024]{1,0:T(8,128)}) custom-call(s32[8]{0:T(128)} %compare_select_fusion.at, bf16[2048,512]{1,0:T(8,128)(2,1)} %get-tuple-element.95.dq, bf16[2048,512]{1,0:T(8,128)(2,1)} %get-tuple-element.96.dk, bf16[2048,512]{1,0:T(8,128)(2,1)} %get-tuple-element.97.dv, ...), custom_call_target="tpu_custom_call" | custom-call | flops 3221225472 | bytes 20000000 | tf_op jit(solution)/shard_map/project_back_keep/pallas_call | solution.py:1245
  479.8 4.6 turn.1
  487.3 11.1 %collective-permute-done.10 = bf16[2048,256]{1,0:T(8,128)(2,1)} collective-permute-done((bf16[2048,256]{1,0:T(8,128)(2,1)S(1)}, bf16[2048,256]{1,0:T(8,128)(2,1)}, u32[]{:S(2)}, u32[]{:S(2)}) %collective-permute-start.10) | collective-permute-done | bytes 1048608 | tf_op jit(solution)/shard_map/ppermute | solution.py:309
  498.4 14.1 %collective-permute-done.9 = bf16[2048,256]{1,0:T(8,128)(2,1)} collective-permute-done((bf16[2048,256]{1,0:T(8,128)(2,1)}, bf16[2048,256]{1,0:T(8,128)(2,1)}, u32[]{:S(2)}, u32[]{:S(2)}) %collective-permute-start.9) | collective-permute-done | bytes 1048608 | tf_op jit(solution)/shard_map/ppermute | solution.py:309
  516.4 20.6 %collective-permute-start.24 = (bf16[2368,128]{1,0:T(8,128)(2,1)S(1)}, bf16[2368,128]{1,0:T(8,128)(2,1)S(1)}, u32[]{:S(2)}, u32[]{:S(2)}) collective-permute-start(bf16[2368,128]{1,0:T(8,128)(2,1)S(1)} %get-tuple-element.160), channel_id=1, source_target_pairs={{0,3},{1,0},{2,1},{3,2},{4,7},{5,4},{6,5},{7,6},{8,11},{9,8},{10,9... | collective-permute-start | bytes 1818632 | tf_op jit(solution)/shard_map/ppermute | solution.py:309
  543.4 12.1 %collective-permute-done.24.d = bf16[2368,128]{1,0:T(8,128)(2,1)S(1)} collective-permute-done((bf16[2368,128]{1,0:T(8,128)(2,1)S(1)}, bf16[2368,128]{1,0:T(8,128)(2,1)S(1)}, u32[]{:S(2)}, u32[]{:S(2)}) %collective-permute-start.24) | collective-permute-done | bytes 606240 | tf_op jit(solution)/shard_map/ppermute | solution.py:309
  566.3 9.4 %collective-permute-done.28 = f32[16,128]{1,0:T(8,128)S(1)} collective-permute-done((f32[16,128]{1,0:T(8,128)S(1)}, f32[16,128]{1,0:T(8,128)S(1)}, u32[]{:S(2)}, u32[]{:S(2)}) %collective-permute-start.28) | collective-permute-done | bytes 8224 | tf_op jit(solution)/shard_map/ppermute | solution.py:309
  575.8 12.9 %collective-permute-start.29 = (f32[16,128]{1,0:T(8,128)S(1)}, f32[16,128]{1,0:T(8,128)S(1)}, u32[]{:S(2)}, u32[]{:S(2)}) collective-permute-start(f32[16,128]{1,0:T(8,128)S(1)} %add.118), channel_id=1, source_target_pairs={{0,2},{1,3},{2,0},{3,1},{4,6},{5,7},{6,4},{7,5},{8,10},{9,11},{10,... | collective-permute-start | bytes 24584 | tf_op jit(solution)/shard_map/ppermute | solution.py:309
  592.8 4.0 collective-permute-done.17.b
  596.7 10.3 %collective-permute-done.18.c = bf16[3,128,256]{2,1,0:T(8,128)(2,1)S(1)} collective-permute-done((bf16[3,128,256]{2,1,0:T(8,128)(2,1)S(1)}, bf16[3,128,256]{2,1,0:T(8,128)(2,1)S(1)}, u32[]{:S(2)}, u32[]{:S(2)}) %collective-permute-start.18) | collective-permute-done | bytes 196640 | tf_op jit(solution)/shard_map/ppermute | solution.py:309
  611.9 3.9 select_convert_fusion
  (129 shorter events, 78.8 us)
Async XLA Ops:
  0.6 173.5 %collective-permute-start = (s32[2,8]{1,0:T(2,128)}, s32[2,8]{1,0:T(2,128)S(1)}, u32[]{:S(2)}, u32[]{:S(2)}) collective-permute-start(s32[2,8]{1,0:T(2,128)} %param.15), channel_id=1, source_target_pairs={{0,4},{1,5},{2,6},{3,7},{4,0},{5,1},{6,2},{7,3},{8,12},{9,13},{10,... | collective-permute-start | bytes 200 | tf_op jit(solution)/shard_map/ppermute | solution.py:309
  171.6 66.4 %collective-permute-start.2 = (bf16[1024,1024]{1,0:T(8,128)(2,1)}, bf16[1024,1024]{1,0:T(8,128)(2,1)}, u32[]{:S(2)}, u32[]{:S(2)}) collective-permute-start(bf16[1024,1024]{1,0:T(8,128)(2,1)} %cot_here), channel_id=1, source_target_pairs={{1,4},{3,6},{4,1},{6,3},{9,12},{11,14},{12,9},{14,11},{17,20},{19,... | collective-permute-start | bytes 6291464 | tf_op jit(solution)/shard_map/ppermute | solution.py:309
  299.1 46.6 %collective-permute-start.4 = (bf16[1024,512]{1,0:T(8,128)(2,1)}, bf16[1024,512]{1,0:T(8,128)(2,1)}, u32[]{:S(2)}, u32[]{:S(2)}) collective-permute-start(bf16[1024,512]{1,0:T(8,128)(2,1)} %get-tuple-element.87), channel_id=1, source_target_pairs={{0,4},{1,5},{2,6},{3,7},{4,0},{5,1},{6,2},{7,3},{8,12},{9,13},{10,... | collective-permute-start | bytes 3145736 | tf_op jit(solution)/shard_map/ppermute | solution.py:309
  299.3 97.5 %collective-permute-start.3 = (bf16[1024,1024]{1,0:T(8,128)(2,1)}, bf16[1024,1024]{1,0:T(8,128)(2,1)}, u32[]{:S(2)}, u32[]{:S(2)}) collective-permute-start(bf16[1024,1024]{1,0:T(8,128)(2,1)} %get-tuple-element.77), channel_id=1, source_target_pairs={{1,4},{3,6},{4,1},{6,3},{9,12},{11,14},{12,9},{14,11},{17,20},{19,... | collective-permute-start | bytes 6291464 | tf_op jit(solution)/shard_map/ppermute | solution.py:309
  349.2 54.6 %collective-permute-start.5 = (bf16[2,128,4736]{2,1,0:T(8,128)(2,1)}, bf16[2,128,4736]{2,1,0:T(8,128)(2,1)}, u32[]{:S(2)}, u32[]{:S(2)}) collective-permute-start(bf16[2,128,4736]{2,1,0:T(8,128)(2,1)} %get-tuple-element.93), channel_id=1, source_target_pairs={{0,8},{1,9},{2,10},{3,11},{4,12},{5,13},{6,14},{7,15},{8,0},{9,1},... | collective-permute-start | bytes 7274504 | tf_op jit(solution)/shard_map/ppermute | solution.py:309
  349.2 54.6 %collective-permute-start.6 = (bf16[2,128,4736]{2,1,0:T(8,128)(2,1)}, bf16[2,128,4736]{2,1,0:T(8,128)(2,1)}, u32[]{:S(2)}, u32[]{:S(2)}) collective-permute-start(bf16[2,128,4736]{2,1,0:T(8,128)(2,1)} %get-tuple-element.94), channel_id=1, source_target_pairs={{0,16},{1,17},{2,18},{3,19},{4,20},{5,21},{6,22},{7,23},{8,24},{9,... | collective-permute-start | bytes 7274504 | tf_op jit(solution)/shard_map/ppermute | solution.py:309
  412.4 33.1 %collective-permute-start.7 = (bf16[1024,1024]{1,0:T(8,128)(2,1)}, bf16[1024,1024]{1,0:T(8,128)(2,1)}, u32[]{:S(2)}, u32[]{:S(2)}) collective-permute-start(bf16[1024,1024]{1,0:T(8,128)(2,1)} %project_back_send.1), channel_id=1, source_target_pairs={{0,4},{1,5},{2,6},{3,7},{4,0},{5,1},{6,2},{7,3},{8,12},{9,13},{10,... | collective-permute-start | bytes 6291464 | tf_op jit(solution)/shard_map/ppermute | solution.py:309
  417.6 60.6 %collective-permute-start.21 = (bf16[128,4736]{1,0:T(8,128)(2,1)}, bf16[128,4736]{1,0:T(8,128)(2,1)}, u32[]{:S(2)}, u32[]{:S(2)}) collective-permute-start(bf16[128,4736]{1,0:T(8,128)(2,1)} %get-tuple-element.154), channel_id=1, source_target_pairs={{0,8},{1,9},{2,10},{3,11},{4,12},{5,13},{6,14},{7,15},{8,0},{9,1},... | collective-permute-start | bytes 3637256 | tf_op jit(solution)/shard_map/ppermute | solution.py:309
  422.6 55.6 %collective-permute-start.20 = (bf16[128,4736]{1,0:T(8,128)(2,1)}, bf16[128,4736]{1,0:T(8,128)(2,1)}, u32[]{:S(2)}, u32[]{:S(2)}) collective-permute-start(bf16[128,4736]{1,0:T(8,128)(2,1)} %get-tuple-element.156), channel_id=1, source_target_pairs={{0,16},{1,17},{2,18},{3,19},{4,20},{5,21},{6,22},{7,23},{8,24},{9,... | collective-permute-start | bytes 3637256 | tf_op jit(solution)/shard_map/ppermute | solution.py:309
  432.4 39.7 %collective-permute-start.14 = (bf16[2,128,1536]{2,1,0:T(8,128)(2,1)}, bf16[2,128,1536]{2,1,0:T(8,128)(2,1)}, u32[]{:S(2)}, u32[]{:S(2)}) collective-permute-start(bf16[2,128,1536]{2,1,0:T(8,128)(2,1)} %get-tuple-element.104), channel_id=1, source_target_pairs={{0,4},{1,5},{2,6},{3,7},{4,0},{5,1},{6,2},{7,3},{8,12},{9,13},{10,... | collective-permute-start | bytes 2359304 | tf_op jit(solution)/shard_map/ppermute | solution.py:309
  442.8 31.9 %collective-permute-start.11 = (bf16[2,128,1536]{2,1,0:T(8,128)(2,1)}, bf16[2,128,1536]{2,1,0:T(8,128)(2,1)}, u32[]{:S(2)}, u32[]{:S(2)}) collective-permute-start(bf16[2,128,1536]{2,1,0:T(8,128)(2,1)} %get-tuple-element.102), channel_id=1, source_target_pairs={{0,8},{1,9},{2,10},{3,11},{4,12},{5,13},{6,14},{7,15},{8,0},{9,1},... | collective-permute-start | bytes 2359304 | tf_op jit(solution)/shard_map/ppermute | solution.py:309
  445.5 52.9 %collective-permute-start.10 = (bf16[2048,256]{1,0:T(8,128)(2,1)S(1)}, bf16[2048,256]{1,0:T(8,128)(2,1)}, u32[]{:S(2)}, u32[]{:S(2)}) collective-permute-start(bf16[2048,256]{1,0:T(8,128)(2,1)S(1)} %get-tuple-element.164), channel_id=1, source_target_pairs={{0,1},{1,5},{2,0},{3,4},{4,3},{5,7},{6,2},{7,6},{8,9},{9,13},{10,8... | collective-permute-start | bytes 3145736 | tf_op jit(solution)/shard_map/ppermute | solution.py:309
  472.1 40.4 %collective-permute-start.9 = (bf16[2048,256]{1,0:T(8,128)(2,1)}, bf16[2048,256]{1,0:T(8,128)(2,1)}, u32[]{:S(2)}, u32[]{:S(2)}) collective-permute-start(bf16[2048,256]{1,0:T(8,128)(2,1)} %get-tuple-element.165), channel_id=1, source_target_pairs={{1,4},{2,1},{3,5},{4,2},{5,6},{6,3},{9,12},{10,9},{11,13},{12,10},... | collective-permute-start | bytes 3145736 | tf_op jit(solution)/shard_map/ppermute | solution.py:309
  478.2 38.2 %collective-permute-start.13 = (bf16[2,128,1536]{2,1,0:T(8,128)(2,1)}, bf16[2,128,1536]{2,1,0:T(8,128)(2,1)S(1)}, u32[]{:S(2)}, u32[]{:S(2)}) collective-permute-start(bf16[2,128,1536]{2,1,0:T(8,128)(2,1)} %get-tuple-element.103), channel_id=1, source_target_pairs={{0,4},{1,5},{2,6},{3,7},{4,0},{5,1},{6,2},{7,3},{8,12},{9,13},{10,... | collective-permute-start | bytes 2359304 | tf_op jit(solution)/shard_map/ppermute | solution.py:309
  478.2 58.9 %collective-permute-start.15 = (bf16[2,128,1536]{2,1,0:T(8,128)(2,1)}, bf16[2,128,1536]{2,1,0:T(8,128)(2,1)}, u32[]{:S(2)}, u32[]{:S(2)}) collective-permute-start(bf16[2,128,1536]{2,1,0:T(8,128)(2,1)} %collective-permute-done.14), channel_id=1, source_target_pairs={{0,16},{1,17},{2,18},{3,19},{4,20},{5,21},{6,22},{7,23},{8,24},{9,... | collective-permute-start | bytes 2359304 | tf_op jit(solution)/shard_map/ppermute | solution.py:309
  484.5 28.0 %collective-permute-start.26 = (f32[16,128]{1,0:T(8,128)S(1)}, f32[16,128]{1,0:T(8,128)S(1)}, u32[]{:S(2)}, u32[]{:S(2)}) collective-permute-start(f32[16,128]{1,0:T(8,128)S(1)} %add.115), channel_id=1, source_target_pairs={{0,8},{1,9},{2,10},{3,11},{4,12},{5,13},{6,14},{7,15},{8,0},{9,1},... | collective-permute-start | bytes 24584 | tf_op jit(solution)/shard_map/ppermute | solution.py:309
  498.4 42.4 %collective-permute-start.22 = (bf16[2368,128]{1,0:T(8,128)(2,1)S(1)}, bf16[2368,128]{1,0:T(8,128)(2,1)S(1)}, u32[]{:S(2)}, u32[]{:S(2)}) collective-permute-start(bf16[2368,128]{1,0:T(8,128)(2,1)S(1)} %get-tuple-element.162), channel_id=1, source_target_pairs={{0,1},{1,2},{2,3},{3,0},{4,5},{5,6},{6,7},{7,4},{8,9},{9,10},{10,1... | collective-permute-start | bytes 1818632 | tf_op jit(solution)/shard_map/ppermute | solution.py:309
  512.4 28.5 %collective-permute-start.23 = (bf16[2368,128]{1,0:T(8,128)(2,1)S(1)}, bf16[2368,128]{1,0:T(8,128)(2,1)S(1)}, u32[]{:S(2)}, u32[]{:S(2)}) collective-permute-start(bf16[2368,128]{1,0:T(8,128)(2,1)S(1)} %get-tuple-element.161), channel_id=1, source_target_pairs={{0,2},{1,3},{2,0},{3,1},{4,6},{5,7},{6,4},{7,5},{8,10},{9,11},{10,... | collective-permute-start | bytes 1818632 | tf_op jit(solution)/shard_map/ppermute | solution.py:309
  512.4 99.4 %collective-permute-start.8 = (bf16[1024,1024]{1,0:T(8,128)(2,1)}, bf16[1024,1024]{1,0:T(8,128)(2,1)}, u32[]{:S(2)}, u32[]{:S(2)}) collective-permute-start(bf16[1024,1024]{1,0:T(8,128)(2,1)} %get-tuple-element.99), channel_id=1, source_target_pairs={{1,4},{3,6},{4,1},{6,3},{9,12},{11,14},{12,9},{14,11},{17,20},{19,... | collective-permute-start | bytes 6291464 | tf_op jit(solution)/shard_map/ppermute | solution.py:309
  516.4 39.1 %collective-permute-start.24 = (bf16[2368,128]{1,0:T(8,128)(2,1)S(1)}, bf16[2368,128]{1,0:T(8,128)(2,1)S(1)}, u32[]{:S(2)}, u32[]{:S(2)}) collective-permute-start(bf16[2368,128]{1,0:T(8,128)(2,1)S(1)} %get-tuple-element.160), channel_id=1, source_target_pairs={{0,3},{1,0},{2,1},{3,2},{4,7},{5,4},{6,5},{7,6},{8,11},{9,8},{10,9... | collective-permute-start | bytes 1818632 | tf_op jit(solution)/shard_map/ppermute | solution.py:309
  540.0 23.1 %collective-permute-start.12 = (bf16[128,1536]{1,0:T(8,128)(2,1)S(1)}, bf16[128,1536]{1,0:T(8,128)(2,1)S(1)}, u32[]{:S(2)}, u32[]{:S(2)}) collective-permute-start(bf16[128,1536]{1,0:T(8,128)(2,1)S(1)} %copy-done.7), channel_id=1, source_target_pairs={{0,16},{1,17},{2,18},{3,19},{4,20},{5,21},{6,22},{7,23},{8,24},{9,... | collective-permute-start | bytes 1179656 | tf_op jit(solution)/shard_map/ppermute | solution.py:309
  540.8 22.3 %collective-permute-start.16 = (bf16[128,1536]{1,0:T(8,128)(2,1)}, bf16[128,1536]{1,0:T(8,128)(2,1)S(1)}, u32[]{:S(2)}, u32[]{:S(2)}) collective-permute-start(bf16[128,1536]{1,0:T(8,128)(2,1)} %get-tuple-element.168), channel_id=1, source_target_pairs={{0,8},{1,9},{2,10},{3,11},{4,12},{5,13},{6,14},{7,15},{8,0},{9,1},... | collective-permute-start | bytes 1179656 | tf_op jit(solution)/shard_map/ppermute | solution.py:309
  541.0 34.8 %collective-permute-start.28 = (f32[16,128]{1,0:T(8,128)S(1)}, f32[16,128]{1,0:T(8,128)S(1)}, u32[]{:S(2)}, u32[]{:S(2)}) collective-permute-start(f32[16,128]{1,0:T(8,128)S(1)} %add.117), channel_id=1, source_target_pairs={{0,1},{1,0},{2,3},{3,2},{4,5},{5,4},{6,7},{7,6},{8,9},{9,8},{10,11... | collective-permute-start | bytes 24584 | tf_op jit(solution)/shard_map/ppermute | solution.py:309
  590.7 18.3 %collective-permute-start.19 = (bf16[3,128,256]{2,1,0:T(8,128)(2,1)S(1)}, bf16[3,128,256]{2,1,0:T(8,128)(2,1)S(1)}, u32[]{:S(2)}, u32[]{:S(2)}) collective-permute-start(bf16[3,128,256]{2,1,0:T(8,128)(2,1)S(1)} %get-tuple-element.172), channel_id=1, source_target_pairs={{0,3},{1,0},{2,1},{3,2},{4,7},{5,4},{6,5},{7,6},{8,11},{9,8},{10,9... | collective-permute-start | bytes 589832 | tf_op jit(solution)/shard_map/ppermute | solution.py:309
  (22 other events, 382.6 us)

commit v3 on v2

--- a/solution.py
+++ b/solution.py
@@ -334,12 +334,13 @@
     small[1] = dot(wk[...], halves[...]).astype(BF16)
     small[2] = wv[...]
     small[3] = wo[...].T
-    for n, turned in enumerate((wg[...].T, wu[...].T, wd[...])):
-        big[n] = turned.reshape(big.shape[1:])
+    for n, units in enumerate((wg, wu, wd)):
+        big[n] = units[...].reshape(big.shape[1:])
 
 
 def pack(wq, wk, wv, wo, wg, wu, wd):
-    rows, part = wg.shape
+    wg, wu = wg.T, wu.T
+    part, rows = wg.shape
     lane = jnp.arange(256, dtype=jnp.int32)
     source = ((lane & 127) >> 5) * 64 + (lane >> 7) * 32 + (lane & 31)
     halves = (lane[:, None] == source[None, :]).astype(BF16)
@@ -354,7 +355,19 @@
     )(wq, wk, wv, wo, wg, wu, wd, halves)
 
 
-def gather_kernel(tok, fv, small, big, row, first, g_small, g_big, send, recv, swap, fsend, frecv, here):
+def meet(plane, c, t, dpx, dpy):
+    barrier = pltpu.get_barrier_semaphore()
+    for e in range(2):
+        for d in range(4):
+            if e or d:
+                other = plane + lax.rem(c + e, 2)
+                pl.semaphore_signal(barrier, inc=1, device_id=(other, lax.rem(t + d, 4)), device_id_type=MESH)
+    pl.semaphore_signal(barrier, inc=1, device_id=(dpx, t), device_id_type=MESH)
+    pl.semaphore_signal(barrier, inc=1, device_id=(dpy, t), device_id_type=MESH)
+    pl.semaphore_wait(barrier, 9)
+
+
+def gather_kernel(tok, fv, small, big, row, first, g_small, g_big, send, recv, relay_send, along_recv, next_send, next_recv, swap, fsend, frecv, here):
     dp, t = lax.axis_index("dp"), lax.axis_index("tensor")
     c, x, y = lax.rem(dp, 2), lax.rem(lax.div(dp, 2), 2), lax.div(dp, 4)
     pair, side = lax.div(t, 2), lax.rem(t, 2)
@@ -362,18 +375,7 @@
     dpx, dpy, dpc = dp + 2 - 4 * x, dp + 4 - 8 * y, dp + 1 - 2 * c
     dpxy = dpx + 4 - 8 * y
 
-    barrier = pltpu.get_barrier_semaphore()
-    for e in range(2):
-        for d in range(4):
-            if e or d:
-                other = plane + (c + e) - 2 * lax.div(c + e, 2)
-                pl.semaphore_signal(barrier, inc=1, device_id=(other, lax.rem(t + d, 4)), device_id_type=MESH)
-    pl.semaphore_signal(barrier, inc=1, device_id=(dpx, t), device_id_type=MESH)
-    pl.semaphore_signal(barrier, inc=1, device_id=(dpy, t), device_id_type=MESH)
-    pl.semaphore_wait(barrier, 9)
-
-    dist = [lax.rem(t + 4 - d, 4) for d in range(4)]
-
+    meet(plane, c, t, dpx, dpy)
     def slot(k, at, owner, h):
         if k == 0:
             return g_small.at[pl.ds(2 * h, 2), at, pl.ds(owner * 128, 128), :]
@@ -412,32 +414,83 @@
 
     chunks = 4
     near, far = (dpx, dpy), (dpy, dpx)
-    along = [[copy(k, d - 1, shard(k), both(k, t, dp), dp, lax.rem(t + d, 4)) for d in (1, 2, 3)] for k in range(chunks)]
-    onward = [[[copy(k, 3 + h, part_of(k, h), slot(k, t, dp, h), near[h], t) for h in range(2)]] for k in range(chunks)]
     kept = [pltpu.make_async_copy(shard(k), both(k, t, dp), here.at[k]) for k in range(chunks)]
-    for k in range(chunks):
-        onward[k] += [
-            [copy(k, 3 + 2 * d + h, slot(k, dist[d], dp, h), slot(k, dist[d], dp, h), near[h], t) for h in range(2)]
-            for d in (1, 2, 3)
-        ]
+
+    def relay(k, at, side, src):
+        return pltpu.make_async_remote_copy(
+            src_ref=src,
+            dst_ref=both(k, at, dp),
+            send_sem=relay_send.at[k, at, side],
+            recv_sem=along_recv.at[k, at],
+            device_id=(dp, t + 2 * side - 1),
+            device_id_type=MESH,
+        )
+
+    def onward(k, at, h, src):
+        return pltpu.make_async_remote_copy(
+            src_ref=src,
+            dst_ref=slot(k, at, dp, h),
+            send_sem=next_send.at[k, at, h],
+            recv_sem=next_recv.at[k, at, h],
+            device_id=(near[h], t),
+            device_id_type=MESH,
+        )
+
+    def start_along(k):
+        @pl.when(t < 3)
+        def _():
+            relay(k, t, 1, shard(k)).start()
+
+        @pl.when(t > 0)
+        def _():
+            relay(k, t, 0, shard(k)).start()
+
+    def pass_along(k, level):
+        for side, at in ((1, t - level), (0, t + level)):
+
+            @pl.when((at >= 0) & (at < 4))
+            def _():
+                block = both(k, at, dp)
+                move = relay(k, at, side, block)
+                move.wait_recv()
+
+                @pl.when((t < 3) if side else (t > 0))
+                def _():
+                    move.start()
+
+                for h in range(2):
+                    onward(k, at, h, slot(k, at, dp, h)).start()
+
+    def end_along(k):
+        for level in range(4):
+            for side, at in ((1, t - level), (0, t + level)):
+
+                @pl.when((at >= 0) & (at < 4) & ((t < 3) if side else (t > 0)))
+                def _():
+                    relay(k, at, side, both(k, at, dp)).wait_send()
+
     across = [
         [
-            copy(k, 11 + 2 * h + i, column(k, owner, h), column(k, owner, h), far[h], t)
+            copy(k, 2 * h + i, column(k, owner, h), column(k, owner, h), far[h], t)
             for h in range(2)
             for i, owner in enumerate((dp, near[h]))
         ]
         for k in range(chunks)
     ]
     over = [
-        [copy(k, 15 + i, all_of(k, owner), all_of(k, owner), dpc, t) for i, owner in enumerate((dp, dpx, dpy, dpxy))]
+        [copy(k, 4 + i, all_of(k, owner), all_of(k, owner), dpc, t) for i, owner in enumerate((dp, dpx, dpy, dpxy))]
         for k in range(chunks)
     ]
 
-    for item in along[0] + onward[0][0] + kept:
+    order = (1, 0, 2, 3)
+    start_along(order[0])
+    for item in kept:
         item.start()
-    for k in range(1, chunks):
-        for item in onward[k][0]:
-            item.start()
+    for k in order:
+        for h in range(2):
+            onward(k, t, h, part_of(k, h)).start()
+        if k == order[0]:
+            start_along(order[1])
 
     moved = side != c
     to_own = pltpu.make_async_copy(tok, row.at[c], here.at[4])
@@ -487,33 +540,38 @@
             def _():
                 first_copy(p).start()
 
-    for step in range(chunks + 2):
-        if step < chunks:
-            for item in along[step]:
-                item.wait_recv()
-            kept[step].wait()
-            if step + 1 < chunks:
-                for item in along[step + 1]:
-                    item.start()
-            if step == 0:
-                start_tokens()
-            if step == 1:
-                start_first()
-            for pair_of in onward[step][1:]:
-                for item in pair_of:
-                    item.start()
-            over[step][0].start()
-        if 0 <= step - 1 < chunks:
-            for pair_of in onward[step - 1]:
-                for item in pair_of:
-                    item.wait_recv()
-            for item in across[step - 1]:
-                item.start()
-        if 0 <= step - 2 < chunks:
-            for item in across[step - 2]:
-                item.wait_recv()
-            for item in over[step - 2][1:]:
-                item.start()
+    def pass_over(k):
+        for item in across[k]:
+            item.wait_recv()
+        for item in over[k][1:]:
+            item.start()
+
+    def pass_next(k):
+        for at in range(4):
+            for h in range(2):
+                onward(k, at, h, slot(k, at, dp, h)).wait_recv()
+        for item in across[k]:
+            item.start()
+
+    for i, k in enumerate(order):
+        pass_along(k, 1)
+        if i + 2 < chunks:
+            start_along(order[i + 2])
+        if i:
+            pass_next(order[i - 1])
+        pass_along(k, 2)
+        pass_along(k, 3)
+        kept[k].wait()
+        over[k][0].start()
+        if i == 2:
+            start_tokens()
+        if i == 3:
+            start_first()
+        if i >= 2:
+            pass_over(order[i - 2])
+    pass_next(order[3])
+    for k in order[2:]:
+        pass_over(k)
 
     @pl.when(moved)
     def _():
@@ -561,11 +619,12 @@
     for k in range(chunks):
         for item in over[k]:
             item.wait_recv()
-        for item in along[k] + across[k] + over[k]:
+        end_along(k)
+        for item in across[k] + over[k]:
             item.wait_send()
-        for pair_of in onward[k]:
-            for item in pair_of:
-                item.wait_send()
+        for at in range(4):
+            for h in range(2):
+                onward(k, at, h, slot(k, at, dp, h)).wait_send()
 
 
 def gather(tok, fv, small, big):
@@ -583,7 +642,14 @@
         ],
         in_specs=[vmem] * 4,
         out_specs=[any_spec()] * 4,
-        scratch_shapes=[sems((4, 19)), sems((4, 19)), sems((4,)), sems((2,)), sems((2,)), sems((6,))],
+        scratch_shapes=[
+            sems((4, 8)),
+            sems((4, 8)),
+            sems((4, 4, 2)),
+            sems((4, 4)),
+            sems((4, 4, 2)),
+            sems((4, 4, 2)),
+            sems((4,)), sems((2,)), sems((2,)), sems((6,))],
         compiler_params=params(collective_id=0, has_side_effects=True),
         name="gather",
     )(tok, fv, small, big)
@@ -665,92 +731,93 @@
     return (lane & 127) >> 5, lane >> 6
 
 
-def attend_kernel(bounds, q_ref, k_ref, v_ref, starts, o_ref, lse_ref, kept, top, total, acc):
-    of_qk, of_v = head_masks(TILE)
+def attend_kernel(bounds, q_ref, k_ref, v_ref, starts, o_ref, lse_ref, kept, turned, acc):
+    tiles = SEQ // TILE
+    of_qk, _ = head_masks(TILE)
     row = lax.broadcasted_iota(jnp.int32, (TILE, TILE), 0)
     lane = lax.broadcasted_iota(jnp.int32, (TILE, TILE), 1)
+    slabs = [slice(0, 256), slice(256, 512)]
+
+    def turn_values(j, carry):
+        there = pl.ds(pl.multiple_of(j * TILE, TILE), TILE)
+        turned[j] = v_ref[there, :].T
+        return carry
+
+    lax.fori_loop(0, tiles, turn_values, 0)
+
+    def eighths(values, reduce):
+        return reduce(values.reshape(TILE // 8, 8, 4 * TILE), axis=0)
 
     def query_tile(i, carry):
         here = pl.ds(pl.multiple_of(i * TILE, TILE), TILE)
-        q = q_ref[here, :]
-        zero = jnp.zeros_like(q)
-        q4 = jnp.concatenate([jnp.where(of_qk == h, q, zero) for h in range(4)], axis=0)
-        begin = starts[here, :]
-        begin = jnp.concatenate([begin, begin], axis=1)
-        at_row = row + i * TILE
+        q4 = []
+        for slab in slabs:
+            q = q_ref[here, slab]
+            zero = jnp.zeros_like(q)
+            q4.append(jnp.concatenate([jnp.where(of_qk == h, q, zero) for h in range(4)], axis=0))
         low = bounds[i]
-        top[...] = jnp.full_like(top, NEG)
-
-        def score(j, carry):
-            keys = k_ref[pl.ds(pl.multiple_of(j * TILE, TILE), TILE), :]
-            s = dot_nt(q4, keys)
-            at_lane = lane + j * TILE
-            ok = (at_lane >= begin) & (at_lane <= at_row)
-            for h in range(4):
-                part = slice(h * TILE, (h + 1) * TILE)
-                one = jnp.where(ok, s[part], NEG)
-                kept[j - low, part, :] = one
-                top[part] = jnp.maximum(top[part], jnp.maximum(one[:, :128], one[:, 128:]))
-            return carry
-
-        lax.fori_loop(low, i + 1, score, 0)
-        highest = jnp.max(top[...], axis=1, keepdims=True)
-        top[...] = jnp.broadcast_to(highest, top.shape)
-        total[...] = jnp.zeros_like(total)
+        begin = starts[pl.ds(i, 1), :]
+        limit = lane + i * TILE
+
+        def score(j, tops):
+            there = pl.ds(pl.multiple_of(j * TILE, TILE), TILE)
+            at_row = row + j * TILE
+            ok = (at_row >= begin) & (at_row <= limit)
+            ok = jnp.concatenate([ok] * 4, axis=1)
+            new = []
+            for u, slab in enumerate(slabs):
+                s = jnp.where(ok, dot_nt(k_ref[there, slab], q4[u]), NEG)
+                kept[j - low, u] = s
+                new.append(jnp.maximum(tops[u], eighths(s, jnp.max)))
+            return tuple(new)
+
+        start = jnp.full((8, 4 * TILE), NEG, F32)
+        tops = lax.fori_loop(low, i + 1, score, (start, start))
+        tops = [jnp.max(top, axis=0, keepdims=True) for top in tops]
         acc[...] = jnp.zeros_like(acc)
 
-        def weigh(j, carry):
-            values = v_ref[pl.ds(pl.multiple_of(j * TILE, TILE), TILE), :]
-            zero = jnp.zeros_like(values)
-            exps, parts = [], []
-            for h in range(4):
-                part = slice(h * TILE, (h + 1) * TILE)
-                peak = top[part]
-                e = jnp.exp(kept[j - low, part, :] - jnp.concatenate([peak, peak], axis=1))
-                total[part] += e[:, :128] + e[:, 128:]
-                exps.append(e.astype(BF16))
-                parts.append(jnp.where(of_v == h, values, zero))
-            acc[...] += dot(jnp.concatenate(exps, axis=1), jnp.concatenate(parts, axis=0))
-            return carry
-
-        lax.fori_loop(low, i + 1, weigh, 0)
-        sums = jnp.sum(total[...], axis=1, keepdims=True)
-        inverse = 1.0 / sums
-        scale = jnp.broadcast_to(inverse[:TILE], (TILE, 256))
-        for h in range(1, 4):
-            scale = jnp.where(of_v == h, inverse[h * TILE : (h + 1) * TILE], scale)
-        o_ref[here, :] = (acc[...] * scale).astype(BF16)
-        logs = top[...] + jnp.log(jnp.broadcast_to(sums, top.shape))
-        for h in range(4):
-            turned = logs[h * TILE : (h + 1) * TILE].T
-            lse_ref[0, pl.ds(i, 1), h * TILE : (h + 1) * TILE] = turned[:1]
+        def weigh(j, totals):
+            new = []
+            for u in range(2):
+                e = jnp.exp(kept[j - low, u] - tops[u])
+                p = e.astype(BF16)
+                for h in range(4):
+                    part = slice(u * 256 + h * 64, u * 256 + h * 64 + 64)
+                    acc[part] += dot(turned[j, part, :], p[:, h * TILE : (h + 1) * TILE])
+                new.append(totals[u] + eighths(e, jnp.sum))
+            return tuple(new)
+
+        zero = jnp.zeros((8, 4 * TILE), F32)
+        totals = lax.fori_loop(low, i + 1, weigh, (zero, zero))
+        for u, slab in enumerate(slabs):
+            total = jnp.sum(totals[u], axis=0, keepdims=True)
+            inverse = 1.0 / total
+            scaled = [
+                acc[u * 256 + h * 64 : u * 256 + h * 64 + 64] * inverse[:, h * TILE : (h + 1) * TILE] for h in range(4)
+            ]
+            o_ref[here, slab] = jnp.concatenate(scaled, axis=0).T.astype(BF16)
+            lse_ref[u, pl.ds(i, 1), :] = tops[u] + jnp.log(total)
         return carry
 
-    lax.fori_loop(0, SEQ // TILE, query_tile, 0)
+    lax.fori_loop(0, tiles, query_tile, 0)
 
 
 def attend(bounds, q, k, v, starts):
-    slab = pl.BlockSpec((SEQ, 256), lambda u, b: (0, u))
     tiles = SEQ // TILE
-    grid = pltpu.PrefetchScalarGridSpec(
-        num_scalar_prefetch=1,
-        grid=(2,),
-        in_specs=[slab, slab, slab, pl.BlockSpec((SEQ, 128), lambda u, b: (0, 0))],
-        out_specs=[slab, pl.BlockSpec((1, tiles, 4 * TILE), lambda u, b: (u, 0, 0))],
-        scratch_shapes=[
-            pltpu.VMEM((tiles, 4 * TILE, TILE), F32),
-            pltpu.VMEM((4 * TILE, 128), F32),
-            pltpu.VMEM((4 * TILE, 128), F32),
-            pltpu.VMEM((TILE, 256), F32),
-        ],
-    )
+    vmem = pl.BlockSpec(memory_space=pltpu.VMEM)
     return pl.pallas_call(
         attend_kernel,
         out_shape=[
             jax.ShapeDtypeStruct((SEQ, 512), BF16),
             jax.ShapeDtypeStruct((2, tiles, 4 * TILE), F32),
         ],
-        grid_spec=grid,
+        in_specs=[pl.BlockSpec(memory_space=pltpu.SMEM)] + [vmem] * 4,
+        out_specs=[vmem] * 2,
+        scratch_shapes=[
+            pltpu.VMEM((tiles, 2, TILE, 4 * TILE), F32),
+            pltpu.VMEM((tiles, 512, TILE), BF16),
+            pltpu.VMEM((512, TILE), F32),
+        ],
         compiler_params=params(),
         cost_estimate=cost(20e9, 12e6, 1e7),
         name="attend",
@@ -764,6 +831,7 @@
     of_qk, of_v = head_masks(TILE)
     row = lax.broadcasted_iota(jnp.int32, (TILE, TILE), 0)
     lane = lax.broadcasted_iota(jnp.int32, (TILE, TILE), 1)
+    slabs = [slice(0, 256), slice(256, 512)]
     pick = (lax.broadcasted_iota(jnp.int32, (8, 256), 1) >> 6) == lax.broadcasted_iota(
         jnp.int32, (8, 256), 0
     )
@@ -772,21 +840,22 @@
 
     def prepare(i, carry):
         here = pl.ds(pl.multiple_of(i * TILE, TILE), TILE)
-        both = do_ref[here, :].astype(F32) * o_ref[here, :].astype(F32)
-        sums = lax.dot_general(
-            pick, both, (((1,), (1,)), ((), ())), precision=lax.Precision.HIGHEST, preferred_element_type=F32
-        )
-        for h in range(4):
-            delta[pl.ds(i, 1), h * TILE : (h + 1) * TILE] = sums[h : h + 1]
+        for u, slab in enumerate(slabs):
+            both = do_ref[here, slab].astype(F32) * o_ref[here, slab].astype(F32)
+            sums = lax.dot_general(
+                pick, both, (((1,), (1,)), ((), ())), precision=lax.Precision.HIGHEST, preferred_element_type=F32
+            )
+            for h in range(4):
+                delta[u, pl.ds(i, 1), h * TILE : (h + 1) * TILE] = sums[h : h + 1]
         return carry
 
     lax.fori_loop(0, tiles, prepare, 0)
 
-    def rotate_out(values, here, out, scale):
+    def rotate_out(values, here, out, low, scale):
         a, b = values[:, :128], values[:, 128:]
         cos, sin = cosine[here, :], sine[here, :]
-        out[here, :128] = ((a * cos + b * sin) * scale).astype(BF16)
-        out[here, 128:] = ((b * cos - a * sin) * scale).astype(BF16)
+        out[here, low : low + 128] = ((a * cos + b * sin) * scale).astype(BF16)
+        out[here, low + 128 : low + 256] = ((b * cos - a * sin) * scale).astype(BF16)
 
     def split(values, of):
         zero = jnp.zeros_like(values)
@@ -794,74 +863,59 @@
 
     def key_tile(j, carry):
         there = pl.ds(pl.multiple_of(j * TILE, TILE), TILE)
-        keys, values = k_ref[there, :], v_ref[there, :]
-        k4 = split(keys, of_qk)
         at_row = row + j * TILE
         dk_acc[...] = jnp.zeros_like(dk_acc)
         dv_acc[...] = jnp.zeros_like(dv_acc)
 
         def query_tile(i, carry):
             here = pl.ds(pl.multiple_of(i * TILE, TILE), TILE)
-            q4 = split(q_ref[here, :], of_qk)
-            do4 = split(do_ref[here, :], of_v)
-            s = dot_nt(keys, q4)
-            dp = dot_nt(values, do4)
             at_lane = lane + i * TILE
             ok = (at_row >= starts[pl.ds(i, 1), :]) & (at_row <= at_lane)
-            lse, shift = lse_ref[0, pl.ds(i, 1), :], delta[pl.ds(i, 1), :]
-            ps, dss = [], []
-            for h in range(4):
-                part = slice(h * TILE, (h + 1) * TILE)
-                p = jnp.exp(jnp.where(ok, s[:, part] - lse[:, part], NEG))
-                ds = p * (dp[:, part] - shift[:, part])
-                ps.append(p.astype(BF16))
-                dss.append(ds.astype(BF16))
-            dv_acc[...] += dot(jnp.concatenate(ps, axis=1), do4)
-            dk_acc[...] += dot(jnp.concatenate(dss, axis=1), q4)
-            dq_acc[here, :] += dot_tn(jnp.concatenate(dss, axis=0), k4)
+            ok = jnp.concatenate([ok] * 4, axis=1)
+            for u, slab in enumerate(slabs):
+                q4 = split(q_ref[here, slab], of_qk)
+                do4 = split(do_ref[here, slab], of_v)
+                s = dot_nt(k_ref[there, slab], q4)
+                dp = dot_nt(v_ref[there, slab], do4)
+                p = jnp.exp(jnp.where(ok, s - lse_ref[u, pl.ds(i, 1), :], NEG))
+                ds = (p * (dp - delta[u, pl.ds(i, 1), :])).astype(BF16)
+                dv_acc[u] += dot(p.astype(BF16), do4)
+                dk_acc[u] += dot(ds, q4)
+                ds4 = jnp.concatenate([ds[:, h * TILE : (h + 1) * TILE] for h in range(4)], axis=0)
+                dq_acc[i, u] += dot_tn(ds4, split(k_ref[there, slab], of_qk))
             return carry
 
         lax.fori_loop(j, bounds[tiles + j] + 1, query_tile, 0)
-        rotate_out(dk_acc[...], there, dk_ref, 1.0)
-        dv_ref[there, :] = (0.5 * dv_acc[...]).astype(BF16)
+        for u, slab in enumerate(slabs):
+            rotate_out(dk_acc[u], there, dk_ref, u * 256, 1.0)
+            dv_ref[there, slab] = (0.5 * dv_acc[u]).astype(BF16)
         return carry
 
     lax.fori_loop(0, tiles, key_tile, 0)
 
-    def finish(i, carry):
+    def finish_tile(i, carry):
         here = pl.ds(pl.multiple_of(i * TILE, TILE), TILE)
-        rotate_out(dq_acc[here, :], here, dq_ref, 0.125)
+        for u in range(2):
+            rotate_out(dq_acc[i, u], here, dq_ref, u * 256, 0.125)
         return carry
 
-    lax.fori_loop(0, tiles, finish, 0)
+    lax.fori_loop(0, tiles, finish_tile, 0)
 
 
 def attend_back(bounds, q, k, v, do, o, lse, starts, cosine, sine):
-    slab = pl.BlockSpec((SEQ, 256), lambda u, b: (0, u))
-    whole = lambda shape: pl.BlockSpec(shape, lambda u, b: (0,) * len(shape))
     tiles = SEQ // TILE
-    grid = pltpu.PrefetchScalarGridSpec(
-        num_scalar_prefetch=1,
-        grid=(2,),
-        in_specs=[slab] * 5
-        + [
-            pl.BlockSpec((1, tiles, 4 * TILE), lambda u, b: (u, 0, 0)),
-            whole((tiles, TILE)),
-            whole((SEQ, 128)),
-            whole((SEQ, 128)),
-        ],
-        out_specs=[slab] * 3,
-        scratch_shapes=[
-            pltpu.VMEM((SEQ, 256), F32),
-            pltpu.VMEM((tiles, 4 * TILE), F32),
-            pltpu.VMEM((TILE, 256), F32),
-            pltpu.VMEM((TILE, 256), F32),
-        ],
-    )
+    vmem = pl.BlockSpec(memory_space=pltpu.VMEM)
     return pl.pallas_call(
         attend_back_kernel,
         out_shape=[jax.ShapeDtypeStruct((SEQ, 512), BF16)] * 3,
-        grid_spec=grid,
+        in_specs=[pl.BlockSpec(memory_space=pltpu.SMEM)] + [vmem] * 9,
+        out_specs=[vmem] * 3,
+        scratch_shapes=[
+            pltpu.VMEM((tiles, 2, TILE, 256), F32),
+            pltpu.VMEM((2, tiles, 4 * TILE), F32),
+            pltpu.VMEM((2, TILE, 256), F32),
+            pltpu.VMEM((2, TILE, 256), F32),
+        ],
         compiler_params=params(),
         cost_estimate=cost(50e9, 20e6, 1e7),
         name="attend_back",
@@ -1114,14 +1168,12 @@
     return (left.astype(F32) + right.astype(F32)).astype(BF16)
 
 
-def scatter_xy(keep1, got1, keep2, got2):
-    last1, last2 = across_y(add(keep1[1], got1[1])), across_x(add(keep2[1], got2[1]))
-    return add(keep1[0], got1[0]), last1, add(keep2[0], got2[0]), last2
-
-
-def turn_kernel(at, kept1, got1, kept2, got2, out, *, units):
+def turn_kernel(at, kept1, got1, last1, kept2, got2, last2, out, *, units):
     t = at[1]
-    sums = [kept1[...].astype(F32) + got1[...].astype(F32), kept2[...].astype(F32) + got2[...].astype(F32)]
+    sums = [
+        kept[0].astype(F32) + got[0].astype(F32) + last[...].astype(F32)
+        for kept, got, last in ((kept1, got1, last1), (kept2, got2, last2))
+    ]
     part = units // 4
     for h in range(2):
         for n in range(3):
@@ -1135,45 +1187,187 @@
 
 
 def turn(at, arrays, units):
-    vmem = pl.BlockSpec(memory_space=pltpu.VMEM)
+    length = arrays[0].shape[2]
     rows = 3 * (units // 2) + 256
+    half = pl.BlockSpec((1, 128, length), lambda i, at: (0, 0, 0))
+    last = pl.BlockSpec((128, length), lambda i, at: (0, 0))
+    grid = pltpu.PrefetchScalarGridSpec(
+        num_scalar_prefetch=1,
+        grid=(1,),
+        in_specs=[half, half, last] * 2,
+        out_specs=pl.BlockSpec((4, rows, 128), lambda i, at: (0, 0, 0)),
+    )
     return pl.pallas_call(
         functools.partial(turn_kernel, units=units),
         out_shape=jax.ShapeDtypeStruct((4, rows, 128), BF16),
-        in_specs=[pl.BlockSpec(memory_space=pltpu.SMEM)] + [vmem] * 4,
-        out_specs=vmem,
+        grid_spec=grid,
         compiler_params=params(),
-        cost_estimate=cost(1e6, 8e6),
+        cost_estimate=cost(1e6, 10e6),
         name="turn",
     )(at, *arrays)
 
 
-def final_kernel(a, b, c, d, gate, up, down, out):
-    total = a[...].astype(F32) + b[...].astype(F32) + c[...].astype(F32) + d[...].astype(F32)
-    part = down.shape[0]
-    gate[...] = total[:part].T
-    up[...] = total[part : 2 * part].T
-    down[...] = total[2 * part : 3 * part]
-    out[...] = total[3 * part :]
-
-
-def scatter_t(pieces):
-    return [pieces[0]] + [along_t(pieces[d], d) for d in (1, 2, 3)]
-
-
-def final(pieces, part):
+def last_kernel(pieces, send1, keep1, send2, keep2, tok, gains, got_pieces, own_heads, got_heads, got_tok, sums, *rest):
+    (got1, got2, part1, part2, last1, last2, heads, held, came, p_sem, h_sem, one_sem, two_sem, swap, g_sem) = rest
+    dp, t = lax.axis_index("dp"), lax.axis_index("tensor")
+    c, x, y = lax.rem(dp, 2), lax.rem(lax.div(dp, 2), 2), lax.div(dp, 4)
+    pair, side = lax.div(t, 2), lax.rem(t, 2)
+    plane = dp - c
+    dpx, dpy, dpc = dp + 2 - 4 * x, dp + 4 - 8 * y, dp + 1 - 2 * c
+    meet(plane, c, t, dpx, dpy)
+
+    def copy(src, dst, sems, n, to):
+        return pltpu.make_async_remote_copy(
+            src_ref=src,
+            dst_ref=dst,
+            send_sem=sems.at[0, n],
+            recv_sem=sems.at[1, n],
+            device_id=to,
+            device_id_type=MESH,
+        )
+
+    ones = [copy(send1, got1, one_sem, 0, (dpx, t)), copy(send2, got2, one_sem, 1, (dpy, t))]
+    for item in ones:
+        item.start()
+    turns = (dpc, t), (dpx, t), (dpy, t), (dp, t + 1 - 2 * side), (dp, lax.rem(t + 2, 4))
+    held[0] = gains[...]
+    zs = [copy(pieces.at[d], got_pieces.at[d - 1], p_sem, d - 1, (dp, lax.rem(t + d, 4))) for d in (1, 2, 3)]
+    for item in zs:
+        item.start()
+    moved = side != c
+    swapped = copy(tok, got_tok, swap, 0, (plane + side, 2 * pair + c))
+
+    @pl.when(moved)
+    def _():
+        swapped.start()
+
+    def gain_step(n):
+        return copy(held.at[n], came.at[n], g_sem, n, turns[n])
+
+    def gain_next(n):
+        gain_step(n).wait_recv()
+        held[n + 1] = held[n] + came[n]
+
+    gain_step(0).start()
+    for item in ones:
+        item.wait_recv()
+    part1[...] = add(keep1[1], got1[1])
+    part2[...] = add(keep2[1], got2[1])
+    gain_next(0)
+    first1 = keep1[0].astype(F32) + got1[0].astype(F32)
+    first2 = keep2[0].astype(F32) + got2[0].astype(F32)
+    twos = [copy(part1, last1, two_sem, 0, (dpy, t)), copy(part2, last2, two_sem, 1, (dpx, t))]
+    for item in twos:
+        item.start()
+    gain_step(1).start()
+    gain_next(1)
+    for item in twos:
+        item.wait_recv()
+    totals = ((first1 + last1[...].astype(F32)).astype(BF16), (first2 + last2[...].astype(F32)).astype(BF16))
+    for e, total in enumerate(totals):
+        core = (c, 1 - c)[e]
+        for u in range(2):
+            d = lax.rem(2 * core + u + 4 - t, 4)
+            for n in range(3):
+                heads[d, n] = total[:, n * 512 + u * 256 : n * 512 + u * 256 + 256]
+    gain_step(2).start()
+    gain_next(2)
+    own_heads[...] = heads[0]
+    hs = [copy(heads.at[d], got_heads.at[d - 1], h_sem, d - 1, (dp, lax.rem(t + d, 4))) for d in (1, 2, 3)]
+    for item in hs:
+        item.start()
+    for n in (3, 4):
+        gain_step(n).start()
+        gain_next(n)
+    sums[...] = held[5]
+    for item in ones + twos:
+        item.wait_send()
+    for n in range(5):
+        gain_step(n).wait_send()
+    for item in zs + hs:
+        item.wait()
+
+    @pl.when(moved)
+    def _():
+        swapped.wait()
+
+
+def last_exchanges(pieces, send1, keep1, send2, keep2, tok, gains):
+    vmem = pl.BlockSpec(memory_space=pltpu.VMEM)
+    sems = pltpu.SemaphoreType.DMA
+    rows = pieces.shape[1]
+    half = send1.shape
     return pl.pallas_call(
-        final_kernel,
+        last_kernel,
         out_shape=[
-            jax.ShapeDtypeStruct((128, part), F32),
-            jax.ShapeDtypeStruct((128, part), F32),
-            jax.ShapeDtypeStruct((part, 128), F32),
-            jax.ShapeDtypeStruct((256, 128), F32),
+            jax.ShapeDtypeStruct((3, rows, 128), BF16),
+            jax.ShapeDtypeStruct((3, 128, 256), BF16),
+            jax.ShapeDtypeStruct((3, 3, 128, 256), BF16),
+            jax.ShapeDtypeStruct(tok.shape, BF16),
+            jax.ShapeDtypeStruct(gains.shape, F32),
         ],
+        in_specs=[vmem] * 7,
+        out_specs=[any_spec(), vmem, any_spec(), any_spec(), vmem],
+        scratch_shapes=[pltpu.VMEM(half, BF16)] * 2
+        + [pltpu.VMEM(half[1:], BF16)] * 4
+        + [pltpu.VMEM((4, 3, 128, 256), BF16), pltpu.VMEM((6,) + gains.shape, F32), pltpu.VMEM((5,) + gains.shape, F32)]
+        + [sems((2, 3)), sems((2, 3)), sems((2, 2)), sems((2, 2)), sems((2, 1)), sems((2, 5))],
+        compiler_params=params(collective_id=2, has_side_effects=True),
+        name="last_exchanges",
+    )(pieces, send1, keep1, send2, keep2, tok, gains)
+
+
+def finish_kernel(at, own, got, own_heads, got_heads, tok, got_tok, gate, up, down, out, query, key, value, tok_out):
+    @pl.when(pl.program_id(0) == 0)
+    def _():
+        part = down.shape[0]
+        for n, ref in enumerate((gate, up, down, out)):
+            rows = slice(n * part, n * part + ref.shape[0])
+            total = own[0, rows, :].astype(F32)
+            for d in range(3):
+                total += got[d, rows, :].astype(F32)
+            ref[...] = total
+        heads = own_heads[...].astype(F32)
+        for d in range(3):
+            heads += got_heads[d].astype(F32)
+        for n, ref in enumerate((query, key)):
+            parts = []
+            for h in range(4):
+                parts += [heads[n, :, h * 32 : h * 32 + 32], heads[n, :, 128 + h * 32 : 160 + h * 32]]
+            ref[...] = jnp.concatenate(parts, axis=1)
+        value[...] = heads[2]
+
+    stays = (at[0] & 1) == (at[1] & 1)
+    tok_out[...] = jnp.where(stays, tok[...], got_tok[...]).astype(F32)
+
+
+def finish(at, pieces, got, own_heads, got_heads, tok, got_tok, part):
+    count, wide = tok.shape
+    rows = 256
+    row = pl.BlockSpec((rows, wide), lambda i, at: (i, 0))
+    whole = lambda *shape: pl.BlockSpec(shape, lambda i, at: (0,) * len(shape))
+    shapes = [(part, 128)] * 3 + [(256, 128)] + [(128, 256)] * 3
+    grid = pltpu.PrefetchScalarGridSpec(
+        num_scalar_prefetch=1,
+        grid=(count // rows,),
+        in_specs=[
+            whole(1, pieces.shape[1], 128),
+            whole(*got.shape),
+            whole(*own_heads.shape),
+            whole(*got_heads.shape),
+            row,
+            row,
+        ],
+        out_specs=[whole(*shape) for shape in shapes] + [row],
+    )
+    return pl.pallas_call(
+        finish_kernel,
+        out_shape=[jax.ShapeDtypeStruct(shape, F32) for shape in shapes + [(count, wide)]],
+        grid_spec=grid,
         compiler_params=params(),
-        cost_estimate=cost(1e6, 4e6),
-        name="final",
-    )(*pieces)
+        cost_estimate=cost(1e6, 18e6),
+        name="finish",
+    )(at, pieces, got, own_heads, got_heads, tok, got_tok)
 
 
 def project_back_kernel(at, dq, dk, dv, held, out):
@@ -1304,49 +1498,6 @@
     )(at, left, dq, dk, dv)
 
 
-def heads_turn_kernel(at, kept1, got1, kept2, got2, out):
-    c, t = at[0] & 1, at[1]
-    for e, (kept, got) in enumerate(((kept1, got1), (kept2, got2))):
-        total = (kept[...].astype(F32) + got[...].astype(F32)).astype(BF16)
-        for u in range(2):
-            d = (2 * (c ^ e) + u - t) & 3
-            for n in range(3):
-                out[d, n] = total[:, n * 512 + u * 256 : n * 512 + u * 256 + 256]
-
-
-def heads_turn(at, arrays):
-    vmem = pl.BlockSpec(memory_space=pltpu.VMEM)
-    return pl.pallas_call(
-        heads_turn_kernel,
-        out_shape=jax.ShapeDtypeStruct((4, 3, 128, 256), BF16),
-        in_specs=[pl.BlockSpec(memory_space=pltpu.SMEM)] + [vmem] * 4,
-        out_specs=vmem,
-        compiler_params=params(),
-        cost_estimate=cost(1e6, 3e6),
-        name="heads_turn",
-    )(at, *arrays)
-
-
-def heads_final_kernel(a, b, c, d, query, key, value):
-    total = a[...].astype(F32) + b[...].astype(F32) + c[...].astype(F32) + d[...].astype(F32)
-    for n, out in enumerate((query, key)):
-        parts = []
-        for h in range(4):
-            parts += [total[n, :, h * 32 : h * 32 + 32], total[n, :, 128 + h * 32 : 160 + h * 32]]
-        out[...] = jnp.concatenate(parts, axis=1)
-    value[...] = total[2]
-
-
-def heads_final(pieces):
-    return pl.pallas_call(
-        heads_final_kernel,
-        out_shape=[jax.ShapeDtypeStruct((128, 256), F32)] * 3,
-        compiler_params=params(),
-        cost_estimate=cost(1e6, 2e6),
-        name="heads_final",
-    )(*pieces)
-
-
 def fast_body(tokens, first_values, doc_lengths, cotangent, w_query, w_key, w_value, w_out, w_gate, w_up, w_down, gain_attn, gain_mlp):
     me, t = lax.axis_index("dp"), lax.axis_index("tensor")
     c = me % 2
@@ -1365,9 +1516,9 @@
     places = jnp.arange(SEQ, dtype=jnp.int32)
     starts = jnp.max(jnp.where(ends[None, :] <= places[:, None], ends[None, :], 0), axis=1)
     last = jnp.arange(tiles, dtype=jnp.int32) * TILE + (TILE - 1)
-    finish = jnp.min(jnp.where(ends[None, :] > last[:, None], ends[None, :], SEQ), axis=1)
-    bounds = jnp.concatenate([starts.reshape(tiles, TILE)[:, 0] // TILE, (finish - 1) // TILE])
-    starts_wide = jnp.broadcast_to(starts[:, None], (SEQ, 128))
+    stop = jnp.min(jnp.where(ends[None, :] > last[:, None], ends[None, :], SEQ), axis=1)
+    bounds = jnp.concatenate([starts.reshape(tiles, TILE)[:, 0] // TILE, (stop - 1) // TILE])
+    starts_by_tile = starts.reshape(tiles, TILE)
     freqs = 10000.0 ** (-(jnp.arange(32, dtype=F32) * 2.0 / HEAD))
     angles = (places - starts).astype(F32)[:, None] * jnp.tile(freqs, 4)[None, :]
     cosine, sine = jnp.cos(angles), jnp.sin(angles)
@@ -1375,7 +1526,7 @@
     row, cotangent = lax.optimization_barrier((row, cotangent))
     moved_cot = swap_halves(cotangent)
     normed_one, q, k, v = project(at, row, first, cosine, sine, gain_attn[None], small)
-    attended, lse = attend(bounds, q, k, v, starts_wide)
+    attended, lse = attend(bounds, q, k, v, starts_by_tile)
     by_half = attended.reshape(2, SEQ // 2, 512)
     att_own = lax.dynamic_index_in_dim(by_half, c, 0, keepdims=False)
     att_other = across_c(lax.dynamic_index_in_dim(by_half, 1 - c, 0, keepdims=False))
@@ -1392,10 +1543,10 @@
     kept, do = lax.optimization_barrier((kept, do))
     got1, got2 = across_x(kept[0]), across_y(kept[2])
 
-    dq, dk, dv = attend_back(bounds, q, k, v, do, attended, lse, starts.reshape(tiles, TILE), cosine, sine)
+    dq, dk, dv = attend_back(bounds, q, k, v, do, attended, lse, starts_by_tile, cosine, sine)
 
     dq, dk, dv, got1, got2 = lax.optimization_barrier((dq, dk, dv, got1, got2))
-    sums = scatter_xy(kept[1], got1, kept[3], got2)
+    last1, last2 = across_y(add(kept[1][1], got1[1])), across_x(add(kept[3][1], got2[1]))
 
     def first_back(r):
         slab = jnp.where(pair == r, dv[:, :256], dv[:, 256:])
@@ -1412,18 +1563,14 @@
     send2, keep2 = heads_gradient(heads_send_kernel, "heads_send", at, normed_one, dq, dk, dv)
     send2, keep2 = across_c(send2), across_c(keep2)
     send1, keep1 = heads_gradient(heads_keep_kernel, "heads_keep", at, normed_one, dq, dk, dv)
-    grad_gate, grad_up, grad_down, grad_out = final(scatter_t(turn(at, sums, hid.shape[2] // 2)), w_gate.shape[1])
-    head_sums = scatter_xy(keep1, across_x(send1), keep2, across_y(send2))
     grad_tokens, gain_one = project_back_keep(at, dq, dk, dv, small, gn_got, row, grad_hidden, gain_attn[None])
-    grad_tokens = jnp.where(stays, grad_tokens, swap_halves(grad_tokens)).astype(F32)
-    gq, gk, gv = heads_final(scatter_t(heads_turn(at, head_sums)))
-
+    pieces = turn(at, (kept[1], got1, last1, kept[3], got2, last2), hid.shape[2] // 2)
     gains = jnp.stack([jnp.sum(gain_one, axis=0), jnp.sum(gain_two, axis=0)]).reshape(16, 128)
-    gains = gains + across_c(gains)
-    gains = gains + across_x(gains)
-    gains = gains + across_y(gains)
-    gains = gains + move(gains, lambda y, x, c, t: (y, x, c, t ^ 1))
-    gains = gains + move(gains, lambda y, x, c, t: (y, x, c, t ^ 2))
+    pieces, grad_first = lax.optimization_barrier((pieces, grad_first))
+    got, own_heads, got_heads, got_tokens, gains = last_exchanges(pieces, send1, keep1, send2, keep2, grad_tokens, gains)
+    grad_gate, grad_up, grad_down, grad_out, gq, gk, gv, grad_tokens = finish(
+        at, pieces, got, own_heads, got_heads, grad_tokens, got_tokens, w_gate.shape[1]
+    )
     gains = gains.reshape(2, wide)
     return (
         layer_out,
@@ -1433,8 +1580,8 @@
         gk,
         gv,
         grad_out,
-        grad_gate,
-        grad_up,
+        grad_gate.T,
+        grad_up.T,
         grad_down,
         gains[0],
         gains[1],

time: 622 us -> 537 us (0.86)
  the two profiles are of different devices: /device:TPU:11 before, /device:TPU:0 now
where the time goes in v3:
time: 537 us; the launch traced here: 531 us
  Pallas kernels  470 us (88%)
  other arithmetic  28.3 us (5%)
  starting transfers between devices  13.7 us (3%)
  waiting for transfers between devices  11.9 us (2%)
  local copies, waits for them, and re-layouts  6.63 us (1%)
    pallas_call x1, Pallas kernels, gather(): pl.pallas_call(gather_kernel, out_shape=[jax.ShapeDtypeStruct((2, SEQ //...  133 us
    pallas_call x1, Pallas kernels, last_exchanges(): pl.pallas_call(last_kernel, out_shape=[jax.ShapeDtypeStruct((3, rows, 128...  95.6 us
    pallas_call x1, Pallas kernels, mlp(): pl.pallas_call(mlp_kernel, out_shape=[tokens(wide), tokens(wide, F32), to...  60.2 us
    pallas_call x1, Pallas kernels, attend_back(): pl.pallas_call(attend_back_kernel, out_shape=[jax.ShapeDtypeStruct((SEQ,...  49.3 us
    pallas_call x1, Pallas kernels, weights(): pl.pallas_call(weights_kernel, out_shape=[jax.ShapeDtypeStruct((2, 128, l...  36.5 us
    pallas_call x1, Pallas kernels, attend(): pl.pallas_call(attend_kernel, out_shape=[jax.ShapeDtypeStruct((SEQ, 512),...  28 us
    pallas_call x2, Pallas kernels, heads_gradient(): pl.pallas_call(kernel, out_shape=[jax.ShapeDtypeStruct((2, 128, 1536), BF...  19.5 us
    ppermute x14, starting transfers between devices, move(): return lax.ppermute(values, AXES, pairs)  13.7 us
  transfers between devices with their start and end apart: 14, of which 3 were waited for; matrix products, arithmetic and copies ran while one was open for 6% of the time, Pallas kernels for 56%

profile of v3, /device:TPU:0, one launch (start us, length us, event | category | flops | bytes accessed | tf_op | source)
XLA Modules:
  0.0 531.1 jit_solution(889624465958411523)
XLA Ops:
  4.1 132.9 %gather.1 = (bf16[2,1024,1024]{2,1,0:T(8,128)(2,1)}, bf16[2,2048,256]{2,1,0:T(8,128)(2,1)}, bf16[4,4,1024,256]{3,2,1,0:T(8,128)(2,1)}, bf16[3,8,2,4,352,128]{5,4,3,2,1,0:T(8,128)(2,1)}) custom-call(bf16[1024,1024]{1,0:T(8,128)(2,1)} %tok.1, bf16[4096,256]{1,0:T(8,128)(2,1)} %fv.1, bf16[4,128,256]{2,1,0:T(8,128)(2,1)} %get-tuple-element.73.small, ...), custom_call_target="tpu_custom_call" | custom-call | tf_op jit(solution)/shard_map/gather/pallas_call | solution.py:635
  140.2 5.6 %multiply_sine_fusion = (f32[2048,128]{1,0:T(8,128)}, f32[2048,128]{1,0:T(8,128)}) fusion(f32[128]{0:T(128)S(1)} %mul.55, f32[2048]{0:T(1024)S(1)} %subtract_convert_fusion), kind=kLoop, calls=%fused_computation.5 | loop fusion | flops 262144 | bytes 2105856 | tf_op jit(solution)/shard_map/sin | solution.py:1524
  146.4 12.8 %project.1 = (bf16[2048,1024]{1,0:T(8,128)(2,1)}, bf16[2048,512]{1,0:T(8,128)(2,1)}, bf16[2048,512]{1,0:T(8,128)(2,1)}, bf16[2048,512]{1,0:T(8,128)(2,1)}) custom-call(s32[8]{0:T(128)} %compare_select_fusion.at, bf16[2,1024,1024]{2,1,0:T(8,128)(2,1)} %get-tuple-element.76.tok, bf16[2,2048,256]{2,1,0:T(8,128)(2,1)} %get-tuple-element.77.first, ...), custom_call_target="tpu_custom_call" | custom-call | flops 6442450944 | bytes 24000000 | tf_op jit(solution)/shard_map/project/pallas_call | solution.py:718
  159.2 28.0 %attend.1 = (bf16[2048,512]{1,0:T(8,128)(2,1)}, f32[2,8,1024]{2,1,0:T(8,128)}) custom-call(s32[16]{0:T(128)} %pad_add_fusion.bounds, bf16[2048,512]{1,0:T(8,128)(2,1)} %get-tuple-element.79.q_ref, bf16[2048,512]{1,0:T(8,128)(2,1)} %get-tuple-element.80.k_ref, bf16[2048,512]{1,0:T(8,128)(2,1)} %get-tuple-element.81.v_ref, s32[8,256]{1,0:T(8,128)} %copy-done.4), custom_call_target="tpu_custom_call" | custom-call | flops 20000000000 | bytes 12000000 | tf_op jit(solution)/shard_map/attend/pallas_call | solution.py:808
  187.1 2.7 dynamic-slice_bitcast_fusion
  190.2 2.3 collective-permute-done.1.att_other.other
  193.4 60.2 %mlp.1 = (bf16[1024,1024]{1,0:T(8,128)(2,1)}, f32[1024,1024]{1,0:T(8,128)}, bf16[1024,1024]{1,0:T(8,128)(2,1)}, bf16[1024,1024]{1,0:T(8,128)(2,1)}, bf16[3,1024,...) custom-call(s32[8]{0:T(128)} %compare_select_fusion.at, ...), custom_call_target="tpu_custom_call" | custom-call | flops 39728447488 | bytes 60000000 | tf_op jit(solution)/shard_map/mlp/pallas_call | solution.py:1015
  256.8 36.5 %weights.1 = (bf16[2,128,4736]{2,1,0:T(8,128)(2,1)}, bf16[2,128,4736]{2,1,0:T(8,128)(2,1)}, bf16[2,128,4736]{2,1,0:T(8,128)(2,1)}, bf16[2,128,4736]{2,1,0:T(8,128)(2,1)}) custom-call(bf16[1024,1024]{1,0:T(8,128)(2,1)} %get-tuple-element.86.n2, bf16[1024,1024]{1,0:T(8,128)(2,1)} %get-tuple-element.87.g, bf16[1024,1024]{1,0:T(8,128)(2,1)} %get-tuple-element.88.branch, ...), custom_call_target="tpu_custom_call" | custom-call | flops 19864223744 | bytes 50000000 | tf_op jit(solution)/shard_map/weights/pallas_call | solution.py:1157
  293.3 3.5 maximum_select_fusion.do_ref
  298.2 2.3 collective-permute-start.6
  300.5 49.3 %attend_back.1 = (bf16[2048,512]{1,0:T(8,128)(2,1)}, bf16[2048,512]{1,0:T(8,128)(2,1)}, bf16[2048,512]{1,0:T(8,128)(2,1)}) custom-call(s32[16]{0:T(128)} %pad_add_fusion.bounds, bf16[2048,512]{1,0:T(8,128)(2,1)} %get-tuple-element.79.q_ref, bf16[2048,512]{1,0:T(8,128)(2,1)} %get-tuple-element.80.k_ref, bf16[2048,512]{1,0:T(8,128)(2,1)} %get-tuple-element.81.v_ref, ...), custom_call_target="tpu_custom_call" | custom-call | flops 49999998976 | bytes 20000000 | tf_op jit(solution)/shard_map/attend_back/pallas_call | solution.py:908
  349.8 3.1 broadcast_select_fusion
  353.3 8.1 %project_back_send.1 = bf16[1024,1024]{1,0:T(8,128)(2,1)} custom-call(s32[8]{0:T(128)} %compare_select_fusion.at, bf16[2048,512]{1,0:T(8,128)(2,1)} %get-tuple-element.110.dq, bf16[2048,512]{1,0:T(8,128)(2,1)} %get-tuple-element.111.dk, bf16[2048,512]{1,0:T(8,128)(2,1)} %get-tuple-element.107.dv, bf16[4,4,1024,256]{3,2,1,0:T(8,128)(2,1)} %get-tuple-element.78.held.wo), custom_call_target="tpu_custom_call" | custom-call | flops 3221225472 | bytes 10000000 | tf_op jit(solution)/shard_map/project_back_send/pallas_call | solution.py:1400
  361.5 2.9 broadcast_select_fusion.1
  367.6 2.7 fusion.1
  370.8 2.7 fusion
  373.9 9.8 %heads_send.1 = (bf16[2,128,1536]{2,1,0:T(8,128)(2,1)}, bf16[2,128,1536]{2,1,0:T(8,128)(2,1)}) custom-call(s32[8]{0:T(128)} %compare_select_fusion.at, bf16[2048,1024]{1,0:T(8,128)(2,1)} %get-tuple-element.109.left, bf16[2048,512]{1,0:T(8,128)(2,1)} %get-tuple-element.110.dq, bf16[2048,512]{1,0:T(8,128)(2,1)} %get-tuple-element.111.dk, ...), custom_call_target="tpu_custom_call" | custom-call | flops 3221225472 | bytes 12000000 | tf_op jit(solution)/shard_map/heads_send/pallas_call | solution.py:1491
  383.7 9.8 %heads_keep.1 = (bf16[2,128,1536]{2,1,0:T(8,128)(2,1)}, bf16[2,128,1536]{2,1,0:T(8,128)(2,1)}) custom-call(s32[8]{0:T(128)} %compare_select_fusion.at, bf16[2048,1024]{1,0:T(8,128)(2,1)} %get-tuple-element.109.left, bf16[2048,512]{1,0:T(8,128)(2,1)} %get-tuple-element.110.dq, bf16[2048,512]{1,0:T(8,128)(2,1)} %get-tuple-element.111.dk, ...), custom_call_target="tpu_custom_call" | custom-call | flops 3221225472 | bytes 12000000 | tf_op jit(solution)/shard_map/heads_keep/pallas_call | solution.py:1491
  393.5 9.2 %collective-permute-done.10 = bf16[2048,256]{1,0:T(8,128)(2,1)} collective-permute-done((bf16[2048,256]{1,0:T(8,128)(2,1)S(1)}, bf16[2048,256]{1,0:T(8,128)(2,1)}, u32[]{:S(2)}, u32[]{:S(2)}) %collective-permute-start.10) | collective-permute-done | bytes 1048608 | tf_op jit(solution)/shard_map/ppermute | solution.py:309
  404.9 2.3 maximum_convert_fusion
  407.3 6.3 %turn.1.pieces.own = bf16[4,2368,128]{2,1,0:T(8,128)(2,1)} custom-call(s32[8]{0:T(128)} %compare_select_fusion.at, bf16[2,128,4736]{2,1,0:T(8,128)(2,1)} %get-tuple-element.96.kept1, bf16[2,128,4736]{2,1,0:T(8,128)(2,1)} %collective-permute-done.5.got1, bf16[128,4736]{1,0:T(8,128)(2,1)} %collective-permute-done.7.last1, ...), custom_call_target="tpu_custom_call" | custom-call | flops 1000000 | bytes 10000000 | tf_op jit(solution)/shard_map/turn/pallas_call | solution.py:1200
  413.6 10.7 %project_back_keep.1 = (bf16[1024,1024]{1,0:T(8,128)(2,1)}, f32[8,1024]{1,0:T(8,128)}) custom-call(s32[8]{0:T(128)} %compare_select_fusion.at, bf16[2048,512]{1,0:T(8,128)(2,1)} %get-tuple-element.110.dq, bf16[2048,512]{1,0:T(8,128)(2,1)} %get-tuple-element.111.dk, bf16[2048,512]{1,0:T(8,128)(2,1)} %get-tuple-element.107.dv, ...), custom_call_target="tpu_custom_call" | custom-call | flops 3221225472 | bytes 20000000 | tf_op jit(solution)/shard_map/project_back_keep/pallas_call | solution.py:1439
  426.6 95.6 %last_exchanges.1 = (bf16[3,2368,128]{2,1,0:T(8,128)(2,1)}, bf16[3,128,256]{2,1,0:T(8,128)(2,1)}, bf16[3,3,128,256]{3,2,1,0:T(8,128)(2,1)}, bf16[1024,1024]{1,0:T(8,128)(2,1)}, f32[16,128]{1,0:T(8,128)}) custom-call(bf16[4,2368,128]{2,1,0:T(8,128)(2,1)} %turn.1.pieces.own, bf16[2,128,1536]{2,1,0:T(8,128)(2,1)} %get-tuple-element.112.send1, ...), custom_call_target="tpu_custom_call" | custom-call | tf_op jit(solution)/shard_map/last_exchanges/pallas_call | solution.py:1300
  523.5 7.5 %finish.1 = (f32[704,128]{1,0:T(8,128)}, f32[704,128]{1,0:T(8,128)}, f32[704,128]{1,0:T(8,128)}, f32[256,128]{1,0:T(8,128)}, f32[128,256]{1,0:T(8,128)}, /*index...) custom-call(s32[8]{0:T(128)} %compare_select_fusion.at, bf16[4,2368,128]{2,1,0:T(8,128)(2,1)} %turn.1.pieces.own, ...), custom_call_target="tpu_custom_call" | custom-call | flops 1000000 | bytes 18000000 | tf_op jit(solution)/shard_map/finish/pallas_call | solution.py:1363
  (63 shorter events, 23.6 us)
Async XLA Ops:
  0.6 139.0 %collective-permute-start = (s32[2,8]{1,0:T(2,128)}, s32[2,8]{1,0:T(2,128)S(1)}, u32[]{:S(2)}, u32[]{:S(2)}) collective-permute-start(s32[2,8]{1,0:T(2,128)} %param.15), channel_id=1, source_target_pairs={{0,4},{1,5},{2,6},{3,7},{4,0},{5,1},{6,2},{7,3},{8,12},{9,13},{10,... | collective-permute-start | bytes 200 | tf_op jit(solution)/shard_map/ppermute | solution.py:309
  4.1 135.5 %copy-start.5 = (s32[2,8]{1,0:T(2,128)S(1)}, s32[2,8]{1,0:T(2,128)}, u32[]{:S(2)}) copy-start(s32[2,8]{1,0:T(2,128)} %param.15) | copy-start | bytes 196
  137.0 55.4 %collective-permute-start.2 = (bf16[1024,1024]{1,0:T(8,128)(2,1)}, bf16[1024,1024]{1,0:T(8,128)(2,1)}, u32[]{:S(2)}, u32[]{:S(2)}) collective-permute-start(bf16[1024,1024]{1,0:T(8,128)(2,1)} %cot_here), channel_id=1, source_target_pairs={{1,4},{3,6},{4,1},{6,3},{9,12},{11,14},{12,9},{14,11},{17,20},{19,... | collective-permute-start | bytes 6291464 | tf_op jit(solution)/shard_map/ppermute | solution.py:309
  139.9 19.2 %copy-start.4 = (s32[8,256]{1,0:T(8,128)}, s32[8,256]{1,0:T(8,128)S(1)}, u32[]{:S(2)}) copy-start(s32[8,256]{1,0:T(8,128)S(1)} %reshape.83.starts) | copy-start | bytes 24580
  189.8 2.7 collective-permute-start.1
  192.5 1.0 copy-start.6
  253.6 39.6 %collective-permute-start.4 = (bf16[1024,512]{1,0:T(8,128)(2,1)}, bf16[1024,512]{1,0:T(8,128)(2,1)}, u32[]{:S(2)}, u32[]{:S(2)}) collective-permute-start(bf16[1024,512]{1,0:T(8,128)(2,1)} %get-tuple-element.95), channel_id=1, source_target_pairs={{0,4},{1,5},{2,6},{3,7},{4,0},{5,1},{6,2},{7,3},{8,12},{9,13},{10,... | collective-permute-start | bytes 3145736 | tf_op jit(solution)/shard_map/ppermute | solution.py:309
  254.1 95.8 %collective-permute-start.3 = (bf16[1024,1024]{1,0:T(8,128)(2,1)}, bf16[1024,1024]{1,0:T(8,128)(2,1)}, u32[]{:S(2)}, u32[]{:S(2)}) collective-permute-start(bf16[1024,1024]{1,0:T(8,128)(2,1)} %get-tuple-element.85), channel_id=1, source_target_pairs={{1,4},{3,6},{4,1},{6,3},{9,12},{11,14},{12,9},{14,11},{17,20},{19,... | collective-permute-start | bytes 6291464 | tf_op jit(solution)/shard_map/ppermute | solution.py:309
  256.8 36.5 %copy-start.2 = (bf16[1024,512]{1,0:T(8,128)(2,1)S(1)}, bf16[1024,512]{1,0:T(8,128)(2,1)}, u32[]{:S(2)}) copy-start(bf16[1024,512]{1,0:T(8,128)(2,1)} %get-tuple-element.94) | copy-start | bytes 3145732
  296.8 56.2 %collective-permute-start.5 = (bf16[2,128,4736]{2,1,0:T(8,128)(2,1)}, bf16[2,128,4736]{2,1,0:T(8,128)(2,1)}, u32[]{:S(2)}, u32[]{:S(2)}) collective-permute-start(bf16[2,128,4736]{2,1,0:T(8,128)(2,1)} %get-tuple-element.102), channel_id=1, source_target_pairs={{0,8},{1,9},{2,10},{3,11},{4,12},{5,13},{6,14},{7,15},{8,0},{9,1},... | collective-permute-start | bytes 7274504 | tf_op jit(solution)/shard_map/ppermute | solution.py:309
  298.2 55.1 %collective-permute-start.6 = (bf16[2,128,4736]{2,1,0:T(8,128)(2,1)}, bf16[2,128,4736]{2,1,0:T(8,128)(2,1)}, u32[]{:S(2)}, u32[]{:S(2)}) collective-permute-start(bf16[2,128,4736]{2,1,0:T(8,128)(2,1)} %get-tuple-element.103), channel_id=1, source_target_pairs={{0,16},{1,17},{2,18},{3,19},{4,20},{5,21},{6,22},{7,23},{8,24},{9,... | collective-permute-start | bytes 7274504 | tf_op jit(solution)/shard_map/ppermute | solution.py:309
  361.4 6.1 %copy-start.1 = (bf16[2,128,4736]{2,1,0:T(8,128)(2,1)S(1)}, bf16[2,128,4736]{2,1,0:T(8,128)(2,1)}, u32[]{:S(2)}) copy-start(bf16[2,128,4736]{2,1,0:T(8,128)(2,1)} %get-tuple-element.105.kept2) | copy-start | bytes 7274500
  361.4 52.1 %collective-permute-start.13 = (bf16[1024,1024]{1,0:T(8,128)(2,1)}, bf16[1024,1024]{1,0:T(8,128)(2,1)}, u32[]{:S(2)}, u32[]{:S(2)}) collective-permute-start(bf16[1024,1024]{1,0:T(8,128)(2,1)} %project_back_send.1), channel_id=1, source_target_pairs={{0,4},{1,5},{2,6},{3,7},{4,0},{5,1},{6,2},{7,3},{8,12},{9,13},{10,... | collective-permute-start | bytes 6291464 | tf_op jit(solution)/shard_map/ppermute | solution.py:309
  364.3 6.5 %copy-start = (bf16[2,128,4736]{2,1,0:T(8,128)(2,1)S(1)}, bf16[2,128,4736]{2,1,0:T(8,128)(2,1)}, u32[]{:S(2)}) copy-start(bf16[2,128,4736]{2,1,0:T(8,128)(2,1)} %get-tuple-element.96.kept1) | copy-start | bytes 7274500
  364.3 38.3 %collective-permute-start.10 = (bf16[2048,256]{1,0:T(8,128)(2,1)S(1)}, bf16[2048,256]{1,0:T(8,128)(2,1)}, u32[]{:S(2)}, u32[]{:S(2)}) collective-permute-start(bf16[2048,256]{1,0:T(8,128)(2,1)S(1)} %get-tuple-element.136), channel_id=1, source_target_pairs={{0,1},{1,5},{2,0},{3,4},{4,3},{5,7},{6,2},{7,6},{8,9},{9,13},{10,8... | collective-permute-start | bytes 3145736 | tf_op jit(solution)/shard_map/ppermute | solution.py:309
  365.9 36.7 %collective-permute-start.9 = (bf16[2048,256]{1,0:T(8,128)(2,1)}, bf16[2048,256]{1,0:T(8,128)(2,1)}, u32[]{:S(2)}, u32[]{:S(2)}) collective-permute-start(bf16[2048,256]{1,0:T(8,128)(2,1)} %get-tuple-element.137), channel_id=1, source_target_pairs={{1,4},{2,1},{3,5},{4,2},{5,6},{6,3},{9,12},{10,9},{11,13},{12,10},... | collective-permute-start | bytes 3145736 | tf_op jit(solution)/shard_map/ppermute | solution.py:309
  370.2 37.0 %collective-permute-start.8 = (bf16[128,4736]{1,0:T(8,128)(2,1)}, bf16[128,4736]{1,0:T(8,128)(2,1)}, u32[]{:S(2)}, u32[]{:S(2)}) collective-permute-start(bf16[128,4736]{1,0:T(8,128)(2,1)} %fusion.1), channel_id=1, source_target_pairs={{0,8},{1,9},{2,10},{3,11},{4,12},{5,13},{6,14},{7,15},{8,0},{9,1},... | collective-permute-start | bytes 3637256 | tf_op jit(solution)/shard_map/ppermute | solution.py:309
  373.5 33.8 %collective-permute-start.7 = (bf16[128,4736]{1,0:T(8,128)(2,1)}, bf16[128,4736]{1,0:T(8,128)(2,1)}, u32[]{:S(2)}, u32[]{:S(2)}) collective-permute-start(bf16[128,4736]{1,0:T(8,128)(2,1)} %fusion), channel_id=1, source_target_pairs={{0,16},{1,17},{2,18},{3,19},{4,20},{5,21},{6,22},{7,23},{8,24},{9,... | collective-permute-start | bytes 3637256 | tf_op jit(solution)/shard_map/ppermute | solution.py:309
  402.6 23.1 %collective-permute-start.11 = (bf16[2,128,1536]{2,1,0:T(8,128)(2,1)}, bf16[2,128,1536]{2,1,0:T(8,128)(2,1)S(1)}, u32[]{:S(2)}, u32[]{:S(2)}) collective-permute-start(bf16[2,128,1536]{2,1,0:T(8,128)(2,1)} %get-tuple-element.114), channel_id=1, source_target_pairs={{0,4},{1,5},{2,6},{3,7},{4,0},{5,1},{6,2},{7,3},{8,12},{9,13},{10,... | collective-permute-start | bytes 2359304 | tf_op jit(solution)/shard_map/ppermute | solution.py:309
  402.6 23.1 %collective-permute-start.12 = (bf16[2,128,1536]{2,1,0:T(8,128)(2,1)}, bf16[2,128,1536]{2,1,0:T(8,128)(2,1)}, u32[]{:S(2)}, u32[]{:S(2)}) collective-permute-start(bf16[2,128,1536]{2,1,0:T(8,128)(2,1)} %get-tuple-element.115), channel_id=1, source_target_pairs={{0,4},{1,5},{2,6},{3,7},{4,0},{5,1},{6,2},{7,3},{8,12},{9,13},{10,... | collective-permute-start | bytes 2359304 | tf_op jit(solution)/shard_map/ppermute | solution.py:309
  425.7 0.9 copy-start.3

commit v4 on v3

--- a/solution.py
+++ b/solution.py
@@ -1168,53 +1168,76 @@
     return (left.astype(F32) + right.astype(F32)).astype(BF16)
 
 
-def turn_kernel(at, kept1, got1, last1, kept2, got2, last2, out, *, units):
-    t = at[1]
-    sums = [
-        kept[0].astype(F32) + got[0].astype(F32) + last[...].astype(F32)
-        for kept, got, last in ((kept1, got1, last1), (kept2, got2, last2))
-    ]
-    part = units // 4
-    for h in range(2):
-        for n in range(3):
-            turned = sums[h][:, n * units : n * units + units].T.astype(BF16)
-            for i in range(4):
-                rows = slice((2 * n + h) * part, (2 * n + h + 1) * part)
-                out[(i - t) & 3, rows, :] = turned[i * part : (i + 1) * part]
-        turned = sums[h][:, 3 * units :].T.astype(BF16)
-        for i in range(2):
-            out[(2 * h + i - t) & 3, 6 * part :, :] = turned[i * 256 : i * 256 + 256]
-
-
-def turn(at, arrays, units):
-    length = arrays[0].shape[2]
-    rows = 3 * (units // 2) + 256
-    half = pl.BlockSpec((1, 128, length), lambda i, at: (0, 0, 0))
-    last = pl.BlockSpec((128, length), lambda i, at: (0, 0))
+def finish_kernel(at, own, got, own_heads, got_heads, tok, got_tok, first, gate, up, down, out, query, key, value, tok_out, first_out):
+    @pl.when(pl.program_id(0) == 0)
+    def _():
+        part = down.shape[0]
+        for n, ref in enumerate((gate, up, down, out)):
+            rows = slice(n * part, n * part + ref.shape[0])
+            total = own[rows, :].astype(F32)
+            for d in range(3):
+                total += got[d, rows, :].astype(F32)
+            ref[...] = total
+        heads = own_heads[...].astype(F32)
+        for d in range(3):
+            heads += got_heads[d].astype(F32)
+        for n, ref in enumerate((query, key)):
+            parts = []
+            for h in range(4):
+                parts += [heads[n, :, h * 32 : h * 32 + 32], heads[n, :, 128 + h * 32 : 160 + h * 32]]
+            ref[...] = jnp.concatenate(parts, axis=1)
+        value[...] = heads[2]
+
+    stays = (at[0] & 1) == (at[1] & 1)
+    tok_out[...] = jnp.where(stays, tok[...], got_tok[...]).astype(F32)
+    first_out[...] = first[...].astype(F32)
+
+
+def finish(at, pieces, got, own_heads, got_heads, tok, got_tok, first, part):
+    count, wide = tok.shape
+    rows = 256
+    row = pl.BlockSpec((rows, wide), lambda i, at: (i, 0))
+    wider = pl.BlockSpec((first.shape[0] * rows // count, first.shape[1]), lambda i, at: (i, 0))
+    whole = lambda *shape: pl.BlockSpec(shape, lambda i, at: (0,) * len(shape))
+    shapes = [(part, 128)] * 3 + [(256, 128)] + [(128, 256)] * 3
     grid = pltpu.PrefetchScalarGridSpec(
         num_scalar_prefetch=1,
-        grid=(1,),
-        in_specs=[half, half, last] * 2,
-        out_specs=pl.BlockSpec((4, rows, 128), lambda i, at: (0, 0, 0)),
+        grid=(count // rows,),
+        in_specs=[
+            whole(*pieces.shape),
+            whole(*got.shape),
+            whole(*own_heads.shape),
+            whole(*got_heads.shape),
+            row,
+            row,
+            wider,
+        ],
+        out_specs=[whole(*shape) for shape in shapes] + [row, wider],
     )
     return pl.pallas_call(
-        functools.partial(turn_kernel, units=units),
-        out_shape=jax.ShapeDtypeStruct((4, rows, 128), BF16),
+        finish_kernel,
+        out_shape=[jax.ShapeDtypeStruct(shape, F32) for shape in shapes + [(count, wide), first.shape]],
         grid_spec=grid,
         compiler_params=params(),
-        cost_estimate=cost(1e6, 10e6),
-        name="turn",
-    )(at, *arrays)
-
-
-def last_kernel(pieces, send1, keep1, send2, keep2, tok, gains, got_pieces, own_heads, got_heads, got_tok, sums, *rest):
-    (got1, got2, part1, part2, last1, last2, heads, held, came, p_sem, h_sem, one_sem, two_sem, swap, g_sem) = rest
+        cost_estimate=cost(1e6, 18e6),
+        name="finish",
+    )(at, pieces, got, own_heads, got_heads, tok, got_tok, first)
+
+
+def tail_kernel(
+    dq, dk, dv, small, normed, row, grad_hidden, keep1, got1, keep2, got2, gain, gain_two,
+    first, own_pieces, got_pieces, own_heads, got_heads, tok, got_tok, sums,
+    q_s, k_s, v_s, w_s, n_s, x_s, gh_s, ks1, gs1, ks2, gs2, last1, last2, pieces, gn_send, gn_got, turned,
+    h_send, h_got, s1, k1, a1, a2, part1, part2, rest1, rest2, heads, held, came,
+    load, f_sem, m_sem, p_sem, n_sem, c_sem, one_sem, two_sem, h_sem, swap, g_sem,
+):
     dp, t = lax.axis_index("dp"), lax.axis_index("tensor")
     c, x, y = lax.rem(dp, 2), lax.rem(lax.div(dp, 2), 2), lax.div(dp, 4)
     pair, side = lax.div(t, 2), lax.rem(t, 2)
     plane = dp - c
     dpx, dpy, dpc = dp + 2 - 4 * x, dp + 4 - 8 * y, dp + 1 - 2 * c
-    meet(plane, c, t, dpx, dpy)
+    half = SEQ // 2
+    units = (ks1.shape[2] - 512) // 3
 
     def copy(src, dst, sems, n, to):
         return pltpu.make_async_remote_copy(
@@ -1226,20 +1249,148 @@
             device_id_type=MESH,
         )
 
-    ones = [copy(send1, got1, one_sem, 0, (dpx, t)), copy(send2, got2, one_sem, 1, (dpy, t))]
+    sources = [(keep1, ks1), (got1, gs1), (keep2, ks2), (got2, gs2), (dq, q_s), (dk, k_s), (dv, v_s)]
+    sources += [(small.at[pl.ds(0, 3), pl.ds(2 * c, 2)], w_s), (normed, n_s), (row.at[c], x_s), (grad_hidden, gh_s)]
+    loads = [pltpu.make_async_copy(src, dst, load.at[n]) for n, (src, dst) in enumerate(sources)]
+    for item in loads:
+        item.start()
+    meet(plane, c, t, dpx, dpy)
+
+    def value_copy(u):
+        src = dv.at[:, pl.ds(u * 256, 256)]
+        return pltpu.make_async_remote_copy(
+            src_ref=src,
+            dst_ref=first.at[pair],
+            send_sem=f_sem.at[0, u],
+            recv_sem=f_sem.at[1, pair],
+            device_id=(plane + side, 2 * c + u),
+            device_id_type=MESH,
+        )
+
+    def value_local(u):
+        return pltpu.make_async_copy(dv.at[:, pl.ds(u * 256, 256)], first.at[pair], load.at[11])
+
+    for u in range(2):
+        stay = (side == c) & (t == 2 * c + u)
+
+        @pl.when(stay)
+        def _():
+            value_local(u).start()
+
+        @pl.when(jnp.logical_not(stay))
+        def _():
+            value_copy(u).start()
+
+    for item in loads[:4]:
+        item.wait()
+    gs1[1] = add(ks1[1], gs1[1])
+    gs2[1] = add(ks2[1], gs2[1])
+    seconds = [copy(gs1.at[1], last1, m_sem, 0, (dpy, t)), copy(gs2.at[1], last2, m_sem, 1, (dpx, t))]
+    for item in loads[4:8]:
+        item.wait()
+    for item in seconds:
+        item.start()
+
+    def back_product(rows):
+        total = None
+        for u in range(2):
+            for n, grad in enumerate((q_s, k_s, v_s)):
+                term = dot_nt(grad[rows, u * 256 : u * 256 + 256], w_s[n, u])
+                total = term if total is None else total + term
+        return total
+
+    ns = []
+    for i in range(2):
+        rows = pl.ds(pl.multiple_of((1 - c) * half + i * 512, 512), 512)
+        gn_send[i] = back_product(rows).astype(BF16)
+        ns.append(copy(gn_send.at[i], gn_got.at[i], n_sem, i, (dpc, t)))
+
+    def turn(parity):
+        for rel in range(4):
+            yy, xx = (y, 1 - y)[rel // 2], (x, 1 - x)[rel % 2]
+            block = pl.multiple_of((yy * 4 + xx * 2 + parity) * 128, 128)
+            turned[rel * 128 : rel * 128 + 128, :] = n_s[:, pl.ds(block, 128)].T
+
+    loads[8].wait()
+    turn(1 - c)
+    for item in ns:
+        item.start()
+    cs = []
+    for n, right in enumerate((q_s, k_s, v_s)):
+        product = dot(turned[...], right[...]).astype(BF16)
+        lanes = slice(n * 512, n * 512 + 512)
+        place_second(h_send.at[0], h_send.at[1], [product[r * 128 : r * 128 + 128] for r in range(4)], lanes)
+        cs.append(copy(h_send.at[:, :, :, pl.ds(n * 512, 512)], h_got.at[:, :, :, pl.ds(n * 512, 512)], c_sem, n, (dpc, t)))
+        if n:
+            cs[n - 1].start()
+    turn(c)
+    cs[2].start()
+    for n, right in enumerate((q_s, k_s, v_s)):
+        product = dot(turned[...], right[...]).astype(BF16)
+        lanes = slice(n * 512, n * 512 + 512)
+        place_first(s1, k1, [product[r * 128 : r * 128 + 128] for r in range(4)], lanes)
+    for item in cs:
+        item.wait_recv()
+    ones = [copy(h_got.at[0], a2, one_sem, 1, (dpy, t)), copy(s1, a1, one_sem, 0, (dpx, t))]
     for item in ones:
         item.start()
-    turns = (dpc, t), (dpx, t), (dpy, t), (dp, t + 1 - 2 * side), (dp, lax.rem(t + 2, 4))
-    held[0] = gains[...]
+
+    for item in seconds:
+        item.wait_recv()
+    part = units // 4
+    for h, (kept, got, last) in enumerate(((ks1, gs1, last1), (ks2, gs2, last2))):
+        for n in range(4):
+            lanes = slice(n * units, n * units + (units if n < 3 else 512))
+            total = kept[0, :, lanes].astype(F32) + got[0, :, lanes].astype(F32) + last[:, lanes].astype(F32)
+            flipped = total.T.astype(BF16)
+            if n < 3:
+                for i in range(4):
+                    rows = slice((2 * n + h) * part, (2 * n + h + 1) * part)
+                    pieces[lax.rem(i + 4 - t, 4), rows, :] = flipped[i * part : (i + 1) * part]
+            else:
+                for i in range(2):
+                    pieces[lax.rem(2 * h + i + 4 - t, 4), 6 * part :, :] = flipped[i * 256 : i * 256 + 256]
+    own_pieces[...] = pieces[0]
     zs = [copy(pieces.at[d], got_pieces.at[d - 1], p_sem, d - 1, (dp, lax.rem(t + d, 4))) for d in (1, 2, 3)]
     for item in zs:
         item.start()
+
+    for item in loads[9:11]:
+        item.wait()
     moved = side != c
-    swapped = copy(tok, got_tok, swap, 0, (plane + side, 2 * pair + c))
+    gained = jnp.zeros((8, tok.shape[2]), F32)
+    for i in range(2):
+        ns[i].wait_recv()
+        rows = pl.ds(pl.multiple_of(c * half + i * 512, 512), 512)
+        here = slice(i * 512, i * 512 + 512)
+        grad = back_product(rows) + gn_got[i].astype(F32)
+        values = x_s[here, :].astype(F32)
+        factor = lax.rsqrt(jnp.mean(values * values, axis=1, keepdims=True) + EPSILON)
+        gained += jnp.sum((grad * values * factor).reshape(-1, 8, grad.shape[1]), axis=0)
+        scaled = grad * gain[...]
+        mean = jnp.mean(scaled * values, axis=1, keepdims=True)
+        tok[i] = (gh_s[here, :] + factor * scaled - values * (factor * factor * factor * mean)).astype(BF16)
+    swaps = [copy(tok.at[i], got_tok.at[i], swap, i, (plane + side, 2 * pair + c)) for i in range(2)]
+
+    for item in ones:
+        item.wait_recv()
+    part1[...] = add(k1[1], a1[1])
+    part2[...] = add(h_got[1, 1], a2[1])
 
     @pl.when(moved)
     def _():
-        swapped.start()
+        for item in swaps:
+            item.start()
+
+    twos = [copy(part1, rest1, two_sem, 0, (dpy, t)), copy(part2, rest2, two_sem, 1, (dpx, t))]
+    for item in twos:
+        item.start()
+
+    turns = (dpc, t), (dpx, t), (dpy, t), (dp, t + 1 - 2 * side), (dp, lax.rem(t + 2, 4))
+    line = lax.broadcasted_iota(jnp.int32, gained.shape, 0)
+    total_one = jnp.sum(gained, axis=0, keepdims=True)
+    total_two = jnp.sum(gain_two[...], axis=0, keepdims=True)
+    held[0] = jnp.where(line == 0, total_one, jnp.where(line == 1, total_two, 0.0))
 
     def gain_step(n):
         return copy(held.at[n], came.at[n], g_sem, n, turns[n])
@@ -1248,22 +1399,15 @@
         gain_step(n).wait_recv()
         held[n + 1] = held[n] + came[n]
 
+    total1 = k1[0].astype(F32) + a1[0].astype(F32)
+    total2 = h_got[1, 0].astype(F32) + a2[0].astype(F32)
     gain_step(0).start()
-    for item in ones:
-        item.wait_recv()
-    part1[...] = add(keep1[1], got1[1])
-    part2[...] = add(keep2[1], got2[1])
     gain_next(0)
-    first1 = keep1[0].astype(F32) + got1[0].astype(F32)
-    first2 = keep2[0].astype(F32) + got2[0].astype(F32)
-    twos = [copy(part1, last1, two_sem, 0, (dpy, t)), copy(part2, last2, two_sem, 1, (dpx, t))]
-    for item in twos:
-        item.start()
     gain_step(1).start()
     gain_next(1)
     for item in twos:
         item.wait_recv()
-    totals = ((first1 + last1[...].astype(F32)).astype(BF16), (first2 + last2[...].astype(F32)).astype(BF16))
+    totals = ((total1 + rest1[...].astype(F32)).astype(BF16), (total2 + rest2[...].astype(F32)).astype(BF16))
     for e, total in enumerate(totals):
         core = (c, 1 - c)[e]
         for u in range(2):
@@ -1280,222 +1424,80 @@
         gain_step(n).start()
         gain_next(n)
     sums[...] = held[5]
-    for item in ones + twos:
+
+    for item in seconds + ns + cs + ones + twos:
         item.wait_send()
     for n in range(5):
         gain_step(n).wait_send()
+    for u in range(2):
+        stay = (side == c) & (t == 2 * c + u)
+
+        @pl.when(stay)
+        def _():
+            value_local(u).wait()
+
+        @pl.when(jnp.logical_not(stay))
+        def _():
+            value_copy(u).wait_send()
+
+    for p in range(2):
+
+        @pl.when((pair != c) | (t != 2 * p + c))
+        def _():
+            pltpu.make_async_remote_copy(
+                src_ref=first.at[p],
+                dst_ref=first.at[p],
+                send_sem=f_sem.at[0, p],
+                recv_sem=f_sem.at[1, p],
+                device_id=(dpc, t),
+                device_id_type=MESH,
+            ).wait_recv()
+
     for item in zs + hs:
         item.wait()
 
     @pl.when(moved)
     def _():
-        swapped.wait()
-
-
-def last_exchanges(pieces, send1, keep1, send2, keep2, tok, gains):
+        for item in swaps:
+            item.wait()
+
+
+def tail(dq, dk, dv, small, normed, row, grad_hidden, keep1, got1, keep2, got2, gain, gain_two):
     vmem = pl.BlockSpec(memory_space=pltpu.VMEM)
     sems = pltpu.SemaphoreType.DMA
-    rows = pieces.shape[1]
-    half = send1.shape
+    wide = normed.shape[1]
+    length = keep1.shape[2]
+    rows = (length - 512) // 2 + 256
+    half = SEQ // 2
+    low = lambda *shape: pltpu.VMEM(shape, BF16)
     return pl.pallas_call(
-        last_kernel,
+        tail_kernel,
         out_shape=[
+            jax.ShapeDtypeStruct((2, SEQ, 256), BF16),
+            jax.ShapeDtypeStruct((rows, 128), BF16),
             jax.ShapeDtypeStruct((3, rows, 128), BF16),
             jax.ShapeDtypeStruct((3, 128, 256), BF16),
             jax.ShapeDtypeStruct((3, 3, 128, 256), BF16),
-            jax.ShapeDtypeStruct(tok.shape, BF16),
-            jax.ShapeDtypeStruct(gains.shape, F32),
+            jax.ShapeDtypeStruct((2, half // 2, wide), BF16),
+            jax.ShapeDtypeStruct((2, half // 2, wide), BF16),
+            jax.ShapeDtypeStruct((8, wide), F32),
         ],
-        in_specs=[vmem] * 7,
-        out_specs=[any_spec(), vmem, any_spec(), any_spec(), vmem],
-        scratch_shapes=[pltpu.VMEM(half, BF16)] * 2
-        + [pltpu.VMEM(half[1:], BF16)] * 4
-        + [pltpu.VMEM((4, 3, 128, 256), BF16), pltpu.VMEM((6,) + gains.shape, F32), pltpu.VMEM((5,) + gains.shape, F32)]
-        + [sems((2, 3)), sems((2, 3)), sems((2, 2)), sems((2, 2)), sems((2, 1)), sems((2, 5))],
+        in_specs=[any_spec()] * 11 + [vmem] * 2,
+        out_specs=[any_spec(), vmem, any_spec(), vmem, any_spec(), vmem, any_spec(), vmem],
+        scratch_shapes=[low(SEQ, 512)] * 3
+        + [low(3, 2, wide, 256), low(SEQ, wide), low(half, wide), pltpu.VMEM((half, wide), F32)]
+        + [low(2, 128, length)] * 4
+        + [low(128, length)] * 2
+        + [low(4, rows, 128), low(2, half // 2, wide), low(2, half // 2, wide), low(512, SEQ)]
+        + [low(2, 2, 128, 1536)] * 2
+        + [low(2, 128, 1536)] * 4
+        + [low(128, 1536)] * 4
+        + [low(4, 3, 128, 256), pltpu.VMEM((6, 8, wide), F32), pltpu.VMEM((5, 8, wide), F32)]
+        + [sems((12,)), sems((2, 2)), sems((2, 2)), sems((2, 3)), sems((2, 2)), sems((2, 3)), sems((2, 2)), sems((2, 2))]
+        + [sems((2, 3)), sems((2, 2)), sems((2, 5))],
         compiler_params=params(collective_id=2, has_side_effects=True),
-        name="last_exchanges",
-    )(pieces, send1, keep1, send2, keep2, tok, gains)
-
-
-def finish_kernel(at, own, got, own_heads, got_heads, tok, got_tok, gate, up, down, out, query, key, value, tok_out):
-    @pl.when(pl.program_id(0) == 0)
-    def _():
-        part = down.shape[0]
-        for n, ref in enumerate((gate, up, down, out)):
-            rows = slice(n * part, n * part + ref.shape[0])
-            total = own[0, rows, :].astype(F32)
-            for d in range(3):
-                total += got[d, rows, :].astype(F32)
-            ref[...] = total
-        heads = own_heads[...].astype(F32)
-        for d in range(3):
-            heads += got_heads[d].astype(F32)
-        for n, ref in enumerate((query, key)):
-            parts = []
-            for h in range(4):
-                parts += [heads[n, :, h * 32 : h * 32 + 32], heads[n, :, 128 + h * 32 : 160 + h * 32]]
-            ref[...] = jnp.concatenate(parts, axis=1)
-        value[...] = heads[2]
-
-    stays = (at[0] & 1) == (at[1] & 1)
-    tok_out[...] = jnp.where(stays, tok[...], got_tok[...]).astype(F32)
-
-
-def finish(at, pieces, got, own_heads, got_heads, tok, got_tok, part):
-    count, wide = tok.shape
-    rows = 256
-    row = pl.BlockSpec((rows, wide), lambda i, at: (i, 0))
-    whole = lambda *shape: pl.BlockSpec(shape, lambda i, at: (0,) * len(shape))
-    shapes = [(part, 128)] * 3 + [(256, 128)] + [(128, 256)] * 3
-    grid = pltpu.PrefetchScalarGridSpec(
-        num_scalar_prefetch=1,
-        grid=(count // rows,),
-        in_specs=[
-            whole(1, pieces.shape[1], 128),
-            whole(*got.shape),
-            whole(*own_heads.shape),
-            whole(*got_heads.shape),
-            row,
-            row,
-        ],
-        out_specs=[whole(*shape) for shape in shapes] + [row],
-    )
-    return pl.pallas_call(
-        finish_kernel,
-        out_shape=[jax.ShapeDtypeStruct(shape, F32) for shape in shapes + [(count, wide)]],
-        grid_spec=grid,
-        compiler_params=params(),
-        cost_estimate=cost(1e6, 18e6),
-        name="finish",
-    )(at, pieces, got, own_heads, got_heads, tok, got_tok)
-
-
-def project_back_kernel(at, dq, dk, dv, held, out):
-    out[...] = back_product(dq, dk, dv, held).astype(out.dtype)
-
-
-def back_product(dq, dk, dv, held):
-    total = None
-    for u in range(2):
-        for n, grad in enumerate((dq, dk, dv)):
-            term = dot_nt(grad[:, u * 256 : u * 256 + 256], held[n, u])
-            total = term if total is None else total + term
-    return total
-
-
-def back_specs(rows, other, wide):
-    half = SEQ // 2 // rows
-    row = pl.BlockSpec((rows, 512), lambda i, at: (((at[0] & 1) ^ other) * half + i, 0))
-    return [row] * 3 + [once((4, 2, wide, 256), lambda i, at: (0, at[0] & 1, 0, 0))]
-
-
-def project_back_send(at, dq, dk, dv, small):
-    rows, wide = 512, small.shape[2]
-    grid = pltpu.PrefetchScalarGridSpec(
-        num_scalar_prefetch=1,
-        grid=(SEQ // 2 // rows,),
-        in_specs=back_specs(rows, 1, wide),
-        out_specs=pl.BlockSpec((rows, wide), lambda i, at: (i, 0)),
-    )
-    return pl.pallas_call(
-        project_back_kernel,
-        out_shape=jax.ShapeDtypeStruct((SEQ // 2, wide), BF16),
-        grid_spec=grid,
-        compiler_params=params(),
-        cost_estimate=cost(SEQ * wide * 1536, 10e6),
-        name="project_back_send",
-    )(at, dq, dk, dv, small)
-
-
-def project_back_keep_kernel(at, dq, dk, dv, held, got, tok, grad_hidden, gain, out, gain_out):
-    @pl.when(pl.program_id(0) == 0)
-    def _():
-        gain_out[...] = jnp.zeros_like(gain_out)
-
-    grad = back_product(dq, dk, dv, held) + got[...].astype(F32)
-    values = tok[0].astype(F32)
-    factor = lax.rsqrt(jnp.mean(values * values, axis=1, keepdims=True) + EPSILON)
-    gain_out[...] += jnp.sum((grad * values * factor).reshape(-1, 8, grad.shape[1]), axis=0)
-    scaled = grad * gain[...]
-    mean = jnp.mean(scaled * values, axis=1, keepdims=True)
-    out[...] = (grad_hidden[...] + factor * scaled - values * (factor * factor * factor * mean)).astype(BF16)
-
-
-def project_back_keep(at, dq, dk, dv, small, got, tok, grad_hidden, gain):
-    rows, wide = 512, small.shape[2]
-    row = pl.BlockSpec((rows, wide), lambda i, at: (i, 0))
-    grid = pltpu.PrefetchScalarGridSpec(
-        num_scalar_prefetch=1,
-        grid=(SEQ // 2 // rows,),
-        in_specs=back_specs(rows, 0, wide)
-        + [
-            row,
-            pl.BlockSpec((1, rows, wide), lambda i, at: (at[0] & 1, i, 0)),
-            row,
-            pl.BlockSpec((1, wide), lambda i, at: (0, 0)),
-        ],
-        out_specs=[row, pl.BlockSpec((8, wide), lambda i, at: (0, 0))],
-    )
-    return pl.pallas_call(
-        project_back_keep_kernel,
-        out_shape=[jax.ShapeDtypeStruct((SEQ // 2, wide), BF16), jax.ShapeDtypeStruct((8, wide), F32)],
-        grid_spec=grid,
-        compiler_params=params(),
-        cost_estimate=cost(SEQ * wide * 1536, 20e6),
-        name="project_back_keep",
-    )(at, dq, dk, dv, small, got, tok, grad_hidden, gain)
-
-
-def heads_send_kernel(at, left, dq, dk, dv, send, keep, turned):
-    n = pl.program_id(0)
-
-    @pl.when(n == 0)
-    def _():
-        turn_rows(left, at[0] >> 1, 1 - (at[0] & 1), turned)
-
-    for k, right in enumerate((dq, dk, dv)):
-
-        @pl.when(n == k)
-        def _():
-            product = dot(turned[...], right[...]).astype(BF16)
-            done = [product[r * 128 : r * 128 + 128] for r in range(4)]
-            place_second(send, keep, done, slice(k * 512, k * 512 + 512))
-
-
-def heads_keep_kernel(at, left, dq, dk, dv, send, keep, turned):
-    n = pl.program_id(0)
-
-    @pl.when(n == 0)
-    def _():
-        turn_rows(left, at[0] >> 1, at[0] & 1, turned)
-
-    for k, right in enumerate((dq, dk, dv)):
-
-        @pl.when(n == k)
-        def _():
-            product = dot(turned[...], right[...]).astype(BF16)
-            done = [product[r * 128 : r * 128 + 128] for r in range(4)]
-            place_first(send, keep, done, slice(k * 512, k * 512 + 512))
-
-
-def heads_gradient(kernel, name, at, left, dq, dk, dv):
-    count, wide = left.shape
-    full = lambda *shape: pl.BlockSpec(shape, lambda n, at: (0,) * len(shape), pipeline_mode=pl.Buffered(1))
-    grid = pltpu.PrefetchScalarGridSpec(
-        num_scalar_prefetch=1,
-        grid=(3,),
-        in_specs=[full(count, wide)] + [full(count, 512)] * 3,
-        out_specs=[full(2, 128, 1536)] * 2,
-        scratch_shapes=[pltpu.VMEM((512, count), BF16)],
-    )
-    return pl.pallas_call(
-        kernel,
-        out_shape=[jax.ShapeDtypeStruct((2, 128, 1536), BF16)] * 2,
-        grid_spec=grid,
-        compiler_params=params(),
-        cost_estimate=cost(2 * count * 512 * 1536, 12e6),
-        name=name,
-    )(at, left, dq, dk, dv)
+        name="tail",
+    )(dq, dk, dv, small, normed, row, grad_hidden, keep1, got1, keep2, got2, gain, gain_two)
 
 
 def fast_body(tokens, first_values, doc_lengths, cotangent, w_query, w_key, w_value, w_out, w_gate, w_up, w_down, gain_attn, gain_mlp):
@@ -1545,33 +1547,13 @@
 
     dq, dk, dv = attend_back(bounds, q, k, v, do, attended, lse, starts_by_tile, cosine, sine)
 
-    dq, dk, dv, got1, got2 = lax.optimization_barrier((dq, dk, dv, got1, got2))
-    last1, last2 = across_y(add(kept[1][1], got1[1])), across_x(add(kept[3][1], got2[1]))
-
-    def first_back(r):
-        slab = jnp.where(pair == r, dv[:, :256], dv[:, 256:])
-        came = move(slab, lambda y, x, c, t: (y, x, t % 2, 2 * c + ((t // 2) ^ r)))
-        return jnp.where(stays & (t == 2 * c + (pair ^ r)), slab, came)
-
-    fb = [first_back(0), first_back(1)]
-    odd = side
-    grad_first = jnp.concatenate(
-        [jnp.where(odd == 0, fb[0], fb[1]), jnp.where(odd == 0, fb[1], fb[0])]
-    ).astype(F32)
-
-    gn_got = across_c(project_back_send(at, dq, dk, dv, small))
-    send2, keep2 = heads_gradient(heads_send_kernel, "heads_send", at, normed_one, dq, dk, dv)
-    send2, keep2 = across_c(send2), across_c(keep2)
-    send1, keep1 = heads_gradient(heads_keep_kernel, "heads_keep", at, normed_one, dq, dk, dv)
-    grad_tokens, gain_one = project_back_keep(at, dq, dk, dv, small, gn_got, row, grad_hidden, gain_attn[None])
-    pieces = turn(at, (kept[1], got1, last1, kept[3], got2, last2), hid.shape[2] // 2)
-    gains = jnp.stack([jnp.sum(gain_one, axis=0), jnp.sum(gain_two, axis=0)]).reshape(16, 128)
-    pieces, grad_first = lax.optimization_barrier((pieces, grad_first))
-    got, own_heads, got_heads, got_tokens, gains = last_exchanges(pieces, send1, keep1, send2, keep2, grad_tokens, gains)
-    grad_gate, grad_up, grad_down, grad_out, gq, gk, gv, grad_tokens = finish(
-        at, pieces, got, own_heads, got_heads, grad_tokens, got_tokens, w_gate.shape[1]
-    )
-    gains = gains.reshape(2, wide)
+    first_back, pieces, got, own_heads, got_heads, grad_tokens, got_tokens, gains = tail(
+        dq, dk, dv, small, normed_one, row, grad_hidden, kept[1], got1, kept[3], got2, gain_attn[None], gain_two
+    )
+    shape = (SEQ // 2, wide)
+    grad_gate, grad_up, grad_down, grad_out, gq, gk, gv, grad_tokens, grad_first = finish(
+        at, pieces, got, own_heads, got_heads, grad_tokens.reshape(shape), got_tokens.reshape(shape), first_back.reshape(2 * SEQ, 256), w_gate.shape[1]
+    )
     return (
         layer_out,
         grad_tokens,

time: 537 us -> 498 us (0.927)
  the two profiles are of different devices: /device:TPU:0 before, /device:TPU:11 now
where the time goes in v4:
time: 498 us; the launch traced here: 492 us
  Pallas kernels  451 us (91%)
  starting transfers between devices  15.7 us (3%)
  other arithmetic  14.6 us (3%)
  local copies, waits for them, and re-layouts  5.27 us (1%)
    pallas_call x1, Pallas kernels, tail(): pl.pallas_call(tail_kernel, out_shape=[jax.ShapeDtypeStruct((2, SEQ, 256)...  131 us
    pallas_call x1, Pallas kernels, gather(): pl.pallas_call(gather_kernel, out_shape=[jax.ShapeDtypeStruct((2, SEQ //...  122 us
    pallas_call x1, Pallas kernels, mlp(): pl.pallas_call(mlp_kernel, out_shape=[tokens(wide), tokens(wide, F32), to...  60.2 us
    pallas_call x1, Pallas kernels, attend_back(): pl.pallas_call(attend_back_kernel, out_shape=[jax.ShapeDtypeStruct((SEQ,...  49.1 us
    pallas_call x1, Pallas kernels, weights(): pl.pallas_call(weights_kernel, out_shape=[jax.ShapeDtypeStruct((2, 128, l...  36.4 us
    pallas_call x1, Pallas kernels, attend(): pl.pallas_call(attend_kernel, out_shape=[jax.ShapeDtypeStruct((SEQ, 512),...  28 us
    ppermute x7, starting transfers between devices, move(): return lax.ppermute(values, AXES, pairs)  15.7 us
    pallas_call x1, Pallas kernels, project(): pl.pallas_call(project_kernel, out_shape=[jax.ShapeDtypeStruct((SEQ, wide...  12.8 us
  transfers between devices with their start and end apart: 7, of which 3 were waited for; matrix products, arithmetic and copies ran while one was open for 4% of the time, Pallas kernels for 51%

profile of v4, /device:TPU:11, one launch (start us, length us, event | category | flops | bytes accessed | tf_op | source)
XLA Modules:
  0.0 491.7 jit_solution(10504075470227464204)
XLA Ops:
  0.6 0.7 collective-permute-start
  1.4 0.7 fusion.halves
  2.1 2.3 pack.1
  4.3 122.1 %gather.1 = (bf16[2,1024,1024]{2,1,0:T(8,128)(2,1)}, bf16[2,2048,256]{2,1,0:T(8,128)(2,1)}, bf16[4,4,1024,256]{3,2,1,0:T(8,128)(2,1)}, bf16[3,8,2,4,352,128]{5,4,3,2,1,0:T(8,128)(2,1)}) custom-call(bf16[1024,1024]{1,0:T(8,128)(2,1)} %tok.1, bf16[4096,256]{1,0:T(8,128)(2,1)} %fv.1, bf16[4,128,256]{2,1,0:T(8,128)(2,1)} %get-tuple-element.64.small, ...), custom_call_target="tpu_custom_call" | custom-call | tf_op jit(solution)/shard_map/gather/pallas_call | solution.py:635
  126.5 2.0 collective-permute-start.2
  129.8 0.6 pad_add_fusion.bounds
  130.4 5.6 %multiply_sine_fusion = (f32[2048,128]{1,0:T(8,128)}, f32[2048,128]{1,0:T(8,128)}) fusion(f32[128]{0:T(128)S(1)} %mul.51, f32[2048]{0:T(1024)S(1)} %subtract_convert_fusion), kind=kLoop, calls=%fused_computation.2 | loop fusion | flops 262144 | bytes 2105856 | tf_op jit(solution)/shard_map/sin | solution.py:1526
  136.0 12.8 %project.1 = (bf16[2048,1024]{1,0:T(8,128)(2,1)}, bf16[2048,512]{1,0:T(8,128)(2,1)}, bf16[2048,512]{1,0:T(8,128)(2,1)}, bf16[2048,512]{1,0:T(8,128)(2,1)}) custom-call(s32[8]{0:T(128)} %compare_select_fusion.at, bf16[2,1024,1024]{2,1,0:T(8,128)(2,1)} %get-tuple-element.67.tok.row, bf16[2,2048,256]{2,1,0:T(8,128)(2,1)} %get-tuple-element.68.first, ...), custom_call_target="tpu_custom_call" | custom-call | flops 6442450944 | bytes 24000000 | tf_op jit(solution)/shard_map/project/pallas_call | solution.py:718
  148.7 28.0 %attend.1 = (bf16[2048,512]{1,0:T(8,128)(2,1)}, f32[2,8,1024]{2,1,0:T(8,128)}) custom-call(s32[16]{0:T(128)} %pad_add_fusion.bounds, bf16[2048,512]{1,0:T(8,128)(2,1)} %get-tuple-element.70.q_ref, bf16[2048,512]{1,0:T(8,128)(2,1)} %get-tuple-element.71.k_ref, bf16[2048,512]{1,0:T(8,128)(2,1)} %get-tuple-element.72.v_ref, s32[8,256]{1,0:T(8,128)} %copy-done.1), custom_call_target="tpu_custom_call" | custom-call | flops 20000000000 | bytes 12000000 | tf_op jit(solution)/shard_map/attend/pallas_call | solution.py:808
  176.7 2.6 dynamic-slice_bitcast_fusion
  179.4 9.1 %collective-permute-start.1 = (bf16[1024,512]{1,0:T(8,128)(2,1)S(1)}, bf16[1024,512]{1,0:T(8,128)(2,1)S(1)}, u32[]{:S(2)}, u32[]{:S(2)}) collective-permute-start(bf16[1024,512]{1,0:T(8,128)(2,1)S(1)} %get-tuple-element.116), channel_id=1, source_target_pairs={{0,4},{1,5},{2,6},{3,7},{4,0},{5,1},{6,2},{7,3},{8,12},{9,13},{10,... | collective-permute-start | bytes 3145736 | tf_op jit(solution)/shard_map/ppermute | solution.py:309
  188.5 2.3 collective-permute-done.1.att_other.other
  190.8 1.0 copy-done.3
  191.8 60.2 %mlp.1 = (bf16[1024,1024]{1,0:T(8,128)(2,1)}, f32[1024,1024]{1,0:T(8,128)}, bf16[1024,1024]{1,0:T(8,128)(2,1)}, bf16[1024,1024]{1,0:T(8,128)(2,1)}, bf16[3,1024,...) custom-call(s32[8]{0:T(128)} %compare_select_fusion.at, ...), custom_call_target="tpu_custom_call" | custom-call | flops 39728447488 | bytes 60000000 | tf_op jit(solution)/shard_map/mlp/pallas_call | solution.py:1015
  252.4 2.0 collective-permute-start.3
  254.4 36.4 %weights.1 = (bf16[2,128,4736]{2,1,0:T(8,128)(2,1)}, bf16[2,128,4736]{2,1,0:T(8,128)(2,1)}, bf16[2,128,4736]{2,1,0:T(8,128)(2,1)}, bf16[2,128,4736]{2,1,0:T(8,128)(2,1)}) custom-call(bf16[1024,1024]{1,0:T(8,128)(2,1)} %get-tuple-element.77.n2, bf16[1024,1024]{1,0:T(8,128)(2,1)} %get-tuple-element.78.g, bf16[1024,1024]{1,0:T(8,128)(2,1)} %get-tuple-element.79.branch, ...), custom_call_target="tpu_custom_call" | custom-call | flops 19864223744 | bytes 50000000 | tf_op jit(solution)/shard_map/weights/pallas_call | solution.py:1157
  290.8 3.6 maximum_select_fusion.do_ref
  294.4 1.3 collective-permute-start.5
  295.9 49.1 %attend_back.1 = (bf16[2048,512]{1,0:T(8,128)(2,1)}, bf16[2048,512]{1,0:T(8,128)(2,1)}, bf16[2048,512]{1,0:T(8,128)(2,1)}) custom-call(s32[16]{0:T(128)} %pad_add_fusion.bounds, bf16[2048,512]{1,0:T(8,128)(2,1)} %get-tuple-element.70.q_ref, bf16[2048,512]{1,0:T(8,128)(2,1)} %get-tuple-element.71.k_ref, bf16[2048,512]{1,0:T(8,128)(2,1)} %get-tuple-element.72.v_ref, ...), custom_call_target="tpu_custom_call" | custom-call | flops 49999998976 | bytes 20000000 | tf_op jit(solution)/shard_map/attend_back/pallas_call | solution.py:908
  345.0 3.1 broadcast_select_fusion
  348.6 1.4 collective-permute-done.6.got2
  350.0 130.8 %tail.1 = (bf16[2,2048,256]{2,1,0:T(8,128)(2,1)}, bf16[2368,128]{1,0:T(8,128)(2,1)}, bf16[3,2368,128]{2,1,0:T(8,128)(2,1)}, bf16[3,128,256]{2,1,0:T(8,128)(2,1)}...) custom-call(bf16[2048,512]{1,0:T(8,128)(2,1)} %get-tuple-element.89., ...), custom_call_target="tpu_custom_call" | custom-call | tf_op jit(solution)/shard_map/tail/pallas_call | solution.py:1473
  480.8 1.4 fusion.7
  482.2 9.3 %finish.1 = (f32[704,128]{1,0:T(8,128)}, f32[704,128]{1,0:T(8,128)}, f32[704,128]{1,0:T(8,128)}, f32[256,128]{1,0:T(8,128)}, f32[128,256]{1,0:T(8,128)}, /*index...) custom-call(s32[8]{0:T(128)} %compare_select_fusion.at, ...), custom_call_target="tpu_custom_call" | custom-call | flops 1000000 | bytes 18000000 | tf_op jit(solution)/shard_map/finish/pallas_call | solution.py:1217
  (29 shorter events, 2.3 us)
Async XLA Ops:
  0.6 128.5 %collective-permute-start = (s32[2,8]{1,0:T(2,128)}, s32[2,8]{1,0:T(2,128)S(1)}, u32[]{:S(2)}, u32[]{:S(2)}) collective-permute-start(s32[2,8]{1,0:T(2,128)} %param.15), channel_id=1, source_target_pairs={{0,4},{1,5},{2,6},{3,7},{4,0},{5,1},{6,2},{7,3},{8,12},{9,13},{10,... | collective-permute-start | bytes 200 | tf_op jit(solution)/shard_map/ppermute | solution.py:309
  4.3 124.8 %copy-start.2 = (s32[2,8]{1,0:T(2,128)S(1)}, s32[2,8]{1,0:T(2,128)}, u32[]{:S(2)}) copy-start(s32[2,8]{1,0:T(2,128)} %param.15) | copy-start | bytes 196
  126.5 64.3 %collective-permute-start.2 = (bf16[1024,1024]{1,0:T(8,128)(2,1)}, bf16[1024,1024]{1,0:T(8,128)(2,1)}, u32[]{:S(2)}, u32[]{:S(2)}) collective-permute-start(bf16[1024,1024]{1,0:T(8,128)(2,1)} %cot_here), channel_id=1, source_target_pairs={{1,4},{3,6},{4,1},{6,3},{9,12},{11,14},{12,9},{14,11},{17,20},{19,... | collective-permute-start | bytes 6291464 | tf_op jit(solution)/shard_map/ppermute | solution.py:309
  129.4 19.3 %copy-start.1 = (s32[8,256]{1,0:T(8,128)}, s32[8,256]{1,0:T(8,128)S(1)}, u32[]{:S(2)}) copy-start(s32[8,256]{1,0:T(8,128)S(1)} %reshape.76.starts) | copy-start | bytes 24580
  179.4 11.4 %collective-permute-start.1 = (bf16[1024,512]{1,0:T(8,128)(2,1)S(1)}, bf16[1024,512]{1,0:T(8,128)(2,1)S(1)}, u32[]{:S(2)}, u32[]{:S(2)}) collective-permute-start(bf16[1024,512]{1,0:T(8,128)(2,1)S(1)} %get-tuple-element.116), channel_id=1, source_target_pairs={{0,4},{1,5},{2,6},{3,7},{4,0},{5,1},{6,2},{7,3},{8,12},{9,13},{10,... | collective-permute-start | bytes 3145736 | tf_op jit(solution)/shard_map/ppermute | solution.py:309
  190.8 1.0 copy-start.3
  251.9 38.9 %collective-permute-start.4 = (bf16[1024,512]{1,0:T(8,128)(2,1)}, bf16[1024,512]{1,0:T(8,128)(2,1)}, u32[]{:S(2)}, u32[]{:S(2)}) collective-permute-start(bf16[1024,512]{1,0:T(8,128)(2,1)} %get-tuple-element.86), channel_id=1, source_target_pairs={{0,4},{1,5},{2,6},{3,7},{4,0},{5,1},{6,2},{7,3},{8,12},{9,13},{10,... | collective-permute-start | bytes 3145736 | tf_op jit(solution)/shard_map/ppermute | solution.py:309
  252.4 92.6 %collective-permute-start.3 = (bf16[1024,1024]{1,0:T(8,128)(2,1)}, bf16[1024,1024]{1,0:T(8,128)(2,1)}, u32[]{:S(2)}, u32[]{:S(2)}) collective-permute-start(bf16[1024,1024]{1,0:T(8,128)(2,1)} %get-tuple-element.76), channel_id=1, source_target_pairs={{1,4},{3,6},{4,1},{6,3},{9,12},{11,14},{12,9},{14,11},{17,20},{19,... | collective-permute-start | bytes 6291464 | tf_op jit(solution)/shard_map/ppermute | solution.py:309
  254.4 36.5 %copy-start = (bf16[1024,512]{1,0:T(8,128)(2,1)S(1)}, bf16[1024,512]{1,0:T(8,128)(2,1)}, u32[]{:S(2)}) copy-start(bf16[1024,512]{1,0:T(8,128)(2,1)} %get-tuple-element.85) | copy-start | bytes 3145732
  294.4 54.2 %collective-permute-start.5 = (bf16[2,128,4736]{2,1,0:T(8,128)(2,1)}, bf16[2,128,4736]{2,1,0:T(8,128)(2,1)}, u32[]{:S(2)}, u32[]{:S(2)}) collective-permute-start(bf16[2,128,4736]{2,1,0:T(8,128)(2,1)} %get-tuple-element.95), channel_id=1, source_target_pairs={{0,8},{1,9},{2,10},{3,11},{4,12},{5,13},{6,14},{7,15},{8,0},{9,1},... | collective-permute-start | bytes 7274504 | tf_op jit(solution)/shard_map/ppermute | solution.py:309
  295.7 54.3 %collective-permute-start.6 = (bf16[2,128,4736]{2,1,0:T(8,128)(2,1)}, bf16[2,128,4736]{2,1,0:T(8,128)(2,1)}, u32[]{:S(2)}, u32[]{:S(2)}) collective-permute-start(bf16[2,128,4736]{2,1,0:T(8,128)(2,1)} %get-tuple-element.97), channel_id=1, source_target_pairs={{0,16},{1,17},{2,18},{3,19},{4,20},{5,21},{6,22},{7,23},{8,24},{9,... | collective-permute-start | bytes 7274504 | tf_op jit(solution)/shard_map/ppermute | solution.py:309

commit v5 on v4

--- a/solution.py
+++ b/solution.py
@@ -367,7 +367,11 @@
     pl.semaphore_wait(barrier, 9)
 
 
-def gather_kernel(tok, fv, small, big, row, first, g_small, g_big, send, recv, relay_send, along_recv, next_send, next_recv, swap, fsend, frecv, here):
+def gather_kernel(
+    ends, tok, fv, small, big, gain, freqs, row_out, g_small, g_big, normed_out, q_out, k_out, v_out, cos_out, sin_out,
+    row, first, w_s, n_s, q_s, k_s, v_s, raw_s, cos_s, sin_s,
+    send, recv, relay_send, along_recv, next_send, next_recv, swap, fsend, frecv, here, tile_sem, end_sem,
+):
     dp, t = lax.axis_index("dp"), lax.axis_index("tensor")
     c, x, y = lax.rem(dp, 2), lax.rem(lax.div(dp, 2), 2), lax.div(dp, 4)
     pair, side = lax.div(t, 2), lax.rem(t, 2)
@@ -552,6 +556,17 @@
                 onward(k, at, h, slot(k, at, dp, h)).wait_recv()
         for item in across[k]:
             item.start()
+
+    for i in range(8):
+        rows = slice(i * TILE, i * TILE + TILE)
+        at_row = lax.broadcasted_iota(jnp.int32, (TILE, 128), 0) + i * TILE
+        begin = jnp.zeros_like(at_row)
+        for k in range(DOCS):
+            begin = jnp.maximum(begin, jnp.where(at_row >= ends[k], ends[k], 0))
+        angles = (at_row - begin).astype(F32) * freqs[...]
+        cos_s[rows, :] = jnp.cos(angles)
+        sin_s[rows, :] = jnp.sin(angles)
+    tables = [pltpu.make_async_copy(cos_s, cos_out, end_sem.at[0]), pltpu.make_async_copy(sin_s, sin_out, end_sem.at[1])]
 
     for i, k in enumerate(order):
         pass_along(k, 1)
@@ -570,8 +585,12 @@
         if i >= 2:
             pass_over(order[i - 2])
     pass_next(order[3])
-    for k in order[2:]:
-        pass_over(k)
+    for item in tables:
+        item.start()
+    for item in over[0]:
+        item.wait_recv()
+    load_w = pltpu.make_async_copy(g_small.at[pl.ds(0, 3), pl.ds(2 * c, 2)], w_s, end_sem.at[2])
+    load_w.start()
 
     @pl.when(moved)
     def _():
@@ -591,6 +610,39 @@
         device_id_type=MESH,
     )
     given.start()
+    load_w.wait()
+    outs = []
+
+    def project(half, n):
+        low = pl.multiple_of(half * (SEQ // 2) + lax.rem(n, 2) * 512, 512)
+        rows = pl.ds(low, 512)
+        values = row[half, n % 2 * 512 : n % 2 * 512 + 512, :].astype(F32)
+        factor = lax.rsqrt(jnp.mean(values * values, axis=1, keepdims=True) + EPSILON)
+        normed = (values * factor * gain[...]).astype(BF16)
+        n_s[rows, :] = normed
+        cos, sin = cos_s[rows, :], sin_s[rows, :]
+        for u in range(2):
+            for m, out, scale in ((0, q_s, 0.125), (1, k_s, 1.0)):
+                raw = dot(normed, w_s[m, u])
+                a, b = raw[:, :128], raw[:, 128:]
+                out[rows, u * 256 : u * 256 + 128] = ((a * cos - b * sin) * scale).astype(BF16)
+                out[rows, u * 256 + 128 : u * 256 + 256] = ((b * cos + a * sin) * scale).astype(BF16)
+            raw_s[rows, u * 256 : u * 256 + 256] = 0.5 * dot(normed, w_s[2, u])
+        for m, (src, dst) in enumerate(((n_s, normed_out), (q_s, q_out), (k_s, k_out))):
+            item = pltpu.make_async_copy(src.at[rows, :], dst.at[rows, :], tile_sem.at[n, m])
+            item.start()
+            outs.append(item)
+
+    project(c, 0)
+    project(c, 1)
+    pass_over(order[2])
+    given.wait_recv()
+    row_copy = pltpu.make_async_copy(row, row_out, end_sem.at[3])
+    row_copy.start()
+    project(1 - c, 2)
+    project(1 - c, 3)
+    pass_over(order[3])
+
     for p in range(2):
 
         @pl.when(stays[p])
@@ -615,44 +667,64 @@
         def _():
             came.wait_recv()
 
-    given.wait()
+    for n in range(4):
+        rows = slice(n * 512, n * 512 + 512)
+        for u in range(2):
+            lanes = slice(u * 256, u * 256 + 256)
+            v_s[rows, lanes] = (raw_s[rows, lanes] + 0.5 * first[u, rows, :].astype(F32)).astype(BF16)
+        item = pltpu.make_async_copy(v_s.at[rows, :], v_out.at[rows, :], tile_sem.at[n, 3])
+        item.start()
+        outs.append(item)
+
+    given.wait_send()
     for k in range(chunks):
-        for item in over[k]:
-            item.wait_recv()
+        if k:
+            for item in over[k]:
+                item.wait_recv()
         end_along(k)
         for item in across[k] + over[k]:
             item.wait_send()
         for at in range(4):
             for h in range(2):
                 onward(k, at, h, slot(k, at, dp, h)).wait_send()
-
-
-def gather(tok, fv, small, big):
+    for item in outs + tables + [row_copy]:
+        item.wait()
+
+
+def gather(ends, tok, fv, small, big, gain, freqs):
     part, rows = big.shape[2:]
     wide = tok.shape[1]
     vmem = pl.BlockSpec(memory_space=pltpu.VMEM)
     sems = pltpu.SemaphoreType.DMA
+    low = lambda *shape: pltpu.VMEM(shape, BF16)
+    shapes = [(2, SEQ // 2, wide), (4, 4, wide, 256), (3, 8, 2, 4, part, rows), (SEQ, wide)] + [(SEQ, 512)] * 3
     return pl.pallas_call(
         gather_kernel,
-        out_shape=[
-            jax.ShapeDtypeStruct((2, SEQ // 2, wide), BF16),
-            jax.ShapeDtypeStruct((2, SEQ, 256), BF16),
-            jax.ShapeDtypeStruct((4, 4, wide, 256), BF16),
-            jax.ShapeDtypeStruct((3, 8, 2, 4, part, rows), BF16),
-        ],
-        in_specs=[vmem] * 4,
-        out_specs=[any_spec()] * 4,
-        scratch_shapes=[
+        out_shape=[jax.ShapeDtypeStruct(shape, BF16) for shape in shapes]
+        + [jax.ShapeDtypeStruct((SEQ, 128), F32)] * 2,
+        in_specs=[pl.BlockSpec(memory_space=pltpu.SMEM)] + [vmem] * 6,
+        out_specs=[any_spec()] * 9,
+        scratch_shapes=[low(2, SEQ // 2, wide), low(2, SEQ, 256), low(3, 2, wide, 256), low(SEQ, wide)]
+        + [low(SEQ, 512)] * 3
+        + [pltpu.VMEM((SEQ, 512), F32)]
+        + [pltpu.VMEM((SEQ, 128), F32)] * 2
+        + [
             sems((4, 8)),
             sems((4, 8)),
             sems((4, 4, 2)),
             sems((4, 4)),
             sems((4, 4, 2)),
             sems((4, 4, 2)),
-            sems((4,)), sems((2,)), sems((2,)), sems((6,))],
+            sems((4,)),
+            sems((2,)),
+            sems((2,)),
+            sems((6,)),
+            sems((4, 4)),
+            sems((4,)),
+        ],
         compiler_params=params(collective_id=0, has_side_effects=True),
         name="gather",
-    )(tok, fv, small, big)
+    )(ends, tok, fv, small, big, gain, freqs)
 
 
 def dot(left, right):
@@ -679,51 +751,8 @@
     return pl.CostEstimate(flops=int(flops), bytes_accessed=int(size), transcendentals=int(exps))
 
 
-def project_kernel(at, tok, first, cosine, sine, gain, held, normed_out, q_out, k_out, v_out):
-    values = tok[0].astype(F32)
-    factor = lax.rsqrt(jnp.mean(values * values, axis=1, keepdims=True) + EPSILON)
-    normed = (values * factor * gain[...]).astype(BF16)
-    normed_out[...] = normed
-    cos, sin = cosine[...], sine[...]
-    for u in range(2):
-        for n, out, scale in ((0, q_out, 0.125), (1, k_out, 1.0)):
-            raw = dot(normed, held[n, u])
-            a, b = raw[:, :128], raw[:, 128:]
-            out[:, u * 256 : u * 256 + 128] = ((a * cos - b * sin) * scale).astype(BF16)
-            out[:, u * 256 + 128 : u * 256 + 256] = ((b * cos + a * sin) * scale).astype(BF16)
-        raw = dot(normed, held[2, u])
-        v_out[:, u * 256 : u * 256 + 256] = (0.5 * raw + 0.5 * first[u].astype(F32)).astype(BF16)
-
-
 def once(shape, place):
     return pl.BlockSpec(shape, place, pipeline_mode=pl.Buffered(1))
-
-
-def project(at, tok, first, cosine, sine, gain, small):
-    rows, wide = 512, tok.shape[2]
-    row = lambda width: pl.BlockSpec((rows, width), lambda i, at: (i, 0))
-    grid = pltpu.PrefetchScalarGridSpec(
-        num_scalar_prefetch=1,
-        grid=(4,),
-        in_specs=[
-            pl.BlockSpec((1, rows, wide), lambda i, at: (i // 2, i % 2, 0)),
-            pl.BlockSpec((2, rows, 256), lambda i, at: (0, i, 0)),
-            row(128),
-            row(128),
-            pl.BlockSpec((1, wide), lambda i, at: (0, 0)),
-            once((4, 2, wide, 256), lambda i, at: (0, at[0] & 1, 0, 0)),
-        ],
-        out_specs=[row(wide), row(512), row(512), row(512)],
-    )
-    return pl.pallas_call(
-        project_kernel,
-        out_shape=[jax.ShapeDtypeStruct((SEQ, wide), BF16)]
-        + [jax.ShapeDtypeStruct((SEQ, 512), BF16)] * 3,
-        grid_spec=grid,
-        compiler_params=params(),
-        cost_estimate=cost(2 * SEQ * wide * 1536, 24e6),
-        name="project",
-    )(at, tok, first, cosine, sine, gain, small)
 
 
 def head_masks(rows):
@@ -731,7 +760,7 @@
     return (lane & 127) >> 5, lane >> 6
 
 
-def attend_kernel(bounds, q_ref, k_ref, v_ref, starts, o_ref, lse_ref, kept, turned, acc):
+def attend_kernel(at, bounds, q_ref, k_ref, v_ref, starts, own_ref, send_ref, lse_ref, kept, turned, acc):
     tiles = SEQ // TILE
     of_qk, _ = head_masks(TILE)
     row = lax.broadcasted_iota(jnp.int32, (TILE, TILE), 0)
@@ -795,24 +824,36 @@
             scaled = [
                 acc[u * 256 + h * 64 : u * 256 + h * 64 + 64] * inverse[:, h * TILE : (h + 1) * TILE] for h in range(4)
             ]
-            o_ref[here, slab] = jnp.concatenate(scaled, axis=0).T.astype(BF16)
+            done = jnp.concatenate(scaled, axis=0).T.astype(BF16)
+            local = pl.ds(pl.multiple_of(lax.rem(i, tiles // 2) * TILE, TILE), TILE)
+            mine = lax.div(i, tiles // 2) == (at[0] & 1)
+
+            @pl.when(mine)
+            def _():
+                own_ref[local, slab] = done
+
+            @pl.when(jnp.logical_not(mine))
+            def _():
+                send_ref[local, slab] = done
+
             lse_ref[u, pl.ds(i, 1), :] = tops[u] + jnp.log(total)
         return carry
 
     lax.fori_loop(0, tiles, query_tile, 0)
 
 
-def attend(bounds, q, k, v, starts):
+def attend(at, bounds, q, k, v, starts):
     tiles = SEQ // TILE
     vmem = pl.BlockSpec(memory_space=pltpu.VMEM)
     return pl.pallas_call(
         attend_kernel,
         out_shape=[
-            jax.ShapeDtypeStruct((SEQ, 512), BF16),
+            jax.ShapeDtypeStruct((SEQ // 2, 512), BF16),
+            jax.ShapeDtypeStruct((SEQ // 2, 512), BF16),
             jax.ShapeDtypeStruct((2, tiles, 4 * TILE), F32),
         ],
-        in_specs=[pl.BlockSpec(memory_space=pltpu.SMEM)] + [vmem] * 4,
-        out_specs=[vmem] * 2,
+        in_specs=[pl.BlockSpec(memory_space=pltpu.SMEM)] * 2 + [vmem] * 4,
+        out_specs=[vmem] * 3,
         scratch_shapes=[
             pltpu.VMEM((tiles, 2, TILE, 4 * TILE), F32),
             pltpu.VMEM((tiles, 512, TILE), BF16),
@@ -821,11 +862,12 @@
         compiler_params=params(),
         cost_estimate=cost(20e9, 12e6, 1e7),
         name="attend",
-    )(bounds, q, k, v, starts)
+    )(at, bounds, q, k, v, starts)
 
 
 def attend_back_kernel(
-    bounds, q_ref, k_ref, v_ref, do_ref, o_ref, lse_ref, starts, cosine, sine, dq_ref, dk_ref, dv_ref, dq_acc, delta, dk_acc, dv_acc
+    at, bounds, q_hbm, k_hbm, v_hbm, do_own, do_other, o_own, o_other, lse_ref, starts, cosine, sine, dq_hbm, dk_hbm, dv_hbm,
+    q_ref, k_ref, v_ref, do_ref, o_ref, dq_ref, dk_ref, dv_ref, dq_acc, delta, dk_acc, dv_acc, load, store,
 ):
     tiles = SEQ // TILE
     of_qk, of_v = head_masks(TILE)
@@ -836,7 +878,26 @@
         jnp.int32, (8, 256), 0
     )
     pick = pick.astype(F32)
+    half = SEQ // 2
+    low = pl.multiple_of((at[0] & 1) * half, half)
+    mine, others = pl.ds(low, half), pl.ds(half - low, half)
+    loads = [
+        pltpu.make_async_copy(src, dst, load.at[n])
+        for n, (src, dst) in enumerate((
+            (do_own, do_ref.at[mine, :]),
+            (do_other, do_ref.at[others, :]),
+            (o_own, o_ref.at[mine, :]),
+            (o_other, o_ref.at[others, :]),
+            (q_hbm, q_ref),
+            (k_hbm, k_ref),
+            (v_hbm, v_ref),
+        ))
+    ]
+    for item in loads:
+        item.start()
     dq_acc[...] = jnp.zeros_like(dq_acc)
+    for item in loads[:4]:
+        item.wait()
 
     def prepare(i, carry):
         here = pl.ds(pl.multiple_of(i * TILE, TILE), TILE)
@@ -850,6 +911,8 @@
         return carry
 
     lax.fori_loop(0, tiles, prepare, 0)
+    for item in loads[4:]:
+        item.wait()
 
     def rotate_out(values, here, out, low, scale):
         a, b = values[:, :128], values[:, 128:]
@@ -889,6 +952,8 @@
         for u, slab in enumerate(slabs):
             rotate_out(dk_acc[u], there, dk_ref, u * 256, 1.0)
             dv_ref[there, slab] = (0.5 * dv_acc[u]).astype(BF16)
+        pltpu.make_async_copy(dk_ref.at[there, :], dk_hbm.at[there, :], store.at[0]).start()
+        pltpu.make_async_copy(dv_ref.at[there, :], dv_hbm.at[there, :], store.at[1]).start()
         return carry
 
     lax.fori_loop(0, tiles, key_tile, 0)
@@ -897,29 +962,36 @@
         here = pl.ds(pl.multiple_of(i * TILE, TILE), TILE)
         for u in range(2):
             rotate_out(dq_acc[i, u], here, dq_ref, u * 256, 0.125)
+        pltpu.make_async_copy(dq_ref.at[here, :], dq_hbm.at[here, :], store.at[2]).start()
         return carry
 
     lax.fori_loop(0, tiles, finish_tile, 0)
-
-
-def attend_back(bounds, q, k, v, do, o, lse, starts, cosine, sine):
+    for n, (src, dst) in enumerate(((dk_ref, dk_hbm), (dv_ref, dv_hbm), (dq_ref, dq_hbm))):
+        pltpu.make_async_copy(src, dst, store.at[n]).wait()
+
+
+def attend_back(at, bounds, q, k, v, do_own, do_other, o_own, o_other, lse, starts, cosine, sine):
     tiles = SEQ // TILE
     vmem = pl.BlockSpec(memory_space=pltpu.VMEM)
+    sems = pltpu.SemaphoreType.DMA
     return pl.pallas_call(
         attend_back_kernel,
         out_shape=[jax.ShapeDtypeStruct((SEQ, 512), BF16)] * 3,
-        in_specs=[pl.BlockSpec(memory_space=pltpu.SMEM)] + [vmem] * 9,
-        out_specs=[vmem] * 3,
-        scratch_shapes=[
+        in_specs=[pl.BlockSpec(memory_space=pltpu.SMEM)] * 2 + [any_spec()] * 7 + [vmem] * 4,
+        out_specs=[any_spec()] * 3,
+        scratch_shapes=[pltpu.VMEM((SEQ, 512), BF16)] * 8
+        + [
             pltpu.VMEM((tiles, 2, TILE, 256), F32),
             pltpu.VMEM((2, tiles, 4 * TILE), F32),
             pltpu.VMEM((2, TILE, 256), F32),
             pltpu.VMEM((2, TILE, 256), F32),
+            sems((7,)),
+            sems((3,)),
         ],
         compiler_params=params(),
         cost_estimate=cost(50e9, 20e6, 1e7),
         name="attend_back",
-    )(bounds, q, k, v, do, o, lse, starts, cosine, sine)
+    )(at, bounds, q, k, v, do_own, do_other, o_own, o_other, lse, starts, cosine, sine)
 
 
 def mlp_kernel(at, att_own, att_other, tok, cot_here, cot_moved, gain, wo, big, *rest):
@@ -1168,7 +1240,7 @@
     return (left.astype(F32) + right.astype(F32)).astype(BF16)
 
 
-def finish_kernel(at, own, got, own_heads, got_heads, tok, got_tok, first, gate, up, down, out, query, key, value, tok_out, first_out):
+def finish_kernel(at, own, got, own_heads, got_heads, tok, got_tok, first, layer, got_layer, gate, up, down, out, query, key, value, tok_out, first_out, layer_out):
     @pl.when(pl.program_id(0) == 0)
     def _():
         part = down.shape[0]
@@ -1191,9 +1263,10 @@
     stays = (at[0] & 1) == (at[1] & 1)
     tok_out[...] = jnp.where(stays, tok[...], got_tok[...]).astype(F32)
     first_out[...] = first[...].astype(F32)
-
-
-def finish(at, pieces, got, own_heads, got_heads, tok, got_tok, first, part):
+    layer_out[...] = jnp.where(stays, layer[...], got_layer[...])
+
+
+def finish(at, pieces, got, own_heads, got_heads, tok, got_tok, first, layer, got_layer, part):
     count, wide = tok.shape
     rows = 256
     row = pl.BlockSpec((rows, wide), lambda i, at: (i, 0))
@@ -1211,17 +1284,20 @@
             row,
             row,
             wider,
+            row,
+            row,
         ],
-        out_specs=[whole(*shape) for shape in shapes] + [row, wider],
+        out_specs=[whole(*shape) for shape in shapes] + [row, wider, row],
     )
     return pl.pallas_call(
         finish_kernel,
-        out_shape=[jax.ShapeDtypeStruct(shape, F32) for shape in shapes + [(count, wide), first.shape]],
+        out_shape=[jax.ShapeDtypeStruct(shape, F32) for shape in shapes + [(count, wide), first.shape]]
+        + [jax.ShapeDtypeStruct((count, wide), BF16)],
         grid_spec=grid,
         compiler_params=params(),
         cost_estimate=cost(1e6, 18e6),
         name="finish",
-    )(at, pieces, got, own_heads, got_heads, tok, got_tok, first)
+    )(at, pieces, got, own_heads, got_heads, tok, got_tok, first, layer, got_layer)
 
 
 def tail_kernel(
@@ -1509,50 +1585,46 @@
     at = jnp.where(jnp.arange(8, dtype=jnp.int32) == 0, me, t).astype(jnp.int32)
 
     small_shard, big_shard = pack(w_query, w_key, w_value, w_out, w_gate, w_up, w_down)
-    row, first, small, big = gather(tokens, first_values, small_shard, big_shard)
-
     lengths = jnp.where(c == side, doc_lengths, across_c(doc_lengths))
     lengths = lax.dynamic_index_in_dim(lengths, pair, 0, keepdims=False)
     order = jnp.arange(DOCS, dtype=jnp.int32)
     ends = jnp.sum(jnp.where(order[None, :] <= order[:, None], lengths[None, :], 0), axis=1)
+    freqs = 10000.0 ** (-(jnp.arange(32, dtype=F32) * 2.0 / HEAD))
+    row, small, big, normed_one, q, k, v, cosine, sine = gather(
+        ends, tokens, first_values, small_shard, big_shard, gain_attn[None], jnp.tile(freqs, 4)[None]
+    )
     places = jnp.arange(SEQ, dtype=jnp.int32)
     starts = jnp.max(jnp.where(ends[None, :] <= places[:, None], ends[None, :], 0), axis=1)
     last = jnp.arange(tiles, dtype=jnp.int32) * TILE + (TILE - 1)
     stop = jnp.min(jnp.where(ends[None, :] > last[:, None], ends[None, :], SEQ), axis=1)
     bounds = jnp.concatenate([starts.reshape(tiles, TILE)[:, 0] // TILE, (stop - 1) // TILE])
     starts_by_tile = starts.reshape(tiles, TILE)
-    freqs = 10000.0 ** (-(jnp.arange(32, dtype=F32) * 2.0 / HEAD))
-    angles = (places - starts).astype(F32)[:, None] * jnp.tile(freqs, 4)[None, :]
-    cosine, sine = jnp.cos(angles), jnp.sin(angles)
 
     row, cotangent = lax.optimization_barrier((row, cotangent))
     moved_cot = swap_halves(cotangent)
-    normed_one, q, k, v = project(at, row, first, cosine, sine, gain_attn[None], small)
-    attended, lse = attend(bounds, q, k, v, starts_by_tile)
-    by_half = attended.reshape(2, SEQ // 2, 512)
-    att_own = lax.dynamic_index_in_dim(by_half, c, 0, keepdims=False)
-    att_other = across_c(lax.dynamic_index_in_dim(by_half, 1 - c, 0, keepdims=False))
+    att_own, att_send, lse = attend(at, bounds, q, k, v, starts_by_tile)
+    att_other = across_c(att_send)
     out, grad_hidden, branch, normed_two, hid, ga_own, ga_other, gain_two, cot = mlp(
         at, att_own, att_other, row, cotangent, moved_cot, gain_mlp[None], small, big
     )
-    stays = c == side
-    layer_out = jnp.where(stays, out, swap_halves(out))
+    moved_out = swap_halves(out)
 
     ga_got = across_c(ga_other)
-    do = jnp.where(c == 0, jnp.concatenate([ga_own, ga_got]), jnp.concatenate([ga_got, ga_own]))
 
     kept = weights(normed_two, cot, branch, hid, att_own, att_other)
-    kept, do = lax.optimization_barrier((kept, do))
+    kept, ga_got = lax.optimization_barrier((kept, ga_got))
     got1, got2 = across_x(kept[0]), across_y(kept[2])
 
-    dq, dk, dv = attend_back(bounds, q, k, v, do, attended, lse, starts_by_tile, cosine, sine)
+    dq, dk, dv = attend_back(
+        at, bounds, q, k, v, ga_own, ga_got, att_own, att_send, lse, starts_by_tile, cosine, sine
+    )
 
     first_back, pieces, got, own_heads, got_heads, grad_tokens, got_tokens, gains = tail(
         dq, dk, dv, small, normed_one, row, grad_hidden, kept[1], got1, kept[3], got2, gain_attn[None], gain_two
     )
     shape = (SEQ // 2, wide)
-    grad_gate, grad_up, grad_down, grad_out, gq, gk, gv, grad_tokens, grad_first = finish(
-        at, pieces, got, own_heads, got_heads, grad_tokens.reshape(shape), got_tokens.reshape(shape), first_back.reshape(2 * SEQ, 256), w_gate.shape[1]
+    grad_gate, grad_up, grad_down, grad_out, gq, gk, gv, grad_tokens, grad_first, layer_out = finish(
+        at, pieces, got, own_heads, got_heads, grad_tokens.reshape(shape), got_tokens.reshape(shape), first_back.reshape(2 * SEQ, 256), out, moved_out, w_gate.shape[1]
     )
     return (
         layer_out,

time: 498 us -> 476 us (0.956)
  Pallas kernels: 451 us -> 432 us
  waiting for transfers between devices: 4.1 us -> 16.5 us
  other arithmetic: 14.6 us -> 2.93 us
    pallas_call x3 -> x2, Pallas kernels: 163 us -> 146 us  [the longest x1 121 us: gather(): pl.pallas_call(gather_kernel, out_shape=[jax.ShapeDtypeStruct(shape, BF16...]
    ppermute x7, waiting for transfers between devices: 4.1 us -> 16.5 us  [move(): return lax.ppermute(values, AXES, pairs)]
    pallas_call x1, Pallas kernels: 49.1 us -> 39.7 us  [attend_back(): pl.pallas_call(attend_back_kernel, out_shape=[jax.ShapeDtypeStruct((SEQ,...]
    select_n x2 -> x0, other arithmetic: 6.74 us -> none  [the longest x1 3.61 us: fast_body(): jnp.where(c == 0, jnp.concatenate([ga_own, ga_got]), jnp.concatenate([ga_...]
    sin x1 -> x0, other arithmetic: 5.6 us -> none  [fast_body(): cosine, sine = (jnp.cos(angles), jnp.sin(angles))]
  transfers between devices with their start and end apart: 7 -> 7, of which waited for: 3 -> 2; matrix products, arithmetic and copies ran while one was open for 4% -> 1% of each run, Pallas kernels for 51% -> 51%
where the time goes in v5:
time: 476 us; the launch traced here: 470 us
  Pallas kernels  432 us (91%)
  waiting for transfers between devices  16.5 us (3%)
  starting transfers between devices  13.5 us (3%)
    pallas_call x1, Pallas kernels, tail(): pl.pallas_call(tail_kernel, out_shape=[jax.ShapeDtypeStruct((2, SEQ, 256)...  132 us
    pallas_call x1, Pallas kernels, gather(): pl.pallas_call(gather_kernel, out_shape=[jax.ShapeDtypeStruct(shape, BF16...  121 us
    pallas_call x1, Pallas kernels, mlp(): pl.pallas_call(mlp_kernel, out_shape=[tokens(wide), tokens(wide, F32), to...  60.2 us
    pallas_call x1, Pallas kernels, weights(): pl.pallas_call(weights_kernel, out_shape=[jax.ShapeDtypeStruct((2, 128, l...  41.2 us
    pallas_call x1, Pallas kernels, attend_back(): pl.pallas_call(attend_back_kernel, out_shape=[jax.ShapeDtypeStruct((SEQ,...  39.7 us
    pallas_call x1, Pallas kernels, attend(): pl.pallas_call(attend_kernel, out_shape=[jax.ShapeDtypeStruct((SEQ // 2,...  25 us
    ppermute x7, waiting for transfers between devices, move(): return lax.ppermute(values, AXES, pairs)  16.5 us
    ppermute x7, starting transfers between devices, move(): return lax.ppermute(values, AXES, pairs)  13.5 us
  transfers between devices with their start and end apart: 7, of which 2 were waited for; matrix products, arithmetic and copies ran while one was open for 1% of the time, Pallas kernels for 51%

profile of v5, /device:TPU:11, one launch (start us, length us, event | category | flops | bytes accessed | tf_op | source)
XLA Modules:
  0.0 469.5 jit_solution(8097368215386944314)
XLA Ops:
  0.6 0.7 collective-permute-start
  1.4 0.5 compare_select_fusion.at
  2.0 0.6 broadcast_in_dim_tile.3.freqs
  2.6 0.7 fusion.halves
  3.2 2.3 pack.1
  5.5 0.7 broadcast_select_fusion
  6.8 120.6 %gather.1 = (bf16[2,1024,1024]{2,1,0:T(8,128)(2,1)}, bf16[4,4,1024,256]{3,2,1,0:T(8,128)(2,1)}, bf16[3,8,2,4,352,128]{5,4,3,2,1,0:T(8,128)(2,1)}, bf16[2048,1024...) custom-call(s32[8]{0:T(128)} %copy-done.1, ...), custom_call_target="tpu_custom_call" | custom-call | tf_op jit(solution)/shard_map/gather/pallas_call | solution.py:701
  127.4 2.0 collective-permute-start.2
  129.5 0.6 pad_add_fusion.bounds
  130.1 25.0 %attend.1 = (bf16[1024,512]{1,0:T(8,128)(2,1)}, bf16[1024,512]{1,0:T(8,128)(2,1)}, f32[2,8,1024]{2,1,0:T(8,128)}) custom-call(s32[8]{0:T(128)} %compare_select_fusion.at, s32[16]{0:T(128)} %pad_add_fusion.bounds, bf16[2048,512]{1,0:T(8,128)(2,1)} %get-tuple-element.69.q_ref.q_hbm, bf16[2048,512]{1,0:T(8,128)(2,1)} %get-tuple-element.70.k_ref.k_hbm, ...), custom_call_target="tpu_custom_call" | custom-call | flops 20000000000 | bytes 12000000 | tf_op jit(solution)/shard_map/attend/pallas_call | solution.py:848
  155.1 7.7 %collective-permute-start.1 = (bf16[1024,512]{1,0:T(8,128)(2,1)}, bf16[1024,512]{1,0:T(8,128)(2,1)S(1)}, u32[]{:S(2)}, u32[]{:S(2)}) collective-permute-start(bf16[1024,512]{1,0:T(8,128)(2,1)} %get-tuple-element.73.o_other), channel_id=1, source_target_pairs={{0,4},{1,5},{2,6},{3,7},{4,0},{5,1},{6,2},{7,3},{8,12},{9,13},{10,... | collective-permute-start | bytes 3145736 | tf_op jit(solution)/shard_map/ppermute | solution.py:309
  162.8 2.5 collective-permute-done.1.att_other.other
  165.4 1.0 copy-done.3
  166.3 60.2 %mlp.1 = (bf16[1024,1024]{1,0:T(8,128)(2,1)}, f32[1024,1024]{1,0:T(8,128)}, bf16[1024,1024]{1,0:T(8,128)(2,1)}, bf16[1024,1024]{1,0:T(8,128)(2,1)}, bf16[3,1024,...) custom-call(s32[8]{0:T(128)} %compare_select_fusion.at, ...), custom_call_target="tpu_custom_call" | custom-call | flops 39728447488 | bytes 60000000 | tf_op jit(solution)/shard_map/mlp/pallas_call | solution.py:1087
  226.5 0.4 collective-permute-start.3
  227.0 2.0 collective-permute-start.6
  229.0 41.2 %weights.1 = (bf16[2,128,4736]{2,1,0:T(8,128)(2,1)}, bf16[2,128,4736]{2,1,0:T(8,128)(2,1)}, bf16[2,128,4736]{2,1,0:T(8,128)(2,1)}, bf16[2,128,4736]{2,1,0:T(8,128)(2,1)}) custom-call(bf16[1024,1024]{1,0:T(8,128)(2,1)} %get-tuple-element.80.n2, bf16[1024,1024]{1,0:T(8,128)(2,1)} %get-tuple-element.81.g, bf16[1024,1024]{1,0:T(8,128)(2,1)} %get-tuple-element.82.branch, ...), custom_call_target="tpu_custom_call" | custom-call | flops 19864223744 | bytes 50000000 | tf_op jit(solution)/shard_map/weights/pallas_call | solution.py:1229
  270.2 0.3 collective-permute-start.4
  270.7 0.5 copy-done.2
  271.2 39.7 %attend_back.1 = (bf16[2048,512]{1,0:T(8,128)(2,1)}, bf16[2048,512]{1,0:T(8,128)(2,1)}, bf16[2048,512]{1,0:T(8,128)(2,1)}) custom-call(s32[8]{0:T(128)} %compare_select_fusion.at, s32[16]{0:T(128)} %pad_add_fusion.bounds, bf16[2048,512]{1,0:T(8,128)(2,1)} %get-tuple-element.69.q_ref.q_hbm, bf16[2048,512]{1,0:T(8,128)(2,1)} %get-tuple-element.70.k_ref.k_hbm, ...), custom_call_target="tpu_custom_call" | custom-call | flops 49999998976 | bytes 20000000 | tf_op jit(solution)/shard_map/attend_back/pallas_call | solution.py:977
  310.9 14.0 %collective-permute-done.4.got1 = bf16[2,128,4736]{2,1,0:T(8,128)(2,1)} collective-permute-done((bf16[2,128,4736]{2,1,0:T(8,128)(2,1)}, bf16[2,128,4736]{2,1,0:T(8,128)(2,1)}, u32[]{:S(2)}, u32[]{:S(2)}) %collective-permute-start.4) | collective-permute-done | bytes 2424864 | tf_op jit(solution)/shard_map/ppermute | solution.py:309
  324.9 132.0 %tail.1 = (bf16[2,2048,256]{2,1,0:T(8,128)(2,1)}, bf16[2368,128]{1,0:T(8,128)(2,1)}, bf16[3,2368,128]{2,1,0:T(8,128)(2,1)}, bf16[3,128,256]{2,1,0:T(8,128)(2,1)}...) custom-call(bf16[2048,512]{1,0:T(8,128)(2,1)} %get-tuple-element.93., ...), custom_call_target="tpu_custom_call" | custom-call | tf_op jit(solution)/shard_map/tail/pallas_call | solution.py:1549
  456.8 1.4 fusion.6
  458.3 11.0 %finish.1 = (f32[704,128]{1,0:T(8,128)}, f32[704,128]{1,0:T(8,128)}, f32[704,128]{1,0:T(8,128)}, f32[256,128]{1,0:T(8,128)}, f32[128,256]{1,0:T(8,128)}, /*index...) custom-call(s32[8]{0:T(128)} %compare_select_fusion.at, ...), custom_call_target="tpu_custom_call" | custom-call | flops 1000000 | bytes 18000000 | tf_op jit(solution)/shard_map/finish/pallas_call | solution.py:1292
  (23 shorter events, 0.9 us)
Async XLA Ops:
  0.6 4.9 %collective-permute-start = (s32[2,8]{1,0:T(2,128)}, s32[2,8]{1,0:T(2,128)S(1)}, u32[]{:S(2)}, u32[]{:S(2)}) collective-permute-start(s32[2,8]{1,0:T(2,128)} %param.15), channel_id=1, source_target_pairs={{0,4},{1,5},{2,6},{3,7},{4,0},{5,1},{6,2},{7,3},{8,12},{9,13},{10,... | collective-permute-start | bytes 200 | tf_op jit(solution)/shard_map/ppermute | solution.py:309
  6.3 0.5 copy-start.1
  6.6 120.8 %copy-start = (s32[8,256]{1,0:T(8,128)}, s32[8,256]{1,0:T(8,128)S(1)}, u32[]{:S(2)}) copy-start(s32[8,256]{1,0:T(8,128)S(1)} %reshape.65.starts) | copy-start | bytes 24580
  127.4 37.9 %collective-permute-start.2 = (bf16[1024,1024]{1,0:T(8,128)(2,1)}, bf16[1024,1024]{1,0:T(8,128)(2,1)}, u32[]{:S(2)}, u32[]{:S(2)}) collective-permute-start(bf16[1024,1024]{1,0:T(8,128)(2,1)} %cot_here), channel_id=1, source_target_pairs={{1,4},{3,6},{4,1},{6,3},{9,12},{11,14},{12,9},{14,11},{17,20},{19,... | collective-permute-start | bytes 6291464 | tf_op jit(solution)/shard_map/ppermute | solution.py:309
  155.1 10.2 %collective-permute-start.1 = (bf16[1024,512]{1,0:T(8,128)(2,1)}, bf16[1024,512]{1,0:T(8,128)(2,1)S(1)}, u32[]{:S(2)}, u32[]{:S(2)}) collective-permute-start(bf16[1024,512]{1,0:T(8,128)(2,1)} %get-tuple-element.73.o_other), channel_id=1, source_target_pairs={{0,4},{1,5},{2,6},{3,7},{4,0},{5,1},{6,2},{7,3},{8,12},{9,13},{10,... | collective-permute-start | bytes 3145736 | tf_op jit(solution)/shard_map/ppermute | solution.py:309
  165.3 1.0 copy-start.3
  226.5 43.6 %collective-permute-start.3 = (bf16[1024,512]{1,0:T(8,128)(2,1)}, bf16[1024,512]{1,0:T(8,128)(2,1)S(1)}, u32[]{:S(2)}, u32[]{:S(2)}) collective-permute-start(bf16[1024,512]{1,0:T(8,128)(2,1)} %get-tuple-element.88), channel_id=1, source_target_pairs={{0,4},{1,5},{2,6},{3,7},{4,0},{5,1},{6,2},{7,3},{8,12},{9,13},{10,... | collective-permute-start | bytes 3145736 | tf_op jit(solution)/shard_map/ppermute | solution.py:309
  227.0 231.3 %collective-permute-start.6 = (bf16[1024,1024]{1,0:T(8,128)(2,1)}, bf16[1024,1024]{1,0:T(8,128)(2,1)}, u32[]{:S(2)}, u32[]{:S(2)}) collective-permute-start(bf16[1024,1024]{1,0:T(8,128)(2,1)} %get-tuple-element.110.layer), channel_id=1, source_target_pairs={{1,4},{3,6},{4,1},{6,3},{9,12},{11,14},{12,9},{14,11},{17,20},{19,... | collective-permute-start | bytes 6291464 | tf_op jit(solution)/shard_map/ppermute | solution.py:309
  270.2 1.0 copy-start.2
  270.2 54.7 %collective-permute-start.4 = (bf16[2,128,4736]{2,1,0:T(8,128)(2,1)}, bf16[2,128,4736]{2,1,0:T(8,128)(2,1)}, u32[]{:S(2)}, u32[]{:S(2)}) collective-permute-start(bf16[2,128,4736]{2,1,0:T(8,128)(2,1)} %get-tuple-element.99), channel_id=1, source_target_pairs={{0,8},{1,9},{2,10},{3,11},{4,12},{5,13},{6,14},{7,15},{8,0},{9,1},... | collective-permute-start | bytes 7274504 | tf_op jit(solution)/shard_map/ppermute | solution.py:309
  270.5 54.3 %collective-permute-start.5 = (bf16[2,128,4736]{2,1,0:T(8,128)(2,1)}, bf16[2,128,4736]{2,1,0:T(8,128)(2,1)}, u32[]{:S(2)}, u32[]{:S(2)}) collective-permute-start(bf16[2,128,4736]{2,1,0:T(8,128)(2,1)} %get-tuple-element.101), channel_id=1, source_target_pairs={{0,16},{1,17},{2,18},{3,19},{4,20},{5,21},{6,22},{7,23},{8,24},{9,... | collective-permute-start | bytes 7274504 | tf_op jit(solution)/shard_map/ppermute | solution.py:309

commit v6 on v5

--- a/solution.py
+++ b/solution.py
@@ -611,12 +611,20 @@
     )
     given.start()
     load_w.wait()
-    outs = []
+
+    def rows_of(half, n):
+        return pl.ds(pl.multiple_of(half * (SEQ // 2) + n * 512, 512), 512)
+
+    def done_copies(half, n):
+        rows = rows_of(half, n)
+        return [
+            pltpu.make_async_copy(src.at[rows, :], dst.at[rows, :], tile_sem.at[2 * half + n, m])
+            for m, (src, dst) in enumerate(((n_s, normed_out), (q_s, q_out), (k_s, k_out)))
+        ]
 
     def project(half, n):
-        low = pl.multiple_of(half * (SEQ // 2) + lax.rem(n, 2) * 512, 512)
-        rows = pl.ds(low, 512)
-        values = row[half, n % 2 * 512 : n % 2 * 512 + 512, :].astype(F32)
+        rows = rows_of(half, n)
+        values = row[half, pl.ds(pl.multiple_of(n * 512, 512), 512), :].astype(F32)
         factor = lax.rsqrt(jnp.mean(values * values, axis=1, keepdims=True) + EPSILON)
         normed = (values * factor * gain[...]).astype(BF16)
         n_s[rows, :] = normed
@@ -628,19 +636,24 @@
                 out[rows, u * 256 : u * 256 + 128] = ((a * cos - b * sin) * scale).astype(BF16)
                 out[rows, u * 256 + 128 : u * 256 + 256] = ((b * cos + a * sin) * scale).astype(BF16)
             raw_s[rows, u * 256 : u * 256 + 256] = 0.5 * dot(normed, w_s[2, u])
-        for m, (src, dst) in enumerate(((n_s, normed_out), (q_s, q_out), (k_s, k_out))):
-            item = pltpu.make_async_copy(src.at[rows, :], dst.at[rows, :], tile_sem.at[n, m])
+        for item in done_copies(half, n):
             item.start()
-            outs.append(item)
-
-    project(c, 0)
-    project(c, 1)
-    pass_over(order[2])
-    given.wait_recv()
+
     row_copy = pltpu.make_async_copy(row, row_out, end_sem.at[3])
-    row_copy.start()
-    project(1 - c, 2)
-    project(1 - c, 3)
+
+    def half_row(i, carry):
+        @pl.when(i == 1)
+        def _():
+            pass_over(order[2])
+            given.wait_recv()
+            row_copy.start()
+
+        half = c + i - 2 * c * i
+        project(half, 0)
+        project(half, 1)
+        return carry
+
+    lax.fori_loop(0, 2, half_row, 0)
     pass_over(order[3])
 
     for p in range(2):
@@ -667,6 +680,7 @@
         def _():
             came.wait_recv()
 
+    outs = []
     for n in range(4):
         rows = slice(n * 512, n * 512 + 512)
         for u in range(2):
@@ -676,6 +690,8 @@
         item.start()
         outs.append(item)
 
+    for n in range(4):
+        outs += done_copies(n // 2, n % 2)
     given.wait_send()
     for k in range(chunks):
         if k:
@@ -866,8 +882,24 @@
 
 
 def attend_back_kernel(
-    at, bounds, q_hbm, k_hbm, v_hbm, do_own, do_other, o_own, o_other, lse_ref, starts, cosine, sine, dq_hbm, dk_hbm, dv_hbm,
-    q_ref, k_ref, v_ref, do_ref, o_ref, dq_ref, dk_ref, dv_ref, dq_acc, delta, dk_acc, dv_acc, load, store,
+    at, bounds, q_hbm, k_hbm, v_hbm, do_own, do_other, o_own, o_other, lse_ref, starts, cosine, sine, *rest, part,
+):
+    if part:
+        held_hbm, rest = rest[0], rest[1:]
+        dq_hbm, dk_hbm, dv_hbm = rest[:3]
+        rest = rest[3:]
+    else:
+        dq_hbm, dk_hbm, dv_hbm, held_hbm = rest[:4]
+        rest = rest[4:]
+    attend_back_part(
+        at, bounds, q_hbm, k_hbm, v_hbm, do_own, do_other, o_own, o_other, lse_ref, starts, cosine, sine, held_hbm, dq_hbm, dk_hbm,
+        dv_hbm, *rest, part=part
+    )
+
+
+def attend_back_part(
+    at, bounds, q_hbm, k_hbm, v_hbm, do_own, do_other, o_own, o_other, lse_ref, starts, cosine, sine, held_hbm, dq_hbm, dk_hbm, dv_hbm,
+    q_ref, k_ref, v_ref, do_ref, o_ref, dq_ref, dk_ref, dv_ref, dq_acc, delta, dk_acc, dv_acc, load, store, *, part,
 ):
     tiles = SEQ // TILE
     of_qk, of_v = head_masks(TILE)
@@ -881,23 +913,39 @@
     half = SEQ // 2
     low = pl.multiple_of((at[0] & 1) * half, half)
     mine, others = pl.ds(low, half), pl.ds(half - low, half)
-    loads = [
-        pltpu.make_async_copy(src, dst, load.at[n])
-        for n, (src, dst) in enumerate((
-            (do_own, do_ref.at[mine, :]),
-            (do_other, do_ref.at[others, :]),
-            (o_own, o_ref.at[mine, :]),
-            (o_other, o_ref.at[others, :]),
-            (q_hbm, q_ref),
-            (k_hbm, k_ref),
-            (v_hbm, v_ref),
-        ))
+    first_half, second_half = pl.ds(0, half), pl.ds(half, half)
+    mine_second = (at[0] & 1) == 1
+    here_half = second_half if part else first_half
+    q_rows = second_half if part else pl.ds(0, SEQ)
+    plain = [
+        (q_hbm.at[q_rows, :], q_ref.at[q_rows, :]),
+        (k_hbm.at[here_half, :], k_ref.at[here_half, :]),
+        (v_hbm.at[here_half, :], v_ref.at[here_half, :]),
     ]
+    if part:
+        plain.append((held_hbm, dq_acc.at[pl.ds(tiles // 2, tiles // 2)]))
+    loads = [pltpu.make_async_copy(src, dst, load.at[4 + n]) for n, (src, dst) in enumerate(plain)]
+
+    def half_loads(own, other, dst, n):
+        pairs = [(own, mine, mine_second), (other, others, jnp.logical_not(mine_second))]
+        for e, (src, rows, wanted) in enumerate(pairs):
+            yield pltpu.make_async_copy(src, dst.at[rows, :], load.at[n + e]), wanted
+
+    parts = list(half_loads(do_own, do_other, do_ref, 0)) + list(half_loads(o_own, o_other, o_ref, 2))
+
+    def each(action):
+        for item, wanted in parts:
+            if part:
+                pl.when(wanted)(functools.partial(action, item))
+            else:
+                action(item)
+
+    each(lambda item: item.start())
     for item in loads:
         item.start()
-    dq_acc[...] = jnp.zeros_like(dq_acc)
-    for item in loads[:4]:
-        item.wait()
+    if not part:
+        dq_acc[...] = jnp.zeros_like(dq_acc)
+    each(lambda item: item.wait())
 
     def prepare(i, carry):
         here = pl.ds(pl.multiple_of(i * TILE, TILE), TILE)
@@ -910,8 +958,9 @@
                 delta[u, pl.ds(i, 1), h * TILE : (h + 1) * TILE] = sums[h : h + 1]
         return carry
 
-    lax.fori_loop(0, tiles, prepare, 0)
-    for item in loads[4:]:
+    middle = tiles // 2
+    lax.fori_loop(middle * part, tiles, prepare, 0)
+    for item in loads:
         item.wait()
 
     def rotate_out(values, here, out, low, scale):
@@ -952,46 +1001,56 @@
         for u, slab in enumerate(slabs):
             rotate_out(dk_acc[u], there, dk_ref, u * 256, 1.0)
             dv_ref[there, slab] = (0.5 * dv_acc[u]).astype(BF16)
-        pltpu.make_async_copy(dk_ref.at[there, :], dk_hbm.at[there, :], store.at[0]).start()
-        pltpu.make_async_copy(dv_ref.at[there, :], dv_hbm.at[there, :], store.at[1]).start()
+        local = pl.ds(pl.multiple_of((j - middle * part) * TILE, TILE), TILE)
+        pltpu.make_async_copy(dk_ref.at[there, :], dk_hbm.at[local, :], store.at[0]).start()
+        pltpu.make_async_copy(dv_ref.at[there, :], dv_hbm.at[local, :], store.at[1]).start()
         return carry
 
-    lax.fori_loop(0, tiles, key_tile, 0)
+    lax.fori_loop(middle * part, middle * part + middle, key_tile, 0)
+    if not part:
+        held = pltpu.make_async_copy(dq_acc.at[pl.ds(middle, middle)], held_hbm, store.at[3])
+        held.start()
 
     def finish_tile(i, carry):
         here = pl.ds(pl.multiple_of(i * TILE, TILE), TILE)
         for u in range(2):
             rotate_out(dq_acc[i, u], here, dq_ref, u * 256, 0.125)
-        pltpu.make_async_copy(dq_ref.at[here, :], dq_hbm.at[here, :], store.at[2]).start()
+        local = pl.ds(pl.multiple_of((i - middle * part) * TILE, TILE), TILE)
+        pltpu.make_async_copy(dq_ref.at[here, :], dq_hbm.at[local, :], store.at[2]).start()
         return carry
 
-    lax.fori_loop(0, tiles, finish_tile, 0)
+    lax.fori_loop(middle * part, middle * part + middle, finish_tile, 0)
     for n, (src, dst) in enumerate(((dk_ref, dk_hbm), (dv_ref, dv_hbm), (dq_ref, dq_hbm))):
-        pltpu.make_async_copy(src, dst, store.at[n]).wait()
-
-
-def attend_back(at, bounds, q, k, v, do_own, do_other, o_own, o_other, lse, starts, cosine, sine):
+        pltpu.make_async_copy(src.at[here_half, :], dst, store.at[n]).wait()
+    if not part:
+        held.wait()
+
+
+def attend_back(part, at, bounds, q, k, v, do_own, do_other, o_own, o_other, lse, starts, cosine, sine, *held):
     tiles = SEQ // TILE
     vmem = pl.BlockSpec(memory_space=pltpu.VMEM)
     sems = pltpu.SemaphoreType.DMA
+    outs = [jax.ShapeDtypeStruct((SEQ // 2, 512), BF16)] * 3
+    if not part:
+        outs.append(jax.ShapeDtypeStruct((tiles // 2, 2, TILE, 256), F32))
     return pl.pallas_call(
-        attend_back_kernel,
-        out_shape=[jax.ShapeDtypeStruct((SEQ, 512), BF16)] * 3,
-        in_specs=[pl.BlockSpec(memory_space=pltpu.SMEM)] * 2 + [any_spec()] * 7 + [vmem] * 4,
-        out_specs=[any_spec()] * 3,
+        functools.partial(attend_back_kernel, part=part),
+        out_shape=outs,
+        in_specs=[pl.BlockSpec(memory_space=pltpu.SMEM)] * 2 + [any_spec()] * 7 + [vmem] * 4 + [any_spec()] * len(held),
+        out_specs=[any_spec()] * len(outs),
         scratch_shapes=[pltpu.VMEM((SEQ, 512), BF16)] * 8
         + [
             pltpu.VMEM((tiles, 2, TILE, 256), F32),
             pltpu.VMEM((2, tiles, 4 * TILE), F32),
             pltpu.VMEM((2, TILE, 256), F32),
             pltpu.VMEM((2, TILE, 256), F32),
-            sems((7,)),
-            sems((3,)),
+            sems((8,)),
+            sems((4,)),
         ],
         compiler_params=params(),
-        cost_estimate=cost(50e9, 20e6, 1e7),
+        cost_estimate=cost(25e9, 12e6, 5e6),
         name="attend_back",
-    )(at, bounds, q, k, v, do_own, do_other, o_own, o_other, lse, starts, cosine, sine)
+    )(at, bounds, q, k, v, do_own, do_other, o_own, o_other, lse, starts, cosine, sine, *held)
 
 
 def mlp_kernel(at, att_own, att_other, tok, cot_here, cot_moved, gain, wo, big, *rest):
@@ -1240,7 +1299,7 @@
     return (left.astype(F32) + right.astype(F32)).astype(BF16)
 
 
-def finish_kernel(at, own, got, own_heads, got_heads, tok, got_tok, first, layer, got_layer, gate, up, down, out, query, key, value, tok_out, first_out, layer_out):
+def finish_kernel(at, own, got, own_heads, got_heads, tok, got_tok, first, came0, came1, slab0, slab1, layer, got_layer, gate, up, down, out, query, key, value, tok_out, first_out, layer_out):
     @pl.when(pl.program_id(0) == 0)
     def _():
         part = down.shape[0]
@@ -1262,15 +1321,30 @@
 
     stays = (at[0] & 1) == (at[1] & 1)
     tok_out[...] = jnp.where(stays, tok[...], got_tok[...]).astype(F32)
-    first_out[...] = first[...].astype(F32)
+    step = pl.program_id(0)
+    c, t = at[0] & 1, at[1]
+    pair, side = t >> 1, t & 1
+    r = (step >> 1) ^ side
+    local = (c == side) & (t == 2 * c + (pair ^ r))
+
+    @pl.when((step & 1) == 0)
+    def _():
+        came = jnp.where(r == 0, came0[...], came1[...])
+        slab = jnp.where(r == 0, slab0[...], slab1[...])
+        first_out[...] = jnp.where(local, slab, came).astype(F32)
+
+    @pl.when((step & 1) == 1)
+    def _():
+        first_out[...] = first[0].astype(F32)
+
     layer_out[...] = jnp.where(stays, layer[...], got_layer[...])
 
 
-def finish(at, pieces, got, own_heads, got_heads, tok, got_tok, first, layer, got_layer, part):
+def finish(at, pieces, got, own_heads, got_heads, tok, got_tok, first, early, layer, got_layer, part):
     count, wide = tok.shape
     rows = 256
     row = pl.BlockSpec((rows, wide), lambda i, at: (i, 0))
-    wider = pl.BlockSpec((first.shape[0] * rows // count, first.shape[1]), lambda i, at: (i, 0))
+    wider = pl.BlockSpec((SEQ // 2, 256), lambda i, at: (i, 0))
     whole = lambda *shape: pl.BlockSpec(shape, lambda i, at: (0,) * len(shape))
     shapes = [(part, 128)] * 3 + [(256, 128)] + [(128, 256)] * 3
     grid = pltpu.PrefetchScalarGridSpec(
@@ -1283,7 +1357,8 @@
             whole(*got_heads.shape),
             row,
             row,
-            wider,
+            pl.BlockSpec((1, SEQ // 2, 256), lambda i, at: (i // 2, 0, 0)),
+            *[whole(SEQ // 2, 256)] * 4,
             row,
             row,
         ],
@@ -1291,19 +1366,19 @@
     )
     return pl.pallas_call(
         finish_kernel,
-        out_shape=[jax.ShapeDtypeStruct(shape, F32) for shape in shapes + [(count, wide), first.shape]]
+        out_shape=[jax.ShapeDtypeStruct(shape, F32) for shape in shapes + [(count, wide), (2 * SEQ, 256)]]
         + [jax.ShapeDtypeStruct((count, wide), BF16)],
         grid_spec=grid,
         compiler_params=params(),
         cost_estimate=cost(1e6, 18e6),
         name="finish",
-    )(at, pieces, got, own_heads, got_heads, tok, got_tok, first, layer, got_layer)
+    )(at, pieces, got, own_heads, got_heads, tok, got_tok, first, *early, layer, got_layer)
 
 
 def tail_kernel(
-    dq, dk, dv, small, normed, row, grad_hidden, keep1, got1, keep2, got2, gain, gain_two,
+    dq0, dk0, dv0, dq1, dk1, dv1, small, normed, row, grad_hidden, keep1, got1, keep2, got2, gain, gain_two,
     first, own_pieces, got_pieces, own_heads, got_heads, tok, got_tok, sums,
-    q_s, k_s, v_s, w_s, n_s, x_s, gh_s, ks1, gs1, ks2, gs2, last1, last2, pieces, gn_send, gn_got, turned,
+    d_s, w_s, n_s, x_s, gh_s, ks1, gs1, ks2, gs2, last1, last2, pieces, gn_send, gn_got, turned,
     h_send, h_got, s1, k1, a1, a2, part1, part2, rest1, rest2, heads, held, came,
     load, f_sem, m_sem, p_sem, n_sem, c_sem, one_sem, two_sem, h_sem, swap, g_sem,
 ):
@@ -1325,15 +1400,17 @@
             device_id_type=MESH,
         )
 
-    sources = [(keep1, ks1), (got1, gs1), (keep2, ks2), (got2, gs2), (dq, q_s), (dk, k_s), (dv, v_s)]
-    sources += [(small.at[pl.ds(0, 3), pl.ds(2 * c, 2)], w_s), (normed, n_s), (row.at[c], x_s), (grad_hidden, gh_s)]
+    sources = [(keep1, ks1), (got1, gs1), (keep2, ks2), (got2, gs2)]
+    for h, arrays in enumerate(((dq0, dk0, dv0), (dq1, dk1, dv1))):
+        sources += [(src, d_s.at[n, pl.ds(h * half, half), :]) for n, src in enumerate(arrays)]
+    sources += [(normed, n_s), (small.at[pl.ds(0, 3), pl.ds(2 * c, 2)], w_s), (row.at[c], x_s), (grad_hidden, gh_s)]
     loads = [pltpu.make_async_copy(src, dst, load.at[n]) for n, (src, dst) in enumerate(sources)]
     for item in loads:
         item.start()
     meet(plane, c, t, dpx, dpy)
 
     def value_copy(u):
-        src = dv.at[:, pl.ds(u * 256, 256)]
+        src = dv1.at[:, pl.ds(u * 256, 256)]
         return pltpu.make_async_remote_copy(
             src_ref=src,
             dst_ref=first.at[pair],
@@ -1344,7 +1421,7 @@
         )
 
     def value_local(u):
-        return pltpu.make_async_copy(dv.at[:, pl.ds(u * 256, 256)], first.at[pair], load.at[11])
+        return pltpu.make_async_copy(dv1.at[:, pl.ds(u * 256, 256)], first.at[pair], load.at[14])
 
     for u in range(2):
         stay = (side == c) & (t == 2 * c + u)
@@ -1361,25 +1438,14 @@
         item.wait()
     gs1[1] = add(ks1[1], gs1[1])
     gs2[1] = add(ks2[1], gs2[1])
-    seconds = [copy(gs1.at[1], last1, m_sem, 0, (dpy, t)), copy(gs2.at[1], last2, m_sem, 1, (dpx, t))]
-    for item in loads[4:8]:
+    seconds = []
+    for n, lanes in enumerate((pl.ds(0, 2 * units), pl.ds(2 * units, units + 512))):
+        seconds.append(copy(gs1.at[1, :, lanes], last1.at[:, lanes], m_sem, 2 * n, (dpy, t)))
+        seconds.append(copy(gs2.at[1, :, lanes], last2.at[:, lanes], m_sem, 2 * n + 1, (dpx, t)))
+    for item in loads[4:11]:
         item.wait()
     for item in seconds:
         item.start()
-
-    def back_product(rows):
-        total = None
-        for u in range(2):
-            for n, grad in enumerate((q_s, k_s, v_s)):
-                term = dot_nt(grad[rows, u * 256 : u * 256 + 256], w_s[n, u])
-                total = term if total is None else total + term
-        return total
-
-    ns = []
-    for i in range(2):
-        rows = pl.ds(pl.multiple_of((1 - c) * half + i * 512, 512), 512)
-        gn_send[i] = back_product(rows).astype(BF16)
-        ns.append(copy(gn_send.at[i], gn_got.at[i], n_sem, i, (dpc, t)))
 
     def turn(parity):
         for rel in range(4):
@@ -1387,58 +1453,114 @@
             block = pl.multiple_of((yy * 4 + xx * 2 + parity) * 128, 128)
             turned[rel * 128 : rel * 128 + 128, :] = n_s[:, pl.ds(block, 128)].T
 
-    loads[8].wait()
+    def heads_copy(n):
+        lanes = pl.ds(pl.multiple_of(n * 512, 512), 512)
+        return copy(h_send.at[:, :, :, lanes], h_got.at[:, :, :, lanes], c_sem, n, (dpc, t))
+
+    def heads_product(n):
+        product = dot(turned[...], d_s[n]).astype(BF16)
+        return [product[r * 128 : r * 128 + 128] for r in range(4)], pl.ds(pl.multiple_of(n * 512, 512), 512)
+
+    def heads_send(n, carry):
+        place_second(h_send.at[0], h_send.at[1], *heads_product(n))
+
+        @pl.when(n > 0)
+        def _():
+            heads_copy(n - 1).start()
+
+        return carry
+
+    def heads_keep(n, carry):
+        place_first(s1, k1, *heads_product(n))
+        return carry
+
     turn(1 - c)
-    for item in ns:
+    lax.fori_loop(0, 3, heads_send, 0)
+
+    part = units // 4
+    low_rows, high_rows = pl.ds(0, 4 * part), pl.ds(4 * part, 2 * part + 256)
+
+    def fill_pieces(which):
+        for h, (kept, got, last) in enumerate(((ks1, gs1, last1), (ks2, gs2, last2))):
+            for n in which:
+                lanes = slice(n * units, n * units + (units if n < 3 else 512))
+                total = kept[0, :, lanes].astype(F32) + got[0, :, lanes].astype(F32) + last[:, lanes].astype(F32)
+                flipped = total.T.astype(BF16)
+                if n < 3:
+                    for i in range(4):
+                        rows = slice((2 * n + h) * part, (2 * n + h + 1) * part)
+                        pieces[lax.rem(i + 4 - t, 4), rows, :] = flipped[i * part : (i + 1) * part]
+                else:
+                    for i in range(2):
+                        pieces[lax.rem(2 * h + i + 4 - t, 4), 6 * part :, :] = flipped[i * 256 : i * 256 + 256]
+
+    def piece_copies(rows, n):
+        return [
+            copy(pieces.at[d, rows, :], got_pieces.at[d - 1, rows, :], p_sem, 3 * n + d - 1, (dp, lax.rem(t + d, 4)))
+            for d in (1, 2, 3)
+        ]
+
+    for item in seconds[:2]:
+        item.wait_recv()
+    fill_pieces((0, 1))
+    turn(c)
+    heads_copy(2).start()
+    zs = piece_copies(low_rows, 0)
+    for item in zs:
         item.start()
-    cs = []
-    for n, right in enumerate((q_s, k_s, v_s)):
-        product = dot(turned[...], right[...]).astype(BF16)
-        lanes = slice(n * 512, n * 512 + 512)
-        place_second(h_send.at[0], h_send.at[1], [product[r * 128 : r * 128 + 128] for r in range(4)], lanes)
-        cs.append(copy(h_send.at[:, :, :, pl.ds(n * 512, 512)], h_got.at[:, :, :, pl.ds(n * 512, 512)], c_sem, n, (dpc, t)))
-        if n:
-            cs[n - 1].start()
-    turn(c)
-    cs[2].start()
-    for n, right in enumerate((q_s, k_s, v_s)):
-        product = dot(turned[...], right[...]).astype(BF16)
-        lanes = slice(n * 512, n * 512 + 512)
-        place_first(s1, k1, [product[r * 128 : r * 128 + 128] for r in range(4)], lanes)
+    lax.fori_loop(0, 3, heads_keep, 0)
+    cs = [heads_copy(n) for n in range(3)]
     for item in cs:
         item.wait_recv()
     ones = [copy(h_got.at[0], a2, one_sem, 1, (dpy, t)), copy(s1, a1, one_sem, 0, (dpx, t))]
     for item in ones:
         item.start()
-
-    for item in seconds:
+    for item in seconds[2:]:
         item.wait_recv()
-    part = units // 4
-    for h, (kept, got, last) in enumerate(((ks1, gs1, last1), (ks2, gs2, last2))):
-        for n in range(4):
-            lanes = slice(n * units, n * units + (units if n < 3 else 512))
-            total = kept[0, :, lanes].astype(F32) + got[0, :, lanes].astype(F32) + last[:, lanes].astype(F32)
-            flipped = total.T.astype(BF16)
-            if n < 3:
-                for i in range(4):
-                    rows = slice((2 * n + h) * part, (2 * n + h + 1) * part)
-                    pieces[lax.rem(i + 4 - t, 4), rows, :] = flipped[i * part : (i + 1) * part]
-            else:
-                for i in range(2):
-                    pieces[lax.rem(2 * h + i + 4 - t, 4), 6 * part :, :] = flipped[i * 256 : i * 256 + 256]
+    fill_pieces((2, 3))
     own_pieces[...] = pieces[0]
-    zs = [copy(pieces.at[d], got_pieces.at[d - 1], p_sem, d - 1, (dp, lax.rem(t + d, 4))) for d in (1, 2, 3)]
-    for item in zs:
+    last_zs = piece_copies(high_rows, 1)
+    for item in last_zs:
         item.start()
-
-    for item in loads[9:11]:
-        item.wait()
+    zs += last_zs
+
+    def back_product(rows):
+        total = None
+        for u in range(2):
+            for n in range(3):
+                term = dot_nt(d_s[n, rows, u * 256 : u * 256 + 256], w_s[n, u])
+                total = term if total is None else total + term
+        return total
+
+    ns = [copy(gn_send.at[i], gn_got.at[i], n_sem, i, (dpc, t)) for i in range(2)]
+
+    def other_half(i, carry):
+        rows = pl.ds(pl.multiple_of((1 - c) * half + i * 512, 512), 512)
+        gn_send[i] = back_product(rows).astype(BF16)
+        return carry
+
+    loads[11].wait()
+    lax.fori_loop(0, 2, other_half, 0)
+
+    for item in ones:
+        item.wait_recv()
+    part1[...] = add(k1[1], a1[1])
+    part2[...] = add(h_got[1, 1], a2[1])
+    for item in ns:
+        item.start()
+    twos = [copy(part1, rest1, two_sem, 0, (dpy, t)), copy(part2, rest2, two_sem, 1, (dpx, t))]
+    for item in twos:
+        item.start()
+
+    loads[12].wait()
+    loads[13].wait()
     moved = side != c
-    gained = jnp.zeros((8, tok.shape[2]), F32)
-    for i in range(2):
-        ns[i].wait_recv()
+    for item in ns:
+        item.wait_recv()
+
+    def own_half(i, gained):
         rows = pl.ds(pl.multiple_of(c * half + i * 512, 512), 512)
-        here = slice(i * 512, i * 512 + 512)
+        here = pl.ds(pl.multiple_of(i * 512, 512), 512)
         grad = back_product(rows) + gn_got[i].astype(F32)
         values = x_s[here, :].astype(F32)
         factor = lax.rsqrt(jnp.mean(values * values, axis=1, keepdims=True) + EPSILON)
@@ -1446,21 +1568,18 @@
         scaled = grad * gain[...]
         mean = jnp.mean(scaled * values, axis=1, keepdims=True)
         tok[i] = (gh_s[here, :] + factor * scaled - values * (factor * factor * factor * mean)).astype(BF16)
+        return gained
+
+    gained = lax.fori_loop(0, 2, own_half, jnp.zeros((8, tok.shape[2]), F32))
     swaps = [copy(tok.at[i], got_tok.at[i], swap, i, (plane + side, 2 * pair + c)) for i in range(2)]
 
-    for item in ones:
-        item.wait_recv()
-    part1[...] = add(k1[1], a1[1])
-    part2[...] = add(h_got[1, 1], a2[1])
+    total1 = k1[0].astype(F32) + a1[0].astype(F32)
+    total2 = h_got[1, 0].astype(F32) + a2[0].astype(F32)
 
     @pl.when(moved)
     def _():
         for item in swaps:
             item.start()
-
-    twos = [copy(part1, rest1, two_sem, 0, (dpy, t)), copy(part2, rest2, two_sem, 1, (dpx, t))]
-    for item in twos:
-        item.start()
 
     turns = (dpc, t), (dpx, t), (dpy, t), (dp, t + 1 - 2 * side), (dp, lax.rem(t + 2, 4))
     line = lax.broadcasted_iota(jnp.int32, gained.shape, 0)
@@ -1475,8 +1594,6 @@
         gain_step(n).wait_recv()
         held[n + 1] = held[n] + came[n]
 
-    total1 = k1[0].astype(F32) + a1[0].astype(F32)
-    total2 = h_got[1, 0].astype(F32) + a2[0].astype(F32)
     gain_step(0).start()
     gain_next(0)
     gain_step(1).start()
@@ -1538,7 +1655,7 @@
             item.wait()
 
 
-def tail(dq, dk, dv, small, normed, row, grad_hidden, keep1, got1, keep2, got2, gain, gain_two):
+def tail(back, small, normed, row, grad_hidden, keep1, got1, keep2, got2, gain, gain_two):
     vmem = pl.BlockSpec(memory_space=pltpu.VMEM)
     sems = pltpu.SemaphoreType.DMA
     wide = normed.shape[1]
@@ -1549,7 +1666,7 @@
     return pl.pallas_call(
         tail_kernel,
         out_shape=[
-            jax.ShapeDtypeStruct((2, SEQ, 256), BF16),
+            jax.ShapeDtypeStruct((2, half, 256), BF16),
             jax.ShapeDtypeStruct((rows, 128), BF16),
             jax.ShapeDtypeStruct((3, rows, 128), BF16),
             jax.ShapeDtypeStruct((3, 128, 256), BF16),
@@ -1558,9 +1675,9 @@
             jax.ShapeDtypeStruct((2, half // 2, wide), BF16),
             jax.ShapeDtypeStruct((8, wide), F32),
         ],
-        in_specs=[any_spec()] * 11 + [vmem] * 2,
+        in_specs=[any_spec()] * 14 + [vmem] * 2,
         out_specs=[any_spec(), vmem, any_spec(), vmem, any_spec(), vmem, any_spec(), vmem],
-        scratch_shapes=[low(SEQ, 512)] * 3
+        scratch_shapes=[low(3, SEQ, 512)]
         + [low(3, 2, wide, 256), low(SEQ, wide), low(half, wide), pltpu.VMEM((half, wide), F32)]
         + [low(2, 128, length)] * 4
         + [low(128, length)] * 2
@@ -1569,11 +1686,11 @@
         + [low(2, 128, 1536)] * 4
         + [low(128, 1536)] * 4
         + [low(4, 3, 128, 256), pltpu.VMEM((6, 8, wide), F32), pltpu.VMEM((5, 8, wide), F32)]
-        + [sems((12,)), sems((2, 2)), sems((2, 2)), sems((2, 3)), sems((2, 2)), sems((2, 3)), sems((2, 2)), sems((2, 2))]
+        + [sems((15,)), sems((2, 2)), sems((2, 4)), sems((2, 6)), sems((2, 2)), sems((2, 3)), sems((2, 2)), sems((2, 2))]
         + [sems((2, 3)), sems((2, 2)), sems((2, 5))],
         compiler_params=params(collective_id=2, has_side_effects=True),
         name="tail",
-    )(dq, dk, dv, small, normed, row, grad_hidden, keep1, got1, keep2, got2, gain, gain_two)
+    )(*back, small, normed, row, grad_hidden, keep1, got1, keep2, got2, gain, gain_two)
 
 
 def fast_body(tokens, first_values, doc_lengths, cotangent, w_query, w_key, w_value, w_out, w_gate, w_up, w_down, gain_attn, gain_mlp):
@@ -1615,16 +1732,22 @@
     kept, ga_got = lax.optimization_barrier((kept, ga_got))
     got1, got2 = across_x(kept[0]), across_y(kept[2])
 
-    dq, dk, dv = attend_back(
-        at, bounds, q, k, v, ga_own, ga_got, att_own, att_send, lse, starts_by_tile, cosine, sine
-    )
+    rest = (att_own, att_send, lse, starts_by_tile, cosine, sine)
+    dq0, dk0, dv0, held = attend_back(0, at, bounds, q, k, v, ga_own, ga_got, *rest)
+
+    slabs = [jnp.where(pair == r, dv0[:, :256], dv0[:, 256:]) for r in range(2)]
+    came = [
+        move(slabs[r], lambda y, x, c, t, r=r: (y, x, t % 2, 2 * c + ((t // 2) ^ r))) for r in range(2)
+    ]
+    dq1, dk1, dv1 = attend_back(1, at, bounds, q, k, v, ga_own, ga_got, *rest, held)
+    dv1, came = lax.optimization_barrier((dv1, came))
 
     first_back, pieces, got, own_heads, got_heads, grad_tokens, got_tokens, gains = tail(
-        dq, dk, dv, small, normed_one, row, grad_hidden, kept[1], got1, kept[3], got2, gain_attn[None], gain_two
+        (dq0, dk0, dv0, dq1, dk1, dv1), small, normed_one, row, grad_hidden, kept[1], got1, kept[3], got2, gain_attn[None], gain_two
     )
     shape = (SEQ // 2, wide)
     grad_gate, grad_up, grad_down, grad_out, gq, gk, gv, grad_tokens, grad_first, layer_out = finish(
-        at, pieces, got, own_heads, got_heads, grad_tokens.reshape(shape), got_tokens.reshape(shape), first_back.reshape(2 * SEQ, 256), out, moved_out, w_gate.shape[1]
+        at, pieces, got, own_heads, got_heads, grad_tokens.reshape(shape), got_tokens.reshape(shape), first_back, (*came, *slabs), out, moved_out, w_gate.shape[1]
     )
     return (
         layer_out,

time: 476 us -> 481 us (1.011)
  waiting for transfers between devices: 16.5 us -> 3.84 us
  starting transfers between devices: 13.5 us -> 25.5 us
    ppermute x7 -> x9, waiting for transfers between devices: 16.5 us -> 3.84 us  [move(): return lax.ppermute(values, AXES, pairs)]
    ppermute x7 -> x9, starting transfers between devices: 13.5 us -> 25.5 us  [move(): return lax.ppermute(values, AXES, pairs)]
    pallas_call x1, Pallas kernels: 25 us -> 29.9 us  [attend(): pl.pallas_call(attend_kernel, out_shape=[jax.ShapeDtypeStruct((SEQ // 2,...]
    pallas_call x2 -> x3, Pallas kernels: 172 us -> 173 us  [the longest x1 118 us: tail(): pl.pallas_call(tail_kernel, out_shape=[jax.ShapeDtypeStruct((2, half, 256...]
  transfers between devices with their start and end apart: 7 -> 9, of which waited for: 2 -> 2; matrix products, arithmetic and copies ran while one was open for 1% -> 1% of each run, Pallas kernels for 51% -> 51%
where the time goes in v6:
time: 481 us; the launch traced here: 472 us
  Pallas kernels  434 us (90%)
  starting transfers between devices  25.5 us (5%)
    pallas_call x1, Pallas kernels, gather(): pl.pallas_call(gather_kernel, out_shape=[jax.ShapeDtypeStruct(shape, BF16...  121 us
    pallas_call x1, Pallas kernels, tail(): pl.pallas_call(tail_kernel, out_shape=[jax.ShapeDtypeStruct((2, half, 256...  118 us
    pallas_call x1, Pallas kernels, mlp(): pl.pallas_call(mlp_kernel, out_shape=[tokens(wide), tokens(wide, F32), to...  60 us
    pallas_call x2, Pallas kernels, attend_back(): pl.pallas_call(functools.partial(attend_back_kernel, part=part), out_shap...  55 us
    pallas_call x1, Pallas kernels, weights(): pl.pallas_call(weights_kernel, out_shape=[jax.ShapeDtypeStruct((2, 128, l...  36.4 us
    pallas_call x1, Pallas kernels, attend(): pl.pallas_call(attend_kernel, out_shape=[jax.ShapeDtypeStruct((SEQ // 2,...  29.9 us
    ppermute x9, starting transfers between devices, move(): return lax.ppermute(values, AXES, pairs)  25.5 us
    pallas_call x1, Pallas kernels, finish(): pl.pallas_call(finish_kernel, out_shape=[jax.ShapeDtypeStruct(shape, F32)...  11.8 us
  transfers between devices with their start and end apart: 9, of which 2 were waited for; matrix products, arithmetic and copies ran while one was open for 1% of the time, Pallas kernels for 51%

profile of v6, /device:TPU:11, one launch (start us, length us, event | category | flops | bytes accessed | tf_op | source)
XLA Modules:
  0.0 472.2 jit_solution(11980382387384392147)
XLA Ops:
  0.6 0.7 collective-permute-start
  1.9 0.7 fusion.halves
  2.6 0.6 broadcast_in_dim_tile.3.freqs
  3.2 2.3 pack.1
  5.4 0.7 broadcast_select_fusion.2
  6.8 120.6 %gather.1 = (bf16[2,1024,1024]{2,1,0:T(8,128)(2,1)}, bf16[4,4,1024,256]{3,2,1,0:T(8,128)(2,1)}, bf16[3,8,2,4,352,128]{5,4,3,2,1,0:T(8,128)(2,1)}, bf16[2048,1024...) custom-call(s32[8]{0:T(128)} %copy-done.4, ...), custom_call_target="tpu_custom_call" | custom-call | tf_op jit(solution)/shard_map/gather/pallas_call | solution.py:717
  127.4 10.9 %collective-permute-start.2 = (bf16[1024,1024]{1,0:T(8,128)(2,1)}, bf16[1024,1024]{1,0:T(8,128)(2,1)}, u32[]{:S(2)}, u32[]{:S(2)}) collective-permute-start(bf16[1024,1024]{1,0:T(8,128)(2,1)} %cot_here), channel_id=1, source_target_pairs={{1,4},{3,6},{4,1},{6,3},{9,12},{11,14},{12,9},{14,11},{17,20},{19,... | collective-permute-start | bytes 6291464 | tf_op jit(solution)/shard_map/ppermute | solution.py:309
  138.3 0.6 pad_add_fusion.bounds
  138.9 29.9 %attend.1 = (bf16[1024,512]{1,0:T(8,128)(2,1)}, bf16[1024,512]{1,0:T(8,128)(2,1)}, f32[2,8,1024]{2,1,0:T(8,128)}) custom-call(s32[8]{0:T(128)} %compare_select_fusion.at, s32[16]{0:T(128)} %pad_add_fusion.bounds, bf16[2048,512]{1,0:T(8,128)(2,1)} %get-tuple-element.76.q_ref.q_hbm, bf16[2048,512]{1,0:T(8,128)(2,1)} %get-tuple-element.77.k_ref.k_hbm, ...), custom_call_target="tpu_custom_call" | custom-call | flops 20000000000 | bytes 12000000 | tf_op jit(solution)/shard_map/attend/pallas_call | solution.py:864
  168.8 8.0 %collective-permute-start.1 = (bf16[1024,512]{1,0:T(8,128)(2,1)}, bf16[1024,512]{1,0:T(8,128)(2,1)S(1)}, u32[]{:S(2)}, u32[]{:S(2)}) collective-permute-start(bf16[1024,512]{1,0:T(8,128)(2,1)} %get-tuple-element.80.o_other), channel_id=1, source_target_pairs={{0,4},{1,5},{2,6},{3,7},{4,0},{5,1},{6,2},{7,3},{8,12},{9,13},{10,... | collective-permute-start | bytes 3145736 | tf_op jit(solution)/shard_map/ppermute | solution.py:309
  176.8 2.5 collective-permute-done.1.att_other.other
  179.3 1.0 copy-done.6
  180.3 60.0 %mlp.1 = (bf16[1024,1024]{1,0:T(8,128)(2,1)}, f32[1024,1024]{1,0:T(8,128)}, bf16[1024,1024]{1,0:T(8,128)(2,1)}, bf16[1024,1024]{1,0:T(8,128)(2,1)}, bf16[3,1024,...) custom-call(s32[8]{0:T(128)} %compare_select_fusion.at, ...), custom_call_target="tpu_custom_call" | custom-call | flops 39728447488 | bytes 60000000 | tf_op jit(solution)/shard_map/mlp/pallas_call | solution.py:1146
  240.7 2.0 collective-permute-start.8
  242.7 36.4 %weights.1 = (bf16[2,128,4736]{2,1,0:T(8,128)(2,1)}, bf16[2,128,4736]{2,1,0:T(8,128)(2,1)}, bf16[2,128,4736]{2,1,0:T(8,128)(2,1)}, bf16[2,128,4736]{2,1,0:T(8,128)(2,1)}) custom-call(bf16[1024,1024]{1,0:T(8,128)(2,1)} %get-tuple-element.87.n2, bf16[1024,1024]{1,0:T(8,128)(2,1)} %get-tuple-element.88.g, bf16[1024,1024]{1,0:T(8,128)(2,1)} %get-tuple-element.89.branch, ...), custom_call_target="tpu_custom_call" | custom-call | flops 19864223744 | bytes 50000000 | tf_op jit(solution)/shard_map/weights/pallas_call | solution.py:1288
  279.2 1.3 collective-permute-start.6
  280.7 34.1 %attend_back.2 = (bf16[1024,512]{1,0:T(8,128)(2,1)}, bf16[1024,512]{1,0:T(8,128)(2,1)}, bf16[1024,512]{1,0:T(8,128)(2,1)}, f32[4,2,256,256]{3,2,1,0:T(8,128)}) custom-call(s32[8]{0:T(128)} %compare_select_fusion.at, s32[16]{0:T(128)} %pad_add_fusion.bounds, bf16[2048,512]{1,0:T(8,128)(2,1)} %get-tuple-element.76.q_ref.q_hbm, ...), custom_call_target="tpu_custom_call" | custom-call | flops 24999999488 | bytes 12000000 | tf_op jit(solution)/shard_map/attend_back/pallas_call | solution.py:1036
  314.8 1.3 broadcast_select_fusion
  316.1 1.9 collective-permute-start.4
  318.1 20.8 %attend_back.3 = (bf16[1024,512]{1,0:T(8,128)(2,1)}, bf16[1024,512]{1,0:T(8,128)(2,1)}, bf16[1024,512]{1,0:T(8,128)(2,1)}) custom-call(s32[8]{0:T(128)} %compare_select_fusion.at, s32[16]{0:T(128)} %pad_add_fusion.bounds, bf16[2048,512]{1,0:T(8,128)(2,1)} %get-tuple-element.76.q_ref.q_hbm, bf16[2048,512]{1,0:T(8,128)(2,1)} %get-tuple-element.77.k_ref.k_hbm, ...), custom_call_target="tpu_custom_call" | custom-call | flops 24999999488 | bytes 12000000 | tf_op jit(solution)/shard_map/attend_back/pallas_call | solution.py:1036
  339.0 1.3 collective-permute-done.5.came1
  340.3 118.5 %tail.1 = (bf16[2,1024,256]{2,1,0:T(8,128)(2,1)}, bf16[2368,128]{1,0:T(8,128)(2,1)}, bf16[3,2368,128]{2,1,0:T(8,128)(2,1)}, bf16[3,128,256]{2,1,0:T(8,128)(2,1)}...) custom-call(bf16[1024,512]{1,0:T(8,128)(2,1)} %get-tuple-element.100, ...), custom_call_target="tpu_custom_call" | custom-call | tf_op jit(solution)/shard_map/tail/pallas_call | solution.py:1666
  458.8 1.4 fusion.6
  460.3 11.8 %finish.1 = (f32[704,128]{1,0:T(8,128)}, f32[704,128]{1,0:T(8,128)}, f32[704,128]{1,0:T(8,128)}, f32[256,128]{1,0:T(8,128)}, f32[128,256]{1,0:T(8,128)}, /*index...) custom-call(s32[8]{0:T(128)} %compare_select_fusion.at, ...), custom_call_target="tpu_custom_call" | custom-call | flops 1000000 | bytes 18000000 | tf_op jit(solution)/shard_map/finish/pallas_call | solution.py:1367
  (35 shorter events, 1.9 us)
Async XLA Ops:
  0.6 4.8 %collective-permute-start = (s32[2,8]{1,0:T(2,128)}, s32[2,8]{1,0:T(2,128)S(1)}, u32[]{:S(2)}, u32[]{:S(2)}) collective-permute-start(s32[2,8]{1,0:T(2,128)} %param.15), channel_id=1, source_target_pairs={{0,4},{1,5},{2,6},{3,7},{4,0},{5,1},{6,2},{7,3},{8,12},{9,13},{10,... | collective-permute-start | bytes 200 | tf_op jit(solution)/shard_map/ppermute | solution.py:309
  6.3 0.5 copy-start.4
  6.4 121.0 %copy-start.3 = (s32[8,256]{1,0:T(8,128)}, s32[8,256]{1,0:T(8,128)S(1)}, u32[]{:S(2)}) copy-start(s32[8,256]{1,0:T(8,128)S(1)} %reshape.62.starts) | copy-start | bytes 24580
  127.4 51.9 %collective-permute-start.2 = (bf16[1024,1024]{1,0:T(8,128)(2,1)}, bf16[1024,1024]{1,0:T(8,128)(2,1)}, u32[]{:S(2)}, u32[]{:S(2)}) collective-permute-start(bf16[1024,1024]{1,0:T(8,128)(2,1)} %cot_here), channel_id=1, source_target_pairs={{1,4},{3,6},{4,1},{6,3},{9,12},{11,14},{12,9},{14,11},{17,20},{19,... | collective-permute-start | bytes 6291464 | tf_op jit(solution)/shard_map/ppermute | solution.py:309
  168.8 10.5 %collective-permute-start.1 = (bf16[1024,512]{1,0:T(8,128)(2,1)}, bf16[1024,512]{1,0:T(8,128)(2,1)S(1)}, u32[]{:S(2)}, u32[]{:S(2)}) collective-permute-start(bf16[1024,512]{1,0:T(8,128)(2,1)} %get-tuple-element.80.o_other), channel_id=1, source_target_pairs={{0,4},{1,5},{2,6},{3,7},{4,0},{5,1},{6,2},{7,3},{8,12},{9,13},{10,... | collective-permute-start | bytes 3145736 | tf_op jit(solution)/shard_map/ppermute | solution.py:309
  179.3 1.0 copy-start.6
  240.3 38.9 %collective-permute-start.3 = (bf16[1024,512]{1,0:T(8,128)(2,1)}, bf16[1024,512]{1,0:T(8,128)(2,1)S(1)}, u32[]{:S(2)}, u32[]{:S(2)}) collective-permute-start(bf16[1024,512]{1,0:T(8,128)(2,1)} %get-tuple-element.95), channel_id=1, source_target_pairs={{0,4},{1,5},{2,6},{3,7},{4,0},{5,1},{6,2},{7,3},{8,12},{9,13},{10,... | collective-permute-start | bytes 3145736 | tf_op jit(solution)/shard_map/ppermute | solution.py:309
  240.7 219.5 %collective-permute-start.8 = (bf16[1024,1024]{1,0:T(8,128)(2,1)}, bf16[1024,1024]{1,0:T(8,128)(2,1)}, u32[]{:S(2)}, u32[]{:S(2)}) collective-permute-start(bf16[1024,1024]{1,0:T(8,128)(2,1)} %get-tuple-element.124.layer), channel_id=1, source_target_pairs={{1,4},{3,6},{4,1},{6,3},{9,12},{11,14},{12,9},{14,11},{17,20},{19,... | collective-permute-start | bytes 6291464 | tf_op jit(solution)/shard_map/ppermute | solution.py:309
  279.2 1.5 copy-start.5
  279.2 61.2 %collective-permute-start.6 = (bf16[2,128,4736]{2,1,0:T(8,128)(2,1)}, bf16[2,128,4736]{2,1,0:T(8,128)(2,1)}, u32[]{:S(2)}, u32[]{:S(2)}) collective-permute-start(bf16[2,128,4736]{2,1,0:T(8,128)(2,1)} %get-tuple-element.111), channel_id=1, source_target_pairs={{0,8},{1,9},{2,10},{3,11},{4,12},{5,13},{6,14},{7,15},{8,0},{9,1},... | collective-permute-start | bytes 7274504 | tf_op jit(solution)/shard_map/ppermute | solution.py:309
  280.5 59.9 %collective-permute-start.7 = (bf16[2,128,4736]{2,1,0:T(8,128)(2,1)}, bf16[2,128,4736]{2,1,0:T(8,128)(2,1)}, u32[]{:S(2)}, u32[]{:S(2)}) collective-permute-start(bf16[2,128,4736]{2,1,0:T(8,128)(2,1)} %get-tuple-element.113), channel_id=1, source_target_pairs={{0,16},{1,17},{2,18},{3,19},{4,20},{5,21},{6,22},{7,23},{8,24},{9,... | collective-permute-start | bytes 7274504 | tf_op jit(solution)/shard_map/ppermute | solution.py:309
  316.1 22.9 %copy-start = (bf16[1024,256]{1,0:T(8,128)(2,1)}, bf16[1024,256]{1,0:T(8,128)(2,1)S(1)}, u32[]{:S(2)}) copy-start(bf16[1024,256]{1,0:T(8,128)(2,1)S(1)} %get-tuple-element.136.slab1) | copy-start | bytes 1572868
  316.1 22.9 %copy-start.1 = (bf16[1024,256]{1,0:T(8,128)(2,1)}, bf16[1024,256]{1,0:T(8,128)(2,1)S(1)}, u32[]{:S(2)}) copy-start(bf16[1024,256]{1,0:T(8,128)(2,1)S(1)} %get-tuple-element.137.slab0) | copy-start | bytes 1572868
  316.1 22.9 %collective-permute-start.4 = (bf16[1024,256]{1,0:T(8,128)(2,1)S(1)}, bf16[1024,256]{1,0:T(8,128)(2,1)S(1)}, u32[]{:S(2)}, u32[]{:S(2)}) collective-permute-start(bf16[1024,256]{1,0:T(8,128)(2,1)S(1)} %get-tuple-element.137.slab0), channel_id=1, source_target_pairs={{1,4},{2,1},{3,5},{4,2},{5,6},{6,3},{9,12},{10,9},{11,13},{12,10},... | collective-permute-start | bytes 1572872 | tf_op jit(solution)/shard_map/ppermute | solution.py:309
  318.0 22.3 %collective-permute-start.5 = (bf16[1024,256]{1,0:T(8,128)(2,1)S(1)}, bf16[1024,256]{1,0:T(8,128)(2,1)}, u32[]{:S(2)}, u32[]{:S(2)}) collective-permute-start(bf16[1024,256]{1,0:T(8,128)(2,1)S(1)} %get-tuple-element.136.slab1), channel_id=1, source_target_pairs={{0,1},{1,5},{2,0},{3,4},{4,3},{5,7},{6,2},{7,6},{8,9},{9,13},{10,8... | collective-permute-start | bytes 1572872 | tf_op jit(solution)/shard_map/ppermute | solution.py:309
  339.0 119.8 %copy-start.2 = (bf16[1024,256]{1,0:T(8,128)(2,1)}, bf16[1024,256]{1,0:T(8,128)(2,1)S(1)}, u32[]{:S(2)}) copy-start(bf16[1024,256]{1,0:T(8,128)(2,1)S(1)} %collective-permute-done.4.came0) | copy-start | bytes 1572868

commit v7 on v6

--- a/solution.py
+++ b/solution.py
@@ -557,8 +557,8 @@
         for item in across[k]:
             item.start()
 
-    for i in range(8):
-        rows = slice(i * TILE, i * TILE + TILE)
+    def table(i, carry):
+        rows = pl.ds(pl.multiple_of(i * TILE, TILE), TILE)
         at_row = lax.broadcasted_iota(jnp.int32, (TILE, 128), 0) + i * TILE
         begin = jnp.zeros_like(at_row)
         for k in range(DOCS):
@@ -566,6 +566,9 @@
         angles = (at_row - begin).astype(F32) * freqs[...]
         cos_s[rows, :] = jnp.cos(angles)
         sin_s[rows, :] = jnp.sin(angles)
+        return carry
+
+    lax.fori_loop(0, SEQ // TILE, table, 0)
     tables = [pltpu.make_async_copy(cos_s, cos_out, end_sem.at[0]), pltpu.make_async_copy(sin_s, sin_out, end_sem.at[1])]
 
     for i, k in enumerate(order):
@@ -638,6 +641,7 @@
             raw_s[rows, u * 256 : u * 256 + 256] = 0.5 * dot(normed, w_s[2, u])
         for item in done_copies(half, n):
             item.start()
+        return 0
 
     row_copy = pltpu.make_async_copy(row, row_out, end_sem.at[3])
 
@@ -649,8 +653,7 @@
             row_copy.start()
 
         half = c + i - 2 * c * i
-        project(half, 0)
-        project(half, 1)
+        lax.fori_loop(0, 2, lambda n, _: project(half, n), 0)
         return carry
 
     lax.fori_loop(0, 2, half_row, 0)
@@ -680,18 +683,22 @@
         def _():
             came.wait_recv()
 
-    outs = []
-    for n in range(4):
-        rows = slice(n * 512, n * 512 + 512)
+    def mixed_copy(n):
+        rows = pl.ds(pl.multiple_of(n * 512, 512), 512)
+        return rows, pltpu.make_async_copy(v_s.at[rows, :], v_out.at[rows, :], tile_sem.at[n, 3])
+
+    def mix(n, carry):
+        rows, item = mixed_copy(n)
         for u in range(2):
             lanes = slice(u * 256, u * 256 + 256)
             v_s[rows, lanes] = (raw_s[rows, lanes] + 0.5 * first[u, rows, :].astype(F32)).astype(BF16)
-        item = pltpu.make_async_copy(v_s.at[rows, :], v_out.at[rows, :], tile_sem.at[n, 3])
         item.start()
-        outs.append(item)
-
+        return carry
+
+    lax.fori_loop(0, 4, mix, 0)
+    outs = []
     for n in range(4):
-        outs += done_copies(n // 2, n % 2)
+        outs += done_copies(n // 2, n % 2) + [mixed_copy(n)[1]]
     given.wait_send()
     for k in range(chunks):
         if k:
@@ -1055,7 +1062,7 @@
 
 def mlp_kernel(at, att_own, att_other, tok, cot_here, cot_moved, gain, wo, big, *rest):
     (out, gh_out, gb_out, n2_out, hid_out, ga_own, ga_other, gg_out, cot_out) = rest[:9]
-    (wg, wu, wd, sems) = rest[9:]
+    (wg, wu, wd, down, back, sems) = rest[9:]
     step = pl.program_id(0)
     c = at[0] & 1
 
@@ -1084,23 +1091,33 @@
         for n, held in enumerate((wg, wu, wd)):
             pltpu.make_async_copy(held, held, sems.at[n]).wait()
 
-    down = jnp.zeros_like(hidden)
-    back = jnp.zeros_like(hidden)
-    units = wg.shape[0]
-    for low in range(0, units, 768):
-        part = slice(low, min(low + 768, units))
-        gate, up, grad_act = dot_nt(normed, wg[part]), dot_nt(normed, wu[part]), dot_nt(g, wd[part])
+    down[...] = hidden
+    back[...] = jnp.zeros_like(back)
+    units, block = wg.shape[0], 768
+
+    def unit_block(low, width):
+        part = pl.ds(low, width)
+        gate, up, grad_act = dot_nt(normed, wg[part, :]), dot_nt(normed, wu[part, :]), dot_nt(g, wd[part, :])
         sig = 1.0 / (1.0 + jnp.exp(-gate))
         silu = gate * sig
         act = (silu * up).astype(BF16)
         grad_up = (grad_act * silu).astype(BF16)
         grad_gate = (grad_act * up * (sig * (1.0 + gate * (1.0 - sig)))).astype(BF16)
         hid_out[0, :, part], hid_out[1, :, part], hid_out[2, :, part] = grad_gate, grad_up, act
-        down += dot(act, wd[part])
-        back += dot(grad_gate, wg[part]) + dot(grad_up, wu[part])
-    out[...] = (hidden + down).astype(BF16)
-    gg_out[...] += jnp.sum((back * hidden * factor).reshape(-1, 8, back.shape[1]), axis=0)
-    scaled = back * gains
+        down[...] += dot(act, wd[part, :])
+        back[...] += dot(grad_gate, wg[part, :]) + dot(grad_up, wu[part, :])
+
+    def whole_block(k, carry):
+        unit_block(pl.multiple_of(k * block, block), block)
+        return carry
+
+    lax.fori_loop(0, units // block, whole_block, 0)
+    if units % block:
+        unit_block(units - units % block, units % block)
+    grad = back[...]
+    out[...] = down[...].astype(BF16)
+    gg_out[...] += jnp.sum((grad * hidden * factor).reshape(-1, 8, grad.shape[1]), axis=0)
+    scaled = grad * gains
     mean = jnp.mean(scaled * hidden, axis=1, keepdims=True)
     grad_hidden = g.astype(F32) + factor * scaled - hidden * (factor * factor * factor * mean)
     gh_out[...] = grad_hidden
@@ -1140,7 +1157,9 @@
             pl.BlockSpec((8, wide), lambda i, at: (0, 0)),
             row(wide),
         ],
-        scratch_shapes=[pltpu.VMEM((units, wide), BF16)] * 3 + [pltpu.SemaphoreType.DMA((3,))],
+        scratch_shapes=[pltpu.VMEM((units, wide), BF16)] * 3
+        + [pltpu.VMEM((rows, wide), F32)] * 2
+        + [pltpu.SemaphoreType.DMA((3,))],
     )
     tokens = lambda width, kind=BF16: jax.ShapeDtypeStruct((count, width), kind)
     return pl.pallas_call(
@@ -1181,57 +1200,68 @@
         send[xr, :, lanes] = done[2 + xr]
 
 
-def weights_kernel(n2, g, branch, hid, own, other, send1, keep1, send2, keep2, turned, given, got, out_sem, in_sem):
+def weights_kernel(
+    n2, g_hbm, branch_hbm, hid, own_hbm, other_hbm, send1_out, keep1_out, send2_out, keep2_out,
+    turned, g, branch, own, other, send1, keep1, send2, keep2, given, got, out_sem, in_sem, load, store,
+):
     step = pl.program_id(0)
     dp, t = lax.axis_index("dp"), lax.axis_index("tensor")
     c = lax.rem(dp, 2)
     plane = lax.div(dp, 2)
     n = lax.rem(step, 4)
     units = hid.shape[2] // 2
+    loads = [
+        pltpu.make_async_copy(src, dst, load.at[m])
+        for m, (src, dst) in enumerate(((g_hbm, g), (branch_hbm, branch), (own_hbm, own), (other_hbm, other)))
+    ]
 
     @pl.when(step == 0)
     def _():
+        for item in loads:
+            item.start()
         barrier = pltpu.get_barrier_semaphore()
         pl.semaphore_signal(barrier, inc=1, device_id=(dp + 1 - 2 * c, t), device_id_type=MESH)
         pl.semaphore_wait(barrier, 1)
 
+    @pl.when(step == 2)
+    def _():
+        for item in loads:
+            item.wait()
+
+    def lanes_of(k):
+        return pl.ds(k * units, units if k < 3 else 512)
+
     def exchange(k):
-        lanes = pl.ds(k * units, units if k < 3 else 512)
         return pltpu.make_async_remote_copy(
-            src_ref=given.at[:, :, :, lanes],
-            dst_ref=got.at[:, :, :, lanes],
+            src_ref=given.at[:, :, :, lanes_of(k)],
+            dst_ref=got.at[:, :, :, lanes_of(k)],
             send_sem=out_sem.at[k],
             recv_sem=in_sem.at[k],
             device_id=(dp + 1 - 2 * c, t),
             device_id_type=MESH,
         )
 
-    for phase, parity in ((0, 1 - c), (1, c)):
-        for at_n, source in ((0, n2), (2, g), (3, branch)):
-
-            @pl.when(step == 4 * phase + at_n)
-            def _():
-                x = lax.rem(plane, 2)
-                y = lax.div(plane, 2)
-                for rel in range(4):
-                    yy, xx = (y, 1 - y)[rel // 2], (x, 1 - x)[rel % 2]
-                    block = pl.multiple_of((yy * 4 + xx * 2 + parity) * 128, 128)
-                    turned[rel * 128 : rel * 128 + 128, :] = source[:, pl.ds(block, 128)].T
-
-    def heads(h):
-        return jnp.where(c == h, own[...], other[...])
-
-    @pl.when(step < 3)
-    def _():
-        for h in range(2):
-            product = dot(turned[...], hid[0, :, h * units : h * units + units]).astype(BF16)
-            given[:, h, :, pl.ds(pl.multiple_of(n * units, 128), units)] = product.reshape(4, 128, units)
-
-    @pl.when(step == 3)
-    def _():
-        for h in range(2):
-            product = dot(turned[...], heads(h)).astype(BF16)
-            given[:, h, :, 3 * units : 3 * units + 512] = product.reshape(4, 128, 512)
+    def stores(k):
+        arrays = ((send1, send1_out), (keep1, keep1_out), (send2, send2_out), (keep2, keep2_out))
+        return [
+            pltpu.make_async_copy(src.at[:, :, lanes_of(k)], dst.at[:, :, lanes_of(k)], store.at[m, k])
+            for m, (src, dst) in enumerate(arrays)
+        ]
+
+    def turn(source, parity):
+        x = lax.rem(plane, 2)
+        y = lax.div(plane, 2)
+        for rel in range(4):
+            yy, xx = (y, 1 - y)[rel // 2], (x, 1 - x)[rel % 2]
+            block = pl.multiple_of((yy * 4 + xx * 2 + parity) * 128, 128)
+            turned[rel * 128 : rel * 128 + 128, :] = source[:, pl.ds(block, 128)].T
+
+    parity = jnp.where(step < 4, 1 - c, c)
+    for at_n, source in ((0, n2), (2, g), (3, branch)):
+
+        @pl.when(n == at_n)
+        def _():
+            turn(source, parity)
 
     for k in range(4):
 
@@ -1243,47 +1273,76 @@
         def _():
             exchange(k).wait_recv()
 
-    def keep(product, h, lanes):
-        done = [(product[r * 128 : r * 128 + 128] + got[r, h, :, lanes].astype(F32)).astype(BF16) for r in range(4)]
-        (place_first, place_second)[h](*((send1, keep1), (send2, keep2))[h], done, lanes)
-
-    @pl.when((step >= 4) & (step < 7))
+        if k < 3:
+
+            @pl.when(step == k + 5)
+            def _():
+                for item in stores(k):
+                    item.start()
+
+    def give_or_keep(product, h, lanes):
+        @pl.when(step < 4)
+        def _():
+            given[:, h, :, lanes] = product.astype(BF16).reshape(4, 128, product.shape[1])
+
+        for e, (place, send, keep) in enumerate(((place_first, send1, keep1), (place_second, send2, keep2))):
+
+            @pl.when((step >= 4) & (h == e))
+            def _():
+                done = [
+                    (product[r * 128 : r * 128 + 128] + got[r, h, :, lanes].astype(F32)).astype(BF16) for r in range(4)
+                ]
+                place(send, keep, done, lanes)
+
+    @pl.when(n < 3)
     def _():
-        for h in range(2):
-            product = dot(turned[...], hid[0, :, h * units : h * units + units])
-            keep(product, h, pl.ds(pl.multiple_of(n * units, 128), units))
+        def one(h, carry):
+            right = hid[0, :, pl.ds(pl.multiple_of(h * units, 128), units)]
+            give_or_keep(dot(turned[...], right), h, pl.ds(pl.multiple_of(n * units, 128), units))
+            return carry
+
+        lax.fori_loop(0, 2, one, 0)
+
+    @pl.when(n == 3)
+    def _():
+        def one(h, carry):
+            right = jnp.where(c == h, own[...], other[...])
+            give_or_keep(dot(turned[...], right), h, lanes_of(3))
+            return carry
+
+        lax.fori_loop(0, 2, one, 0)
 
     @pl.when(step == 7)
     def _():
-        for h in range(2):
-            keep(dot(turned[...], heads(h)), h, pl.ds(3 * units, 512))
+        for item in stores(3):
+            item.start()
         for k in range(4):
             exchange(k).wait_send()
+            for item in stores(k):
+                item.wait()
 
 
 def weights(n2, g, branch, hid, own, other):
     count, wide = n2.shape
     units = hid.shape[2] // 2
-    full = lambda *shape: pl.BlockSpec(shape, lambda s: (0,) * len(shape), pipeline_mode=pl.Buffered(1))
     length = 3 * units + 512
+    low = lambda *shape: pltpu.VMEM(shape, BF16)
+    sems = pltpu.SemaphoreType.DMA
     grid = pl.GridSpec(
         grid=(8,),
         in_specs=[
-            full(count, wide),
-            full(count, wide),
-            full(count, wide),
+            pl.BlockSpec((count, wide), lambda s: (0, 0), pipeline_mode=pl.Buffered(1)),
+            any_spec(),
+            any_spec(),
             pl.BlockSpec((1, count, 2 * units), lambda s: (jnp.minimum(lax.rem(s, 4), 2), 0, 0)),
-            full(count, 512),
-            full(count, 512),
+            any_spec(),
+            any_spec(),
         ],
-        out_specs=[full(2, 128, length)] * 4,
-        scratch_shapes=[
-            pltpu.VMEM((512, count), BF16),
-            pltpu.VMEM((4, 2, 128, length), BF16),
-            pltpu.VMEM((4, 2, 128, length), BF16),
-            pltpu.SemaphoreType.DMA((4,)),
-            pltpu.SemaphoreType.DMA((4,)),
-        ],
+        out_specs=[any_spec()] * 4,
+        scratch_shapes=[low(512, count), low(count, wide), low(count, wide), low(count, 512), low(count, 512)]
+        + [low(2, 128, length)] * 4
+        + [low(4, 2, 128, length)] * 2
+        + [sems((4,)), sems((4,)), sems((4,)), sems((4, 4))],
     )
     return pl.pallas_call(
         weights_kernel,

time: 481 us -> 463 us (0.963); the launches traced: 472 us -> 460 us
  Pallas kernels: 434 us -> 419 us
    pallas_call x2, Pallas kernels: 55 us -> 46.5 us  [attend_back(): pl.pallas_call(functools.partial(attend_back_kernel, part=part), out_shap...]
    pallas_call x1, Pallas kernels: 118 us -> 113 us  [tail(): pl.pallas_call(tail_kernel, out_shape=[jax.ShapeDtypeStruct((2, half, 256...]
    pallas_call x1, Pallas kernels: 29.9 us -> 25 us  [attend(): pl.pallas_call(attend_kernel, out_shape=[jax.ShapeDtypeStruct((SEQ // 2,...]
  transfers between devices with their start and end apart: 9 -> 9, of which waited for: 2 -> 1; matrix products, arithmetic and copies ran while one was open for 1% -> 1% of each run, Pallas kernels for 51% -> 49%
where the time goes in v7:
time: 463 us; the launch traced here: 460 us
  Pallas kernels  419 us (90%)
  starting transfers between devices  30.3 us (7%)
    pallas_call x1, Pallas kernels, gather(): pl.pallas_call(gather_kernel, out_shape=[jax.ShapeDtypeStruct(shape, BF16...  121 us
    pallas_call x1, Pallas kernels, tail(): pl.pallas_call(tail_kernel, out_shape=[jax.ShapeDtypeStruct((2, half, 256...  113 us
    pallas_call x1, Pallas kernels, mlp(): pl.pallas_call(mlp_kernel, out_shape=[tokens(wide), tokens(wide, F32), to...  59.5 us
    pallas_call x2, Pallas kernels, attend_back(): pl.pallas_call(functools.partial(attend_back_kernel, part=part), out_shap...  46.5 us
    pallas_call x1, Pallas kernels, weights(): pl.pallas_call(weights_kernel, out_shape=[jax.ShapeDtypeStruct((2, 128, l...  40 us
    ppermute x9, starting transfers between devices, move(): return lax.ppermute(values, AXES, pairs)  30.3 us
    pallas_call x1, Pallas kernels, attend(): pl.pallas_call(attend_kernel, out_shape=[jax.ShapeDtypeStruct((SEQ // 2,...  25 us
    pallas_call x1, Pallas kernels, finish(): pl.pallas_call(finish_kernel, out_shape=[jax.ShapeDtypeStruct(shape, F32)...  11.8 us
  transfers between devices with their start and end apart: 9, of which 1 were waited for; matrix products, arithmetic and copies ran while one was open for 1% of the time, Pallas kernels for 49%

profile of v7, /device:TPU:11, one launch (start us, length us, event | category | flops | bytes accessed | tf_op | source)
XLA Modules:
  0.0 460.0 jit_solution(14361171566075059326)
XLA Ops:
  0.6 0.7 collective-permute-start
  1.4 0.5 compare_select_fusion.at
  1.9 0.7 fusion.halves
  2.6 0.6 broadcast_in_dim_tile.3.freqs
  3.2 2.3 pack.1
  5.4 0.7 broadcast_select_fusion.2
  6.8 120.6 %gather.1 = (bf16[2,1024,1024]{2,1,0:T(8,128)(2,1)}, bf16[4,4,1024,256]{3,2,1,0:T(8,128)(2,1)}, bf16[3,8,2,4,352,128]{5,4,3,2,1,0:T(8,128)(2,1)}, bf16[2048,1024...) custom-call(s32[8]{0:T(128)} %copy-done.4, ...), custom_call_target="tpu_custom_call" | custom-call | tf_op jit(solution)/shard_map/gather/pallas_call | solution.py:724
  127.4 2.1 collective-permute-start.2
  129.5 0.6 pad_add_fusion.bounds
  130.0 25.0 %attend.1 = (bf16[1024,512]{1,0:T(8,128)(2,1)}, bf16[1024,512]{1,0:T(8,128)(2,1)}, f32[2,8,1024]{2,1,0:T(8,128)}) custom-call(s32[8]{0:T(128)} %compare_select_fusion.at, s32[16]{0:T(128)} %pad_add_fusion.bounds, bf16[2048,512]{1,0:T(8,128)(2,1)} %get-tuple-element.76.q_ref.q_hbm, bf16[2048,512]{1,0:T(8,128)(2,1)} %get-tuple-element.77.k_ref.k_hbm, ...), custom_call_target="tpu_custom_call" | custom-call | flops 20000000000 | bytes 12000000 | tf_op jit(solution)/shard_map/attend/pallas_call | solution.py:871
  155.1 7.9 %collective-permute-start.1 = (bf16[1024,512]{1,0:T(8,128)(2,1)}, bf16[1024,512]{1,0:T(8,128)(2,1)S(1)}, u32[]{:S(2)}, u32[]{:S(2)}) collective-permute-start(bf16[1024,512]{1,0:T(8,128)(2,1)} %get-tuple-element.80.o_other), channel_id=1, source_target_pairs={{0,4},{1,5},{2,6},{3,7},{4,0},{5,1},{6,2},{7,3},{8,12},{9,13},{10,... | collective-permute-start | bytes 3145736 | tf_op jit(solution)/shard_map/ppermute | solution.py:309
  163.0 2.5 collective-permute-done.1.att_other.other_hbm
  165.5 1.0 copy-done.6
  166.4 59.5 %mlp.1 = (bf16[1024,1024]{1,0:T(8,128)(2,1)}, f32[1024,1024]{1,0:T(8,128)}, bf16[1024,1024]{1,0:T(8,128)(2,1)}, bf16[1024,1024]{1,0:T(8,128)(2,1)}, bf16[3,1024,...) custom-call(s32[8]{0:T(128)} %compare_select_fusion.at, ...), custom_call_target="tpu_custom_call" | custom-call | flops 39728447488 | bytes 60000000 | tf_op jit(solution)/shard_map/mlp/pallas_call | solution.py:1165
  226.4 2.0 collective-permute-start.8
  228.3 40.0 %weights.1 = (bf16[2,128,4736]{2,1,0:T(8,128)(2,1)}, bf16[2,128,4736]{2,1,0:T(8,128)(2,1)}, bf16[2,128,4736]{2,1,0:T(8,128)(2,1)}, bf16[2,128,4736]{2,1,0:T(8,128)(2,1)}) custom-call(bf16[1024,1024]{1,0:T(8,128)(2,1)} %get-tuple-element.87.n2, bf16[1024,1024]{1,0:T(8,128)(2,1)} %get-tuple-element.88.g_hbm, bf16[1024,1024]{1,0:T(8,128)(2,1)} %get-tuple-element.89.branch_hbm, ...), custom_call_target="tpu_custom_call" | custom-call | flops 19864223744 | bytes 50000000 | tf_op jit(solution)/shard_map/weights/pallas_call | solution.py:1347
  268.5 1.5 collective-permute-start.7
  269.9 22.5 %attend_back.2 = (bf16[1024,512]{1,0:T(8,128)(2,1)}, bf16[1024,512]{1,0:T(8,128)(2,1)}, bf16[1024,512]{1,0:T(8,128)(2,1)}, f32[4,2,256,256]{3,2,1,0:T(8,128)}) custom-call(s32[8]{0:T(128)} %compare_select_fusion.at, s32[16]{0:T(128)} %pad_add_fusion.bounds, bf16[2048,512]{1,0:T(8,128)(2,1)} %get-tuple-element.76.q_ref.q_hbm, ...), custom_call_target="tpu_custom_call" | custom-call | flops 24999999488 | bytes 12000000 | tf_op jit(solution)/shard_map/attend_back/pallas_call | solution.py:1043
  292.5 1.3 broadcast_select_fusion
  293.8 15.3 %collective-permute-start.4 = (bf16[1024,256]{1,0:T(8,128)(2,1)S(1)}, bf16[1024,256]{1,0:T(8,128)(2,1)S(1)}, u32[]{:S(2)}, u32[]{:S(2)}) collective-permute-start(bf16[1024,256]{1,0:T(8,128)(2,1)S(1)} %get-tuple-element.137.slab0), channel_id=1, source_target_pairs={{1,4},{2,1},{3,5},{4,2},{5,6},{6,3},{9,12},{10,9},{11,13},{12,10},... | collective-permute-start | bytes 1572872 | tf_op jit(solution)/shard_map/ppermute | solution.py:309
  309.5 24.0 %attend_back.3 = (bf16[1024,512]{1,0:T(8,128)(2,1)}, bf16[1024,512]{1,0:T(8,128)(2,1)}, bf16[1024,512]{1,0:T(8,128)(2,1)}) custom-call(s32[8]{0:T(128)} %compare_select_fusion.at, s32[16]{0:T(128)} %pad_add_fusion.bounds, bf16[2048,512]{1,0:T(8,128)(2,1)} %get-tuple-element.76.q_ref.q_hbm, bf16[2048,512]{1,0:T(8,128)(2,1)} %get-tuple-element.77.k_ref.k_hbm, ...), custom_call_target="tpu_custom_call" | custom-call | flops 24999999488 | bytes 12000000 | tf_op jit(solution)/shard_map/attend_back/pallas_call | solution.py:1043
  333.5 113.1 %tail.1 = (bf16[2,1024,256]{2,1,0:T(8,128)(2,1)}, bf16[2368,128]{1,0:T(8,128)(2,1)}, bf16[3,2368,128]{2,1,0:T(8,128)(2,1)}, bf16[3,128,256]{2,1,0:T(8,128)(2,1)}...) custom-call(bf16[1024,512]{1,0:T(8,128)(2,1)} %get-tuple-element.100, ...), custom_call_target="tpu_custom_call" | custom-call | tf_op jit(solution)/shard_map/tail/pallas_call | solution.py:1725
  446.6 1.4 fusion.6
  448.1 11.8 %finish.1 = (f32[704,128]{1,0:T(8,128)}, f32[704,128]{1,0:T(8,128)}, f32[704,128]{1,0:T(8,128)}, f32[256,128]{1,0:T(8,128)}, f32[128,256]{1,0:T(8,128)}, /*index...) custom-call(s32[8]{0:T(128)} %compare_select_fusion.at, ...), custom_call_target="tpu_custom_call" | custom-call | flops 1000000 | bytes 18000000 | tf_op jit(solution)/shard_map/finish/pallas_call | solution.py:1426
  (35 shorter events, 1.5 us)
Async XLA Ops:
  0.6 4.8 %collective-permute-start = (s32[2,8]{1,0:T(2,128)}, s32[2,8]{1,0:T(2,128)S(1)}, u32[]{:S(2)}, u32[]{:S(2)}) collective-permute-start(s32[2,8]{1,0:T(2,128)} %param.15), channel_id=1, source_target_pairs={{0,4},{1,5},{2,6},{3,7},{4,0},{5,1},{6,2},{7,3},{8,12},{9,13},{10,... | collective-permute-start | bytes 200 | tf_op jit(solution)/shard_map/ppermute | solution.py:309
  6.3 0.5 copy-start.4
  6.4 121.0 %copy-start.3 = (s32[8,256]{1,0:T(8,128)}, s32[8,256]{1,0:T(8,128)S(1)}, u32[]{:S(2)}) copy-start(s32[8,256]{1,0:T(8,128)S(1)} %reshape.62.starts) | copy-start | bytes 24580
  127.4 38.1 %collective-permute-start.2 = (bf16[1024,1024]{1,0:T(8,128)(2,1)}, bf16[1024,1024]{1,0:T(8,128)(2,1)}, u32[]{:S(2)}, u32[]{:S(2)}) collective-permute-start(bf16[1024,1024]{1,0:T(8,128)(2,1)} %cot_here), channel_id=1, source_target_pairs={{1,4},{3,6},{4,1},{6,3},{9,12},{11,14},{12,9},{14,11},{17,20},{19,... | collective-permute-start | bytes 6291464 | tf_op jit(solution)/shard_map/ppermute | solution.py:309
  155.1 10.4 %collective-permute-start.1 = (bf16[1024,512]{1,0:T(8,128)(2,1)}, bf16[1024,512]{1,0:T(8,128)(2,1)S(1)}, u32[]{:S(2)}, u32[]{:S(2)}) collective-permute-start(bf16[1024,512]{1,0:T(8,128)(2,1)} %get-tuple-element.80.o_other), channel_id=1, source_target_pairs={{0,4},{1,5},{2,6},{3,7},{4,0},{5,1},{6,2},{7,3},{8,12},{9,13},{10,... | collective-permute-start | bytes 3145736 | tf_op jit(solution)/shard_map/ppermute | solution.py:309
  165.4 1.0 copy-start.6
  225.9 42.4 %collective-permute-start.3 = (bf16[1024,512]{1,0:T(8,128)(2,1)}, bf16[1024,512]{1,0:T(8,128)(2,1)S(1)}, u32[]{:S(2)}, u32[]{:S(2)}) collective-permute-start(bf16[1024,512]{1,0:T(8,128)(2,1)} %get-tuple-element.95), channel_id=1, source_target_pairs={{0,4},{1,5},{2,6},{3,7},{4,0},{5,1},{6,2},{7,3},{8,12},{9,13},{10,... | collective-permute-start | bytes 3145736 | tf_op jit(solution)/shard_map/ppermute | solution.py:309
  226.4 221.7 %collective-permute-start.8 = (bf16[1024,1024]{1,0:T(8,128)(2,1)}, bf16[1024,1024]{1,0:T(8,128)(2,1)}, u32[]{:S(2)}, u32[]{:S(2)}) collective-permute-start(bf16[1024,1024]{1,0:T(8,128)(2,1)} %get-tuple-element.124.layer), channel_id=1, source_target_pairs={{1,4},{3,6},{4,1},{6,3},{9,12},{11,14},{12,9},{14,11},{17,20},{19,... | collective-permute-start | bytes 6291464 | tf_op jit(solution)/shard_map/ppermute | solution.py:309
  268.4 1.6 copy-start.5
  268.4 65.1 %collective-permute-start.6 = (bf16[2,128,4736]{2,1,0:T(8,128)(2,1)}, bf16[2,128,4736]{2,1,0:T(8,128)(2,1)}, u32[]{:S(2)}, u32[]{:S(2)}) collective-permute-start(bf16[2,128,4736]{2,1,0:T(8,128)(2,1)} %get-tuple-element.111), channel_id=1, source_target_pairs={{0,8},{1,9},{2,10},{3,11},{4,12},{5,13},{6,14},{7,15},{8,0},{9,1},... | collective-permute-start | bytes 7274504 | tf_op jit(solution)/shard_map/ppermute | solution.py:309
  268.5 65.1 %collective-permute-start.7 = (bf16[2,128,4736]{2,1,0:T(8,128)(2,1)}, bf16[2,128,4736]{2,1,0:T(8,128)(2,1)}, u32[]{:S(2)}, u32[]{:S(2)}) collective-permute-start(bf16[2,128,4736]{2,1,0:T(8,128)(2,1)} %get-tuple-element.113), channel_id=1, source_target_pairs={{0,16},{1,17},{2,18},{3,19},{4,20},{5,21},{6,22},{7,23},{8,24},{9,... | collective-permute-start | bytes 7274504 | tf_op jit(solution)/shard_map/ppermute | solution.py:309
  293.7 39.7 %copy-start = (bf16[1024,256]{1,0:T(8,128)(2,1)}, bf16[1024,256]{1,0:T(8,128)(2,1)S(1)}, u32[]{:S(2)}) copy-start(bf16[1024,256]{1,0:T(8,128)(2,1)S(1)} %get-tuple-element.136.slab1) | copy-start | bytes 1572868
  293.8 39.7 %copy-start.1 = (bf16[1024,256]{1,0:T(8,128)(2,1)}, bf16[1024,256]{1,0:T(8,128)(2,1)S(1)}, u32[]{:S(2)}) copy-start(bf16[1024,256]{1,0:T(8,128)(2,1)S(1)} %get-tuple-element.137.slab0) | copy-start | bytes 1572868
  293.8 39.7 %collective-permute-start.4 = (bf16[1024,256]{1,0:T(8,128)(2,1)S(1)}, bf16[1024,256]{1,0:T(8,128)(2,1)S(1)}, u32[]{:S(2)}, u32[]{:S(2)}) collective-permute-start(bf16[1024,256]{1,0:T(8,128)(2,1)S(1)} %get-tuple-element.137.slab0), channel_id=1, source_target_pairs={{1,4},{2,1},{3,5},{4,2},{5,6},{6,3},{9,12},{10,9},{11,13},{12,10},... | collective-permute-start | bytes 1572872 | tf_op jit(solution)/shard_map/ppermute | solution.py:309
  309.1 24.4 %collective-permute-start.5 = (bf16[1024,256]{1,0:T(8,128)(2,1)S(1)}, bf16[1024,256]{1,0:T(8,128)(2,1)}, u32[]{:S(2)}, u32[]{:S(2)}) collective-permute-start(bf16[1024,256]{1,0:T(8,128)(2,1)S(1)} %get-tuple-element.136.slab1), channel_id=1, source_target_pairs={{0,1},{1,5},{2,0},{3,4},{4,3},{5,7},{6,2},{7,6},{8,9},{9,13},{10,8... | collective-permute-start | bytes 1572872 | tf_op jit(solution)/shard_map/ppermute | solution.py:309
  333.5 113.1 %copy-start.2 = (bf16[1024,256]{1,0:T(8,128)(2,1)}, bf16[1024,256]{1,0:T(8,128)(2,1)S(1)}, u32[]{:S(2)}) copy-start(bf16[1024,256]{1,0:T(8,128)(2,1)S(1)} %collective-permute-done.4.came0) | copy-start | bytes 1572868

commit v8 on v7

--- a/solution.py
+++ b/solution.py
@@ -1082,9 +1082,9 @@
     factor = lax.rsqrt(jnp.mean(hidden * hidden, axis=1, keepdims=True) + EPSILON)
     gains = gain[...]
     normed = (hidden * factor * gains).astype(BF16)
-    n2_out[...] = normed
+    n2_out[...] = normed.T
     g = jnp.where((at[1] & 1) == c, cot_here[...], cot_moved[...])
-    cot_out[...] = g
+    cot_out[...] = g.T
 
     @pl.when(step == 0)
     def _():
@@ -1122,7 +1122,7 @@
     grad_hidden = g.astype(F32) + factor * scaled - hidden * (factor * factor * factor * mean)
     gh_out[...] = grad_hidden
     branch = grad_hidden.astype(BF16)
-    gb_out[...] = branch
+    gb_out[...] = branch.T
     for e, ga in enumerate((ga_own, ga_other)):
         for u in range(2):
             ga[:, u * 256 : u * 256 + 256] = dot(branch, wo[0, 2 * (c ^ e) + u]).astype(BF16)
@@ -1133,6 +1133,7 @@
     big = big.reshape(3, 8, -1, 128)
     rows, units = 256, big.shape[2]
     row = lambda width: pl.BlockSpec((rows, width), lambda i, at: (i, 0))
+    turned = pl.BlockSpec((wide, rows), lambda i, at: (0, i))
     grid = pltpu.PrefetchScalarGridSpec(
         num_scalar_prefetch=1,
         grid=(count // rows,),
@@ -1149,13 +1150,13 @@
         out_specs=[
             row(wide),
             row(wide),
-            row(wide),
-            row(wide),
+            turned,
+            turned,
             pl.BlockSpec((3, rows, units), lambda i, at: (0, i, 0)),
             row(512),
             row(512),
             pl.BlockSpec((8, wide), lambda i, at: (0, 0)),
-            row(wide),
+            turned,
         ],
         scratch_shapes=[pltpu.VMEM((units, wide), BF16)] * 3
         + [pltpu.VMEM((rows, wide), F32)] * 2
@@ -1167,13 +1168,13 @@
         out_shape=[
             tokens(wide),
             tokens(wide, F32),
-            tokens(wide),
-            tokens(wide),
+            jax.ShapeDtypeStruct((wide, count), BF16),
+            jax.ShapeDtypeStruct((wide, count), BF16),
             jax.ShapeDtypeStruct((3, count, units), BF16),
             tokens(512),
             tokens(512),
             jax.ShapeDtypeStruct((8, wide), F32),
-            tokens(wide),
+            jax.ShapeDtypeStruct((wide, count), BF16),
         ],
         grid_spec=grid,
         compiler_params=params(),
@@ -1208,7 +1209,6 @@
     dp, t = lax.axis_index("dp"), lax.axis_index("tensor")
     c = lax.rem(dp, 2)
     plane = lax.div(dp, 2)
-    n = lax.rem(step, 4)
     units = hid.shape[2] // 2
     loads = [
         pltpu.make_async_copy(src, dst, load.at[m])
@@ -1248,20 +1248,39 @@
             for m, (src, dst) in enumerate(arrays)
         ]
 
-    def turn(source, parity):
+    def turn(source):
         x = lax.rem(plane, 2)
         y = lax.div(plane, 2)
-        for rel in range(4):
-            yy, xx = (y, 1 - y)[rel // 2], (x, 1 - x)[rel % 2]
-            block = pl.multiple_of((yy * 4 + xx * 2 + parity) * 128, 128)
-            turned[rel * 128 : rel * 128 + 128, :] = source[:, pl.ds(block, 128)].T
-
-    parity = jnp.where(step < 4, 1 - c, c)
-    for at_n, source in ((0, n2), (2, g), (3, branch)):
-
-        @pl.when(n == at_n)
+        for e, parity in enumerate((1 - c, c)):
+            for rel in range(4):
+                yy, xx = (y, 1 - y)[rel // 2], (x, 1 - x)[rel % 2]
+                block = pl.multiple_of((yy * 4 + xx * 2 + parity) * 128, 128)
+                low = e * 512 + rel * 128
+                turned[low : low + 128, :] = source[pl.ds(block, 128), :]
+
+    for at_step, source in ((0, n2), (2, g), (3, branch)):
+
+        @pl.when(step == at_step)
         def _():
-            turn(source, parity)
+            turn(source)
+
+    places = ((place_first, send1, keep1), (place_second, send2, keep2))
+
+    def take(product, h, lanes):
+        rows = product.astype(BF16)
+        given[:, h, :, lanes] = rows[:512].reshape(4, 128, rows.shape[1])
+        for e, (place, send, keep) in enumerate(places):
+
+            @pl.when(h == e)
+            def _():
+                place(send, keep, [rows[512 + r * 128 : 640 + r * 128] for r in range(4)], lanes)
+
+    def add_got(lanes):
+        for yr in range(2):
+            keep1[yr, :, lanes] = add(keep1[yr, :, lanes], got[2 * yr, 0, :, lanes])
+            send1[yr, :, lanes] = add(send1[yr, :, lanes], got[2 * yr + 1, 0, :, lanes])
+            keep2[yr, :, lanes] = add(keep2[yr, :, lanes], got[yr, 1, :, lanes])
+            send2[yr, :, lanes] = add(send2[yr, :, lanes], got[2 + yr, 1, :, lanes])
 
     for k in range(4):
 
@@ -1269,53 +1288,34 @@
         def _():
             exchange(k).start()
 
-        @pl.when(step == k + 4)
-        def _():
-            exchange(k).wait_recv()
-
-        if k < 3:
-
-            @pl.when(step == k + 5)
-            def _():
-                for item in stores(k):
-                    item.start()
-
-    def give_or_keep(product, h, lanes):
-        @pl.when(step < 4)
-        def _():
-            given[:, h, :, lanes] = product.astype(BF16).reshape(4, 128, product.shape[1])
-
-        for e, (place, send, keep) in enumerate(((place_first, send1, keep1), (place_second, send2, keep2))):
-
-            @pl.when((step >= 4) & (h == e))
-            def _():
-                done = [
-                    (product[r * 128 : r * 128 + 128] + got[r, h, :, lanes].astype(F32)).astype(BF16) for r in range(4)
-                ]
-                place(send, keep, done, lanes)
-
-    @pl.when(n < 3)
+    @pl.when(step < 3)
     def _():
         def one(h, carry):
             right = hid[0, :, pl.ds(pl.multiple_of(h * units, 128), units)]
-            give_or_keep(dot(turned[...], right), h, pl.ds(pl.multiple_of(n * units, 128), units))
+            take(dot(turned[...], right), h, pl.ds(pl.multiple_of(step * units, 128), units))
             return carry
 
         lax.fori_loop(0, 2, one, 0)
 
-    @pl.when(n == 3)
+    @pl.when(step == 3)
     def _():
         def one(h, carry):
-            right = jnp.where(c == h, own[...], other[...])
-            give_or_keep(dot(turned[...], right), h, lanes_of(3))
+            take(dot(turned[...], jnp.where(c == h, own[...], other[...])), h, lanes_of(3))
             return carry
 
         lax.fori_loop(0, 2, one, 0)
 
-    @pl.when(step == 7)
+    for k in range(4):
+
+        @pl.when(step == k + 2)
+        def _():
+            exchange(k).wait_recv()
+            add_got(lanes_of(k))
+            for item in stores(k):
+                item.start()
+
+    @pl.when(step == 5)
     def _():
-        for item in stores(3):
-            item.start()
         for k in range(4):
             exchange(k).wait_send()
             for item in stores(k):
@@ -1323,23 +1323,23 @@
 
 
 def weights(n2, g, branch, hid, own, other):
-    count, wide = n2.shape
+    wide, count = n2.shape
     units = hid.shape[2] // 2
     length = 3 * units + 512
     low = lambda *shape: pltpu.VMEM(shape, BF16)
     sems = pltpu.SemaphoreType.DMA
     grid = pl.GridSpec(
-        grid=(8,),
+        grid=(6,),
         in_specs=[
-            pl.BlockSpec((count, wide), lambda s: (0, 0), pipeline_mode=pl.Buffered(1)),
+            pl.BlockSpec((wide, count), lambda s: (0, 0), pipeline_mode=pl.Buffered(1)),
             any_spec(),
             any_spec(),
-            pl.BlockSpec((1, count, 2 * units), lambda s: (jnp.minimum(lax.rem(s, 4), 2), 0, 0)),
+            pl.BlockSpec((1, count, 2 * units), lambda s: (jnp.minimum(s, 2), 0, 0)),
             any_spec(),
             any_spec(),
         ],
         out_specs=[any_spec()] * 4,
-        scratch_shapes=[low(512, count), low(count, wide), low(count, wide), low(count, 512), low(count, 512)]
+        scratch_shapes=[low(wide, count), low(wide, count), low(wide, count), low(count, 512), low(count, 512)]
         + [low(2, 128, length)] * 4
         + [low(4, 2, 128, length)] * 2
         + [sems((4,)), sems((4,)), sems((4,)), sems((4, 4))],
@@ -1359,15 +1359,19 @@
 
 
 def finish_kernel(at, own, got, own_heads, got_heads, tok, got_tok, first, came0, came1, slab0, slab1, layer, got_layer, gate, up, down, out, query, key, value, tok_out, first_out, layer_out):
-    @pl.when(pl.program_id(0) == 0)
-    def _():
-        part = down.shape[0]
-        for n, ref in enumerate((gate, up, down, out)):
+    part = down.shape[0]
+    for n, ref in enumerate((gate, up, down, out)):
+
+        @pl.when(pl.program_id(0) == n)
+        def _():
             rows = slice(n * part, n * part + ref.shape[0])
             total = own[rows, :].astype(F32)
             for d in range(3):
                 total += got[d, rows, :].astype(F32)
             ref[...] = total
+
+    @pl.when(pl.program_id(0) == 3)
+    def _():
         heads = own_heads[...].astype(F32)
         for d in range(3):
             heads += got_heads[d].astype(F32)

time: 463 us -> 462 us (level)
  starting transfers between devices: 30.3 us -> 15.7 us
  Pallas kernels: 419 us -> 431 us
    ppermute x9, starting transfers between devices: 30.3 us -> 15.7 us  [move(): return lax.ppermute(values, AXES, pairs)]
    pallas_call x2, Pallas kernels: 46.5 us -> 54.8 us  [attend_back(): pl.pallas_call(functools.partial(attend_back_kernel, part=part), out_shap...]
    pallas_call x1, Pallas kernels: 113 us -> 119 us  [tail(): pl.pallas_call(tail_kernel, out_shape=[jax.ShapeDtypeStruct((2, half, 256...]
    pallas_call x1, Pallas kernels: 40 us -> 34.2 us  [weights(): pl.pallas_call(weights_kernel, out_shape=[jax.ShapeDtypeStruct((2, 128, l...]
    pallas_call x1, Pallas kernels: 25 us -> 29.9 us  [attend(): pl.pallas_call(attend_kernel, out_shape=[jax.ShapeDtypeStruct((SEQ // 2,...]
  transfers between devices with their start and end apart: 9 -> 9, of which waited for: 1 -> 2; matrix products, arithmetic and copies ran while one was open for 1% -> 1% of each run, Pallas kernels for 49% -> 52%
where the time goes in v8:
time: 462 us; the launch traced here: 459 us
  Pallas kernels  431 us (93%)
  starting transfers between devices  15.7 us (3%)
    pallas_call x1, Pallas kernels, gather(): pl.pallas_call(gather_kernel, out_shape=[jax.ShapeDtypeStruct(shape, BF16...  121 us
    pallas_call x1, Pallas kernels, tail(): pl.pallas_call(tail_kernel, out_shape=[jax.ShapeDtypeStruct((2, half, 256...  119 us
    pallas_call x1, Pallas kernels, mlp(): pl.pallas_call(mlp_kernel, out_shape=[tokens(wide), tokens(wide, F32), ja...  59.4 us
    pallas_call x2, Pallas kernels, attend_back(): pl.pallas_call(functools.partial(attend_back_kernel, part=part), out_shap...  54.8 us
    pallas_call x1, Pallas kernels, weights(): pl.pallas_call(weights_kernel, out_shape=[jax.ShapeDtypeStruct((2, 128, l...  34.2 us
    pallas_call x1, Pallas kernels, attend(): pl.pallas_call(attend_kernel, out_shape=[jax.ShapeDtypeStruct((SEQ // 2,...  29.9 us
    ppermute x9, starting transfers between devices, move(): return lax.ppermute(values, AXES, pairs)  15.7 us
    pallas_call x1, Pallas kernels, finish(): pl.pallas_call(finish_kernel, out_shape=[jax.ShapeDtypeStruct(shape, F32)...  11.3 us
  transfers between devices with their start and end apart: 9, of which 2 were waited for; matrix products, arithmetic and copies ran while one was open for 1% of the time, Pallas kernels for 52%

profile of v8, /device:TPU:11, one launch (start us, length us, event | category | flops | bytes accessed | tf_op | source)
XLA Modules:
  0.0 459.3 jit_solution(17494557834777872500)
XLA Ops:
  0.6 0.7 collective-permute-start
  1.9 0.7 fusion.halves
  2.6 0.6 broadcast_in_dim_tile.3.freqs
  3.2 2.3 pack.1
  5.4 0.7 broadcast_select_fusion.2
  6.8 120.6 %gather.1 = (bf16[2,1024,1024]{2,1,0:T(8,128)(2,1)}, bf16[4,4,1024,256]{3,2,1,0:T(8,128)(2,1)}, bf16[3,8,2,4,352,128]{5,4,3,2,1,0:T(8,128)(2,1)}, bf16[2048,1024...) custom-call(s32[8]{0:T(128)} %copy-done.4, ...), custom_call_target="tpu_custom_call" | custom-call | tf_op jit(solution)/shard_map/gather/pallas_call | solution.py:724
  127.4 2.1 collective-permute-start.2
  129.5 0.6 pad_add_fusion.bounds
  130.0 29.9 %attend.1 = (bf16[1024,512]{1,0:T(8,128)(2,1)}, bf16[1024,512]{1,0:T(8,128)(2,1)}, f32[2,8,1024]{2,1,0:T(8,128)}) custom-call(s32[8]{0:T(128)} %compare_select_fusion.at, s32[16]{0:T(128)} %pad_add_fusion.bounds, bf16[2048,512]{1,0:T(8,128)(2,1)} %get-tuple-element.76.q_ref.q_hbm, bf16[2048,512]{1,0:T(8,128)(2,1)} %get-tuple-element.77.k_ref.k_hbm, ...), custom_call_target="tpu_custom_call" | custom-call | flops 20000000000 | bytes 12000000 | tf_op jit(solution)/shard_map/attend/pallas_call | solution.py:871
  160.0 7.9 %collective-permute-start.1 = (bf16[1024,512]{1,0:T(8,128)(2,1)}, bf16[1024,512]{1,0:T(8,128)(2,1)S(1)}, u32[]{:S(2)}, u32[]{:S(2)}) collective-permute-start(bf16[1024,512]{1,0:T(8,128)(2,1)} %get-tuple-element.80.o_other), channel_id=1, source_target_pairs={{0,4},{1,5},{2,6},{3,7},{4,0},{5,1},{6,2},{7,3},{8,12},{9,13},{10,... | collective-permute-start | bytes 3145736 | tf_op jit(solution)/shard_map/ppermute | solution.py:309
  167.9 2.5 collective-permute-done.1.att_other.other_hbm
  170.4 1.0 copy-done.6
  171.3 59.4 %mlp.1 = (bf16[1024,1024]{1,0:T(8,128)(2,1)}, f32[1024,1024]{1,0:T(8,128)}, bf16[1024,1024]{1,0:T(8,128)(2,1)}, bf16[1024,1024]{1,0:T(8,128)(2,1)}, bf16[3,1024,...) custom-call(s32[8]{0:T(128)} %compare_select_fusion.at, ...), custom_call_target="tpu_custom_call" | custom-call | flops 39728447488 | bytes 60000000 | tf_op jit(solution)/shard_map/mlp/pallas_call | solution.py:1166
  231.2 2.0 collective-permute-start.8
  233.2 34.2 %weights.1 = (bf16[2,128,4736]{2,1,0:T(8,128)(2,1)}, bf16[2,128,4736]{2,1,0:T(8,128)(2,1)}, bf16[2,128,4736]{2,1,0:T(8,128)(2,1)}, bf16[2,128,4736]{2,1,0:T(8,128)(2,1)}) custom-call(bf16[1024,1024]{1,0:T(8,128)(2,1)} %get-tuple-element.87.n2, bf16[1024,1024]{1,0:T(8,128)(2,1)} %get-tuple-element.88.g_hbm, bf16[1024,1024]{1,0:T(8,128)(2,1)} %get-tuple-element.89.branch_hbm, ...), custom_call_target="tpu_custom_call" | custom-call | flops 19864223744 | bytes 50000000 | tf_op jit(solution)/shard_map/weights/pallas_call | solution.py:1347
  267.8 0.5 copy-done.5
  268.3 34.1 %attend_back.2 = (bf16[1024,512]{1,0:T(8,128)(2,1)}, bf16[1024,512]{1,0:T(8,128)(2,1)}, bf16[1024,512]{1,0:T(8,128)(2,1)}, f32[4,2,256,256]{3,2,1,0:T(8,128)}) custom-call(s32[8]{0:T(128)} %compare_select_fusion.at, s32[16]{0:T(128)} %pad_add_fusion.bounds, bf16[2048,512]{1,0:T(8,128)(2,1)} %get-tuple-element.76.q_ref.q_hbm, ...), custom_call_target="tpu_custom_call" | custom-call | flops 24999999488 | bytes 12000000 | tf_op jit(solution)/shard_map/attend_back/pallas_call | solution.py:1043
  302.5 1.3 broadcast_select_fusion
  303.8 1.9 collective-permute-start.4
  306.0 20.7 %attend_back.3 = (bf16[1024,512]{1,0:T(8,128)(2,1)}, bf16[1024,512]{1,0:T(8,128)(2,1)}, bf16[1024,512]{1,0:T(8,128)(2,1)}) custom-call(s32[8]{0:T(128)} %compare_select_fusion.at, s32[16]{0:T(128)} %pad_add_fusion.bounds, bf16[2048,512]{1,0:T(8,128)(2,1)} %get-tuple-element.76.q_ref.q_hbm, bf16[2048,512]{1,0:T(8,128)(2,1)} %get-tuple-element.77.k_ref.k_hbm, ...), custom_call_target="tpu_custom_call" | custom-call | flops 24999999488 | bytes 12000000 | tf_op jit(solution)/shard_map/attend_back/pallas_call | solution.py:1043
  326.8 0.7 collective-permute-done.5.came1
  327.4 118.9 %tail.1 = (bf16[2,1024,256]{2,1,0:T(8,128)(2,1)}, bf16[2368,128]{1,0:T(8,128)(2,1)}, bf16[3,2368,128]{2,1,0:T(8,128)(2,1)}, bf16[3,128,256]{2,1,0:T(8,128)(2,1)}...) custom-call(bf16[1024,512]{1,0:T(8,128)(2,1)} %get-tuple-element.100, ...), custom_call_target="tpu_custom_call" | custom-call | tf_op jit(solution)/shard_map/tail/pallas_call | solution.py:1729
  446.4 1.4 fusion.6
  447.8 11.3 %finish.1 = (f32[704,128]{1,0:T(8,128)}, f32[704,128]{1,0:T(8,128)}, f32[704,128]{1,0:T(8,128)}, f32[256,128]{1,0:T(8,128)}, f32[128,256]{1,0:T(8,128)}, /*index...) custom-call(s32[8]{0:T(128)} %compare_select_fusion.at, ...), custom_call_target="tpu_custom_call" | custom-call | flops 1000000 | bytes 18000000 | tf_op jit(solution)/shard_map/finish/pallas_call | solution.py:1430
  (35 shorter events, 2.3 us)
Async XLA Ops:
  0.6 4.8 %collective-permute-start = (s32[2,8]{1,0:T(2,128)}, s32[2,8]{1,0:T(2,128)S(1)}, u32[]{:S(2)}, u32[]{:S(2)}) collective-permute-start(s32[2,8]{1,0:T(2,128)} %param.15), channel_id=1, source_target_pairs={{0,4},{1,5},{2,6},{3,7},{4,0},{5,1},{6,2},{7,3},{8,12},{9,13},{10,... | collective-permute-start | bytes 200 | tf_op jit(solution)/shard_map/ppermute | solution.py:309
  6.3 0.5 copy-start.4
  6.4 121.0 %copy-start.3 = (s32[8,256]{1,0:T(8,128)}, s32[8,256]{1,0:T(8,128)S(1)}, u32[]{:S(2)}) copy-start(s32[8,256]{1,0:T(8,128)S(1)} %reshape.62.starts) | copy-start | bytes 24580
  127.4 43.0 %collective-permute-start.2 = (bf16[1024,1024]{1,0:T(8,128)(2,1)}, bf16[1024,1024]{1,0:T(8,128)(2,1)}, u32[]{:S(2)}, u32[]{:S(2)}) collective-permute-start(bf16[1024,1024]{1,0:T(8,128)(2,1)} %cot_here), channel_id=1, source_target_pairs={{1,4},{3,6},{4,1},{6,3},{9,12},{11,14},{12,9},{14,11},{17,20},{19,... | collective-permute-start | bytes 6291464 | tf_op jit(solution)/shard_map/ppermute | solution.py:309
  160.0 10.4 %collective-permute-start.1 = (bf16[1024,512]{1,0:T(8,128)(2,1)}, bf16[1024,512]{1,0:T(8,128)(2,1)S(1)}, u32[]{:S(2)}, u32[]{:S(2)}) collective-permute-start(bf16[1024,512]{1,0:T(8,128)(2,1)} %get-tuple-element.80.o_other), channel_id=1, source_target_pairs={{0,4},{1,5},{2,6},{3,7},{4,0},{5,1},{6,2},{7,3},{8,12},{9,13},{10,... | collective-permute-start | bytes 3145736 | tf_op jit(solution)/shard_map/ppermute | solution.py:309
  170.4 1.0 copy-start.6
  230.8 36.6 %collective-permute-start.3 = (bf16[1024,512]{1,0:T(8,128)(2,1)}, bf16[1024,512]{1,0:T(8,128)(2,1)S(1)}, u32[]{:S(2)}, u32[]{:S(2)}) collective-permute-start(bf16[1024,512]{1,0:T(8,128)(2,1)} %get-tuple-element.95), channel_id=1, source_target_pairs={{0,4},{1,5},{2,6},{3,7},{4,0},{5,1},{6,2},{7,3},{8,12},{9,13},{10,... | collective-permute-start | bytes 3145736 | tf_op jit(solution)/shard_map/ppermute | solution.py:309
  231.2 216.6 %collective-permute-start.8 = (bf16[1024,1024]{1,0:T(8,128)(2,1)}, bf16[1024,1024]{1,0:T(8,128)(2,1)}, u32[]{:S(2)}, u32[]{:S(2)}) collective-permute-start(bf16[1024,1024]{1,0:T(8,128)(2,1)} %get-tuple-element.124.layer), channel_id=1, source_target_pairs={{1,4},{3,6},{4,1},{6,3},{9,12},{11,14},{12,9},{14,11},{17,20},{19,... | collective-permute-start | bytes 6291464 | tf_op jit(solution)/shard_map/ppermute | solution.py:309
  267.4 1.0 copy-start.5
  267.4 60.0 %collective-permute-start.6 = (bf16[2,128,4736]{2,1,0:T(8,128)(2,1)}, bf16[2,128,4736]{2,1,0:T(8,128)(2,1)}, u32[]{:S(2)}, u32[]{:S(2)}) collective-permute-start(bf16[2,128,4736]{2,1,0:T(8,128)(2,1)} %get-tuple-element.111), channel_id=1, source_target_pairs={{0,8},{1,9},{2,10},{3,11},{4,12},{5,13},{6,14},{7,15},{8,0},{9,1},... | collective-permute-start | bytes 7274504 | tf_op jit(solution)/shard_map/ppermute | solution.py:309
  267.7 59.7 %collective-permute-start.7 = (bf16[2,128,4736]{2,1,0:T(8,128)(2,1)}, bf16[2,128,4736]{2,1,0:T(8,128)(2,1)}, u32[]{:S(2)}, u32[]{:S(2)}) collective-permute-start(bf16[2,128,4736]{2,1,0:T(8,128)(2,1)} %get-tuple-element.113), channel_id=1, source_target_pairs={{0,16},{1,17},{2,18},{3,19},{4,20},{5,21},{6,22},{7,23},{8,24},{9,... | collective-permute-start | bytes 7274504 | tf_op jit(solution)/shard_map/ppermute | solution.py:309
  303.7 23.0 %copy-start = (bf16[1024,256]{1,0:T(8,128)(2,1)}, bf16[1024,256]{1,0:T(8,128)(2,1)S(1)}, u32[]{:S(2)}) copy-start(bf16[1024,256]{1,0:T(8,128)(2,1)S(1)} %get-tuple-element.136.slab1) | copy-start | bytes 1572868
  303.8 23.0 %copy-start.1 = (bf16[1024,256]{1,0:T(8,128)(2,1)}, bf16[1024,256]{1,0:T(8,128)(2,1)S(1)}, u32[]{:S(2)}) copy-start(bf16[1024,256]{1,0:T(8,128)(2,1)S(1)} %get-tuple-element.137.slab0) | copy-start | bytes 1572868
  303.8 23.0 %collective-permute-start.4 = (bf16[1024,256]{1,0:T(8,128)(2,1)S(1)}, bf16[1024,256]{1,0:T(8,128)(2,1)S(1)}, u32[]{:S(2)}, u32[]{:S(2)}) collective-permute-start(bf16[1024,256]{1,0:T(8,128)(2,1)S(1)} %get-tuple-element.137.slab0), channel_id=1, source_target_pairs={{1,4},{2,1},{3,5},{4,2},{5,6},{6,3},{9,12},{10,9},{11,13},{12,10},... | collective-permute-start | bytes 1572872 | tf_op jit(solution)/shard_map/ppermute | solution.py:309
  305.7 21.7 %collective-permute-start.5 = (bf16[1024,256]{1,0:T(8,128)(2,1)S(1)}, bf16[1024,256]{1,0:T(8,128)(2,1)}, u32[]{:S(2)}, u32[]{:S(2)}) collective-permute-start(bf16[1024,256]{1,0:T(8,128)(2,1)S(1)} %get-tuple-element.136.slab1), channel_id=1, source_target_pairs={{0,1},{1,5},{2,0},{3,4},{4,3},{5,7},{6,2},{7,6},{8,9},{9,13},{10,8... | collective-permute-start | bytes 1572872 | tf_op jit(solution)/shard_map/ppermute | solution.py:309
  326.8 119.6 %copy-start.2 = (bf16[1024,256]{1,0:T(8,128)(2,1)}, bf16[1024,256]{1,0:T(8,128)(2,1)S(1)}, u32[]{:S(2)}) copy-start(bf16[1024,256]{1,0:T(8,128)(2,1)S(1)} %collective-permute-done.4.came0) | copy-start | bytes 1572868

commit v9 on v8

--- a/solution.py
+++ b/solution.py
@@ -1803,7 +1803,6 @@
         move(slabs[r], lambda y, x, c, t, r=r: (y, x, t % 2, 2 * c + ((t // 2) ^ r))) for r in range(2)
     ]
     dq1, dk1, dv1 = attend_back(1, at, bounds, q, k, v, ga_own, ga_got, *rest, held)
-    dv1, came = lax.optimization_barrier((dv1, came))
 
     first_back, pieces, got, own_heads, got_heads, grad_tokens, got_tokens, gains = tail(
         (dq0, dk0, dv0, dq1, dk1, dv1), small, normed_one, row, grad_hidden, kept[1], got1, kept[3], got2, gain_attn[None], gain_two

time: 462 us -> 461 us (level)
  starting transfers between devices: 15.7 us -> 26.8 us
  Pallas kernels: 431 us -> 421 us
    ppermute x9, starting transfers between devices: 15.7 us -> 26.8 us  [move(): return lax.ppermute(values, AXES, pairs)]
    pallas_call x2, Pallas kernels: 54.8 us -> 46.5 us  [attend_back(): pl.pallas_call(functools.partial(attend_back_kernel, part=part), out_shap...]
    pallas_call x1, Pallas kernels: 29.9 us -> 25 us  [attend(): pl.pallas_call(attend_kernel, out_shape=[jax.ShapeDtypeStruct((SEQ // 2,...]
  transfers between devices with their start and end apart: 9 -> 9, of which waited for: 2 -> 1; matrix products, arithmetic and copies ran while one was open for 1% -> 1% of each run, Pallas kernels for 52% -> 50%
where the time goes in v9:
time: 461 us; the launch traced here: 459 us
  Pallas kernels  421 us (91%)
  starting transfers between devices  26.8 us (6%)
    pallas_call x1, Pallas kernels, tail(): pl.pallas_call(tail_kernel, out_shape=[jax.ShapeDtypeStruct((2, half, 256...  122 us
    pallas_call x1, Pallas kernels, gather(): pl.pallas_call(gather_kernel, out_shape=[jax.ShapeDtypeStruct(shape, BF16...  121 us
    pallas_call x1, Pallas kernels, mlp(): pl.pallas_call(mlp_kernel, out_shape=[tokens(wide), tokens(wide, F32), ja...  59.4 us
    pallas_call x2, Pallas kernels, attend_back(): pl.pallas_call(functools.partial(attend_back_kernel, part=part), out_shap...  46.5 us
    pallas_call x1, Pallas kernels, weights(): pl.pallas_call(weights_kernel, out_shape=[jax.ShapeDtypeStruct((2, 128, l...  34.2 us
    ppermute x9, starting transfers between devices, move(): return lax.ppermute(values, AXES, pairs)  26.8 us
    pallas_call x1, Pallas kernels, attend(): pl.pallas_call(attend_kernel, out_shape=[jax.ShapeDtypeStruct((SEQ // 2,...  25 us
    pallas_call x1, Pallas kernels, finish(): pl.pallas_call(finish_kernel, out_shape=[jax.ShapeDtypeStruct(shape, F32)...  11.3 us
  transfers between devices with their start and end apart: 9, of which 1 were waited for; matrix products, arithmetic and copies ran while one was open for 1% of the time, Pallas kernels for 50%

profile of v9, /device:TPU:11, one launch (start us, length us, event | category | flops | bytes accessed | tf_op | source)
XLA Modules:
  0.0 459.4 jit_solution(6230756666906260223)
XLA Ops:
  0.6 0.7 collective-permute-start
  1.9 0.7 fusion.halves
  2.6 0.6 broadcast_in_dim_tile.3.freqs
  3.2 2.3 pack.1
  5.4 0.7 broadcast_select_fusion.2
  6.8 120.6 %gather.1 = (bf16[2,1024,1024]{2,1,0:T(8,128)(2,1)}, bf16[4,4,1024,256]{3,2,1,0:T(8,128)(2,1)}, bf16[3,8,2,4,352,128]{5,4,3,2,1,0:T(8,128)(2,1)}, bf16[2048,1024...) custom-call(s32[8]{0:T(128)} %copy-done.4, ...), custom_call_target="tpu_custom_call" | custom-call | tf_op jit(solution)/shard_map/gather/pallas_call | solution.py:724
  127.4 2.1 collective-permute-start.2
  130.0 25.0 %attend.1 = (bf16[1024,512]{1,0:T(8,128)(2,1)}, bf16[1024,512]{1,0:T(8,128)(2,1)}, f32[2,8,1024]{2,1,0:T(8,128)}) custom-call(s32[8]{0:T(128)} %compare_select_fusion.at, s32[16]{0:T(128)} %pad_add_fusion.bounds, bf16[2048,512]{1,0:T(8,128)(2,1)} %get-tuple-element.73.q_ref.q_hbm, bf16[2048,512]{1,0:T(8,128)(2,1)} %get-tuple-element.74.k_ref.k_hbm, ...), custom_call_target="tpu_custom_call" | custom-call | flops 20000000000 | bytes 12000000 | tf_op jit(solution)/shard_map/attend/pallas_call | solution.py:871
  155.1 7.9 %collective-permute-start.1 = (bf16[1024,512]{1,0:T(8,128)(2,1)}, bf16[1024,512]{1,0:T(8,128)(2,1)S(1)}, u32[]{:S(2)}, u32[]{:S(2)}) collective-permute-start(bf16[1024,512]{1,0:T(8,128)(2,1)} %get-tuple-element.77.o_other), channel_id=1, source_target_pairs={{0,4},{1,5},{2,6},{3,7},{4,0},{5,1},{6,2},{7,3},{8,12},{9,13},{10,... | collective-permute-start | bytes 3145736 | tf_op jit(solution)/shard_map/ppermute | solution.py:309
  163.0 2.5 collective-permute-done.1.att_other.other_hbm
  165.5 1.0 copy-done.6
  166.4 59.4 %mlp.1 = (bf16[1024,1024]{1,0:T(8,128)(2,1)}, f32[1024,1024]{1,0:T(8,128)}, bf16[1024,1024]{1,0:T(8,128)(2,1)}, bf16[1024,1024]{1,0:T(8,128)(2,1)}, bf16[3,1024,...) custom-call(s32[8]{0:T(128)} %compare_select_fusion.at, ...), custom_call_target="tpu_custom_call" | custom-call | flops 39728447488 | bytes 60000000 | tf_op jit(solution)/shard_map/mlp/pallas_call | solution.py:1166
  226.3 2.0 collective-permute-start.8
  228.3 34.2 %weights.1 = (bf16[2,128,4736]{2,1,0:T(8,128)(2,1)}, bf16[2,128,4736]{2,1,0:T(8,128)(2,1)}, bf16[2,128,4736]{2,1,0:T(8,128)(2,1)}, bf16[2,128,4736]{2,1,0:T(8,128)(2,1)}) custom-call(bf16[1024,1024]{1,0:T(8,128)(2,1)} %get-tuple-element.84.n2, bf16[1024,1024]{1,0:T(8,128)(2,1)} %get-tuple-element.85.g_hbm, bf16[1024,1024]{1,0:T(8,128)(2,1)} %get-tuple-element.86.branch_hbm, ...), custom_call_target="tpu_custom_call" | custom-call | flops 19864223744 | bytes 50000000 | tf_op jit(solution)/shard_map/weights/pallas_call | solution.py:1347
  262.5 5.2 %collective-permute-start.4 = (bf16[2,128,4736]{2,1,0:T(8,128)(2,1)}, bf16[2,128,4736]{2,1,0:T(8,128)(2,1)}, u32[]{:S(2)}, u32[]{:S(2)}) collective-permute-start(bf16[2,128,4736]{2,1,0:T(8,128)(2,1)} %get-tuple-element.107), channel_id=1, source_target_pairs={{0,8},{1,9},{2,10},{3,11},{4,12},{5,13},{6,14},{7,15},{8,0},{9,1},... | collective-permute-start | bytes 7274504 | tf_op jit(solution)/shard_map/ppermute | solution.py:309
  267.9 27.5 %attend_back.2 = (bf16[1024,512]{1,0:T(8,128)(2,1)}, bf16[1024,512]{1,0:T(8,128)(2,1)}, bf16[1024,512]{1,0:T(8,128)(2,1)}, f32[4,2,256,256]{3,2,1,0:T(8,128)}) custom-call(s32[8]{0:T(128)} %compare_select_fusion.at, s32[16]{0:T(128)} %pad_add_fusion.bounds, bf16[2048,512]{1,0:T(8,128)(2,1)} %get-tuple-element.73.q_ref.q_hbm, ...), custom_call_target="tpu_custom_call" | custom-call | flops 24999999488 | bytes 12000000 | tf_op jit(solution)/shard_map/attend_back/pallas_call | solution.py:1043
  295.4 1.3 broadcast_select_fusion
  296.7 4.7 %collective-permute-start.6 = (bf16[1024,256]{1,0:T(8,128)(2,1)S(1)}, bf16[1024,256]{1,0:T(8,128)(2,1)S(1)}, u32[]{:S(2)}, u32[]{:S(2)}) collective-permute-start(bf16[1024,256]{1,0:T(8,128)(2,1)S(1)} %get-tuple-element.131.slab0), channel_id=1, source_target_pairs={{1,4},{2,1},{3,5},{4,2},{5,6},{6,3},{9,12},{10,9},{11,13},{12,10},... | collective-permute-start | bytes 1572872 | tf_op jit(solution)/shard_map/ppermute | solution.py:309
  301.5 3.6 collective-permute-start.7
  305.0 19.0 %attend_back.3 = (bf16[1024,512]{1,0:T(8,128)(2,1)}, bf16[1024,512]{1,0:T(8,128)(2,1)}, bf16[1024,512]{1,0:T(8,128)(2,1)}) custom-call(s32[8]{0:T(128)} %compare_select_fusion.at, s32[16]{0:T(128)} %pad_add_fusion.bounds, bf16[2048,512]{1,0:T(8,128)(2,1)} %get-tuple-element.73.q_ref.q_hbm, bf16[2048,512]{1,0:T(8,128)(2,1)} %get-tuple-element.74.k_ref.k_hbm, ...), custom_call_target="tpu_custom_call" | custom-call | flops 24999999488 | bytes 12000000 | tf_op jit(solution)/shard_map/attend_back/pallas_call | solution.py:1043
  324.1 121.5 %tail.1 = (bf16[2,1024,256]{2,1,0:T(8,128)(2,1)}, bf16[2368,128]{1,0:T(8,128)(2,1)}, bf16[3,2368,128]{2,1,0:T(8,128)(2,1)}, bf16[3,128,256]{2,1,0:T(8,128)(2,1)}...) custom-call(bf16[1024,512]{1,0:T(8,128)(2,1)} %get-tuple-element.97., ...), custom_call_target="tpu_custom_call" | custom-call | tf_op jit(solution)/shard_map/tail/pallas_call | solution.py:1729
  445.6 1.4 fusion.6
  447.1 0.8 copy-done.2
  447.9 11.3 %finish.1 = (f32[704,128]{1,0:T(8,128)}, f32[704,128]{1,0:T(8,128)}, f32[704,128]{1,0:T(8,128)}, f32[256,128]{1,0:T(8,128)}, f32[128,256]{1,0:T(8,128)}, /*index...) custom-call(s32[8]{0:T(128)} %compare_select_fusion.at, ...), custom_call_target="tpu_custom_call" | custom-call | flops 1000000 | bytes 18000000 | tf_op jit(solution)/shard_map/finish/pallas_call | solution.py:1430
  (35 shorter events, 2.4 us)
Async XLA Ops:
  0.6 4.8 %collective-permute-start = (s32[2,8]{1,0:T(2,128)}, s32[2,8]{1,0:T(2,128)S(1)}, u32[]{:S(2)}, u32[]{:S(2)}) collective-permute-start(s32[2,8]{1,0:T(2,128)} %param.15), channel_id=1, source_target_pairs={{0,4},{1,5},{2,6},{3,7},{4,0},{5,1},{6,2},{7,3},{8,12},{9,13},{10,... | collective-permute-start | bytes 200 | tf_op jit(solution)/shard_map/ppermute | solution.py:309
  6.3 0.5 copy-start.4
  6.4 121.0 %copy-start.3 = (s32[8,256]{1,0:T(8,128)}, s32[8,256]{1,0:T(8,128)S(1)}, u32[]{:S(2)}) copy-start(s32[8,256]{1,0:T(8,128)S(1)} %reshape.62.starts) | copy-start | bytes 24580
  127.4 38.1 %collective-permute-start.2 = (bf16[1024,1024]{1,0:T(8,128)(2,1)}, bf16[1024,1024]{1,0:T(8,128)(2,1)}, u32[]{:S(2)}, u32[]{:S(2)}) collective-permute-start(bf16[1024,1024]{1,0:T(8,128)(2,1)} %cot_here), channel_id=1, source_target_pairs={{1,4},{3,6},{4,1},{6,3},{9,12},{11,14},{12,9},{14,11},{17,20},{19,... | collective-permute-start | bytes 6291464 | tf_op jit(solution)/shard_map/ppermute | solution.py:309
  155.1 10.4 %collective-permute-start.1 = (bf16[1024,512]{1,0:T(8,128)(2,1)}, bf16[1024,512]{1,0:T(8,128)(2,1)S(1)}, u32[]{:S(2)}, u32[]{:S(2)}) collective-permute-start(bf16[1024,512]{1,0:T(8,128)(2,1)} %get-tuple-element.77.o_other), channel_id=1, source_target_pairs={{0,4},{1,5},{2,6},{3,7},{4,0},{5,1},{6,2},{7,3},{8,12},{9,13},{10,... | collective-permute-start | bytes 3145736 | tf_op jit(solution)/shard_map/ppermute | solution.py:309
  165.4 1.0 copy-start.6
  225.9 36.6 %collective-permute-start.3 = (bf16[1024,512]{1,0:T(8,128)(2,1)}, bf16[1024,512]{1,0:T(8,128)(2,1)S(1)}, u32[]{:S(2)}, u32[]{:S(2)}) collective-permute-start(bf16[1024,512]{1,0:T(8,128)(2,1)} %get-tuple-element.92), channel_id=1, source_target_pairs={{0,4},{1,5},{2,6},{3,7},{4,0},{5,1},{6,2},{7,3},{8,12},{9,13},{10,... | collective-permute-start | bytes 3145736 | tf_op jit(solution)/shard_map/ppermute | solution.py:309
  226.3 220.8 %collective-permute-start.8 = (bf16[1024,1024]{1,0:T(8,128)(2,1)}, bf16[1024,1024]{1,0:T(8,128)(2,1)}, u32[]{:S(2)}, u32[]{:S(2)}) collective-permute-start(bf16[1024,1024]{1,0:T(8,128)(2,1)} %get-tuple-element.118.layer), channel_id=1, source_target_pairs={{1,4},{3,6},{4,1},{6,3},{9,12},{11,14},{12,9},{14,11},{17,20},{19,... | collective-permute-start | bytes 6291464 | tf_op jit(solution)/shard_map/ppermute | solution.py:309
  262.5 5.5 %copy-start.5 = (bf16[1024,512]{1,0:T(8,128)(2,1)}, bf16[1024,512]{1,0:T(8,128)(2,1)S(1)}, u32[]{:S(2)}) copy-start(bf16[1024,512]{1,0:T(8,128)(2,1)S(1)} %collective-permute-done.3.do_other) | copy-start | bytes 3145732
  262.5 61.6 %collective-permute-start.4 = (bf16[2,128,4736]{2,1,0:T(8,128)(2,1)}, bf16[2,128,4736]{2,1,0:T(8,128)(2,1)}, u32[]{:S(2)}, u32[]{:S(2)}) collective-permute-start(bf16[2,128,4736]{2,1,0:T(8,128)(2,1)} %get-tuple-element.107), channel_id=1, source_target_pairs={{0,8},{1,9},{2,10},{3,11},{4,12},{5,13},{6,14},{7,15},{8,0},{9,1},... | collective-permute-start | bytes 7274504 | tf_op jit(solution)/shard_map/ppermute | solution.py:309
  267.7 56.4 %collective-permute-start.5 = (bf16[2,128,4736]{2,1,0:T(8,128)(2,1)}, bf16[2,128,4736]{2,1,0:T(8,128)(2,1)}, u32[]{:S(2)}, u32[]{:S(2)}) collective-permute-start(bf16[2,128,4736]{2,1,0:T(8,128)(2,1)} %get-tuple-element.109), channel_id=1, source_target_pairs={{0,16},{1,17},{2,18},{3,19},{4,20},{5,21},{6,22},{7,23},{8,24},{9,... | collective-permute-start | bytes 7274504 | tf_op jit(solution)/shard_map/ppermute | solution.py:309
  296.7 27.3 %copy-start = (bf16[1024,256]{1,0:T(8,128)(2,1)}, bf16[1024,256]{1,0:T(8,128)(2,1)S(1)}, u32[]{:S(2)}) copy-start(bf16[1024,256]{1,0:T(8,128)(2,1)S(1)} %get-tuple-element.130.slab1) | copy-start | bytes 1572868
  296.7 27.3 %copy-start.1 = (bf16[1024,256]{1,0:T(8,128)(2,1)}, bf16[1024,256]{1,0:T(8,128)(2,1)S(1)}, u32[]{:S(2)}) copy-start(bf16[1024,256]{1,0:T(8,128)(2,1)S(1)} %get-tuple-element.131.slab0) | copy-start | bytes 1572868
  296.7 150.3 %collective-permute-start.6 = (bf16[1024,256]{1,0:T(8,128)(2,1)S(1)}, bf16[1024,256]{1,0:T(8,128)(2,1)S(1)}, u32[]{:S(2)}, u32[]{:S(2)}) collective-permute-start(bf16[1024,256]{1,0:T(8,128)(2,1)S(1)} %get-tuple-element.131.slab0), channel_id=1, source_target_pairs={{1,4},{2,1},{3,5},{4,2},{5,6},{6,3},{9,12},{10,9},{11,13},{12,10},... | collective-permute-start | bytes 1572872 | tf_op jit(solution)/shard_map/ppermute | solution.py:309
  301.5 145.6 %collective-permute-start.7 = (bf16[1024,256]{1,0:T(8,128)(2,1)S(1)}, bf16[1024,256]{1,0:T(8,128)(2,1)}, u32[]{:S(2)}, u32[]{:S(2)}) collective-permute-start(bf16[1024,256]{1,0:T(8,128)(2,1)S(1)} %get-tuple-element.130.slab1), channel_id=1, source_target_pairs={{0,1},{1,5},{2,0},{3,4},{4,3},{5,7},{6,2},{7,6},{8,9},{9,13},{10,8... | collective-permute-start | bytes 1572872 | tf_op jit(solution)/shard_map/ppermute | solution.py:309
  447.1 0.8 copy-start.2
